TPU v7x, 512 devices: a whole 4x4x16 slice. The times are simulated.
512 devices in a mesh: dp: 32 (over z, x_hi), txt: 16 (over y, x_lo, core).
Axes of the slice: x: 4 (x_hi: 2, x_lo: 2; x = x_hi * 2 + x_lo), y: 4, z: 16, core: 2. Of those that a mesh axis runs over, the one named last changes fastest.
Arguments:
- resid: bfloat16 [8192, 1024], P('dp', 'txt'), may hold values from -40 to 40
- prenorm_gain: float32 [1024], replicated, may hold values from 0.25 to 1.75
- prenorm_bias: float32 [1024], replicated, may hold values from -3 to 3
- up_weight: bfloat16 [1024, 4096], P('dp', 'txt'), may hold values from -0.1875 to 0.1875
- up_bias: float32 [4096], P('txt'), may hold values from -3 to 3
- down_weight: bfloat16 [4096, 1024], P('txt', 'dp'), may hold values from -0.09375 to 0.09375
- down_bias: float32 [1024], replicated, may hold values from -3 to 3
- post_gain: float32 [1024], P('txt'), may hold values from 0.25 to 1.75
- post_bias: float32 [1024], P('txt'), may hold values from -3 to 3
- projection: bfloat16 [1024, 768], P('txt'), may hold values from -1 to 1
- texts: bfloat16 [20480, 768], P('txt'), may hold values from -48 to 48
- labels: int32 [8192], P('dp'), may hold values from 0 to 20479
- step_size: float32 [1], replicated, may hold values from 0.5 to 2
Outputs:
- adversarial: float32 [8192, 1024], P('dp', 'txt')
All inputs are finite; a program needn't handle non-finite values.
Results may differ from a plain program's by a relative error of at most 0.0036.
Values may be sent and summed in bfloat16 or wider, within the bound.
No kernel may reach another device: no remote copies, remote signals or barrier semaphores. Data moves between devices by JAX's collectives and lax.ppermute only.
A program may use at most 64 MiB of HBM per device.

v0:
```python
import jax
import jax.numpy as jnp
from jax import lax
from jax.sharding import PartitionSpec as P

MODEL_WIDTH = 1024


def sent_to_all(x, axis):
    copies = jnp.broadcast_to(x, (lax.axis_size(axis), *x.shape))
    return lax.all_to_all(copies, axis, split_axis=0, concat_axis=0, tiled=True)


def joined_along(tiles, dim):
    tiles = jnp.moveaxis(tiles, 0, dim)
    lengths = tiles.shape
    return tiles.reshape(*lengths[:dim], lengths[dim] * lengths[dim + 1], *lengths[dim + 2 :])


def gathered_copies(x, axis, dim):
    tiles = sent_to_all(x, axis)
    return joined_along(tiles, dim)


def in_blocks(x, dim, size):
    lengths = x.shape
    tiles = x.reshape(*lengths[:dim], size, lengths[dim] // size, *lengths[dim + 1 :])
    return jnp.moveaxis(tiles, dim, 0)


def summed_on_arrival(x, axis, dim):
    size = lax.axis_size(axis)
    tiles = lax.all_to_all(in_blocks(x, dim, size), axis, 0, 0, tiled=True)
    return jnp.sum(tiles, axis=0)


def over_copies(x, axis):
    everything = sent_to_all(x, axis)
    return jnp.sum(everything, axis=0)


def packed_total(arrays, axis):
    ends = [0]
    for a in arrays:
        ends.append(ends[-1] + a.size)
    subtotal = over_copies(jnp.concatenate([a.ravel() for a in arrays]), axis)
    return tuple((subtotal[b:e].reshape(a.shape) for a, b, e in zip(arrays, ends, ends[1:])))


def gathered_once(x, axis):
    leaves = jax.tree.leaves(x)
    order = sorted(range(len(leaves)), key=lambda k: -leaves[k].size)
    width = (1, *leaves[order[0]].shape)[-1]
    lines = [
        jnp.pad(leaves[k].reshape(-1), (0, -leaves[k].size % width)).reshape(-1, width)
        for k in order
    ]
    both, at, found = (sent_to_all(jnp.concatenate(lines), axis), 0, {})
    for k, line in zip(order, lines):
        share = both[:, at : at + len(line)].reshape(len(both), -1)
        found[k] = share[:, : leaves[k].size].reshape(-1, *leaves[k].shape)
        at += len(line)
    numbers = iter(range(len(leaves)))
    return jax.tree.map(lambda _: found[next(numbers)], x)


def combined_pairwise(pieces, combine):
    while len(jax.tree.leaves(pieces)[0]) > 1:
        pieces = jax.vmap(combine)(
            *(jax.tree.map(lambda part: part[side::2], pieces) for side in (0, 1))
        )
    return jax.tree.map(lambda part: part[0], pieces)


def combined_all(x, axis, combine):
    pieces = gathered_once(x, axis)
    return combined_pairwise(pieces, combine)


def merge_softmax(first, second):
    top_val = jnp.maximum(first[0], second[0])
    return (
        top_val,
        first[1] * jnp.exp(first[0] - top_val) + second[1] * jnp.exp(second[0] - top_val),
    )


def local(
    resid,
    prenorm_gain,
    prenorm_bias,
    up_weight,
    up_bias,
    down_weight,
    down_bias,
    post_gain,
    post_bias,
    projection,
    texts,
    labels,
    step_size,
):
    feature_width = resid.shape[1]
    shift_amount = lax.axis_index("txt") * feature_width
    gathered = gathered_copies(resid, "txt", 1)
    input_rows = gathered.astype(jnp.float32)
    input_mean = jnp.mean(input_rows, axis=1, keepdims=True)
    var_in = jnp.mean(input_rows * input_rows, axis=1, keepdims=True) - input_mean * input_mean
    input_inverse_deviation = lax.rsqrt(var_in + 1e-05)
    centered_input = (input_rows - input_mean) * input_inverse_deviation
    normed_input = (centered_input * prenorm_gain + prenorm_bias).astype(jnp.bfloat16)
    w_up = gathered_copies(up_weight, "dp", 0)
    w_down = gathered_copies(down_weight, "dp", 1)
    pre_act = jnp.dot(normed_input, w_up, preferred_element_type=jnp.float32) + up_bias
    gate_sig = jax.nn.sigmoid(1.702 * pre_act)
    hidden = (pre_act * gate_sig).astype(jnp.bfloat16)
    mixed_part = jnp.dot(hidden, w_down, preferred_element_type=jnp.float32)
    mixed = summed_on_arrival(mixed_part, "txt", 1)
    own_rows = resid.astype(jnp.float32)
    block_out = own_rows + mixed + lax.dynamic_slice_in_dim(down_bias, shift_amount, feature_width)
    out_sums = packed_total(
        (jnp.sum(block_out, axis=1), jnp.sum(block_out * block_out, axis=1)), "txt"
    )
    mean_out = out_sums[0][:, None] / MODEL_WIDTH
    var_out = out_sums[1][:, None] / MODEL_WIDTH - mean_out * mean_out
    rstd_out = lax.rsqrt(var_out + 1e-05)
    yhat = (block_out - mean_out) * rstd_out
    post_normed = (yhat * post_gain + post_bias).astype(jnp.bfloat16)
    emb_part = jnp.dot(post_normed, projection, preferred_element_type=jnp.float32)
    embedding = summed_on_arrival(emb_part, "txt", 0)
    emb_norm = jnp.sqrt(jnp.sum(embedding * embedding, axis=1, keepdims=True) + 1e-06)
    unit_vec = embedding / emb_norm
    unit_low = gathered_copies(unit_vec.astype(jnp.bfloat16), "txt", 0)
    text_f = texts.astype(jnp.float32)
    text_unit = (text_f / jnp.sqrt(jnp.sum(text_f * text_f, axis=1, keepdims=True) + 1e-06)).astype(
        jnp.bfloat16
    )
    logits = 100.0 * jnp.einsum(
        "ie,je->ij", unit_low, text_unit, preferred_element_type=jnp.float32
    )
    local_top = jnp.max(logits, axis=1)
    local_total = jnp.sum(jnp.exp(logits - local_top[:, None]), axis=1)
    row_top, row_total = combined_all((local_top, local_total), "txt", merge_softmax)
    exponent = jnp.exp(logits - row_top[:, None])
    prob = exponent / row_total[:, None]
    local_label = labels - lax.axis_index("txt") * texts.shape[0]
    columns = lax.broadcasted_iota(jnp.int32, logits.shape, 1)
    target = (columns == local_label[:, None]).astype(jnp.float32)
    score_grad = (100.0 * (prob - target)).astype(jnp.bfloat16)
    back_part = jnp.dot(score_grad, text_unit, preferred_element_type=jnp.float32)
    unit_grad = summed_on_arrival(back_part, "txt", 0)
    along = jnp.sum(unit_vec * unit_grad, axis=1, keepdims=True)
    grad_share = ((unit_grad - unit_vec * along) / emb_norm).astype(jnp.bfloat16)
    emb_grad = gathered_copies(grad_share, "txt", 0)
    post_grad = jnp.einsum("ie,de->id", emb_grad, projection, preferred_element_type=jnp.float32)
    scaled = post_grad * post_gain
    back_sums = packed_total((jnp.sum(scaled, axis=1), jnp.sum(scaled * yhat, axis=1)), "txt")
    output_gradient = (
        scaled - back_sums[0][:, None] / MODEL_WIDTH - yhat * (back_sums[1][:, None] / MODEL_WIDTH)
    ) * rstd_out
    out_full = gathered_copies(output_gradient.astype(jnp.bfloat16), "txt", 1)
    hid_grad = jnp.einsum("id,fd->if", out_full, w_down, preferred_element_type=jnp.float32)
    act_grad = (hid_grad * (gate_sig + 1.702 * pre_act * gate_sig * (1.0 - gate_sig))).astype(
        jnp.bfloat16
    )
    normed_part = jnp.einsum("if,df->id", act_grad, w_up, preferred_element_type=jnp.float32)
    normed_gradient = summed_on_arrival(normed_part, "txt", 1)
    centered_input_portion = lax.dynamic_slice_in_dim(
        centered_input, shift_amount, feature_width, 1
    )
    scaled_input = normed_gradient * lax.dynamic_slice_in_dim(
        prenorm_gain, shift_amount, feature_width
    )
    input_row_sums = packed_total(
        (jnp.sum(scaled_input, axis=1), jnp.sum(scaled_input * centered_input_portion, axis=1)),
        "txt",
    )
    input_gradient = (
        output_gradient
        + (
            scaled_input
            - input_row_sums[0][:, None] / MODEL_WIDTH
            - centered_input_portion * (input_row_sums[1][:, None] / MODEL_WIDTH)
        )
        * input_inverse_deviation
    )
    square_sum = over_copies(jnp.sum(input_gradient * input_gradient, axis=1), "txt")
    grad_rms = jnp.sqrt(square_sum[:, None] / MODEL_WIDTH + 1e-06)
    return own_rows + step_size[0] * input_gradient / grad_rms


def solution(mesh):
    placed = (
        P("dp", "txt"),
        P(),
        P(),
        P("dp", "txt"),
        P("txt"),
        P("txt", "dp"),
        P(),
        P("txt"),
        P("txt"),
        P("txt", None),
        P("txt", None),
        P("dp"),
        P(),
    )
    return jax.shard_map(
        local, mesh=mesh, in_specs=placed, out_specs=P("dp", "txt"), check_vma=False
    )
```

profile of v0, /device:TPU:1, one launch (start us, length us, event | category | flops | bytes accessed | tf_op | source)
XLA Modules:
  0.0 280.2 jit_solution(1755771523890583014)
XLA Ops:
  0.0 0.8 broadcast_in_dim.22
  0.9 19.2 %all_to_all.79 = bf16[16,256,64]{1,2,0:T(8,128)(2,1)S(1)} all-to-all(bf16[16,256,64]{1,2,0:T(8,128)(2,1)S(1)} %broadcast_in_dim.22), channel_id=1, replica_groups=mesh['dp'=32,'txt'=16] {'txt'}, dimensions={0} | all-to-all | bytes 1048576 | tf_op jit(solution)/shard_map/all_to_all | solution.py:11
  20.2 44.9 %all_to_all.80 = bf16[32,32,256]{2,1,0:T(8,128)(2,1)S(1)} all-to-all(bf16[32,32,256]{2,1,0:T(8,128)(2,1)S(1)} %broadcast_in_dim.23), channel_id=1, replica_groups=mesh['dp'=32,'txt'=16] {'dp'}, dimensions={0} | all-to-all | bytes 1048576 | tf_op jit(solution)/shard_map/all_to_all | solution.py:11
  65.1 0.9 broadcast_in_dim.24
  66.0 7.1 %all-to-all-start.2 = ((bf16[32,256,32]{1,2,0:T(8,128)(2,1)}), bf16[32,256,32]{1,2,0:T(8,128)(2,1)S(1)}, u32[]{:S(2)}, u32[]{:S(2)}) async-start(bf16[32,256,32]{1,2,0:T(8,128)(2,1)} %broadcast_in_dim.24), calls=%async_computation.2 | async-start | bytes 1048576 | tf_op jit(solution)/shard_map/all_to_all | solution.py:11
  74.2 29.4 %all-to-all-done.2 = bf16[32,256,32]{1,2,0:T(8,128)(2,1)S(1)} async-done(((bf16[32,256,32]{1,2,0:T(8,128)(2,1)}), bf16[32,256,32]{1,2,0:T(8,128)(2,1)S(1)}, u32[]{:S(2)}, u32[]{:S(2)}) %all-to-all-start.2) | async-done | bytes 524320 | tf_op jit(solution)/shard_map/all_to_all | solution.py:11
  103.6 1.3 convolution_bitcast_fusion.1
  104.9 7.1 %all-to-all-start.3 = ((f32[16,256,64]{1,2,0:T(8,128)}), f32[16,256,64]{1,2,0:T(8,128)S(1)}, u32[]{:S(2)}, u32[]{:S(2)}) async-start(f32[16,256,64]{1,2,0:T(8,128)} %convolution_bitcast_fusion.1), calls=%async_computation.3 | async-start | bytes 2097152 | tf_op jit(solution)/shard_map/all_to_all | solution.py:33
  112.8 15.2 %all-to-all-done.3 = f32[16,256,64]{1,2,0:T(8,128)S(1)} async-done(((f32[16,256,64]{1,2,0:T(8,128)}), f32[16,256,64]{1,2,0:T(8,128)S(1)}, u32[]{:S(2)}, u32[]{:S(2)}) %all-to-all-start.3) | async-done | bytes 1048608 | tf_op jit(solution)/shard_map/all_to_all | solution.py:33
  128.2 9.3 %all_to_all.81 = f32[16,1,512]{2,1,0:T(1,128)S(1)} all-to-all(f32[16,1,512]{2,1,0:T(1,128)S(1)} %broadcast_in_dim.25), channel_id=1, replica_groups=mesh['dp'=32,'txt'=16] {'txt'}, dimensions={0} | all-to-all | bytes 65536 | tf_op jit(solution)/shard_map/all_to_all | solution.py:11
  137.5 1.2 fusion.20
  138.7 3.8 %all-to-all-start.5 = ((f32[16,16,768]{2,1,0:T(8,128)}), f32[16,16,768]{2,1,0:T(8,128)S(1)}, u32[]{:S(2)}, u32[]{:S(2)}) async-start(f32[16,16,768]{2,1,0:T(8,128)} %bitcast.55), calls=%async_computation.5 | async-start | bytes 1572864 | tf_op jit(solution)/shard_map/all_to_all | solution.py:33
  143.0 12.6 %all-to-all-done.5 = f32[16,16,768]{2,1,0:T(8,128)S(1)} async-done(((f32[16,16,768]{2,1,0:T(8,128)}), f32[16,16,768]{2,1,0:T(8,128)S(1)}, u32[]{:S(2)}, u32[]{:S(2)}) %all-to-all-start.5) | async-done | bytes 786464 | tf_op jit(solution)/shard_map/all_to_all | solution.py:33
  155.9 0.8 broadcast_in_dim.26
  156.7 4.2 %all-to-all-start.6 = ((bf16[16,16,768]{2,1,0:T(8,128)(2,1)}), bf16[16,16,768]{2,1,0:T(8,128)(2,1)S(1)}, u32[]{:S(2)}, u32[]{:S(2)}) async-start(bf16[16,16,768]{2,1,0:T(8,128)(2,1)} %broadcast_in_dim.26), calls=%async_computation.6 | async-start | bytes 786432 | tf_op jit(solution)/shard_map/all_to_all | solution.py:11
  160.9 1.7 fusion.1
  162.6 6.7 %all-to-all-done.6 = bf16[16,16,768]{2,1,0:T(8,128)(2,1)S(1)} async-done(((bf16[16,16,768]{2,1,0:T(8,128)(2,1)}), bf16[16,16,768]{2,1,0:T(8,128)(2,1)S(1)}, u32[]{:S(2)}, u32[]{:S(2)}) %all-to-all-start.6) | async-done | bytes 393248 | tf_op jit(solution)/shard_map/all_to_all | solution.py:11
  169.4 2.5 fusion.37
  171.9 1.1 copy-done.3
  173.9 4.5 %all-to-all-start.7 = ((f32[16,2,256]{2,1,0:T(2,128)}), f32[16,2,256]{2,1,0:T(2,128)S(1)}, u32[]{:S(2)}, u32[]{:S(2)}) async-start(f32[16,2,256]{2,1,0:T(2,128)} %broadcast_in_dim.27), calls=%async_computation.7 | async-start | bytes 65536 | tf_op jit(solution)/shard_map/all_to_all | solution.py:11
  178.4 5.8 %all-to-all-done.7 = f32[16,2,256]{2,1,0:T(2,128)S(1)} async-done(((f32[16,2,256]{2,1,0:T(2,128)}), f32[16,2,256]{2,1,0:T(2,128)S(1)}, u32[]{:S(2)}, u32[]{:S(2)}) %all-to-all-start.7) | async-done | bytes 32800 | tf_op jit(solution)/shard_map/all_to_all | solution.py:11
  184.6 2.3 fusion.4
  186.9 15.7 %all_to_all.82 = f32[16,16,768]{2,1,0:T(8,128)S(1)} all-to-all(f32[16,16,768]{2,1,0:T(8,128)S(1)} %bitcast.62), channel_id=1, replica_groups=mesh['dp'=32,'txt'=16] {'txt'}, dimensions={0} | all-to-all | bytes 1572864 | tf_op jit(solution)/shard_map/all_to_all | solution.py:33
  202.9 11.9 %all_to_all.83 = bf16[16,16,768]{2,1,0:T(8,128)(2,1)S(1)} all-to-all(bf16[16,16,768]{2,1,0:T(8,128)(2,1)S(1)} %broadcast_in_dim.28), channel_id=1, replica_groups=mesh['dp'=32,'txt'=16] {'txt'}, dimensions={0} | all-to-all | bytes 786432 | tf_op jit(solution)/shard_map/all_to_all | solution.py:11
  215.2 9.5 %all_to_all.84 = f32[16,1,512]{2,1,0:T(1,128)S(1)} all-to-all(f32[16,1,512]{2,1,0:T(1,128)S(1)} %broadcast_in_dim.29), channel_id=1, replica_groups=mesh['dp'=32,'txt'=16] {'txt'}, dimensions={0} | all-to-all | bytes 65536 | tf_op jit(solution)/shard_map/all_to_all | solution.py:11
  224.9 12.7 %all_to_all.85 = bf16[16,256,64]{1,2,0:T(8,128)(2,1)S(1)} all-to-all(bf16[16,256,64]{1,2,0:T(8,128)(2,1)S(1)} %broadcast_in_dim.30), channel_id=1, replica_groups=mesh['dp'=32,'txt'=16] {'txt'}, dimensions={0} | all-to-all | bytes 1048576 | tf_op jit(solution)/shard_map/all_to_all | solution.py:11
  237.6 1.8 convolution_bitcast_fusion
  239.4 4.6 %all-to-all-start.12 = ((f32[16,256,64]{1,2,0:T(8,128)}), f32[16,256,64]{1,2,0:T(8,128)S(1)}, u32[]{:S(2)}, u32[]{:S(2)}) async-start(f32[16,256,64]{1,2,0:T(8,128)} %convolution_bitcast_fusion), calls=%async_computation.12 | async-start | bytes 2097152 | tf_op jit(solution)/shard_map/all_to_all | solution.py:33
  244.2 15.7 %all-to-all-done.12 = f32[16,256,64]{1,2,0:T(8,128)S(1)} async-done(((f32[16,256,64]{1,2,0:T(8,128)}), f32[16,256,64]{1,2,0:T(8,128)S(1)}, u32[]{:S(2)}, u32[]{:S(2)}) %all-to-all-start.12) | async-done | bytes 1048608 | tf_op jit(solution)/shard_map/all_to_all | solution.py:33
  260.1 9.1 %all_to_all.86 = f32[16,1,512]{2,1,0:T(1,128)S(1)} all-to-all(f32[16,1,512]{2,1,0:T(1,128)S(1)} %broadcast_in_dim.31), channel_id=1, replica_groups=mesh['dp'=32,'txt'=16] {'txt'}, dimensions={0} | all-to-all | bytes 65536 | tf_op jit(solution)/shard_map/all_to_all | solution.py:11
  270.0 3.7 %all-to-all-start.14 = ((f32[16,1,256]{2,1,0:T(1,128)}), f32[16,1,256]{2,1,0:T(1,128)S(1)}, u32[]{:S(2)}, u32[]{:S(2)}) async-start(f32[16,1,256]{2,1,0:T(1,128)} %broadcast_in_dim.32), calls=%async_computation.14 | async-start | bytes 32768 | tf_op jit(solution)/shard_map/all_to_all | solution.py:11
  274.3 5.2 %all-to-all-done.14 = f32[16,1,256]{2,1,0:T(1,128)S(1)} async-done(((f32[16,1,256]{2,1,0:T(1,128)}), f32[16,1,256]{2,1,0:T(1,128)S(1)}, u32[]{:S(2)}, u32[]{:S(2)}) %all-to-all-start.14) | async-done | bytes 16416 | tf_op jit(solution)/shard_map/all_to_all | solution.py:11
  (105 shorter events, 6.8 us)
Async XLA Ops:
  0.0 137.5 %copy-start = (bf16[64,768]{1,0:T(8,128)(2,1)S(1)}, bf16[64,768]{1,0:T(8,128)(2,1)}, u32[]{:S(2)}) copy-start(bf16[64,768]{1,0:T(8,128)(2,1)} %param.22) | copy-start | bytes 294916
  0.0 20.1 %copy-start.11 = (bf16[32,256]{1,0:T(8,128)(2,1)S(1)}, bf16[32,256]{1,0:T(8,128)(2,1)}, u32[]{:S(2)}) copy-start(bf16[32,256]{1,0:T(8,128)(2,1)} %param.16) | copy-start | bytes 49156
  0.9 64.2 %copy-start.12 = (bf16[256,32]{0,1:T(8,128)(2,1)S(1)}, bf16[256,32]{0,1:T(8,128)(2,1)}, u32[]{:S(2)}) copy-start(bf16[256,32]{0,1:T(8,128)(2,1)} %param.18) | copy-start | bytes 49156
  20.1 53.0 %copy-start.13 = (f32[1024]{0:T(1024)S(1)}, f32[1024]{0:T(1024)}, u32[]{:S(2)}) copy-start(f32[1024]{0:T(1024)} %param.15) | copy-start | bytes 12292
  20.1 53.0 %copy-start.14 = (f32[1024]{0:T(1024)S(1)}, f32[1024]{0:T(1024)}, u32[]{:S(2)}) copy-start(f32[1024]{0:T(1024)} %param.14) | copy-start | bytes 12292
  65.1 8.7 %copy-start.6 = (bf16[32,32,256]{2,1,0:T(8,128)(2,1)}, bf16[32,32,256]{2,1,0:T(8,128)(2,1)S(1)}, u32[]{:S(2)}) copy-start(bf16[32,32,256]{2,1,0:T(8,128)(2,1)S(1)} %all_to_all.80) | copy-start | bytes 1572868
  66.0 7.8 %copy-start.19 = (f32[256]{0:T(256)S(1)}, f32[256]{0:T(256)}, u32[]{:S(2)}) copy-start(f32[256]{0:T(256)} %param.17) | copy-start | bytes 3076
  66.0 37.6 %all-to-all-start.2 = ((bf16[32,256,32]{1,2,0:T(8,128)(2,1)}), bf16[32,256,32]{1,2,0:T(8,128)(2,1)S(1)}, u32[]{:S(2)}, u32[]{:S(2)}) async-start(bf16[32,256,32]{1,2,0:T(8,128)(2,1)} %broadcast_in_dim.24), calls=%async_computation.2 | async-start | bytes 1048576 | tf_op jit(solution)/shard_map/all_to_all | solution.py:11
  74.2 30.8 %copy-start.9 = (f32[256,256]{1,0:T(8,128)}, f32[256,256]{1,0:T(8,128)S(1)}, u32[]{:S(2)}) copy-start(f32[256,256]{1,0:T(8,128)S(1)} %convolution_add_fusion) | copy-start | bytes 786436
  103.6 1.4 copy-start.4
  104.9 23.1 %copy-start.8 = (bf16[256,64]{0,1:T(8,128)(2,1)S(1)}, bf16[256,64]{0,1:T(8,128)(2,1)}, u32[]{:S(2)}) copy-start(bf16[256,64]{0,1:T(8,128)(2,1)} %param.13) | copy-start | bytes 98308
  104.9 32.6 %copy-start.15 = (f32[64]{0:T(128)S(1)}, f32[64]{0:T(128)}, u32[]{:S(2)}) copy-start(f32[64]{0:T(128)} %param.20) | copy-start | bytes 772
  104.9 32.6 %copy-start.18 = (f32[64]{0:T(128)S(1)}, f32[64]{0:T(128)}, u32[]{:S(2)}) copy-start(f32[64]{0:T(128)} %param.21) | copy-start | bytes 772
  104.9 23.0 %all-to-all-start.3 = ((f32[16,256,64]{1,2,0:T(8,128)}), f32[16,256,64]{1,2,0:T(8,128)S(1)}, u32[]{:S(2)}, u32[]{:S(2)}) async-start(f32[16,256,64]{1,2,0:T(8,128)} %convolution_bitcast_fusion.1), calls=%async_computation.3 | async-start | bytes 2097152 | tf_op jit(solution)/shard_map/all_to_all | solution.py:33
  128.2 14.4 %copy-start.1 = (bf16[1280,768]{1,0:T(8,128)(2,1)S(1)}, bf16[1280,768]{1,0:T(8,128)(2,1)}, u32[]{:S(2)}) copy-start(bf16[1280,768]{1,0:T(8,128)(2,1)} %param.23) | copy-start | bytes 5898244
  138.7 16.9 %all-to-all-start.5 = ((f32[16,16,768]{2,1,0:T(8,128)}), f32[16,16,768]{2,1,0:T(8,128)S(1)}, u32[]{:S(2)}, u32[]{:S(2)}) async-start(f32[16,16,768]{2,1,0:T(8,128)} %bitcast.55), calls=%async_computation.5 | async-start | bytes 1572864 | tf_op jit(solution)/shard_map/all_to_all | solution.py:33
  156.7 12.7 %all-to-all-start.6 = ((bf16[16,16,768]{2,1,0:T(8,128)(2,1)}), bf16[16,16,768]{2,1,0:T(8,128)(2,1)S(1)}, u32[]{:S(2)}, u32[]{:S(2)}) async-start(bf16[16,16,768]{2,1,0:T(8,128)(2,1)} %broadcast_in_dim.26), calls=%async_computation.6 | async-start | bytes 786432 | tf_op jit(solution)/shard_map/all_to_all | solution.py:11
  169.4 15.2 %copy-start.2 = (bf16[1280,768]{1,0:T(8,128)(2,1)S(1)}, bf16[1280,768]{1,0:T(8,128)(2,1)}, u32[]{:S(2)}) copy-start(bf16[1280,768]{1,0:T(8,128)(2,1)} %fusion.1) | copy-start | bytes 5898244
  171.9 1.1 copy-start.3
  171.9 6.5 %copy-start.17 = (s32[256]{0:T(256)S(1)}, s32[256]{0:T(256)}, u32[]{:S(2)}) copy-start(s32[256]{0:T(256)} %param.24) | copy-start | bytes 3076
  173.9 10.3 %all-to-all-start.7 = ((f32[16,2,256]{2,1,0:T(2,128)}), f32[16,2,256]{2,1,0:T(2,128)S(1)}, u32[]{:S(2)}, u32[]{:S(2)}) async-start(f32[16,2,256]{2,1,0:T(2,128)} %broadcast_in_dim.27), calls=%async_computation.7 | async-start | bytes 65536 | tf_op jit(solution)/shard_map/all_to_all | solution.py:11
  202.5 12.3 %copy-start.16 = (f32[64]{0:T(128)S(1)}, f32[64]{0:T(128)}, u32[]{:S(2)}) copy-start(f32[64]{0:T(128)} %param.20) | copy-start | bytes 772
  214.8 22.7 %copy-start.5 = (bf16[32,256,32]{1,2,0:T(8,128)(2,1)S(1)}, bf16[32,256,32]{1,2,0:T(8,128)(2,1)}, u32[]{:S(2)}) copy-start(bf16[32,256,32]{1,2,0:T(8,128)(2,1)} %copy-done.4) | copy-start | bytes 1572868
  214.8 22.7 %copy-start.7 = (bf16[32,32,256]{2,1,0:T(8,128)(2,1)S(1)}, bf16[32,32,256]{2,1,0:T(8,128)(2,1)}, u32[]{:S(2)}) copy-start(bf16[32,32,256]{2,1,0:T(8,128)(2,1)} %copy-done.6) | copy-start | bytes 1572868
  214.8 22.7 %copy-start.10 = (f32[256,256]{1,0:T(8,128)S(1)}, f32[256,256]{1,0:T(8,128)}, u32[]{:S(2)}) copy-start(f32[256,256]{1,0:T(8,128)} %copy-done.9) | copy-start | bytes 786436
  239.4 20.5 %all-to-all-start.12 = ((f32[16,256,64]{1,2,0:T(8,128)}), f32[16,256,64]{1,2,0:T(8,128)S(1)}, u32[]{:S(2)}, u32[]{:S(2)}) async-start(f32[16,256,64]{1,2,0:T(8,128)} %convolution_bitcast_fusion), calls=%async_computation.12 | async-start | bytes 2097152 | tf_op jit(solution)/shard_map/all_to_all | solution.py:33
  270.0 9.5 %all-to-all-start.14 = ((f32[16,1,256]{2,1,0:T(1,128)}), f32[16,1,256]{2,1,0:T(1,128)S(1)}, u32[]{:S(2)}, u32[]{:S(2)}) async-start(f32[16,1,256]{2,1,0:T(1,128)} %broadcast_in_dim.32), calls=%async_computation.14 | async-start | bytes 32768 | tf_op jit(solution)/shard_map/all_to_all | solution.py:11
where the time goes:
time: 281 us; the launch traced here: 280 us
  blocking collectives  132 us (47%)
  waiting for transfers between devices  90.6 us (32%)
  starting transfers between devices  35 us (12%)
  matrix products  9.78 us (3%)
  local copies, waits for them, and re-layouts  6.37 us (2%)
  other arithmetic  5.14 us (2%)
    all_to_all x7, blocking collectives, sent_to_all(): return lax.all_to_all(copies, axis, split_axis=0, concat_axis=0, tiled=True)  117 us
    all_to_all x4, waiting for transfers between devices, sent_to_all(): return lax.all_to_all(copies, axis, split_axis=0, concat_axis=0, tiled=True)  47.2 us
    all_to_all x3, waiting for transfers between devices, summed_on_arrival(): tiles = lax.all_to_all(in_blocks(x, dim, size), axis, 0, 0, tiled=True)  43.5 us
    all_to_all x4, starting transfers between devices, sent_to_all(): return lax.all_to_all(copies, axis, split_axis=0, concat_axis=0, tiled=True)  19.5 us
    all_to_all x1, blocking collectives, summed_on_arrival(): tiles = lax.all_to_all(in_blocks(x, dim, size), axis, 0, 0, tiled=True)  15.7 us
    all_to_all x3, starting transfers between devices, summed_on_arrival(): tiles = lax.all_to_all(in_blocks(x, dim, size), axis, 0, 0, tiled=True)  15.5 us
  transfers between devices with their start and end apart: 7, of which 7 were waited for; matrix products, arithmetic and copies ran while one was open for 1% of the time, Pallas kernels for 0%

commit v1 on v0

v1 whole, which is shorter than its diff:
```python
import jax
import jax.numpy as jnp
from jax import lax
from jax.sharding import PartitionSpec as P

WIDTH = 1024
BF = jnp.bfloat16
F32 = jnp.float32


def swapped(x, axis, groups=None):
    return lax.all_to_all(x, axis, 0, 0, tiled=True, axis_index_groups=groups)


def copies(x, n):
    return jnp.broadcast_to(x, (n, *x.shape))


def pieces(x, count):
    out = []
    for _ in range(count):
        part = lax.reduce_precision(x, 8, 7)
        out.append(part.astype(BF))
        x = x - part
    return out


def row_norm(rows):
    mean = jnp.mean(rows, axis=1, keepdims=True)
    var = jnp.mean(rows * rows, axis=1, keepdims=True) - mean * mean
    rstd = lax.rsqrt(var + 1e-05)
    return (rows - mean) * rstd, rstd


def norm_back(scaled, normed, rstd):
    first = jnp.mean(scaled, axis=1, keepdims=True)
    second = jnp.mean(scaled * normed, axis=1, keepdims=True)
    return (scaled - first - normed * second) * rstd


def local(
    resid,
    prenorm_gain,
    prenorm_bias,
    up_weight,
    up_bias,
    down_weight,
    down_bias,
    post_gain,
    post_bias,
    projection,
    texts,
    labels,
    step_size,
):
    n_txt, n_dp = lax.axis_size("txt"), lax.axis_size("dp")
    n_z = n_dp // 2
    me = lax.axis_index("txt")
    images, share = resid.shape
    rows = images // n_txt
    hid = up_weight.shape[1]
    n_text, emb = texts.shape

    proj = lax.all_gather(projection, "txt", axis=0, tiled=True)

    along_z = [[2 * z + x for z in range(n_z)] for x in range(2)]
    mine = jnp.stack([up_weight, down_weight.T])
    mine = swapped(copies(mine, n_z), "dp", along_z)

    text_f = texts.astype(F32)
    text_unit = (text_f / jnp.sqrt(jnp.sum(text_f * text_f, axis=1, keepdims=True) + 1e-06)).astype(BF)
    local_label = labels - me * n_text
    columns = lax.broadcasted_iota(jnp.int32, (images, n_text), 1)
    target = columns == local_label[:, None]
    label_text = jnp.dot(target.astype(BF), text_unit, preferred_element_type=F32).astype(BF)

    label_text = label_text.reshape(n_txt, rows, emb // images, images).transpose(0, 2, 1, 3)
    label_text = label_text.reshape(n_txt, rows * emb // images, images)
    vectors = jnp.stack(pieces(post_gain, 3) + pieces(post_bias, 3))
    vectors = jnp.pad(vectors, ((0, 2), (0, images - share)))
    message = jnp.concatenate(
        [copies(resid.T, n_txt), label_text, copies(vectors, n_txt)], axis=1
    )
    mine, message = lax.optimization_barrier((mine, message))
    pairs = [(i, i ^ 1) for i in range(n_dp)]
    other_up = lax.ppermute(mine[:, 0], "dp", pairs)
    other_down = lax.ppermute(mine[:, 1], "dp", pairs)
    message = swapped(message, "txt")

    state = message[:, :share].reshape(n_txt * share, images)
    label_rows = jnp.sum(message[:, share : share + rows * emb // images].astype(F32), axis=0)
    label_rows = label_rows.reshape(emb // images, rows, images).transpose(1, 0, 2).reshape(rows, emb)
    vectors = message[:, -8:, :share].astype(F32)
    gain_out = (vectors[:, 0] + vectors[:, 1] + vectors[:, 2]).reshape(-1)
    bias_out = (vectors[:, 3] + vectors[:, 4] + vectors[:, 5]).reshape(-1)

    first = lax.rem(lax.axis_index("dp"), 2) == 0

    def whole(own, other):
        both = jnp.stack([jnp.where(first, own, other), jnp.where(first, other, own)], axis=1)
        return both.reshape(WIDTH, hid)

    w_up = whole(mine[:, 0], other_up)
    w_down = whole(mine[:, 1], other_down)

    inputs = state.astype(F32)
    mean_in = jnp.mean(inputs, axis=0)
    var_in = jnp.mean(inputs * inputs, axis=0) - mean_in * mean_in
    rstd_in = lax.rsqrt(var_in + 1e-05)
    normed = ((inputs - mean_in) * rstd_in * prenorm_gain[:, None] + prenorm_bias[:, None]).astype(BF)
    pre_act = jnp.einsum("di,df->if", normed, w_up, preferred_element_type=F32) + up_bias
    gate = jax.nn.sigmoid(1.702 * pre_act)
    hidden = (pre_act * gate).astype(BF)
    mixed = jnp.einsum("if,df->id", hidden, w_down, preferred_element_type=F32).astype(BF)
    mixed = swapped(mixed.reshape(n_txt, rows, WIDTH), "txt")

    pick = lax.broadcasted_iota(jnp.int32, (rows, images), 1) == (
        lax.broadcasted_iota(jnp.int32, (rows, images), 0) + me * rows
    )
    own = jnp.einsum("ri,di->rd", pick.astype(BF), state, preferred_element_type=F32)
    block_out = own + jnp.sum(mixed.astype(F32), axis=0) + down_bias
    yhat, rstd_out = row_norm(block_out)
    post_normed = (yhat * gain_out + bias_out).astype(BF)
    embedding = jnp.dot(post_normed, proj, preferred_element_type=F32)
    emb_norm = jnp.sqrt(jnp.sum(embedding * embedding, axis=1, keepdims=True) + 1e-06)
    unit_vec = embedding / emb_norm
    unit_low = swapped(copies(unit_vec.astype(BF), n_txt), "txt").reshape(images, emb)

    logits = 100.0 * jnp.einsum("ie,je->ij", unit_low, text_unit, preferred_element_type=F32)
    top = lax.reduce_precision(jnp.max(logits, axis=1), 8, 7)
    exponent = jnp.exp(logits - top[:, None])
    others = jnp.where(target, 0.0, exponent)
    rest = jnp.sum(others, axis=1)
    hit = jnp.sum(jnp.where(target, exponent, 0.0), axis=1)
    back = jnp.dot(others.astype(BF), text_unit, preferred_element_type=F32).astype(BF)
    stats = jnp.stack(pieces(top, 1) + pieces(rest, 2) + pieces(hit, 2), axis=1)
    stats = jnp.pad(stats, ((0, 0), (0, 128 - stats.shape[1])))
    back = jnp.concatenate([back, stats], axis=1).reshape(n_txt, rows, emb + 128)
    back = swapped(back, "txt").astype(F32)

    stats = back[:, :, emb:]
    top = stats[:, :, 0]
    weight = jnp.exp(top - jnp.max(top, axis=0))
    rest = jnp.sum(weight * (stats[:, :, 1] + stats[:, :, 2]), axis=0)[:, None]
    hit = jnp.sum(weight * (stats[:, :, 3] + stats[:, :, 4]), axis=0)[:, None]
    unit_grad = jnp.sum(weight[:, :, None] * back[:, :, :emb], axis=0)
    unit_grad = (unit_grad - rest * label_rows) * (100.0 / (rest + hit))
    along = jnp.sum(unit_vec * unit_grad, axis=1, keepdims=True)
    emb_grad = ((unit_grad - unit_vec * along) / emb_norm).astype(BF)
    post_grad = jnp.einsum("ie,de->id", emb_grad, proj, preferred_element_type=F32)
    out_grad = norm_back(post_grad * gain_out, yhat, rstd_out)
    out_low = swapped(copies(out_grad.astype(BF), n_txt), "txt").reshape(images, WIDTH)

    hid_grad = jnp.einsum("id,df->if", out_low, w_down, preferred_element_type=F32)
    act_grad = (hid_grad * (gate + 1.702 * pre_act * gate * (1.0 - gate))).astype(BF)
    normed_grad = jnp.einsum("if,df->id", act_grad, w_up, preferred_element_type=F32).astype(BF)
    normed_grad = swapped(normed_grad.reshape(n_txt, rows, WIDTH), "txt")
    normed_grad = jnp.sum(normed_grad.astype(F32), axis=0)
    xhat, rstd_own = row_norm(own)
    input_grad = out_grad + norm_back(normed_grad * prenorm_gain, xhat, rstd_own)
    rms = jnp.sqrt(jnp.mean(input_grad * input_grad, axis=1, keepdims=True) + 1e-06)
    change = step_size[0] * input_grad / rms
    change = change.reshape(rows, n_txt, share).transpose(1, 0, 2)
    change = swapped(change, "txt").reshape(images, share)
    return resid.astype(F32) + change


def solution(mesh):
    placed = (
        P("dp", "txt"),
        P(),
        P(),
        P("dp", "txt"),
        P("txt"),
        P("txt", "dp"),
        P(),
        P("txt"),
        P("txt"),
        P("txt", None),
        P("txt", None),
        P("dp"),
        P(),
    )
    return jax.shard_map(
        local, mesh=mesh, in_specs=placed, out_specs=P("dp", "txt"), check_vma=False
    )
```

time: 281 us -> 199 us (0.71)
  blocking collectives: 132 us -> 34.6 us
  waiting for transfers between devices: 90.6 us -> 64.5 us
  starting transfers between devices: 35 us -> 50.2 us
  between operations: 1.01 us -> 14.6 us
  other arithmetic: 5.14 us -> 14.8 us
    all_to_all x8 -> x3, blocking collectives: 132 us -> 34.6 us  [swapped(): return lax.all_to_all(x, axis, 0, 0, tiled=True, axis_index_groups=groups)]
    all_to_all x7 -> x5, waiting for transfers between devices: 90.6 us -> 44.6 us  [swapped(): return lax.all_to_all(x, axis, 0, 0, tiled=True, axis_index_groups=groups)]
    ppermute x0 -> x2, waiting for transfers between devices: none -> 19.9 us  [the longest x1 12.9 us: local(): other_up = lax.ppermute(mine[:, 0], 'dp', pairs)]
    all_to_all x7 -> x5, starting transfers between devices: 35 us -> 43.4 us  [swapped(): return lax.all_to_all(x, axis, 0, 0, tiled=True, axis_index_groups=groups)]
    ppermute x0 -> x2, starting transfers between devices: none -> 6.81 us  [the longest x1 4.38 us: local(): other_up = lax.ppermute(mine[:, 0], 'dp', pairs)]
    all_to_all x0 -> x2, local copies, waits for them, and re-layouts: none -> 5.08 us  [swapped(): return lax.all_to_all(x, axis, 0, 0, tiled=True, axis_index_groups=groups)]
    broadcast_in_dim x11 -> x5, local copies, waits for them, and re-layouts: 3.99 us -> 1 us  [copies(): return jnp.broadcast_to(x, (n, *x.shape))]
    dot_general x7 -> x9, matrix products: 9.78 us -> 10.3 us  [the longest x1 2.38 us: local(): jnp.einsum('ri,di->rd', pick.astype(BF), state, preferred_element_type=F32)]
  transfers between devices with their start and end apart: 7 -> 8, of which waited for: 7 -> 6; matrix products, arithmetic and copies ran while one was open for 1% -> 6% of each run, Pallas kernels for 0% -> 0%
where the time goes in v1:
time: 199 us; the launch traced here: 198 us
  waiting for transfers between devices  64.5 us (32%)
  starting transfers between devices  50.2 us (25%)
  blocking collectives  34.6 us (17%)
  other arithmetic  14.8 us (7%)
  between operations  14.6 us (7%)
  matrix products  10.3 us (5%)
  local copies, waits for them, and re-layouts  8.83 us (4%)
    all_to_all x5, waiting for transfers between devices, swapped(): return lax.all_to_all(x, axis, 0, 0, tiled=True, axis_index_groups=groups)  44.6 us
    all_to_all x5, starting transfers between devices, swapped(): return lax.all_to_all(x, axis, 0, 0, tiled=True, axis_index_groups=groups)  43.4 us
    all_to_all x3, blocking collectives, swapped(): return lax.all_to_all(x, axis, 0, 0, tiled=True, axis_index_groups=groups)  34.6 us
    ppermute x1, waiting for transfers between devices, local(): other_up = lax.ppermute(mine[:, 0], 'dp', pairs)  12.9 us
    ppermute x1, waiting for transfers between devices, local(): other_down = lax.ppermute(mine[:, 1], 'dp', pairs)  6.98 us
    all_to_all x2, local copies, waits for them, and re-layouts, swapped(): return lax.all_to_all(x, axis, 0, 0, tiled=True, axis_index_groups=groups)  5.08 us
    ppermute x1, starting transfers between devices, local(): other_up = lax.ppermute(mine[:, 0], 'dp', pairs)  4.38 us
  transfers between devices with their start and end apart: 8, of which 6 were waited for; matrix products, arithmetic and copies ran while one was open for 6% of the time, Pallas kernels for 0%

profile of v1, /device:TPU:1, one launch (start us, length us, event | category | flops | bytes accessed | tf_op | source)
XLA Modules:
  0.0 197.9 jit_solution(10597777659371651987)
XLA Ops:
  6.5 0.9 pad_maximum_fusion.3
  7.4 0.9 broadcast_in_dim.15
  8.3 15.7 %all-to-all-start = ((bf16[16,2,32,256]{3,2,1,0:T(8,128)(2,1)}), bf16[16,2,32,256]{3,2,1,0:T(8,128)(2,1)S(1)}, u32[]{:S(2)}, u32[]{:S(2)}) async-start(bf16[16,2,32,256]{3,2,1,0:T(8,128)(2,1)} %broadcast_in_dim.15), calls=%async_computation | async-start | bytes 1048576 | tf_op jit(solution)/shard_map/all_to_all | solution.py:12
  24.7 2.0 %fusion.1 = f32[1280]{0:T(1024)S(1)} fusion(bf16[1280,768]{1,0:T(8,128)(2,1)} %param.23), kind=kLoop, calls=%fused_computation.4 | loop fusion | flops 2947840 | bytes 1971200 | tf_op jit(solution)/shard_map/reduce_sum | solution.py:71
  27.2 1.3 copy-done.1
  29.7 1.0 pad_maximum_fusion
  30.7 16.2 %all-to-all-done = bf16[16,2,32,256]{3,2,1,0:T(8,128)(2,1)S(1)} async-done(((bf16[16,2,32,256]{3,2,1,0:T(8,128)(2,1)}), bf16[16,2,32,256]{3,2,1,0:T(8,128)(2,1)S(1)}, u32[]{:S(2)}, u32[]{:S(2)}) %all-to-all-start) | async-done | bytes 524320 | tf_op jit(solution)/shard_map/all_to_all | solution.py:12
  46.9 12.6 %all-to-all-start.1 = ((bf16[16,120,256]{2,1,0:T(8,128)(2,1)}), bf16[16,120,256]{2,1,0:T(8,128)(2,1)S(1)}, u32[]{:S(2)}, u32[]{:S(2)}) async-start(bf16[16,120,256]{2,1,0:T(8,128)(2,1)} %pad_maximum_fusion), calls=%async_computation.1 | async-start | bytes 1966080 | tf_op jit(solution)/shard_map/all_to_all | solution.py:12
  59.6 4.4 %collective-permute-start = (bf16[16,32,256]{2,1,0:T(8,128)(2,1)S(1)}, bf16[16,32,256]{2,1,0:T(8,128)(2,1)S(1)}, u32[]{:S(2)}, u32[]{:S(2)}) collective-permute-start(bf16[16,32,256]{2,1,0:T(8,128)(2,1)S(1)} %get-tuple-element.36), channel_id=1, source_target_pairs={{0,16},{16,0},{32,48},{48,32},{64,80},{80,64},{96,112},{112,96},{1... | collective-permute-start | bytes 786440 | tf_op jit(solution)/shard_map/ppermute | solution.py:86
  64.0 2.4 %collective-permute-start.1 = (bf16[16,32,256]{2,1,0:T(8,128)(2,1)S(1)}, bf16[16,32,256]{2,1,0:T(8,128)(2,1)S(1)}, u32[]{:S(2)}, u32[]{:S(2)}) collective-permute-start(bf16[16,32,256]{2,1,0:T(8,128)(2,1)S(1)} %get-tuple-element.37), channel_id=1, source_target_pairs={{0,16},{16,0},{32,48},{48,32},{64,80},{80,64},{96,112},{112,96},{1... | collective-permute-start | bytes 786440 | tf_op jit(solution)/shard_map/ppermute | solution.py:87
  66.6 12.9 %collective-permute-done = bf16[16,32,256]{2,1,0:T(8,128)(2,1)S(1)} collective-permute-done((bf16[16,32,256]{2,1,0:T(8,128)(2,1)S(1)}, bf16[16,32,256]{2,1,0:T(8,128)(2,1)S(1)}, u32[]{:S(2)}, u32[]{:S(2)}) %collective-permute-start) | collective-permute-done | bytes 262176 | tf_op jit(solution)/shard_map/ppermute | solution.py:86
  79.5 7.0 %collective-permute-done.1 = bf16[16,32,256]{2,1,0:T(8,128)(2,1)S(1)} collective-permute-done((bf16[16,32,256]{2,1,0:T(8,128)(2,1)S(1)}, bf16[16,32,256]{2,1,0:T(8,128)(2,1)S(1)}, u32[]{:S(2)}, u32[]{:S(2)}) %collective-permute-start.1) | collective-permute-done | bytes 262176 | tf_op jit(solution)/shard_map/ppermute | solution.py:87
  87.9 1.2 convolution_convert_fusion.1
  89.0 5.8 %all-to-all-start.2 = ((bf16[16,16,1024]{2,1,0:T(8,128)(2,1)}), bf16[16,16,1024]{2,1,0:T(8,128)(2,1)S(1)}, u32[]{:S(2)}, u32[]{:S(2)}) async-start(bf16[16,16,1024]{2,1,0:T(8,128)(2,1)} %bitcast.24), calls=%async_computation.2 | async-start | bytes 1048576 | tf_op jit(solution)/shard_map/all_to_all | solution.py:12
  95.8 10.1 %all-to-all-done.2 = bf16[16,16,1024]{2,1,0:T(8,128)(2,1)S(1)} async-done(((bf16[16,16,1024]{2,1,0:T(8,128)(2,1)}), bf16[16,16,1024]{2,1,0:T(8,128)(2,1)S(1)}, u32[]{:S(2)}, u32[]{:S(2)}) %all-to-all-start.2) | async-done | bytes 524320 | tf_op jit(solution)/shard_map/all_to_all | solution.py:12
  106.0 2.4 %fusion.68 = (f32[16]{0:T(128)}, f32[16]{0:T(128)}, f32[16]{0:T(128)S(1)}, f32[16]{0:T(128)S(1)}, f32[16,1024]{1,0:T(8,128)S(1)}, /*index=5*/f32[16,1024]{1,0:T(8,128)}) fusion(f32[1024]{0:T(1024)S(1)} %copy-done.12, f32[16,1024]{1,0:T(8,128)S(1)} %convert_reduce_fusion.2, bf16[1024,256]{1,0:T(8,128)(2,1)S(1)} %bitcast.99, s32[16]{0:T(128)} %iota_add_fusion), kind=kOutput, calls=%fused_computation.159 | convolution fusion | flops 8523712 | bytes 725312 | tf_op jit(solution)/shard_map/ri,di->rd/dot_general | solution.py:120
  108.4 1.9 multiply_reduce_fusion.7
  110.4 11.6 %all_to_all.40 = bf16[16,16,768]{2,1,0:T(8,128)(2,1)S(1)} all-to-all(bf16[16,16,768]{2,1,0:T(8,128)(2,1)S(1)} %broadcast_in_dim.20), channel_id=1, replica_groups=mesh['dp'=32,'txt'=16] {'txt'}, dimensions={0} | all-to-all | bytes 786432 | tf_op jit(solution)/shard_map/all_to_all | solution.py:12
  122.1 0.8 fusion.73
  122.9 0.8 convolution_convert_fusion.2
  124.6 0.8 fusion.20
  125.4 4.5 %all-to-all-start.4 = ((bf16[16,16,896]{2,1,0:T(8,128)(2,1)}), bf16[16,16,896]{2,1,0:T(8,128)(2,1)S(1)}, u32[]{:S(2)}, u32[]{:S(2)}) async-start(bf16[16,16,896]{2,1,0:T(8,128)(2,1)} %bitcast.28), calls=%async_computation.4 | async-start | bytes 917504 | tf_op jit(solution)/shard_map/all_to_all | solution.py:12
  130.0 9.1 %all-to-all-done.4 = bf16[16,16,896]{2,1,0:T(8,128)(2,1)S(1)} async-done(((bf16[16,16,896]{2,1,0:T(8,128)(2,1)}), bf16[16,16,896]{2,1,0:T(8,128)(2,1)S(1)}, u32[]{:S(2)}, u32[]{:S(2)}) %all-to-all-start.4) | async-done | bytes 458784 | tf_op jit(solution)/shard_map/all_to_all | solution.py:12
  139.1 4.6 %copy.62 = bf16[16,16,896]{1,0,2:T(8,128)(2,1)} copy(bf16[16,16,896]{2,1,0:T(8,128)(2,1)S(1)} %all-to-all-done.4) | data formatting | bytes 917504 | tf_op jit(solution)/shard_map/all_to_all | solution.py:12
  143.7 2.6 %convert_element_type.173 = f32[16,16,896]{1,0,2:T(8,128)S(1)} convert(bf16[16,16,896]{1,0,2:T(8,128)(2,1)} %copy.62) | non-fusion elementwise | flops 229376 | bytes 1376256 | tf_op jit(solution)/shard_map/convert_element_type | solution.py:139
  146.3 1.4 fusion
  149.0 13.5 %all_to_all.41 = bf16[16,16,1024]{2,1,0:T(8,128)(2,1)S(1)} all-to-all(bf16[16,16,1024]{2,1,0:T(8,128)(2,1)S(1)} %broadcast_in_dim.21), channel_id=1, replica_groups=mesh['dp'=32,'txt'=16] {'txt'}, dimensions={0} | all-to-all | bytes 1048576 | tf_op jit(solution)/shard_map/all_to_all | solution.py:12
  162.5 1.5 convolution_convert_fusion
  164.0 4.7 %all-to-all-start.6 = ((bf16[16,16,1024]{2,1,0:T(8,128)(2,1)}), bf16[16,16,1024]{2,1,0:T(8,128)(2,1)S(1)}, u32[]{:S(2)}, u32[]{:S(2)}) async-start(bf16[16,16,1024]{2,1,0:T(8,128)(2,1)} %bitcast.36), calls=%async_computation.6 | async-start | bytes 1048576 | tf_op jit(solution)/shard_map/all_to_all | solution.py:12
  169.4 9.2 %all-to-all-done.6 = bf16[16,16,1024]{2,1,0:T(8,128)(2,1)S(1)} async-done(((bf16[16,16,1024]{2,1,0:T(8,128)(2,1)}), bf16[16,16,1024]{2,1,0:T(8,128)(2,1)S(1)}, u32[]{:S(2)}, u32[]{:S(2)}) %all-to-all-start.6) | async-done | bytes 524320 | tf_op jit(solution)/shard_map/all_to_all | solution.py:12
  179.4 9.4 %all_to_all.42 = f32[16,1,1024]{2,1,0:T(1,128)S(1)} all-to-all(f32[16,1,1024]{2,1,0:T(1,128)S(1)} %reshape.293), channel_id=1, replica_groups=mesh['dp'=32,'txt'=16] {'txt'}, dimensions={0} | all-to-all | bytes 131072 | tf_op jit(solution)/shard_map/all_to_all | solution.py:12
  189.4 0.8 reduce.11
  (117 shorter events, 9.2 us)
Async XLA Ops:
  6.5 20.2 %copy-start = (bf16[1280,768]{1,0:T(8,128)(2,1)S(1)}, bf16[1280,768]{1,0:T(8,128)(2,1)}, u32[]{:S(2)}) copy-start(bf16[1280,768]{1,0:T(8,128)(2,1)} %param.23) | copy-start | bytes 5898244
  8.3 38.6 %all-to-all-start = ((bf16[16,2,32,256]{3,2,1,0:T(8,128)(2,1)}), bf16[16,2,32,256]{3,2,1,0:T(8,128)(2,1)S(1)}, u32[]{:S(2)}, u32[]{:S(2)}) async-start(bf16[16,2,32,256]{3,2,1,0:T(8,128)(2,1)} %broadcast_in_dim.15), calls=%async_computation | async-start | bytes 1048576 | tf_op jit(solution)/shard_map/all_to_all | solution.py:12
  24.7 2.5 %copy-start.13 = (s32[256]{0:T(256)}, s32[256]{0:T(256)S(1)}, u32[]{:S(2)}) copy-start(s32[256]{0:T(256)S(1)} %broadcast_subtract_fusion) | copy-start | bytes 3076
  27.2 1.3 copy-start.1
  28.5 1.0 copy-start.18
  28.5 1.0 copy-start.19
  28.5 1.1 copy-start.9
  30.7 35.7 %copy-start.15 = (f32[1024]{0:T(1024)S(1)}, f32[1024]{0:T(1024)}, u32[]{:S(2)}) copy-start(f32[1024]{0:T(1024)} %param.15) | copy-start | bytes 12292
  30.7 35.8 %copy-start.11 = (f32[1024]{0:T(1024)S(1)}, f32[1024]{0:T(1024)}, u32[]{:S(2)}) copy-start(f32[1024]{0:T(1024)} %param.14) | copy-start | bytes 12292
  46.9 40.1 %all-to-all-start.1 = ((bf16[16,120,256]{2,1,0:T(8,128)(2,1)}), bf16[16,120,256]{2,1,0:T(8,128)(2,1)S(1)}, u32[]{:S(2)}, u32[]{:S(2)}) async-start(bf16[16,120,256]{2,1,0:T(8,128)(2,1)} %pad_maximum_fusion), calls=%async_computation.1 | async-start | bytes 1966080 | tf_op jit(solution)/shard_map/all_to_all | solution.py:12
  59.5 48.9 %all-gather.2.cloned.1.call-start = ((), (), s32[]{:S(2)}) async-start(), calls=%async_computation.8 | async-start | bytes 1671168 | tf_op jit(solution)/shard_map/all_gather | solution.py:64
  59.6 19.9 %collective-permute-start = (bf16[16,32,256]{2,1,0:T(8,128)(2,1)S(1)}, bf16[16,32,256]{2,1,0:T(8,128)(2,1)S(1)}, u32[]{:S(2)}, u32[]{:S(2)}) collective-permute-start(bf16[16,32,256]{2,1,0:T(8,128)(2,1)S(1)} %get-tuple-element.36), channel_id=1, source_target_pairs={{0,16},{16,0},{32,48},{48,32},{64,80},{80,64},{96,112},{112,96},{1... | collective-permute-start | bytes 786440 | tf_op jit(solution)/shard_map/ppermute | solution.py:86
  64.0 22.5 %collective-permute-start.1 = (bf16[16,32,256]{2,1,0:T(8,128)(2,1)S(1)}, bf16[16,32,256]{2,1,0:T(8,128)(2,1)S(1)}, u32[]{:S(2)}, u32[]{:S(2)}) collective-permute-start(bf16[16,32,256]{2,1,0:T(8,128)(2,1)S(1)} %get-tuple-element.37), channel_id=1, source_target_pairs={{0,16},{16,0},{32,48},{48,32},{64,80},{80,64},{96,112},{112,96},{1... | collective-permute-start | bytes 786440 | tf_op jit(solution)/shard_map/ppermute | solution.py:87
  86.8 0.7 copy-start.20
  86.9 1.0 copy-start.5
  86.9 2.1 %copy-start.7 = (bf16[16,2,32,256]{3,2,1,0:T(8,128)(2,1)}, bf16[16,2,32,256]{3,2,1,0:T(8,128)(2,1)S(1)}, u32[]{:S(2)}) copy-start(bf16[16,2,32,256]{3,2,1,0:T(8,128)(2,1)S(1)} %pad_maximum_fusion.1) | copy-start | bytes 1572868
  87.9 7.9 %copy-start.21 = (f32[256,256]{1,0:T(8,128)}, f32[256,256]{1,0:T(8,128)S(1)}, u32[]{:S(2)}) copy-start(f32[256,256]{1,0:T(8,128)S(1)} %convolution_add_fusion) | copy-start | bytes 786436
  87.9 18.1 %copy-start.12 = (f32[1024]{0:T(1024)S(1)}, f32[1024]{0:T(1024)}, u32[]{:S(2)}) copy-start(f32[1024]{0:T(1024)} %param.19) | copy-start | bytes 12292
  89.0 16.9 %all-to-all-start.2 = ((bf16[16,16,1024]{2,1,0:T(8,128)(2,1)}), bf16[16,16,1024]{2,1,0:T(8,128)(2,1)S(1)}, u32[]{:S(2)}, u32[]{:S(2)}) async-start(bf16[16,16,1024]{2,1,0:T(8,128)(2,1)} %bitcast.24), calls=%async_computation.2 | async-start | bytes 1048576 | tf_op jit(solution)/shard_map/all_to_all | solution.py:12
  106.0 16.1 %copy-start.2 = (bf16[1280,768]{1,0:T(8,128)(2,1)S(1)}, bf16[1280,768]{1,0:T(8,128)(2,1)}, u32[]{:S(2)}) copy-start(bf16[1280,768]{1,0:T(8,128)(2,1)} %copy-done.1) | copy-start | bytes 5898244
  122.0 0.8 copy-start.14
  125.4 13.7 %all-to-all-start.4 = ((bf16[16,16,896]{2,1,0:T(8,128)(2,1)}), bf16[16,16,896]{2,1,0:T(8,128)(2,1)S(1)}, u32[]{:S(2)}, u32[]{:S(2)}) async-start(bf16[16,16,896]{2,1,0:T(8,128)(2,1)} %bitcast.28), calls=%async_computation.4 | async-start | bytes 917504 | tf_op jit(solution)/shard_map/all_to_all | solution.py:12
  146.3 1.8 copy-start.3
  147.9 14.5 %copy-start.6 = (bf16[16,2,32,256]{3,2,1,0:T(8,128)(2,1)S(1)}, bf16[16,2,32,256]{3,2,1,0:T(8,128)(2,1)}, u32[]{:S(2)}) copy-start(bf16[16,2,32,256]{3,2,1,0:T(8,128)(2,1)} %copy-done.5) | copy-start | bytes 1572868
  147.9 14.5 %copy-start.8 = (bf16[16,2,32,256]{3,2,1,0:T(8,128)(2,1)S(1)}, bf16[16,2,32,256]{3,2,1,0:T(8,128)(2,1)}, u32[]{:S(2)}) copy-start(bf16[16,2,32,256]{3,2,1,0:T(8,128)(2,1)} %copy-done.7) | copy-start | bytes 1572868
  147.9 14.5 %copy-start.22 = (f32[256,256]{1,0:T(8,128)S(1)}, f32[256,256]{1,0:T(8,128)}, u32[]{:S(2)}) copy-start(f32[256,256]{1,0:T(8,128)} %copy-done.21) | copy-start | bytes 786436
  162.5 6.9 %copy-start.16 = (f32[16]{0:T(128)S(1)}, f32[16]{0:T(128)}, u32[]{:S(2)}) copy-start(f32[16]{0:T(128)} %get-tuple-element.17) | copy-start | bytes 196
  162.5 6.9 %copy-start.17 = (f32[16]{0:T(128)S(1)}, f32[16]{0:T(128)}, u32[]{:S(2)}) copy-start(f32[16]{0:T(128)} %get-tuple-element.18) | copy-start | bytes 196
  162.5 16.2 %copy-start.4 = (f32[16,1024]{1,0:T(8,128)S(1)}, f32[16,1024]{1,0:T(8,128)}, u32[]{:S(2)}) copy-start(f32[16,1024]{1,0:T(8,128)} %get-tuple-element.59) | copy-start | bytes 196612
  164.0 26.4 %copy-start.10 = (bf16[256,64]{0,1:T(8,128)(2,1)S(1)}, bf16[256,64]{0,1:T(8,128)(2,1)}, u32[]{:S(2)}) copy-start(bf16[256,64]{0,1:T(8,128)(2,1)} %param.13) | copy-start | bytes 98308
  164.0 14.5 %all-to-all-start.6 = ((bf16[16,16,1024]{2,1,0:T(8,128)(2,1)}), bf16[16,16,1024]{2,1,0:T(8,128)(2,1)S(1)}, u32[]{:S(2)}, u32[]{:S(2)}) async-start(bf16[16,16,1024]{2,1,0:T(8,128)(2,1)} %bitcast.36), calls=%async_computation.6 | async-start | bytes 1048576 | tf_op jit(solution)/shard_map/all_to_all | solution.py:12
Sparse Core Ops, SparseCore 0:
  66.5 39.8 all-gather.1

commit v2 on v1

--- a/solution.py
+++ b/solution.py
@@ -1,6 +1,8 @@
 import jax
 import jax.numpy as jnp
 from jax import lax
+from jax.experimental import pallas as pl
+from jax.experimental.pallas import tpu as pltpu
 from jax.sharding import PartitionSpec as P
 
 WIDTH = 1024
@@ -36,6 +38,77 @@
     first = jnp.mean(scaled, axis=1, keepdims=True)
     second = jnp.mean(scaled * normed, axis=1, keepdims=True)
     return (scaled - first - normed * second) * rstd
+
+
+def vmem_call(body, outs, *args):
+    return pl.pallas_call(
+        body,
+        out_shape=[jax.ShapeDtypeStruct(s, d) for s, d in outs],
+        in_specs=[pl.BlockSpec(memory_space=pltpu.VMEM)] * len(args),
+        out_specs=[pl.BlockSpec(memory_space=pltpu.VMEM)] * len(outs),
+        compiler_params=pltpu.CompilerParams(vmem_limit_bytes=32 << 20),
+    )(*args)
+
+
+def embed_kernel(mixed, own, bias, gain_out, bias_out, proj, sent, unit, norm, yhat, rstd):
+    n = mixed.shape[0]
+    total = own[...] + bias[...]
+    for j in range(n):
+        total += mixed[j].astype(F32)
+    normed, scale = row_norm(total)
+    yhat[...] = normed
+    rstd[...] = jnp.broadcast_to(scale, rstd.shape)
+    post_normed = (normed * gain_out[...] + bias_out[...]).astype(BF)
+    embedding = jnp.dot(post_normed, proj[...], preferred_element_type=F32)
+    length = jnp.sqrt(jnp.sum(embedding * embedding, axis=1, keepdims=True) + 1e-06)
+    norm[...] = jnp.broadcast_to(length, norm.shape)
+    vec = embedding / length
+    unit[...] = vec
+    low = vec.astype(BF)
+    for j in range(n):
+        sent[j] = low
+
+
+def embed_back_kernel(back, label_rows, unit, norm, yhat, rstd, gain_out, proj, sent, grad):
+    n = back.shape[0]
+    emb = unit.shape[1]
+    stats = [back[j, :, emb:].astype(F32) for j in range(n)]
+    top = stats[0][:, 0:1]
+    for j in range(1, n):
+        top = jnp.maximum(top, stats[j][:, 0:1])
+    rest = jnp.zeros_like(top)
+    hit = jnp.zeros_like(top)
+    unit_grad = jnp.zeros(unit.shape, F32)
+    for j in range(n):
+        weight = jnp.exp(stats[j][:, 0:1] - top)
+        rest += weight * (stats[j][:, 1:2] + stats[j][:, 2:3])
+        hit += weight * (stats[j][:, 3:4] + stats[j][:, 4:5])
+        unit_grad += weight * back[j, :, :emb].astype(F32)
+    unit_grad = (unit_grad - rest * label_rows[...]) * (100.0 / (rest + hit))
+    vec = unit[...]
+    along = jnp.sum(vec * unit_grad, axis=1, keepdims=True)
+    emb_grad = ((unit_grad - vec * along) / norm[:, 0:1]).astype(BF)
+    post_grad = lax.dot_general(
+        emb_grad, proj[...], (((1,), (1,)), ((), ())), preferred_element_type=F32
+    )
+    out_grad = norm_back(post_grad * gain_out[...], yhat[...], rstd[:, 0:1])
+    grad[...] = out_grad
+    low = out_grad.astype(BF)
+    for j in range(n):
+        sent[j] = low
+
+
+def result_kernel(parts, gain, own, out_grad, step, sent):
+    n, _, share = sent.shape
+    total = parts[0].astype(F32)
+    for j in range(1, n):
+        total += parts[j].astype(F32)
+    xhat, scale = row_norm(own[...])
+    grad = out_grad[...] + norm_back(total * gain[...], xhat, scale)
+    rms = jnp.sqrt(jnp.mean(grad * grad, axis=1, keepdims=True) + 1e-06)
+    change = step[0:1, 0:1] * grad / rms
+    for j in range(n):
+        sent[j] = change[:, j * share : (j + 1) * share]
 
 
 def local(
@@ -78,21 +151,32 @@
     label_text = label_text.reshape(n_txt, rows * emb // images, images)
     vectors = jnp.stack(pieces(post_gain, 3) + pieces(post_bias, 3))
     vectors = jnp.pad(vectors, ((0, 2), (0, images - share)))
-    message = jnp.concatenate(
-        [copies(resid.T, n_txt), label_text, copies(vectors, n_txt)], axis=1
-    )
+    message = jnp.concatenate([label_text, copies(vectors, n_txt)], axis=1)
+
+    def from_partner(x, bits):
+        return lax.ppermute(x, "txt", [(i, i ^ bits) for i in range(n_txt)])
+
+    state = resid.T
+    state = jnp.stack([state] + [from_partner(state, 4 * k) for k in (1, 2, 3)])
+    state = jnp.stack([state, from_partner(state, 2)], axis=1)
+    state = jnp.stack([state, from_partner(state, 1)], axis=2)
+    state = state.reshape(2, 2, 2, 2, share, images)
+    for axis in range(4):
+        bit = lax.rem(lax.shift_right_logical(me, 3 - axis), 2) == 1
+        state = jnp.where(bit, jnp.flip(state, axis), state)
+    state = state.reshape(n_txt * share, images)
+
     mine, message = lax.optimization_barrier((mine, message))
     pairs = [(i, i ^ 1) for i in range(n_dp)]
     other_up = lax.ppermute(mine[:, 0], "dp", pairs)
     other_down = lax.ppermute(mine[:, 1], "dp", pairs)
     message = swapped(message, "txt")
 
-    state = message[:, :share].reshape(n_txt * share, images)
-    label_rows = jnp.sum(message[:, share : share + rows * emb // images].astype(F32), axis=0)
+    label_rows = jnp.sum(message[:, : rows * emb // images].astype(F32), axis=0)
     label_rows = label_rows.reshape(emb // images, rows, images).transpose(1, 0, 2).reshape(rows, emb)
     vectors = message[:, -8:, :share].astype(F32)
-    gain_out = (vectors[:, 0] + vectors[:, 1] + vectors[:, 2]).reshape(-1)
-    bias_out = (vectors[:, 3] + vectors[:, 4] + vectors[:, 5]).reshape(-1)
+    gain_out = (vectors[:, 0] + vectors[:, 1] + vectors[:, 2]).reshape(1, WIDTH)
+    bias_out = (vectors[:, 3] + vectors[:, 4] + vectors[:, 5]).reshape(1, WIDTH)
 
     first = lax.rem(lax.axis_index("dp"), 2) == 0
 
@@ -118,13 +202,23 @@
         lax.broadcasted_iota(jnp.int32, (rows, images), 0) + me * rows
     )
     own = jnp.einsum("ri,di->rd", pick.astype(BF), state, preferred_element_type=F32)
-    block_out = own + jnp.sum(mixed.astype(F32), axis=0) + down_bias
-    yhat, rstd_out = row_norm(block_out)
-    post_normed = (yhat * gain_out + bias_out).astype(BF)
-    embedding = jnp.dot(post_normed, proj, preferred_element_type=F32)
-    emb_norm = jnp.sqrt(jnp.sum(embedding * embedding, axis=1, keepdims=True) + 1e-06)
-    unit_vec = embedding / emb_norm
-    unit_low = swapped(copies(unit_vec.astype(BF), n_txt), "txt").reshape(images, emb)
+    sent, unit_vec, emb_norm, yhat, rstd_out = vmem_call(
+        embed_kernel,
+        (
+            ((n_txt, rows, emb), BF),
+            ((rows, emb), F32),
+            ((rows, 128), F32),
+            ((rows, WIDTH), F32),
+            ((rows, 128), F32),
+        ),
+        mixed,
+        own,
+        down_bias[None],
+        gain_out,
+        bias_out,
+        proj,
+    )
+    unit_low = swapped(sent, "txt").reshape(images, emb)
 
     logits = 100.0 * jnp.einsum("ie,je->ij", unit_low, text_unit, preferred_element_type=F32)
     top = lax.reduce_precision(jnp.max(logits, axis=1), 8, 7)
@@ -136,31 +230,35 @@
     stats = jnp.stack(pieces(top, 1) + pieces(rest, 2) + pieces(hit, 2), axis=1)
     stats = jnp.pad(stats, ((0, 0), (0, 128 - stats.shape[1])))
     back = jnp.concatenate([back, stats], axis=1).reshape(n_txt, rows, emb + 128)
-    back = swapped(back, "txt").astype(F32)
-
-    stats = back[:, :, emb:]
-    top = stats[:, :, 0]
-    weight = jnp.exp(top - jnp.max(top, axis=0))
-    rest = jnp.sum(weight * (stats[:, :, 1] + stats[:, :, 2]), axis=0)[:, None]
-    hit = jnp.sum(weight * (stats[:, :, 3] + stats[:, :, 4]), axis=0)[:, None]
-    unit_grad = jnp.sum(weight[:, :, None] * back[:, :, :emb], axis=0)
-    unit_grad = (unit_grad - rest * label_rows) * (100.0 / (rest + hit))
-    along = jnp.sum(unit_vec * unit_grad, axis=1, keepdims=True)
-    emb_grad = ((unit_grad - unit_vec * along) / emb_norm).astype(BF)
-    post_grad = jnp.einsum("ie,de->id", emb_grad, proj, preferred_element_type=F32)
-    out_grad = norm_back(post_grad * gain_out, yhat, rstd_out)
-    out_low = swapped(copies(out_grad.astype(BF), n_txt), "txt").reshape(images, WIDTH)
+    back = swapped(back, "txt")
+
+    sent, out_grad = vmem_call(
+        embed_back_kernel,
+        (((n_txt, rows, WIDTH), BF), ((rows, WIDTH), F32)),
+        back,
+        label_rows,
+        unit_vec,
+        emb_norm,
+        yhat,
+        rstd_out,
+        gain_out,
+        proj,
+    )
+    out_low = swapped(sent, "txt").reshape(images, WIDTH)
 
     hid_grad = jnp.einsum("id,df->if", out_low, w_down, preferred_element_type=F32)
     act_grad = (hid_grad * (gate + 1.702 * pre_act * gate * (1.0 - gate))).astype(BF)
     normed_grad = jnp.einsum("if,df->id", act_grad, w_up, preferred_element_type=F32).astype(BF)
     normed_grad = swapped(normed_grad.reshape(n_txt, rows, WIDTH), "txt")
-    normed_grad = jnp.sum(normed_grad.astype(F32), axis=0)
-    xhat, rstd_own = row_norm(own)
-    input_grad = out_grad + norm_back(normed_grad * prenorm_gain, xhat, rstd_own)
-    rms = jnp.sqrt(jnp.mean(input_grad * input_grad, axis=1, keepdims=True) + 1e-06)
-    change = step_size[0] * input_grad / rms
-    change = change.reshape(rows, n_txt, share).transpose(1, 0, 2)
+    (change,) = vmem_call(
+        result_kernel,
+        (((n_txt, rows, share), F32),),
+        normed_grad,
+        prenorm_gain[None],
+        own,
+        out_grad,
+        step_size[None],
+    )
     change = swapped(change, "txt").reshape(images, share)
     return resid.astype(F32) + change
 

time: 199 us -> 182 us (0.915)
  waiting for transfers between devices: 64.5 us -> 40.7 us
  starting transfers between devices: 50.2 us -> 65.9 us
  other arithmetic: 14.8 us -> 9.82 us
  local copies, waits for them, and re-layouts: 8.83 us -> 4.55 us
  matrix products: 10.3 us -> 8.12 us
    ppermute x0 -> x5, starting transfers between devices: none -> 18.4 us  [from_partner(): return lax.ppermute(x, 'txt', [(i, i ^ bits) for i in range(n_txt)])]
    ppermute x1, waiting for transfers between devices: 12.9 us -> 0.01 us  [local(): other_up = lax.ppermute(mine[:, 0], 'dp', pairs)]
    ppermute x1, waiting for transfers between devices: 6.98 us -> 0.01 us  [local(): other_down = lax.ppermute(mine[:, 1], 'dp', pairs)]
    all_to_all x2 -> x1, local copies, waits for them, and re-layouts: 5.08 us -> 0.51 us  [swapped(): return lax.all_to_all(x, axis, 0, 0, tiled=True, axis_index_groups=groups)]
    all_to_all x5, waiting for transfers between devices: 44.6 us -> 40.1 us  [swapped(): return lax.all_to_all(x, axis, 0, 0, tiled=True, axis_index_groups=groups)]
    convert_element_type x3 -> x0, other arithmetic: 2.78 us -> none  [the longest x1 2.61 us: local(): back = swapped(back, 'txt').astype(F32)]
    all_to_all x5, starting transfers between devices: 43.4 us -> 40.7 us  [swapped(): return lax.all_to_all(x, axis, 0, 0, tiled=True, axis_index_groups=groups)]
    dot_general x2 -> x0, matrix products: 2.53 us -> none  [the longest x1 1.88 us: local(): embedding = jnp.dot(post_normed, proj, preferred_element_type=F32)]
  transfers between devices with their start and end apart: 8 -> 13, of which waited for: 6 -> 6; matrix products, arithmetic and copies ran while one was open for 6% -> 7% of each run, Pallas kernels for 0% -> 0%
where the time goes in v2:
time: 182 us; the launch traced here: 180 us
  starting transfers between devices  65.9 us (36%)
  waiting for transfers between devices  40.7 us (22%)
  blocking collectives  35 us (19%)
  between operations  14.6 us (8%)
  other arithmetic  9.82 us (5%)
  matrix products  8.12 us (4%)
  local copies, waits for them, and re-layouts  4.55 us (2%)
  Pallas kernels  1.91 us (1%)
    all_to_all x5, starting transfers between devices, swapped(): return lax.all_to_all(x, axis, 0, 0, tiled=True, axis_index_groups=groups)  40.7 us
    all_to_all x5, waiting for transfers between devices, swapped(): return lax.all_to_all(x, axis, 0, 0, tiled=True, axis_index_groups=groups)  40.1 us
    all_to_all x3, blocking collectives, swapped(): return lax.all_to_all(x, axis, 0, 0, tiled=True, axis_index_groups=groups)  35 us
    ppermute x5, starting transfers between devices, from_partner(): return lax.ppermute(x, 'txt', [(i, i ^ bits) for i in range(n_txt)])  18.4 us
    ppermute x1, starting transfers between devices, local(): other_down = lax.ppermute(mine[:, 1], 'dp', pairs)  4.65 us
  transfers between devices with their start and end apart: 13, of which 6 were waited for; matrix products, arithmetic and copies ran while one was open for 7% of the time, Pallas kernels for 0%

profile of v2, /device:TPU:1, one launch (start us, length us, event | category | flops | bytes accessed | tf_op | source)
XLA Modules:
  0.0 180.5 jit_solution(17246678403197577807)
XLA Ops:
  6.5 5.6 %collective-permute-start.1 = (bf16[64,256]{1,0:T(8,128)(2,1)}, bf16[64,256]{1,0:T(8,128)(2,1)S(1)}, u32[]{:S(2)}, u32[]{:S(2)}) collective-permute-start(bf16[64,256]{1,0:T(8,128)(2,1)} %bitcast.103), channel_id=1, source_target_pairs={{0,8},{1,9},{2,10},{3,11},{4,12},{5,13},{6,14},{7,15},{8,0},{9,1},... | collective-permute-start | bytes 98312 | tf_op jit(solution)/shard_map/ppermute | solution.py:157
  12.2 2.3 %collective-permute-start = (bf16[64,256]{1,0:T(8,128)(2,1)}, bf16[64,256]{1,0:T(8,128)(2,1)S(1)}, u32[]{:S(2)}, u32[]{:S(2)}) collective-permute-start(bf16[64,256]{1,0:T(8,128)(2,1)} %bitcast.104), channel_id=1, source_target_pairs={{0,4},{1,5},{2,6},{3,7},{4,0},{5,1},{6,2},{7,3},{8,12},{9,13},{10,... | collective-permute-start | bytes 98312 | tf_op jit(solution)/shard_map/ppermute | solution.py:157
  14.5 2.3 %collective-permute-start.2 = (bf16[64,256]{1,0:T(8,128)(2,1)}, bf16[64,256]{1,0:T(8,128)(2,1)S(1)}, u32[]{:S(2)}, u32[]{:S(2)}) collective-permute-start(bf16[64,256]{1,0:T(8,128)(2,1)} %bitcast.105), channel_id=1, source_target_pairs={{0,12},{1,13},{2,14},{3,15},{4,8},{5,9},{6,10},{7,11},{8,4},{9,5},... | collective-permute-start | bytes 98312 | tf_op jit(solution)/shard_map/ppermute | solution.py:157
  17.6 0.9 broadcast_in_dim.30
  18.4 15.0 %all-to-all-start = ((bf16[16,2,32,256]{3,2,1,0:T(8,128)(2,1)}), bf16[16,2,32,256]{3,2,1,0:T(8,128)(2,1)S(1)}, u32[]{:S(2)}, u32[]{:S(2)}) async-start(bf16[16,2,32,256]{3,2,1,0:T(8,128)(2,1)} %broadcast_in_dim.30), calls=%async_computation | async-start | bytes 1048576 | tf_op jit(solution)/shard_map/all_to_all | solution.py:14
  33.5 2.0 %fusion = f32[1280]{0:T(1024)S(1)} fusion(bf16[1280,768]{1,0:T(8,128)(2,1)} %param.23), kind=kLoop, calls=%fused_computation.2 | loop fusion | flops 2947840 | bytes 1971200 | tf_op jit(solution)/shard_map/reduce_sum | solution.py:144
  35.5 1.7 fusion.1
  37.4 3.3 %collective-permute-start.3 = (bf16[4,64,256]{2,1,0:T(8,128)(2,1)S(1)}, bf16[4,64,256]{2,1,0:T(8,128)(2,1)S(1)}, u32[]{:S(2)}, u32[]{:S(2)}) collective-permute-start(bf16[4,64,256]{2,1,0:T(8,128)(2,1)S(1)} %get-tuple-element.39), channel_id=1, source_target_pairs={{0,2},{1,3},{2,0},{3,1},{4,6},{5,7},{6,4},{7,5},{8,10},{9,11},{10,... | collective-permute-start | bytes 393224 | tf_op jit(solution)/shard_map/ppermute | solution.py:157
  40.7 2.3 %fusion.4 = bf16[256,768]{1,0:T(8,128)(2,1)S(1)} fusion(bf16[1280,768]{1,0:T(8,128)(2,1)} %fusion.1, s32[256]{0:T(256)S(1)} %broadcast_subtract_fusion), kind=kOutput, calls=%fused_computation.15 | convolution fusion | flops 503840768 | bytes 2360320 | tf_op jit(solution)/shard_map/dot_general | solution.py:148
  43.6 4.9 %collective-permute-start.4 = (bf16[4,2,64,256]{3,2,0,1:T(8,128)(2,1)S(1)}, bf16[4,2,64,256]{3,2,0,1:T(8,128)(2,1)S(1)}, u32[]{:S(2)}, u32[]{:S(2)}) collective-permute-start(bf16[4,2,64,256]{3,2,0,1:T(8,128)(2,1)S(1)} %pad_maximum_fusion.4), channel_id=1, source_target_pairs={{0,1},{1,0},{2,3},{3,2},{4,5},{5,4},{6,7},{7,6},{8,9},{9,8},{10,11... | collective-permute-start | bytes 786440 | tf_op jit(solution)/shard_map/ppermute | solution.py:157
  49.0 0.8 pad_maximum_fusion.3
  50.6 5.8 %all-to-all-done = bf16[16,2,32,256]{3,2,1,0:T(8,128)(2,1)S(1)} async-done(((bf16[16,2,32,256]{3,2,1,0:T(8,128)(2,1)}), bf16[16,2,32,256]{3,2,1,0:T(8,128)(2,1)S(1)}, u32[]{:S(2)}, u32[]{:S(2)}) %all-to-all-start) | async-done | bytes 524320 | tf_op jit(solution)/shard_map/all_to_all | solution.py:14
  56.3 4.7 %collective-permute-start.6 = (bf16[16,32,256]{2,1,0:T(8,128)(2,1)S(1)}, bf16[16,32,256]{2,1,0:T(8,128)(2,1)S(1)}, u32[]{:S(2)}, u32[]{:S(2)}) collective-permute-start(bf16[16,32,256]{2,1,0:T(8,128)(2,1)S(1)} %get-tuple-element.36), channel_id=1, source_target_pairs={{0,16},{16,0},{32,48},{48,32},{64,80},{80,64},{96,112},{112,96},{1... | collective-permute-start | bytes 786440 | tf_op jit(solution)/shard_map/ppermute | solution.py:172
  61.0 2.1 %collective-permute-start.5 = (bf16[16,32,256]{2,1,0:T(8,128)(2,1)S(1)}, bf16[16,32,256]{2,1,0:T(8,128)(2,1)S(1)}, u32[]{:S(2)}, u32[]{:S(2)}) collective-permute-start(bf16[16,32,256]{2,1,0:T(8,128)(2,1)S(1)} %get-tuple-element.37), channel_id=1, source_target_pairs={{0,16},{16,0},{32,48},{48,32},{64,80},{80,64},{96,112},{112,96},{1... | collective-permute-start | bytes 786440 | tf_op jit(solution)/shard_map/ppermute | solution.py:171
  63.5 12.0 %all-to-all-start.2 = ((bf16[16,56,256]{2,1,0:T(8,128)(2,1)}), bf16[16,56,256]{2,1,0:T(8,128)(2,1)S(1)}, u32[]{:S(2)}, u32[]{:S(2)}) async-start(bf16[16,56,256]{2,1,0:T(8,128)(2,1)} %pad_maximum_fusion.3), calls=%async_computation.2 | async-start | bytes 917504 | tf_op jit(solution)/shard_map/all_to_all | solution.py:14
  76.9 1.1 convolution_convert_fusion.1
  78.1 6.6 %all-to-all-done.2 = bf16[16,56,256]{2,1,0:T(8,128)(2,1)S(1)} async-done(((bf16[16,56,256]{2,1,0:T(8,128)(2,1)}), bf16[16,56,256]{2,1,0:T(8,128)(2,1)S(1)}, u32[]{:S(2)}, u32[]{:S(2)}) %all-to-all-start.2) | async-done | bytes 458784 | tf_op jit(solution)/shard_map/all_to_all | solution.py:14
  84.6 4.5 %all-to-all-start.1 = ((bf16[16,16,1024]{2,1,0:T(8,128)(2,1)}), bf16[16,16,1024]{2,1,0:T(8,128)(2,1)S(1)}, u32[]{:S(2)}, u32[]{:S(2)}) async-start(bf16[16,16,1024]{2,1,0:T(8,128)(2,1)} %bitcast.31), calls=%async_computation.1 | async-start | bytes 1048576 | tf_op jit(solution)/shard_map/all_to_all | solution.py:14
  89.7 9.4 %all-to-all-done.1.mixed = bf16[16,16,1024]{2,1,0:T(8,128)(2,1)S(1)} async-done(((bf16[16,16,1024]{2,1,0:T(8,128)(2,1)}), bf16[16,16,1024]{2,1,0:T(8,128)(2,1)S(1)}, u32[]{:S(2)}, u32[]{:S(2)}) %all-to-all-start.1) | async-done | bytes 524320 | tf_op jit(solution)/shard_map/all_to_all | solution.py:14
  99.1 1.4 copy-done
  101.1 12.1 %all_to_all.40 = bf16[16,16,768]{2,1,0:T(8,128)(2,1)S(1)} all-to-all(bf16[16,16,768]{2,1,0:T(8,128)(2,1)S(1)} %get-tuple-element.16), channel_id=1, replica_groups=mesh['dp'=32,'txt'=16] {'txt'}, dimensions={0} | all-to-all | bytes 786432 | tf_op jit(solution)/shard_map/all_to_all | solution.py:14
  114.0 0.8 convolution_convert_fusion.2
  115.7 0.8 fusion.19
  116.5 4.5 %all-to-all-start.4 = ((bf16[16,16,896]{2,1,0:T(8,128)(2,1)}), bf16[16,16,896]{2,1,0:T(8,128)(2,1)S(1)}, u32[]{:S(2)}, u32[]{:S(2)}) async-start(bf16[16,16,896]{2,1,0:T(8,128)(2,1)} %bitcast.37), calls=%async_computation.4 | async-start | bytes 917504 | tf_op jit(solution)/shard_map/all_to_all | solution.py:14
  121.1 9.1 %all-to-all-done.4.back = bf16[16,16,896]{2,1,0:T(8,128)(2,1)S(1)} async-done(((bf16[16,16,896]{2,1,0:T(8,128)(2,1)}), bf16[16,16,896]{2,1,0:T(8,128)(2,1)S(1)}, u32[]{:S(2)}, u32[]{:S(2)}) %all-to-all-start.4) | async-done | bytes 458784 | tf_op jit(solution)/shard_map/all_to_all | solution.py:14
  130.2 1.0 shard_map.128
  131.2 13.5 %all_to_all.41 = bf16[16,16,1024]{2,1,0:T(8,128)(2,1)S(1)} all-to-all(bf16[16,16,1024]{2,1,0:T(8,128)(2,1)S(1)} %get-tuple-element.21), channel_id=1, replica_groups=mesh['dp'=32,'txt'=16] {'txt'}, dimensions={0} | all-to-all | bytes 1048576 | tf_op jit(solution)/shard_map/all_to_all | solution.py:14
  144.7 2.5 %convolution_convert_fusion = bf16[256,1024]{1,0:T(8,128)(2,1)} fusion(bf16[1024,256]{1,0:T(8,128)(2,1)S(1)} %bitcast.96, bf16[256,1024]{1,0:T(8,128)(2,1)S(1)} %bitcast.98, bf16[1024,256]{1,0:T(8,128)(2,1)S(1)} %bitcast.94, f32[256,256]{1,0:T(8,128)} %copy-done.14), kind=kOutput, calls=%fused_computation.13 | convolution fusion | flops 269352960 | bytes 2359296 | tf_op jit(solution)/shard_map/if,df->id/dot_general | solution.py:251
  147.1 4.5 %all-to-all-start.6 = ((bf16[16,16,1024]{2,1,0:T(8,128)(2,1)}), bf16[16,16,1024]{2,1,0:T(8,128)(2,1)S(1)}, u32[]{:S(2)}, u32[]{:S(2)}) async-start(bf16[16,16,1024]{2,1,0:T(8,128)(2,1)} %bitcast.41), calls=%async_computation.6 | async-start | bytes 1048576 | tf_op jit(solution)/shard_map/all_to_all | solution.py:14
  152.3 9.2 %all-to-all-done.6.parts = bf16[16,16,1024]{2,1,0:T(8,128)(2,1)S(1)} async-done(((bf16[16,16,1024]{2,1,0:T(8,128)(2,1)}), bf16[16,16,1024]{2,1,0:T(8,128)(2,1)S(1)}, u32[]{:S(2)}, u32[]{:S(2)}) %all-to-all-start.6) | async-done | bytes 524320 | tf_op jit(solution)/shard_map/all_to_all | solution.py:14
  162.1 9.4 %all_to_all.42 = f32[16,1,1024]{2,1,0:T(1,128)S(1)} all-to-all(f32[16,1,1024]{2,1,0:T(1,128)S(1)} %reshape.240), channel_id=1, replica_groups=mesh['dp'=32,'txt'=16] {'txt'}, dimensions={0} | all-to-all | bytes 131072 | tf_op jit(solution)/shard_map/all_to_all | solution.py:14
  172.0 0.8 reduce.10
  (89 shorter events, 8.9 us)
Async XLA Ops:
  6.5 92.5 %all-gather.2.cloned.1.call-start = ((), (), s32[]{:S(2)}) async-start(), calls=%async_computation.8 | async-start | bytes 1671168 | tf_op jit(solution)/shard_map/all_gather | solution.py:137
  6.5 30.7 %collective-permute-start.1 = (bf16[64,256]{1,0:T(8,128)(2,1)}, bf16[64,256]{1,0:T(8,128)(2,1)S(1)}, u32[]{:S(2)}, u32[]{:S(2)}) collective-permute-start(bf16[64,256]{1,0:T(8,128)(2,1)} %bitcast.103), channel_id=1, source_target_pairs={{0,8},{1,9},{2,10},{3,11},{4,12},{5,13},{6,14},{7,15},{8,0},{9,1},... | collective-permute-start | bytes 98312 | tf_op jit(solution)/shard_map/ppermute | solution.py:157
  12.2 25.1 %collective-permute-start = (bf16[64,256]{1,0:T(8,128)(2,1)}, bf16[64,256]{1,0:T(8,128)(2,1)S(1)}, u32[]{:S(2)}, u32[]{:S(2)}) collective-permute-start(bf16[64,256]{1,0:T(8,128)(2,1)} %bitcast.104), channel_id=1, source_target_pairs={{0,4},{1,5},{2,6},{3,7},{4,0},{5,1},{6,2},{7,3},{8,12},{9,13},{10,... | collective-permute-start | bytes 98312 | tf_op jit(solution)/shard_map/ppermute | solution.py:157
  14.5 22.8 %collective-permute-start.2 = (bf16[64,256]{1,0:T(8,128)(2,1)}, bf16[64,256]{1,0:T(8,128)(2,1)S(1)}, u32[]{:S(2)}, u32[]{:S(2)}) collective-permute-start(bf16[64,256]{1,0:T(8,128)(2,1)} %bitcast.105), channel_id=1, source_target_pairs={{0,12},{1,13},{2,14},{3,15},{4,8},{5,9},{6,10},{7,11},{8,4},{9,5},... | collective-permute-start | bytes 98312 | tf_op jit(solution)/shard_map/ppermute | solution.py:157
  18.4 17.1 %copy-start.4 = (bf16[1280,768]{1,0:T(8,128)(2,1)S(1)}, bf16[1280,768]{1,0:T(8,128)(2,1)}, u32[]{:S(2)}) copy-start(bf16[1280,768]{1,0:T(8,128)(2,1)} %param.23) | copy-start | bytes 5898244
  18.4 37.9 %all-to-all-start = ((bf16[16,2,32,256]{3,2,1,0:T(8,128)(2,1)}), bf16[16,2,32,256]{3,2,1,0:T(8,128)(2,1)S(1)}, u32[]{:S(2)}, u32[]{:S(2)}) async-start(bf16[16,2,32,256]{3,2,1,0:T(8,128)(2,1)} %broadcast_in_dim.30), calls=%async_computation | async-start | bytes 1048576 | tf_op jit(solution)/shard_map/all_to_all | solution.py:14
  35.5 1.8 copy-start.10
  35.5 1.8 copy-start.8
  37.4 11.2 %copy-start.11 = (f32[64]{0:T(128)S(1)}, f32[64]{0:T(128)}, u32[]{:S(2)}) copy-start(f32[64]{0:T(128)} %param.20) | copy-start | bytes 772
  37.4 11.2 %copy-start.12 = (f32[64]{0:T(128)S(1)}, f32[64]{0:T(128)}, u32[]{:S(2)}) copy-start(f32[64]{0:T(128)} %param.21) | copy-start | bytes 772
  37.4 11.2 %copy-start.9 = (f32[1024]{0:T(1024)S(1)}, f32[1024]{0:T(1024)}, u32[]{:S(2)}) copy-start(f32[1024]{0:T(1024)} %param.15) | copy-start | bytes 12292
  37.4 11.3 %copy-start.2 = (f32[1024]{0:T(1024)S(1)}, f32[1024]{0:T(1024)}, u32[]{:S(2)}) copy-start(f32[1024]{0:T(1024)} %param.14) | copy-start | bytes 12292
  37.4 6.1 %collective-permute-start.3 = (bf16[4,64,256]{2,1,0:T(8,128)(2,1)S(1)}, bf16[4,64,256]{2,1,0:T(8,128)(2,1)S(1)}, u32[]{:S(2)}, u32[]{:S(2)}) collective-permute-start(bf16[4,64,256]{2,1,0:T(8,128)(2,1)S(1)} %get-tuple-element.39), channel_id=1, source_target_pairs={{0,2},{1,3},{2,0},{3,1},{4,6},{5,7},{6,4},{7,5},{8,10},{9,11},{10,... | collective-permute-start | bytes 393224 | tf_op jit(solution)/shard_map/ppermute | solution.py:157
  43.6 6.3 %collective-permute-start.4 = (bf16[4,2,64,256]{3,2,0,1:T(8,128)(2,1)S(1)}, bf16[4,2,64,256]{3,2,0,1:T(8,128)(2,1)S(1)}, u32[]{:S(2)}, u32[]{:S(2)}) collective-permute-start(bf16[4,2,64,256]{3,2,0,1:T(8,128)(2,1)S(1)} %pad_maximum_fusion.4), channel_id=1, source_target_pairs={{0,1},{1,0},{2,3},{3,2},{4,5},{5,4},{6,7},{7,6},{8,9},{9,8},{10,11... | collective-permute-start | bytes 786440 | tf_op jit(solution)/shard_map/ppermute | solution.py:157
  56.3 19.2 %collective-permute-start.6 = (bf16[16,32,256]{2,1,0:T(8,128)(2,1)S(1)}, bf16[16,32,256]{2,1,0:T(8,128)(2,1)S(1)}, u32[]{:S(2)}, u32[]{:S(2)}) collective-permute-start(bf16[16,32,256]{2,1,0:T(8,128)(2,1)S(1)} %get-tuple-element.36), channel_id=1, source_target_pairs={{0,16},{16,0},{32,48},{48,32},{64,80},{80,64},{96,112},{112,96},{1... | collective-permute-start | bytes 786440 | tf_op jit(solution)/shard_map/ppermute | solution.py:172
  61.0 14.6 %collective-permute-start.5 = (bf16[16,32,256]{2,1,0:T(8,128)(2,1)S(1)}, bf16[16,32,256]{2,1,0:T(8,128)(2,1)S(1)}, u32[]{:S(2)}, u32[]{:S(2)}) collective-permute-start(bf16[16,32,256]{2,1,0:T(8,128)(2,1)S(1)} %get-tuple-element.37), channel_id=1, source_target_pairs={{0,16},{16,0},{32,48},{48,32},{64,80},{80,64},{96,112},{112,96},{1... | collective-permute-start | bytes 786440 | tf_op jit(solution)/shard_map/ppermute | solution.py:171
  63.5 21.1 %all-to-all-start.2 = ((bf16[16,56,256]{2,1,0:T(8,128)(2,1)}), bf16[16,56,256]{2,1,0:T(8,128)(2,1)S(1)}, u32[]{:S(2)}, u32[]{:S(2)}) async-start(bf16[16,56,256]{2,1,0:T(8,128)(2,1)} %pad_maximum_fusion.3), calls=%async_computation.2 | async-start | bytes 917504 | tf_op jit(solution)/shard_map/all_to_all | solution.py:14
  75.9 0.7 copy-start.13
  76.0 2.1 %copy-start.6 = (bf16[16,2,32,256]{3,2,1,0:T(8,128)(2,1)}, bf16[16,2,32,256]{3,2,1,0:T(8,128)(2,1)S(1)}, u32[]{:S(2)}) copy-start(bf16[16,2,32,256]{3,2,1,0:T(8,128)(2,1)S(1)} %pad_maximum_fusion.1) | copy-start | bytes 1572868
  76.9 37.0 %copy-start.14 = (f32[256,256]{1,0:T(8,128)}, f32[256,256]{1,0:T(8,128)S(1)}, u32[]{:S(2)}) copy-start(f32[256,256]{1,0:T(8,128)S(1)} %convolution_add_fusion) | copy-start | bytes 786436
  78.1 21.0 %copy-start.3 = (f32[1024]{0:T(1024)S(1)}, f32[1024]{0:T(1024)}, u32[]{:S(2)}) copy-start(f32[1024]{0:T(1024)} %param.19) | copy-start | bytes 12292
  84.6 14.4 %all-to-all-start.1 = ((bf16[16,16,1024]{2,1,0:T(8,128)(2,1)}), bf16[16,16,1024]{2,1,0:T(8,128)(2,1)S(1)}, u32[]{:S(2)}, u32[]{:S(2)}) async-start(bf16[16,16,1024]{2,1,0:T(8,128)(2,1)} %bitcast.31), calls=%async_computation.1 | async-start | bytes 1048576 | tf_op jit(solution)/shard_map/all_to_all | solution.py:14
  99.1 1.4 copy-start
  100.5 12.7 %copy-start.5 = (bf16[1280,768]{1,0:T(8,128)(2,1)S(1)}, bf16[1280,768]{1,0:T(8,128)(2,1)}, u32[]{:S(2)}) copy-start(bf16[1280,768]{1,0:T(8,128)(2,1)} %fusion.1) | copy-start | bytes 5898244
  115.5 14.7 %copy-start.1 = (bf16[1024,768]{1,0:T(8,128)(2,1)S(1)}, bf16[1024,768]{1,0:T(8,128)(2,1)}, u32[]{:S(2)}) copy-start(bf16[1024,768]{1,0:T(8,128)(2,1)} %all-gather.2.cloned.1.call-done.proj) | copy-start | bytes 4718596
  116.5 13.7 %all-to-all-start.4 = ((bf16[16,16,896]{2,1,0:T(8,128)(2,1)}), bf16[16,16,896]{2,1,0:T(8,128)(2,1)S(1)}, u32[]{:S(2)}, u32[]{:S(2)}) async-start(bf16[16,16,896]{2,1,0:T(8,128)(2,1)} %bitcast.37), calls=%async_computation.4 | async-start | bytes 917504 | tf_op jit(solution)/shard_map/all_to_all | solution.py:14
  130.2 14.5 %copy-start.7 = (bf16[16,2,32,256]{3,2,1,0:T(8,128)(2,1)S(1)}, bf16[16,2,32,256]{3,2,1,0:T(8,128)(2,1)}, u32[]{:S(2)}) copy-start(bf16[16,2,32,256]{3,2,1,0:T(8,128)(2,1)} %copy-done.6) | copy-start | bytes 1572868
  147.1 14.4 %all-to-all-start.6 = ((bf16[16,16,1024]{2,1,0:T(8,128)(2,1)}), bf16[16,16,1024]{2,1,0:T(8,128)(2,1)S(1)}, u32[]{:S(2)}, u32[]{:S(2)}) async-start(bf16[16,16,1024]{2,1,0:T(8,128)(2,1)} %bitcast.41), calls=%async_computation.6 | async-start | bytes 1048576 | tf_op jit(solution)/shard_map/all_to_all | solution.py:14
Sparse Core Ops, SparseCore 0:
  17.0 46.2 all-gather.1

commit v3 on v2

v3 whole, which is shorter than its diff:
```python
import jax
import jax.numpy as jnp
from jax import lax
from jax.experimental import pallas as pl
from jax.experimental.pallas import tpu as pltpu
from jax.sharding import PartitionSpec as P

WIDTH = 1024
BF = jnp.bfloat16
F32 = jnp.float32
NT = (((1,), (1,)), ((), ()))
SMALL = pl.CostEstimate(flops=1024, bytes_accessed=1024, transcendentals=0)


def swapped(x, axis, groups=None):
    return lax.all_to_all(x, axis, 0, 0, tiled=True, axis_index_groups=groups)


def copies(x, n):
    return jnp.broadcast_to(x, (n, *x.shape))


def from_partner(x, axis, bits):
    pairs = [(i, i ^ bits) for i in range(lax.axis_size(axis))]
    return lax.ppermute(x, axis, pairs)


def pieces(x, count):
    out = []
    for _ in range(count):
        part = lax.reduce_precision(x, 8, 7)
        out.append(part.astype(BF))
        x = x - part
    return out


def row_norm(rows):
    mean = jnp.mean(rows, axis=1, keepdims=True)
    var = jnp.mean(rows * rows, axis=1, keepdims=True) - mean * mean
    rstd = lax.rsqrt(var + 1e-05)
    return (rows - mean) * rstd, rstd


def norm_back(scaled, normed, rstd):
    first = jnp.mean(scaled, axis=1, keepdims=True)
    second = jnp.mean(scaled * normed, axis=1, keepdims=True)
    return (scaled - first - normed * second) * rstd


def vmem_call(body, outs, *args, scalars=0, cost=None):
    smem = pl.BlockSpec(memory_space=pltpu.SMEM)
    vmem = pl.BlockSpec(memory_space=pltpu.VMEM)
    return pl.pallas_call(
        body,
        out_shape=[jax.ShapeDtypeStruct(s, d) for s, d in outs],
        in_specs=[smem] * scalars + [vmem] * (len(args) - scalars),
        out_specs=[vmem] * len(outs),
        compiler_params=pltpu.CompilerParams(vmem_limit_bytes=32 << 20),
        cost_estimate=cost,
    )(*args)


def text_kernel(near, far, label, unit, label_text):
    n_text = near.shape[0]
    half = label_text.shape[0]
    step = n_text // 5
    total = jnp.zeros(label_text.shape, F32)
    for side, texts in enumerate((near, far)):
        for k in range(5):
            block = texts[k * step : (k + 1) * step, :].astype(F32)
            squares = jnp.sum(block * block, axis=1, keepdims=True)
            low = (block / jnp.sqrt(squares + 1e-06)).astype(BF)
            start = side * n_text + k * step
            unit[start : start + step, :] = low
            columns = lax.broadcasted_iota(jnp.int32, (half, step), 1) + start
            pick = jnp.where(columns == label[...], 1.0, 0.0).astype(BF)
            total += jnp.dot(pick, low, preferred_element_type=F32)
    label_text[...] = total.astype(BF)


def order_kernel(me, near, far, proj, state, vectors):
    emb = proj.shape[1]
    share = near.shape[1]
    half = state.shape[1]
    at = me[0]
    first = lax.rem(at, 2) == 0
    for c, side in enumerate((near, far)):
        for k in range(side.shape[0]):
            x, y = k // 4, k % 4
            there = pl.multiple_of((at ^ (4 * y + 2 * x + c)) * share, share)
            block = side[k]
            proj[pl.ds(there, share), :] = block[:, :emb]
            left = block[:, emb : emb + half]
            right = block[:, emb + half : emb + 2 * half]
            state[pl.ds(there, share), :] = jnp.where(first, left, right)
            vectors[pl.ds(there, share), :] = block[:, emb + 2 * half :]


def rows_kernel(me, state, vectors, own, lines):
    rows, half = own.shape[0], state.shape[1]
    start = (me[0] // 2) * rows
    at = lax.broadcasted_iota(jnp.int32, (rows, half), 1)
    line = lax.broadcasted_iota(jnp.int32, (rows, half), 0)
    own[...] = lax.dot_general(
        (at == line + start).astype(F32).astype(BF), state[...], NT, preferred_element_type=F32
    )
    at = lax.broadcasted_iota(jnp.int32, (16, half), 1)
    line = lax.broadcasted_iota(jnp.int32, (16, half), 0)
    pick = (at >= 3 * line) & (at < 3 * line + 3) & (line < 2)
    lines[...] = lax.dot_general(
        pick.astype(F32).astype(BF), vectors[...], NT, preferred_element_type=F32
    )


def embed_kernel(mixed, own, bias, lines, proj, sent, unit, norm, yhat, rstd):
    n = mixed.shape[0]
    total = own[...] + bias[...]
    for j in range(n):
        total += mixed[j].astype(F32)
    normed, scale = row_norm(total)
    yhat[...] = normed
    rstd[...] = jnp.broadcast_to(scale, rstd.shape)
    post_normed = (normed * lines[0:1, :] + lines[1:2, :]).astype(BF)
    embedding = jnp.dot(post_normed, proj[...], preferred_element_type=F32)
    length = jnp.sqrt(jnp.sum(embedding * embedding, axis=1, keepdims=True) + 1e-06)
    norm[...] = jnp.broadcast_to(length, norm.shape)
    vec = embedding / length
    unit[...] = vec
    low = vec.astype(BF)
    for j in range(n):
        sent[j] = low


def embed_back_kernel(back, label_parts, unit, norm, yhat, rstd, lines, proj, sent, grad):
    n = back.shape[0]
    emb = unit.shape[1]
    stats = [back[j, :, emb:].astype(F32) for j in range(n)]
    top = stats[0][:, 0:1]
    label_rows = label_parts[0].astype(F32)
    for j in range(1, n):
        top = jnp.maximum(top, stats[j][:, 0:1])
        label_rows += label_parts[j].astype(F32)
    rest = jnp.zeros_like(top)
    hit = jnp.zeros_like(top)
    unit_grad = jnp.zeros(unit.shape, F32)
    for j in range(n):
        weight = jnp.exp(stats[j][:, 0:1] - top)
        rest += weight * (stats[j][:, 1:2] + stats[j][:, 2:3])
        hit += weight * (stats[j][:, 3:4] + stats[j][:, 4:5])
        unit_grad += weight * back[j, :, :emb].astype(F32)
    unit_grad = (unit_grad - rest * label_rows) * (100.0 / (rest + hit))
    vec = unit[...]
    along = jnp.sum(vec * unit_grad, axis=1, keepdims=True)
    emb_grad = ((unit_grad - vec * along) / norm[:, 0:1]).astype(BF)
    post_grad = lax.dot_general(emb_grad, proj[...], NT, preferred_element_type=F32)
    out_grad = norm_back(post_grad * lines[0:1, :], yhat[...], rstd[:, 0:1])
    grad[...] = out_grad
    low = out_grad.astype(BF)
    for j in range(n):
        sent[j] = low


def change_kernel(parts, gain, own, out_grad, step, sent):
    n, half, _ = sent.shape
    share = own.shape[1] // n
    total = parts[0].astype(F32)
    for j in range(1, parts.shape[0]):
        total += parts[j].astype(F32)
    xhat, scale = row_norm(own[...])
    grad = out_grad[...] + norm_back(total * gain[...], xhat, scale)
    rms = jnp.sqrt(jnp.mean(grad * grad, axis=1, keepdims=True) + 1e-06)
    change = step[0:1, 0:1] * grad / rms
    for j in range(n):
        block = change[:, j * share : (j + 1) * share]
        sent[j, :, :share] = block[:half]
        sent[j, :, share:] = block[half:]


def result_kernel(parts, resid, out):
    n, _, width = parts.shape
    share = width // 2
    blocks = []
    for c in range(2):
        for g in range(n // 2):
            block = parts[2 * g + c]
            blocks += [block[:, :share], block[:, share:]]
    change = jnp.concatenate(blocks, axis=0)
    out[...] = resid[...].astype(F32) + change.T


def local(
    resid,
    prenorm_gain,
    prenorm_bias,
    up_weight,
    up_bias,
    down_weight,
    down_bias,
    post_gain,
    post_bias,
    projection,
    texts,
    labels,
    step_size,
):
    n_txt, n_dp = lax.axis_size("txt"), lax.axis_size("dp")
    n_z, n_pair = n_dp // 2, n_txt // 2
    me = lax.axis_index("txt")
    core = lax.rem(me, 2)
    images, share = resid.shape
    half = images // 2
    rows = images // n_txt
    hid = up_weight.shape[1]
    n_text, emb = texts.shape
    cores = [[2 * i + c for i in range(n_pair)] for c in range(2)]
    along_z = [[2 * z + x for z in range(n_z)] for x in range(2)]

    mine = jnp.stack([up_weight, down_weight.T])
    mine = swapped(copies(mine, n_z), "dp", along_z)

    vectors = jnp.stack(pieces(post_gain, 3) + pieces(post_bias, 3), axis=1)
    vectors = jnp.pad(vectors, ((0, 0), (0, 128 - vectors.shape[1])))
    chain = jnp.concatenate([projection, resid.T, vectors], axis=1)
    far_texts = from_partner(texts, "txt", 1)
    far_bias = from_partner(up_bias, "txt", 1)
    chain = jnp.stack([chain] + [from_partner(chain, "txt", 4 * k) for k in (1, 2, 3)])
    chain = jnp.concatenate([chain, from_partner(chain, "txt", 2)])
    far_chain = from_partner(chain, "txt", 1)
    here = me.astype(jnp.int32).reshape(1)
    proj, state, vectors = vmem_call(
        order_kernel,
        (((WIDTH, emb), BF), ((WIDTH, half), BF), ((WIDTH, 128), BF)),
        here,
        chain,
        far_chain,
        scalars=1,
        cost=SMALL,
    )
    own, lines = vmem_call(
        rows_kernel,
        (((rows, WIDTH), F32), ((16, WIDTH), F32)),
        here,
        state,
        vectors,
        scalars=1,
    )

    label = lax.dynamic_slice_in_dim(labels, core * half, half) - (me - core) * n_text
    inside = (label >= 0) & (label < 2 * n_text)
    label = jnp.where(core == 0, label, jnp.where(label < n_text, label + n_text, label - n_text))
    label = jnp.where(inside, label, -1)
    text_unit, label_text = vmem_call(
        text_kernel,
        (((2 * n_text, emb), BF), ((half, emb), BF)),
        texts,
        far_texts,
        label[:, None],
        cost=SMALL,
    )
    target = lax.broadcasted_iota(jnp.int32, (half, 2 * n_text), 1) == label[:, None]
    mine, label_text = lax.optimization_barrier((mine, label_text))
    other_up = from_partner(mine[:, 0], "dp", 1)
    other_down = from_partner(mine[:, 1], "dp", 1)
    label_text = swapped(label_text.reshape(n_pair, rows, emb), "txt", cores)
    first = lax.rem(lax.axis_index("dp"), 2) == 0

    def whole(own, other):
        both = jnp.stack([jnp.where(first, own, other), jnp.where(first, other, own)], axis=1)
        return both.reshape(WIDTH, hid)

    w_up = whole(mine[:, 0], other_up)
    w_down = whole(mine[:, 1], other_down)
    w_up = (w_up, from_partner(w_up, "txt", 1))
    w_down = (w_down, from_partner(w_down, "txt", 1))

    inputs = state.astype(F32)
    mean_in = jnp.mean(inputs, axis=0)
    var_in = jnp.mean(inputs * inputs, axis=0) - mean_in * mean_in
    rstd_in = lax.rsqrt(var_in + 1e-05)
    normed = ((inputs - mean_in) * rstd_in * prenorm_gain[:, None] + prenorm_bias[:, None]).astype(BF)
    pre_act = [
        jnp.einsum("di,df->if", normed, w, preferred_element_type=F32) + b
        for w, b in zip(w_up, (up_bias, far_bias))
    ]
    gate = [jax.nn.sigmoid(1.702 * p) for p in pre_act]
    hidden = [(p * g).astype(BF) for p, g in zip(pre_act, gate)]
    mixed = sum(
        jnp.einsum("if,df->id", h, w, preferred_element_type=F32) for h, w in zip(hidden, w_down)
    )
    mixed = mixed.astype(BF).reshape(n_pair, rows, WIDTH)
    mixed, label_text = lax.optimization_barrier((mixed, label_text))
    mixed = swapped(mixed, "txt", cores)

    sent, unit_vec, emb_norm, yhat, rstd_out = vmem_call(
        embed_kernel,
        (
            ((n_pair, rows, emb), BF),
            ((rows, emb), F32),
            ((rows, 128), F32),
            ((rows, WIDTH), F32),
            ((rows, 128), F32),
        ),
        mixed,
        own,
        down_bias[None],
        lines,
        proj,
    )
    unit_low = swapped(sent, "txt", cores).reshape(half, emb)

    logits = 100.0 * jnp.einsum("ie,je->ij", unit_low, text_unit, preferred_element_type=F32)
    top = lax.reduce_precision(jnp.max(logits, axis=1), 8, 7)
    exponent = jnp.exp(logits - top[:, None])
    others = jnp.where(target, 0.0, exponent)
    rest = jnp.sum(others, axis=1)
    hit = jnp.sum(jnp.where(target, exponent, 0.0), axis=1)
    back = jnp.dot(others.astype(BF), text_unit, preferred_element_type=F32).astype(BF)
    stats = jnp.stack(pieces(top, 1) + pieces(rest, 2) + pieces(hit, 2), axis=1)
    stats = jnp.pad(stats, ((0, 0), (0, 128 - stats.shape[1])))
    back = jnp.concatenate([back, stats], axis=1).reshape(n_pair, rows, emb + 128)
    back = swapped(back, "txt", cores)

    sent, out_grad = vmem_call(
        embed_back_kernel,
        (((n_pair, rows, WIDTH), BF), ((rows, WIDTH), F32)),
        back,
        label_text,
        unit_vec,
        emb_norm,
        yhat,
        rstd_out,
        lines,
        proj,
    )
    out_low = swapped(sent, "txt", cores).reshape(half, WIDTH)

    normed_grad = 0.0
    for p, g, up, down in zip(pre_act, gate, w_up, w_down):
        hid_grad = jnp.einsum("id,df->if", out_low, down, preferred_element_type=F32)
        act_grad = (hid_grad * (g + 1.702 * p * g * (1.0 - g))).astype(BF)
        normed_grad += jnp.einsum("if,df->id", act_grad, up, preferred_element_type=F32)
    normed_grad = swapped(normed_grad.astype(BF).reshape(n_pair, rows, WIDTH), "txt", cores)
    (change,) = vmem_call(
        change_kernel,
        (((n_txt, rows // 2, 2 * share), F32),),
        normed_grad,
        prenorm_gain[None],
        own,
        out_grad,
        step_size[None],
    )
    change = swapped(change, "txt")
    (out,) = vmem_call(result_kernel, (((share, images), F32),), change, resid.T)
    return out.T


def solution(mesh):
    placed = (
        P("dp", "txt"),
        P(),
        P(),
        P("dp", "txt"),
        P("txt"),
        P("txt", "dp"),
        P(),
        P("txt"),
        P("txt"),
        P("txt", None),
        P("txt", None),
        P("dp"),
        P(),
    )
    return jax.shard_map(
        local, mesh=mesh, in_specs=placed, out_specs=P("dp", "txt"), check_vma=False
    )
```

time: 182 us -> 174 us (0.956)
  between operations: 14.6 us -> 1.18 us
  Pallas kernels: 1.91 us -> 9.44 us
  waiting for transfers between devices: 40.7 us -> 33.2 us
  local copies, waits for them, and re-layouts: 4.55 us -> 11.4 us
  blocking collectives: 35 us -> 31.7 us
  matrix products: 8.12 us -> 10.8 us
    all_to_all x5, waiting for transfers between devices: 40.1 us -> 17.5 us  [swapped(): return lax.all_to_all(x, axis, 0, 0, tiled=True, axis_index_groups=groups)]
    ppermute x7 -> x11, waiting for transfers between devices: 0.58 us -> 15.7 us  [from_partner(): return lax.ppermute(x, axis, pairs)]
    ppermute x7 -> x11, starting transfers between devices: 25.2 us -> 33.9 us  [from_partner(): return lax.ppermute(x, axis, pairs)]
    all_to_all x5, starting transfers between devices: 40.7 us -> 32.1 us  [swapped(): return lax.all_to_all(x, axis, 0, 0, tiled=True, axis_index_groups=groups)]
    pallas_call x3 -> x7, Pallas kernels: 1.91 us -> 9.44 us  [vmem_call(): pl.pallas_call(body, out_shape=[jax.ShapeDtypeStruct(s, d) for s, d in ou...]
    unnamed x32 -> x55, local copies, waits for them, and re-layouts: 2.25 us -> 8.26 us
    another operation x4 -> x3, other arithmetic: 0.12 us -> 3.49 us  [the longest x2 2.67 us: local(): jnp.stack([chain] + [from_partner(chain, 'txt', 4 * k) for k in (1, 2, 3)])]
    all_to_all x3, blocking collectives: 35 us -> 31.7 us  [swapped(): return lax.all_to_all(x, axis, 0, 0, tiled=True, axis_index_groups=groups)]
  transfers between devices with their start and end apart: 13 -> 16, of which waited for: 6 -> 6; matrix products, arithmetic and copies ran while one was open for 7% -> 7% of each run, Pallas kernels for 0% -> 4%
where the time goes in v3:
time: 174 us; the launch traced here: 173 us
  starting transfers between devices  66 us (38%)
  waiting for transfers between devices  33.2 us (19%)
  blocking collectives  31.7 us (18%)
  local copies, waits for them, and re-layouts  11.4 us (7%)
  matrix products  10.8 us (6%)
  Pallas kernels  9.44 us (5%)
  other arithmetic  9.33 us (5%)
    ppermute x11, starting transfers between devices, from_partner(): return lax.ppermute(x, axis, pairs)  33.9 us
    all_to_all x5, starting transfers between devices, swapped(): return lax.all_to_all(x, axis, 0, 0, tiled=True, axis_index_groups=groups)  32.1 us
    all_to_all x3, blocking collectives, swapped(): return lax.all_to_all(x, axis, 0, 0, tiled=True, axis_index_groups=groups)  31.7 us
    all_to_all x5, waiting for transfers between devices, swapped(): return lax.all_to_all(x, axis, 0, 0, tiled=True, axis_index_groups=groups)  17.5 us
    ppermute x11, waiting for transfers between devices, from_partner(): return lax.ppermute(x, axis, pairs)  15.7 us
    pallas_call x7, Pallas kernels, vmem_call(): pl.pallas_call(body, out_shape=[jax.ShapeDtypeStruct(s, d) for s, d in ou...  9.44 us
    unnamed x55, local copies, waits for them, and re-layouts  8.26 us
    dot_general x1, matrix products, local(): jnp.einsum('ie,je->ij', unit_low, text_unit, preferred_element_type=F32)  3.83 us
  transfers between devices with their start and end apart: 16, of which 6 were waited for; matrix products, arithmetic and copies ran while one was open for 7% of the time, Pallas kernels for 4%

profile of v3, /device:TPU:1, one launch (start us, length us, event | category | flops | bytes accessed | tf_op | source)
XLA Modules:
  0.0 173.0 jit_solution(9966547602324855686)
XLA Ops:
  1.0 1.6 fusion.65
  2.6 5.6 %collective-permute-start.1 = (bf16[64,1152]{1,0:T(8,128)(2,1)}, bf16[64,1152]{1,0:T(8,128)(2,1)S(1)}, u32[]{:S(2)}, u32[]{:S(2)}) collective-permute-start(bf16[64,1152]{1,0:T(8,128)(2,1)} %get-tuple-element.54), channel_id=1, source_target_pairs={{0,8},{1,9},{2,10},{3,11},{4,12},{5,13},{6,14},{7,15},{8,0},{9,1},... | collective-permute-start | bytes 442376 | tf_op jit(solution)/shard_map/ppermute | solution.py:25
  8.2 2.3 %collective-permute-start = (bf16[64,1152]{1,0:T(8,128)(2,1)}, bf16[64,1152]{1,0:T(8,128)(2,1)}, u32[]{:S(2)}, u32[]{:S(2)}) collective-permute-start(bf16[64,1152]{1,0:T(8,128)(2,1)} %get-tuple-element.54), channel_id=1, source_target_pairs={{0,4},{1,5},{2,6},{3,7},{4,0},{5,1},{6,2},{7,3},{8,12},{9,13},{10,... | collective-permute-start | bytes 442376 | tf_op jit(solution)/shard_map/ppermute | solution.py:25
  10.5 2.3 %collective-permute-start.2 = (bf16[64,1152]{1,0:T(8,128)(2,1)}, bf16[64,1152]{1,0:T(8,128)(2,1)}, u32[]{:S(2)}, u32[]{:S(2)}) collective-permute-start(bf16[64,1152]{1,0:T(8,128)(2,1)} %get-tuple-element.54), channel_id=1, source_target_pairs={{0,12},{1,13},{2,14},{3,15},{4,8},{5,9},{6,10},{7,11},{8,4},{9,5},... | collective-permute-start | bytes 442376 | tf_op jit(solution)/shard_map/ppermute | solution.py:25
  14.4 15.0 %all-to-all-start = ((bf16[16,2,32,256]{3,2,1,0:T(8,128)(2,1)}), bf16[16,2,32,256]{3,2,1,0:T(8,128)(2,1)}, u32[]{:S(2)}, u32[]{:S(2)}) async-start(bf16[16,2,32,256]{3,2,1,0:T(8,128)(2,1)} %broadcast_in_dim.35), calls=%async_computation | async-start | bytes 1048576 | tf_op jit(solution)/shard_map/all_to_all | solution.py:16
  29.4 3.4 %collective-permute-start.5 = (bf16[1280,768]{1,0:T(8,128)(2,1)S(1)}, bf16[1280,768]{1,0:T(8,128)(2,1)}, u32[]{:S(2)}, u32[]{:S(2)}) collective-permute-start(bf16[1280,768]{1,0:T(8,128)(2,1)S(1)} %copy-done.2), channel_id=1, source_target_pairs={{0,1},{1,0},{2,3},{3,2},{4,5},{5,4},{6,7},{7,6},{8,9},{9,8},{10,11... | collective-permute-start | bytes 5898248 | tf_op jit(solution)/shard_map/ppermute | solution.py:25
  34.9 3.1 %collective-permute-start.3 = (bf16[4,64,1152]{2,1,0:T(8,128)(2,1)S(1)}, bf16[4,64,1152]{2,1,0:T(8,128)(2,1)S(1)}, u32[]{:S(2)}, u32[]{:S(2)}) collective-permute-start(bf16[4,64,1152]{2,1,0:T(8,128)(2,1)S(1)} %pad_maximum_fusion), channel_id=1, source_target_pairs={{0,2},{1,3},{2,0},{3,1},{4,6},{5,7},{6,4},{7,5},{8,10},{9,11},{10,... | collective-permute-start | bytes 1769480 | tf_op jit(solution)/shard_map/ppermute | solution.py:25
  39.9 11.9 %collective-permute-done.3 = bf16[4,64,1152]{2,1,0:T(8,128)(2,1)S(1)} collective-permute-done((bf16[4,64,1152]{2,1,0:T(8,128)(2,1)S(1)}, bf16[4,64,1152]{2,1,0:T(8,128)(2,1)S(1)}, u32[]{:S(2)}, u32[]{:S(2)}) %collective-permute-start.3) | collective-permute-done | bytes 589856 | tf_op jit(solution)/shard_map/ppermute | solution.py:25
  51.9 2.6 %collective-permute-start.4 = (bf16[8,64,1152]{2,1,0:T(8,128)(2,1)S(1)}, bf16[8,64,1152]{2,1,0:T(8,128)(2,1)}, u32[]{:S(2)}, u32[]{:S(2)}) collective-permute-start(bf16[8,64,1152]{2,1,0:T(8,128)(2,1)S(1)} %constant_dynamic-update-slice_fusion.near), channel_id=1, source_target_pairs={{0,1},{1,0},{2,3},{3,2},{4,5},{5,4},{6,7},{7,6},{8,9},{9,8},{10,11... | collective-permute-start | bytes 3538952 | tf_op jit(solution)/shard_map/ppermute | solution.py:25
  55.6 1.9 %collective-permute-start.9 = (f32[256]{0:T(256)S(1)}, f32[256]{0:T(256)S(1)}, u32[]{:S(2)}, u32[]{:S(2)}) collective-permute-start(f32[256]{0:T(256)S(1)} %copy-done.25), channel_id=1, source_target_pairs={{0,1},{1,0},{2,3},{3,2},{4,5},{5,4},{6,7},{7,6},{8,9},{9,8},{10,11... | collective-permute-start | bytes 3080 | tf_op jit(solution)/shard_map/ppermute | solution.py:25
  59.6 1.5 shard_map.127
  62.6 4.5 %shard_map.128 = (bf16[2560,768]{1,0:T(8,128)(2,1)S(1)}, bf16[128,768]{1,0:T(8,128)(2,1)}) custom-call(bf16[1280,768]{1,0:T(8,128)(2,1)S(1)} %copy-done.2, bf16[1280,768]{1,0:T(8,128)(2,1)} %collective-permute-done.5.far, s32[128,1]{1,0:T(8,128)S(1)} %copy-done.9), custom_call_target="tpu_custom_call" | custom-call | flops 1024 | bytes 1024 | tf_op jit(solution)/shard_map/pallas_call | solution.py:53
  67.0 1.9 %copy-done = bf16[2560,768]{1,0:T(8,128)(2,1)} copy-done((bf16[2560,768]{1,0:T(8,128)(2,1)}, bf16[2560,768]{1,0:T(8,128)(2,1)S(1)}, u32[]{:S(2)}) %copy-start) | copy-done | bytes 3932184
  70.0 4.7 %collective-permute-start.7 = (bf16[16,32,256]{2,1,0:T(8,128)(2,1)S(1)}, bf16[16,32,256]{2,1,0:T(8,128)(2,1)S(1)}, u32[]{:S(2)}, u32[]{:S(2)}) collective-permute-start(bf16[16,32,256]{2,1,0:T(8,128)(2,1)S(1)} %get-tuple-element.51), channel_id=1, source_target_pairs={{0,16},{16,0},{32,48},{48,32},{64,80},{80,64},{96,112},{112,96},{1... | collective-permute-start | bytes 786440 | tf_op jit(solution)/shard_map/ppermute | solution.py:25
  74.6 2.1 %collective-permute-start.6 = (bf16[16,32,256]{2,1,0:T(8,128)(2,1)S(1)}, bf16[16,32,256]{2,1,0:T(8,128)(2,1)S(1)}, u32[]{:S(2)}, u32[]{:S(2)}) collective-permute-start(bf16[16,32,256]{2,1,0:T(8,128)(2,1)S(1)} %get-tuple-element.52), channel_id=1, source_target_pairs={{0,16},{16,0},{32,48},{48,32},{64,80},{80,64},{96,112},{112,96},{1... | collective-permute-start | bytes 786440 | tf_op jit(solution)/shard_map/ppermute | solution.py:25
  77.9 5.0 %all-to-all-start.1 = ((bf16[8,16,768]{2,1,0:T(8,128)(2,1)}), bf16[8,16,768]{2,1,0:T(8,128)(2,1)S(1)}, u32[]{:S(2)}, u32[]{:S(2)}) async-start(bf16[8,16,768]{2,1,0:T(8,128)(2,1)} %bitcast.26), calls=%async_computation.1 | async-start | bytes 393216 | tf_op jit(solution)/shard_map/all_to_all | solution.py:16
  82.9 3.5 %collective-permute-done.6 = bf16[16,32,256]{2,1,0:T(8,128)(2,1)S(1)} collective-permute-done((bf16[16,32,256]{2,1,0:T(8,128)(2,1)S(1)}, bf16[16,32,256]{2,1,0:T(8,128)(2,1)S(1)}, u32[]{:S(2)}, u32[]{:S(2)}) %collective-permute-start.6) | collective-permute-done | bytes 262176 | tf_op jit(solution)/shard_map/ppermute | solution.py:25
  86.4 1.3 select_bitcast_fusion.1
  87.8 3.9 %collective-permute-start.8 = (bf16[1024,256]{1,0:T(8,128)(2,1)S(1)}, bf16[1024,256]{1,0:T(8,128)(2,1)S(1)}, u32[]{:S(2)}, u32[]{:S(2)}) collective-permute-start(bf16[1024,256]{1,0:T(8,128)(2,1)S(1)} %bitcast.95), channel_id=1, source_target_pairs={{0,1},{1,0},{2,3},{3,2},{4,5},{5,4},{6,7},{7,6},{8,9},{9,8},{10,11... | collective-permute-start | bytes 1572872 | tf_op jit(solution)/shard_map/ppermute | solution.py:25
  91.8 1.9 %collective-permute-start.10 = (bf16[1024,256]{1,0:T(8,128)(2,1)S(1)}, bf16[1024,256]{1,0:T(8,128)(2,1)S(1)}, u32[]{:S(2)}, u32[]{:S(2)}) collective-permute-start(bf16[1024,256]{1,0:T(8,128)(2,1)S(1)} %bitcast.90), channel_id=1, source_target_pairs={{0,1},{1,0},{2,3},{3,2},{4,5},{5,4},{6,7},{7,6},{8,9},{9,8},{10,11... | collective-permute-start | bytes 1572872 | tf_op jit(solution)/shard_map/ppermute | solution.py:25
  96.6 5.4 %all-to-all-start.2 = ((bf16[8,16,1024]{2,1,0:T(8,128)(2,1)}), bf16[8,16,1024]{2,1,0:T(8,128)(2,1)S(1)}, u32[]{:S(2)}, u32[]{:S(2)}) async-start(bf16[8,16,1024]{2,1,0:T(8,128)(2,1)} %bitcast.25), calls=%async_computation.2 | async-start | bytes 524288 | tf_op jit(solution)/shard_map/all_to_all | solution.py:16
  102.3 6.4 %all-to-all-done.2.mixed = bf16[8,16,1024]{2,1,0:T(8,128)(2,1)S(1)} async-done(((bf16[8,16,1024]{2,1,0:T(8,128)(2,1)}), bf16[8,16,1024]{2,1,0:T(8,128)(2,1)S(1)}, u32[]{:S(2)}, u32[]{:S(2)}) %all-to-all-start.2) | async-done | bytes 262176 | tf_op jit(solution)/shard_map/all_to_all | solution.py:16
  109.9 3.4 %all-to-all-start.3 = ((bf16[8,16,768]{2,1,0:T(8,128)(2,1)}), bf16[8,16,768]{2,1,0:T(8,128)(2,1)S(1)}, u32[]{:S(2)}, u32[]{:S(2)}) async-start(bf16[8,16,768]{2,1,0:T(8,128)(2,1)} %get-tuple-element.32), calls=%async_computation.3 | async-start | bytes 393216 | tf_op jit(solution)/shard_map/all_to_all | solution.py:16
  113.4 5.7 %all-to-all-done.3 = bf16[8,16,768]{2,1,0:T(8,128)(2,1)S(1)} async-done(((bf16[8,16,768]{2,1,0:T(8,128)(2,1)}), bf16[8,16,768]{2,1,0:T(8,128)(2,1)S(1)}, u32[]{:S(2)}, u32[]{:S(2)}) %all-to-all-start.3) | async-done | bytes 196640 | tf_op jit(solution)/shard_map/all_to_all | solution.py:16
  119.7 3.8 %fusion.67 = (f32[128]{0:T(128)S(1)}, f32[128,2560]{1,0:T(8,128)S(1)}) fusion(bf16[128,768]{1,0:T(8,128)(2,1)} %bitcast.99, bf16[2560,768]{1,0:T(8,128)(2,1)} %copy-done), kind=kOutput, calls=%fused_computation.117 | convolution fusion | flops 503971712 | bytes 5440000 | tf_op jit(solution)/shard_map/ie,je->ij/dot_general | solution.py:311
  123.6 1.5 convolution_convert_fusion
  126.7 8.4 %all_to_all.40.back = bf16[8,16,896]{2,1,0:T(8,128)(2,1)S(1)} all-to-all(bf16[8,16,896]{2,1,0:T(8,128)(2,1)S(1)} %bitcast.98), channel_id=1, replica_groups={{0,2,4,6,8,10,12,14},{1,3,5,7,9,11,13,15},{16,18,20,22,24,26,28,30},{17..., dimensions={0} | all-to-all | bytes 458752 | tf_op jit(solution)/shard_map/all_to_all | solution.py:16
  136.1 8.7 %all_to_all.41 = bf16[8,16,1024]{2,1,0:T(8,128)(2,1)S(1)} all-to-all(bf16[8,16,1024]{2,1,0:T(8,128)(2,1)S(1)} %get-tuple-element.39), channel_id=1, replica_groups={{0,2,4,6,8,10,12,14},{1,3,5,7,9,11,13,15},{16,18,20,22,24,26,28,30},{17..., dimensions={0} | all-to-all | bytes 524288 | tf_op jit(solution)/shard_map/all_to_all | solution.py:16
  144.8 1.7 fusion.7
  147.8 3.4 %all-to-all-start.6 = ((bf16[8,16,1024]{2,1,0:T(8,128)(2,1)}), bf16[8,16,1024]{2,1,0:T(8,128)(2,1)S(1)}, u32[]{:S(2)}, u32[]{:S(2)}) async-start(bf16[8,16,1024]{2,1,0:T(8,128)(2,1)} %bitcast.34), calls=%async_computation.6 | async-start | bytes 524288 | tf_op jit(solution)/shard_map/all_to_all | solution.py:16
  151.8 5.4 %all-to-all-done.6.parts = bf16[8,16,1024]{2,1,0:T(8,128)(2,1)S(1)} async-done(((bf16[8,16,1024]{2,1,0:T(8,128)(2,1)}), bf16[8,16,1024]{2,1,0:T(8,128)(2,1)S(1)}, u32[]{:S(2)}, u32[]{:S(2)}) %all-to-all-start.6) | async-done | bytes 262176 | tf_op jit(solution)/shard_map/all_to_all | solution.py:16
  157.6 14.6 %all_to_all.42.parts = f32[16,8,128]{2,1,0:T(8,128)S(1)} all-to-all(f32[16,8,128]{2,1,0:T(8,128)S(1)} %shard_map.132), channel_id=1, replica_groups=mesh['dp'=32,'txt'=16] {'txt'}, dimensions={0} | all-to-all | bytes 131072 | tf_op jit(solution)/shard_map/all_to_all | solution.py:16
  (99 shorter events, 23.5 us)
Async XLA Ops:
  0.0 32.9 %copy-start.7 = (bf16[256,64]{0,1:T(8,128)(2,1)S(1)}, bf16[256,64]{0,1:T(8,128)(2,1)}, u32[]{:S(2)}) copy-start(bf16[256,64]{0,1:T(8,128)(2,1)} %param.13) | copy-start | bytes 98308
  0.0 29.4 %copy-start.2 = (bf16[1280,768]{1,0:T(8,128)(2,1)S(1)}, bf16[1280,768]{1,0:T(8,128)(2,1)}, u32[]{:S(2)}) copy-start(bf16[1280,768]{1,0:T(8,128)(2,1)} %near.1) | copy-start | bytes 5898244
  2.6 31.2 %collective-permute-start.1 = (bf16[64,1152]{1,0:T(8,128)(2,1)}, bf16[64,1152]{1,0:T(8,128)(2,1)S(1)}, u32[]{:S(2)}, u32[]{:S(2)}) collective-permute-start(bf16[64,1152]{1,0:T(8,128)(2,1)} %get-tuple-element.54), channel_id=1, source_target_pairs={{0,8},{1,9},{2,10},{3,11},{4,12},{5,13},{6,14},{7,15},{8,0},{9,1},... | collective-permute-start | bytes 442376 | tf_op jit(solution)/shard_map/ppermute | solution.py:25
  8.2 25.6 %collective-permute-start = (bf16[64,1152]{1,0:T(8,128)(2,1)}, bf16[64,1152]{1,0:T(8,128)(2,1)}, u32[]{:S(2)}, u32[]{:S(2)}) collective-permute-start(bf16[64,1152]{1,0:T(8,128)(2,1)} %get-tuple-element.54), channel_id=1, source_target_pairs={{0,4},{1,5},{2,6},{3,7},{4,0},{5,1},{6,2},{7,3},{8,12},{9,13},{10,... | collective-permute-start | bytes 442376 | tf_op jit(solution)/shard_map/ppermute | solution.py:25
  10.5 23.3 %collective-permute-start.2 = (bf16[64,1152]{1,0:T(8,128)(2,1)}, bf16[64,1152]{1,0:T(8,128)(2,1)}, u32[]{:S(2)}, u32[]{:S(2)}) collective-permute-start(bf16[64,1152]{1,0:T(8,128)(2,1)} %get-tuple-element.54), channel_id=1, source_target_pairs={{0,12},{1,13},{2,14},{3,15},{4,8},{5,9},{6,10},{7,11},{8,4},{9,5},... | collective-permute-start | bytes 442376 | tf_op jit(solution)/shard_map/ppermute | solution.py:25
  14.4 54.5 %all-to-all-start = ((bf16[16,2,32,256]{3,2,1,0:T(8,128)(2,1)}), bf16[16,2,32,256]{3,2,1,0:T(8,128)(2,1)}, u32[]{:S(2)}, u32[]{:S(2)}) async-start(bf16[16,2,32,256]{3,2,1,0:T(8,128)(2,1)} %broadcast_in_dim.35), calls=%async_computation | async-start | bytes 1048576 | tf_op jit(solution)/shard_map/all_to_all | solution.py:16
  29.4 33.1 %collective-permute-start.5 = (bf16[1280,768]{1,0:T(8,128)(2,1)S(1)}, bf16[1280,768]{1,0:T(8,128)(2,1)}, u32[]{:S(2)}, u32[]{:S(2)}) collective-permute-start(bf16[1280,768]{1,0:T(8,128)(2,1)S(1)} %copy-done.2), channel_id=1, source_target_pairs={{0,1},{1,0},{2,3},{3,2},{4,5},{5,4},{6,7},{7,6},{8,9},{9,8},{10,11... | collective-permute-start | bytes 5898248 | tf_op jit(solution)/shard_map/ppermute | solution.py:25
  34.9 20.7 %copy-start.25 = (f32[256]{0:T(256)S(1)}, f32[256]{0:T(256)}, u32[]{:S(2)}) copy-start(f32[256]{0:T(256)} %param.17) | copy-start | bytes 3076
  34.9 22.6 %copy-start.23 = (s32[256]{0:T(256)S(1)}, s32[256]{0:T(256)}, u32[]{:S(2)}) copy-start(s32[256]{0:T(256)} %param.24) | copy-start | bytes 3076
  34.9 16.9 %collective-permute-start.3 = (bf16[4,64,1152]{2,1,0:T(8,128)(2,1)S(1)}, bf16[4,64,1152]{2,1,0:T(8,128)(2,1)S(1)}, u32[]{:S(2)}, u32[]{:S(2)}) collective-permute-start(bf16[4,64,1152]{2,1,0:T(8,128)(2,1)S(1)} %pad_maximum_fusion), channel_id=1, source_target_pairs={{0,2},{1,3},{2,0},{3,1},{4,6},{5,7},{6,4},{7,5},{8,10},{9,11},{10,... | collective-permute-start | bytes 1769480 | tf_op jit(solution)/shard_map/ppermute | solution.py:25
  51.9 6.4 %collective-permute-start.4 = (bf16[8,64,1152]{2,1,0:T(8,128)(2,1)S(1)}, bf16[8,64,1152]{2,1,0:T(8,128)(2,1)}, u32[]{:S(2)}, u32[]{:S(2)}) collective-permute-start(bf16[8,64,1152]{2,1,0:T(8,128)(2,1)S(1)} %constant_dynamic-update-slice_fusion.near), channel_id=1, source_target_pairs={{0,1},{1,0},{2,3},{3,2},{4,5},{5,4},{6,7},{7,6},{8,9},{9,8},{10,11... | collective-permute-start | bytes 3538952 | tf_op jit(solution)/shard_map/ppermute | solution.py:25
  55.6 39.1 %collective-permute-start.9 = (f32[256]{0:T(256)S(1)}, f32[256]{0:T(256)S(1)}, u32[]{:S(2)}, u32[]{:S(2)}) collective-permute-start(f32[256]{0:T(256)S(1)} %copy-done.25), channel_id=1, source_target_pairs={{0,1},{1,0},{2,3},{3,2},{4,5},{5,4},{6,7},{7,6},{8,9},{9,8},{10,11... | collective-permute-start | bytes 3080 | tf_op jit(solution)/shard_map/ppermute | solution.py:25
  70.0 12.9 %collective-permute-start.7 = (bf16[16,32,256]{2,1,0:T(8,128)(2,1)S(1)}, bf16[16,32,256]{2,1,0:T(8,128)(2,1)S(1)}, u32[]{:S(2)}, u32[]{:S(2)}) collective-permute-start(bf16[16,32,256]{2,1,0:T(8,128)(2,1)S(1)} %get-tuple-element.51), channel_id=1, source_target_pairs={{0,16},{16,0},{32,48},{48,32},{64,80},{80,64},{96,112},{112,96},{1... | collective-permute-start | bytes 786440 | tf_op jit(solution)/shard_map/ppermute | solution.py:25
  74.6 11.7 %collective-permute-start.6 = (bf16[16,32,256]{2,1,0:T(8,128)(2,1)S(1)}, bf16[16,32,256]{2,1,0:T(8,128)(2,1)S(1)}, u32[]{:S(2)}, u32[]{:S(2)}) collective-permute-start(bf16[16,32,256]{2,1,0:T(8,128)(2,1)S(1)} %get-tuple-element.52), channel_id=1, source_target_pairs={{0,16},{16,0},{32,48},{48,32},{64,80},{80,64},{96,112},{112,96},{1... | collective-permute-start | bytes 786440 | tf_op jit(solution)/shard_map/ppermute | solution.py:25
  77.9 18.7 %all-to-all-start.1 = ((bf16[8,16,768]{2,1,0:T(8,128)(2,1)}), bf16[8,16,768]{2,1,0:T(8,128)(2,1)S(1)}, u32[]{:S(2)}, u32[]{:S(2)}) async-start(bf16[8,16,768]{2,1,0:T(8,128)(2,1)} %bitcast.26), calls=%async_computation.1 | async-start | bytes 393216 | tf_op jit(solution)/shard_map/all_to_all | solution.py:16
  87.7 6.6 %copy-start.18 = (bf16[16,2,32,256]{3,2,1,0:T(8,128)(2,1)}, bf16[16,2,32,256]{3,2,1,0:T(8,128)(2,1)S(1)}, u32[]{:S(2)}) copy-start(bf16[16,2,32,256]{3,2,1,0:T(8,128)(2,1)S(1)} %pad_maximum_fusion.1) | copy-start | bytes 1572868
  87.8 6.0 %copy-start.6 = (bf16[1024,128]{1,0:T(8,128)(2,1)S(1)}, bf16[1024,128]{1,0:T(8,128)(2,1)}, u32[]{:S(2)}) copy-start(bf16[1024,128]{1,0:T(8,128)(2,1)} %copy-done.5) | copy-start | bytes 786436
  87.8 6.0 %copy-start.13 = (f32[1024]{0:T(1024)S(1)}, f32[1024]{0:T(1024)}, u32[]{:S(2)}) copy-start(f32[1024]{0:T(1024)} %param.14) | copy-start | bytes 12292
  87.8 6.0 %copy-start.24 = (f32[1024]{0:T(1024)S(1)}, f32[1024]{0:T(1024)}, u32[]{:S(2)}) copy-start(f32[1024]{0:T(1024)} %param.15) | copy-start | bytes 12292
  87.8 6.9 %collective-permute-start.8 = (bf16[1024,256]{1,0:T(8,128)(2,1)S(1)}, bf16[1024,256]{1,0:T(8,128)(2,1)S(1)}, u32[]{:S(2)}, u32[]{:S(2)}) collective-permute-start(bf16[1024,256]{1,0:T(8,128)(2,1)S(1)} %bitcast.95), channel_id=1, source_target_pairs={{0,1},{1,0},{2,3},{3,2},{4,5},{5,4},{6,7},{7,6},{8,9},{9,8},{10,11... | collective-permute-start | bytes 1572872 | tf_op jit(solution)/shard_map/ppermute | solution.py:25
  91.8 3.8 %collective-permute-start.10 = (bf16[1024,256]{1,0:T(8,128)(2,1)S(1)}, bf16[1024,256]{1,0:T(8,128)(2,1)S(1)}, u32[]{:S(2)}, u32[]{:S(2)}) collective-permute-start(bf16[1024,256]{1,0:T(8,128)(2,1)S(1)} %bitcast.90), channel_id=1, source_target_pairs={{0,1},{1,0},{2,3},{3,2},{4,5},{5,4},{6,7},{7,6},{8,9},{9,8},{10,11... | collective-permute-start | bytes 1572872 | tf_op jit(solution)/shard_map/ppermute | solution.py:25
  94.7 7.3 %copy-start.11 = (bf16[1024,128]{1,0:T(8,128)(2,1)S(1)}, bf16[1024,128]{1,0:T(8,128)(2,1)}, u32[]{:S(2)}) copy-start(bf16[1024,128]{1,0:T(8,128)(2,1)} %copy-done.10) | copy-start | bytes 786436
  95.3 13.3 %copy-start.12 = (f32[1024]{0:T(1024)S(1)}, f32[1024]{0:T(1024)}, u32[]{:S(2)}) copy-start(f32[1024]{0:T(1024)} %param.19) | copy-start | bytes 12292
  95.6 14.3 %copy-start.16 = (bf16[1024,256]{1,0:T(8,128)(2,1)}, bf16[1024,256]{1,0:T(8,128)(2,1)S(1)}, u32[]{:S(2)}) copy-start(bf16[1024,256]{1,0:T(8,128)(2,1)S(1)} %collective-permute-done.10) | copy-start | bytes 1572868
  96.6 12.0 %all-to-all-start.2 = ((bf16[8,16,1024]{2,1,0:T(8,128)(2,1)}), bf16[8,16,1024]{2,1,0:T(8,128)(2,1)S(1)}, u32[]{:S(2)}, u32[]{:S(2)}) async-start(bf16[8,16,1024]{2,1,0:T(8,128)(2,1)} %bitcast.25), calls=%async_computation.2 | async-start | bytes 524288 | tf_op jit(solution)/shard_map/all_to_all | solution.py:16
  109.9 9.1 %all-to-all-start.3 = ((bf16[8,16,768]{2,1,0:T(8,128)(2,1)}), bf16[8,16,768]{2,1,0:T(8,128)(2,1)S(1)}, u32[]{:S(2)}, u32[]{:S(2)}) async-start(bf16[8,16,768]{2,1,0:T(8,128)(2,1)} %get-tuple-element.32), calls=%async_computation.3 | async-start | bytes 393216 | tf_op jit(solution)/shard_map/all_to_all | solution.py:16
  119.7 3.8 %copy-start.1 = (bf16[2560,768]{1,0:T(8,128)(2,1)S(1)}, bf16[2560,768]{1,0:T(8,128)(2,1)}, u32[]{:S(2)}) copy-start(bf16[2560,768]{1,0:T(8,128)(2,1)} %copy-done) | copy-start | bytes 11796484
  135.2 9.6 %copy-start.15 = (bf16[16,2,32,256]{3,2,1,0:T(8,128)(2,1)S(1)}, bf16[16,2,32,256]{3,2,1,0:T(8,128)(2,1)}, u32[]{:S(2)}) copy-start(bf16[16,2,32,256]{3,2,1,0:T(8,128)(2,1)} %copy-done.14) | copy-start | bytes 1572868
  136.1 10.4 %copy-start.17 = (bf16[1024,256]{1,0:T(8,128)(2,1)S(1)}, bf16[1024,256]{1,0:T(8,128)(2,1)}, u32[]{:S(2)}) copy-start(bf16[1024,256]{1,0:T(8,128)(2,1)} %copy-done.16) | copy-start | bytes 1572868
  136.1 10.4 %copy-start.21 = (bf16[1024,256]{1,0:T(8,128)(2,1)S(1)}, bf16[1024,256]{1,0:T(8,128)(2,1)}, u32[]{:S(2)}) copy-start(bf16[1024,256]{1,0:T(8,128)(2,1)} %copy-done.20) | copy-start | bytes 1572868
  146.5 25.8 %copy-start.8 = (bf16[256,64]{0,1:T(8,128)(2,1)S(1)}, bf16[256,64]{0,1:T(8,128)(2,1)}, u32[]{:S(2)}) copy-start(bf16[256,64]{0,1:T(8,128)(2,1)} %param.13) | copy-start | bytes 98308
  147.8 9.5 %all-to-all-start.6 = ((bf16[8,16,1024]{2,1,0:T(8,128)(2,1)}), bf16[8,16,1024]{2,1,0:T(8,128)(2,1)S(1)}, u32[]{:S(2)}, u32[]{:S(2)}) async-start(bf16[8,16,1024]{2,1,0:T(8,128)(2,1)} %bitcast.34), calls=%async_computation.6 | async-start | bytes 524288 | tf_op jit(solution)/shard_map/all_to_all | solution.py:16
  (10 other events, 15.9 us)

commit v4 on v3

--- a/solution.py
+++ b/solution.py
@@ -47,7 +47,7 @@
     return (scaled - first - normed * second) * rstd
 
 
-def vmem_call(body, outs, *args, scalars=0, cost=None):
+def vmem_call(body, outs, *args, scalars=0, cost=None, scratch=()):
     smem = pl.BlockSpec(memory_space=pltpu.SMEM)
     vmem = pl.BlockSpec(memory_space=pltpu.VMEM)
     return pl.pallas_call(
@@ -57,6 +57,7 @@
         out_specs=[vmem] * len(outs),
         compiler_params=pltpu.CompilerParams(vmem_limit_bytes=32 << 20),
         cost_estimate=cost,
+        scratch_shapes=[pltpu.VMEM(*spec) for spec in scratch],
     )(*args)
 
 
@@ -78,38 +79,119 @@
     label_text[...] = total.astype(BF)
 
 
-def order_kernel(me, near, far, proj, state, vectors):
+def stack_kernel(*refs):
+    out = refs[-1]
+    for k, part in enumerate(refs[:-1]):
+        out[k] = part[...]
+
+
+def order_kernel(me, *refs):
+    sides, (proj, state, vectors, far_bias) = refs[:4], refs[4:]
     emb = proj.shape[1]
-    share = near.shape[1]
+    share = sides[0].shape[1]
     half = state.shape[1]
     at = me[0]
     first = lax.rem(at, 2) == 0
-    for c, side in enumerate((near, far)):
-        for k in range(side.shape[0]):
-            x, y = k // 4, k % 4
-            there = pl.multiple_of((at ^ (4 * y + 2 * x + c)) * share, share)
-            block = side[k]
-            proj[pl.ds(there, share), :] = block[:, :emb]
-            left = block[:, emb : emb + half]
-            right = block[:, emb + half : emb + 2 * half]
+    for side, bits in zip(sides, (0, 2, 1, 3)):
+        for y in range(side.shape[0]):
+            owner = at ^ (4 * y + bits)
+            there = pl.multiple_of(owner * share, share)
+            proj[pl.ds(there, share), :] = side[y, :, :emb]
+            left = side[y, :, emb : emb + half]
+            right = side[y, :, emb + half : emb + 2 * half]
             state[pl.ds(there, share), :] = jnp.where(first, left, right)
-            vectors[pl.ds(there, share), :] = block[:, emb + 2 * half :]
-
-
-def rows_kernel(me, state, vectors, own, lines):
+            vectors[owner] = side[y, :8, emb + 2 * half :].astype(F32)
+    parts = sides[2][0, 8:16, emb + 2 * half :].astype(F32)
+    for k in range(2):
+        far_bias[:, 128 * k : 128 * k + 128] = (
+            parts[k : k + 1] + parts[k + 2 : k + 3] + parts[k + 4 : k + 5]
+        )
+
+
+def rows_kernel(me, state, vectors, gain, bias, own, lines, normed):
     rows, half = own.shape[0], state.shape[1]
+    share = state.shape[0] // vectors.shape[0]
     start = (me[0] // 2) * rows
     at = lax.broadcasted_iota(jnp.int32, (rows, half), 1)
     line = lax.broadcasted_iota(jnp.int32, (rows, half), 0)
-    own[...] = lax.dot_general(
-        (at == line + start).astype(F32).astype(BF), state[...], NT, preferred_element_type=F32
-    )
-    at = lax.broadcasted_iota(jnp.int32, (16, half), 1)
-    line = lax.broadcasted_iota(jnp.int32, (16, half), 0)
-    pick = (at >= 3 * line) & (at < 3 * line + 3) & (line < 2)
-    lines[...] = lax.dot_general(
-        pick.astype(F32).astype(BF), vectors[...], NT, preferred_element_type=F32
-    )
+    pick = jnp.where(at == line + start, 1.0, 0.0).astype(BF)
+    own[...] = lax.dot_general(pick, state[...], NT, preferred_element_type=F32)
+    for first in range(2):
+        line = [
+            vectors[t, 3 * first : 3 * first + 1, :share]
+            + vectors[t, 3 * first + 1 : 3 * first + 2, :share]
+            + vectors[t, 3 * first + 2 : 3 * first + 3, :share]
+            for t in range(vectors.shape[0])
+        ]
+        lines[first : first + 1, :] = jnp.concatenate(line, axis=1)
+    xhat, _ = row_norm(state[...].astype(F32).T)
+    normed[...] = (xhat * gain[...] + bias[...]).astype(BF)
+
+
+def mlp_kernel(side, own, other, far_own, far_other, normed, bias, far_bias, *outs):
+    w_up, w_down, pre_act, mixed = outs
+    depth = own.shape[2]
+    for k, (mine, theirs) in enumerate(((own, other), (far_own, far_other))):
+        for z in range(own.shape[0]):
+            here = pl.multiple_of(2 * depth * z + depth * side[0], depth)
+            there = pl.multiple_of(2 * depth * z + depth * (1 - side[0]), depth)
+            w_up[k, pl.ds(here, depth), :] = mine[z, 0]
+            w_down[k, pl.ds(here, depth), :] = mine[z, 1]
+            w_up[k, pl.ds(there, depth), :] = theirs[z, 0]
+            w_down[k, pl.ds(there, depth), :] = theirs[z, 1]
+    total = jnp.zeros(mixed.shape, F32)
+    for k, add in enumerate((bias, far_bias)):
+        pre = jnp.dot(normed[...], w_up[k], preferred_element_type=F32) + add[...]
+        pre_act[k] = pre
+        hidden = (pre * jax.nn.sigmoid(1.702 * pre)).astype(BF)
+        total += lax.dot_general(hidden, w_down[k], NT, preferred_element_type=F32)
+    mixed[...] = total.astype(BF)
+
+
+def mlp_back_kernel(out_low, pre_act, w_up, w_down, normed_grad):
+    total = jnp.zeros(normed_grad.shape, F32)
+    for k in range(2):
+        hid_grad = jnp.dot(out_low[...], w_down[k], preferred_element_type=F32)
+        pre = pre_act[k]
+        gate = jax.nn.sigmoid(1.702 * pre)
+        act_grad = (hid_grad * (gate + 1.702 * pre * gate * (1.0 - gate))).astype(BF)
+        total += lax.dot_general(act_grad, w_up[k], NT, preferred_element_type=F32)
+    normed_grad[...] = total.astype(BF)
+
+
+def softmax_kernel(unit_low, text_unit, label, back, logits):
+    half, emb = unit_low.shape
+    n_block = 5
+    step = text_unit.shape[0] // n_block
+    top = None
+    for k in range(n_block):
+        texts = text_unit[k * step : (k + 1) * step, :]
+        block = 100.0 * lax.dot_general(unit_low[...], texts, NT, preferred_element_type=F32)
+        logits[:, k * step : (k + 1) * step] = block
+        block = jnp.max(block, axis=1, keepdims=True)
+        top = block if top is None else jnp.maximum(top, block)
+    top = top.astype(BF).astype(F32)
+    rest = jnp.zeros_like(top)
+    hit = jnp.zeros_like(top)
+    total = jnp.zeros((half, emb), F32)
+    for k in range(n_block):
+        block = jnp.exp(logits[:, k * step : (k + 1) * step] - top)
+        columns = lax.broadcasted_iota(jnp.int32, (half, step), 1) + k * step
+        target = columns == label[...]
+        others = jnp.where(target, 0.0, block)
+        rest += jnp.sum(others, axis=1, keepdims=True)
+        hit += jnp.sum(jnp.where(target, block, 0.0), axis=1, keepdims=True)
+        total += jnp.dot(
+            others.astype(BF), text_unit[k * step : (k + 1) * step, :], preferred_element_type=F32
+        )
+    back[:, :emb] = total.astype(BF)
+    lane = lax.broadcasted_iota(jnp.int32, (half, 128), 1)
+    rest_high = rest.astype(BF).astype(F32)
+    hit_high = hit.astype(BF).astype(F32)
+    stats = jnp.zeros((half, 128), F32)
+    for k, value in enumerate((top, rest_high, rest - rest_high, hit_high, hit - hit_high)):
+        stats = jnp.where(lane == k, value, stats)
+    back[:, emb:] = stats.astype(BF)
 
 
 def embed_kernel(mixed, own, bias, lines, proj, sent, unit, norm, yhat, rstd):
@@ -218,31 +300,47 @@
     mine = jnp.stack([up_weight, down_weight.T])
     mine = swapped(copies(mine, n_z), "dp", along_z)
 
-    vectors = jnp.stack(pieces(post_gain, 3) + pieces(post_bias, 3), axis=1)
-    vectors = jnp.pad(vectors, ((0, 0), (0, 128 - vectors.shape[1])))
+    vectors = jnp.stack(pieces(post_gain, 3) + pieces(post_bias, 3))
+    vectors = jnp.pad(vectors, ((0, 2), (0, 128 - share)))
+    bias_parts = jnp.stack(pieces(up_bias, 3)).reshape(3 * hid // 128, 128)
+    vectors = jnp.concatenate([vectors, bias_parts])
+    vectors = jnp.pad(vectors, ((0, share - vectors.shape[0]), (0, 0)))
     chain = jnp.concatenate([projection, resid.T, vectors], axis=1)
     far_texts = from_partner(texts, "txt", 1)
-    far_bias = from_partner(up_bias, "txt", 1)
-    chain = jnp.stack([chain] + [from_partner(chain, "txt", 4 * k) for k in (1, 2, 3)])
-    chain = jnp.concatenate([chain, from_partner(chain, "txt", 2)])
+    chain = [chain] + [from_partner(chain, "txt", 4 * k) for k in (1, 2, 3)]
+    (chain,) = vmem_call(
+        stack_kernel, (((len(chain), *chain[0].shape), BF),), *chain, cost=SMALL
+    )
+    chain_x = from_partner(chain, "txt", 2)
     far_chain = from_partner(chain, "txt", 1)
+    far_chain_x = from_partner(chain_x, "txt", 1)
     here = me.astype(jnp.int32).reshape(1)
-    proj, state, vectors = vmem_call(
+    proj, state, vectors, far_bias = vmem_call(
         order_kernel,
-        (((WIDTH, emb), BF), ((WIDTH, half), BF), ((WIDTH, 128), BF)),
+        (
+            ((WIDTH, emb), BF),
+            ((WIDTH, half), BF),
+            ((n_txt, 8, 128), F32),
+            ((1, hid), F32),
+        ),
         here,
         chain,
+        chain_x,
         far_chain,
+        far_chain_x,
         scalars=1,
         cost=SMALL,
     )
-    own, lines = vmem_call(
+    own, lines, normed = vmem_call(
         rows_kernel,
-        (((rows, WIDTH), F32), ((16, WIDTH), F32)),
+        (((rows, WIDTH), F32), ((8, WIDTH), F32), ((half, WIDTH), BF)),
         here,
         state,
         vectors,
+        prenorm_gain[None],
+        prenorm_bias[None],
         scalars=1,
+        cost=SMALL,
     )
 
     label = lax.dynamic_slice_in_dim(labels, core * half, half) - (me - core) * n_text
@@ -257,39 +355,32 @@
         label[:, None],
         cost=SMALL,
     )
-    target = lax.broadcasted_iota(jnp.int32, (half, 2 * n_text), 1) == label[:, None]
-    mine, label_text = lax.optimization_barrier((mine, label_text))
-    other_up = from_partner(mine[:, 0], "dp", 1)
-    other_down = from_partner(mine[:, 1], "dp", 1)
+    mine, label_text, normed = lax.optimization_barrier((mine, label_text, normed))
+    other = from_partner(mine, "dp", 1)
+    far_mine = from_partner(mine, "txt", 1)
     label_text = swapped(label_text.reshape(n_pair, rows, emb), "txt", cores)
-    first = lax.rem(lax.axis_index("dp"), 2) == 0
-
-    def whole(own, other):
-        both = jnp.stack([jnp.where(first, own, other), jnp.where(first, other, own)], axis=1)
-        return both.reshape(WIDTH, hid)
-
-    w_up = whole(mine[:, 0], other_up)
-    w_down = whole(mine[:, 1], other_down)
-    w_up = (w_up, from_partner(w_up, "txt", 1))
-    w_down = (w_down, from_partner(w_down, "txt", 1))
-
-    inputs = state.astype(F32)
-    mean_in = jnp.mean(inputs, axis=0)
-    var_in = jnp.mean(inputs * inputs, axis=0) - mean_in * mean_in
-    rstd_in = lax.rsqrt(var_in + 1e-05)
-    normed = ((inputs - mean_in) * rstd_in * prenorm_gain[:, None] + prenorm_bias[:, None]).astype(BF)
-    pre_act = [
-        jnp.einsum("di,df->if", normed, w, preferred_element_type=F32) + b
-        for w, b in zip(w_up, (up_bias, far_bias))
-    ]
-    gate = [jax.nn.sigmoid(1.702 * p) for p in pre_act]
-    hidden = [(p * g).astype(BF) for p, g in zip(pre_act, gate)]
-    mixed = sum(
-        jnp.einsum("if,df->id", h, w, preferred_element_type=F32) for h, w in zip(hidden, w_down)
-    )
-    mixed = mixed.astype(BF).reshape(n_pair, rows, WIDTH)
-    mixed, label_text = lax.optimization_barrier((mixed, label_text))
-    mixed = swapped(mixed, "txt", cores)
+    other, label_text = lax.optimization_barrier((other, label_text))
+    far_other = from_partner(other, "txt", 1)
+    side = lax.rem(lax.axis_index("dp"), 2).astype(jnp.int32).reshape(1)
+    w_up, w_down, pre_act, mixed = vmem_call(
+        mlp_kernel,
+        (
+            ((2, WIDTH, hid), BF),
+            ((2, WIDTH, hid), BF),
+            ((2, half, hid), F32),
+            ((half, WIDTH), BF),
+        ),
+        side,
+        mine,
+        other,
+        far_mine,
+        far_other,
+        normed,
+        up_bias[None],
+        far_bias,
+        scalars=1,
+    )
+    mixed = swapped(mixed.reshape(n_pair, rows, WIDTH), "txt", cores)
 
     sent, unit_vec, emb_norm, yhat, rstd_out = vmem_call(
         embed_kernel,
@@ -308,16 +399,15 @@
     )
     unit_low = swapped(sent, "txt", cores).reshape(half, emb)
 
-    logits = 100.0 * jnp.einsum("ie,je->ij", unit_low, text_unit, preferred_element_type=F32)
-    top = lax.reduce_precision(jnp.max(logits, axis=1), 8, 7)
-    exponent = jnp.exp(logits - top[:, None])
-    others = jnp.where(target, 0.0, exponent)
-    rest = jnp.sum(others, axis=1)
-    hit = jnp.sum(jnp.where(target, exponent, 0.0), axis=1)
-    back = jnp.dot(others.astype(BF), text_unit, preferred_element_type=F32).astype(BF)
-    stats = jnp.stack(pieces(top, 1) + pieces(rest, 2) + pieces(hit, 2), axis=1)
-    stats = jnp.pad(stats, ((0, 0), (0, 128 - stats.shape[1])))
-    back = jnp.concatenate([back, stats], axis=1).reshape(n_pair, rows, emb + 128)
+    (back,) = vmem_call(
+        softmax_kernel,
+        (((half, emb + 128), BF),),
+        unit_low,
+        text_unit,
+        label[:, None],
+        scratch=(((half, 2 * n_text), F32),),
+    )
+    back = back.reshape(n_pair, rows, emb + 128)
     back = swapped(back, "txt", cores)
 
     sent, out_grad = vmem_call(
@@ -334,12 +424,10 @@
     )
     out_low = swapped(sent, "txt", cores).reshape(half, WIDTH)
 
-    normed_grad = 0.0
-    for p, g, up, down in zip(pre_act, gate, w_up, w_down):
-        hid_grad = jnp.einsum("id,df->if", out_low, down, preferred_element_type=F32)
-        act_grad = (hid_grad * (g + 1.702 * p * g * (1.0 - g))).astype(BF)
-        normed_grad += jnp.einsum("if,df->id", act_grad, up, preferred_element_type=F32)
-    normed_grad = swapped(normed_grad.astype(BF).reshape(n_pair, rows, WIDTH), "txt", cores)
+    (normed_grad,) = vmem_call(
+        mlp_back_kernel, (((half, WIDTH), BF),), out_low, pre_act, w_up, w_down
+    )
+    normed_grad = swapped(normed_grad.reshape(n_pair, rows, WIDTH), "txt", cores)
     (change,) = vmem_call(
         change_kernel,
         (((n_txt, rows // 2, 2 * share), F32),),

time: 174 us -> 165 us (0.948)
  blocking collectives: 31.7 us -> 49.4 us
  matrix products: 10.8 us -> 0 us
  starting transfers between devices: 66 us -> 58.8 us
  other arithmetic: 9.33 us -> 3.15 us
  Pallas kernels: 9.44 us -> 13.7 us
  waiting for transfers between devices: 33.2 us -> 29.4 us
  local copies, waits for them, and re-layouts: 11.4 us -> 8.24 us
    all_to_all x3 -> x5, blocking collectives: 31.7 us -> 49.4 us  [swapped(): return lax.all_to_all(x, axis, 0, 0, tiled=True, axis_index_groups=groups)]
    all_to_all x5 -> x3, starting transfers between devices: 32.1 us -> 17.1 us  [swapped(): return lax.all_to_all(x, axis, 0, 0, tiled=True, axis_index_groups=groups)]
    dot_general x8 -> x0, matrix products: 10.8 us -> none  [the longest x1 3.83 us: local(): jnp.einsum('ie,je->ij', unit_low, text_unit, preferred_element_type=F32)]
    ppermute x11 -> x10, starting transfers between devices: 33.9 us -> 41.7 us  [from_partner(): return lax.ppermute(x, axis, pairs)]
    pallas_call x7 -> x11, Pallas kernels: 9.44 us -> 13.7 us  [vmem_call(): pl.pallas_call(body, out_shape=[jax.ShapeDtypeStruct(s, d) for s, d in ou...]
    another operation x6 -> x2, other arithmetic: 4.9 us -> 0.69 us  [the longest x1 0.68 us: local(): vectors = jnp.stack(pieces(post_gain, 3) + pieces(post_bias, 3))]
    all_to_all x5 -> x3, waiting for transfers between devices: 17.5 us -> 13.7 us  [swapped(): return lax.all_to_all(x, axis, 0, 0, tiled=True, axis_index_groups=groups)]
    unnamed x55 -> x26, local copies, waits for them, and re-layouts: 8.26 us -> 7.2 us
  transfers between devices with their start and end apart: 16 -> 13, of which waited for: 6 -> 7; matrix products, arithmetic and copies ran while one was open for 7% -> 3% of each run, Pallas kernels for 4% -> 3%
where the time goes in v4:
time: 165 us; the launch traced here: 164 us
  starting transfers between devices  58.8 us (36%)
  blocking collectives  49.4 us (30%)
  waiting for transfers between devices  29.4 us (18%)
  Pallas kernels  13.7 us (8%)
  local copies, waits for them, and re-layouts  8.24 us (5%)
  other arithmetic  3.15 us (2%)
    all_to_all x5, blocking collectives, swapped(): return lax.all_to_all(x, axis, 0, 0, tiled=True, axis_index_groups=groups)  49.4 us
    ppermute x10, starting transfers between devices, from_partner(): return lax.ppermute(x, axis, pairs)  41.7 us
    all_to_all x3, starting transfers between devices, swapped(): return lax.all_to_all(x, axis, 0, 0, tiled=True, axis_index_groups=groups)  17.1 us
    ppermute x10, waiting for transfers between devices, from_partner(): return lax.ppermute(x, axis, pairs)  15.7 us
    pallas_call x11, Pallas kernels, vmem_call(): pl.pallas_call(body, out_shape=[jax.ShapeDtypeStruct(s, d) for s, d in ou...  13.7 us
    all_to_all x3, waiting for transfers between devices, swapped(): return lax.all_to_all(x, axis, 0, 0, tiled=True, axis_index_groups=groups)  13.7 us
    unnamed x26, local copies, waits for them, and re-layouts  7.2 us
  transfers between devices with their start and end apart: 13, of which 7 were waited for; matrix products, arithmetic and copies ran while one was open for 3% of the time, Pallas kernels for 3%

profile of v4, /device:TPU:1, one launch (start us, length us, event | category | flops | bytes accessed | tf_op | source)
XLA Modules:
  0.0 163.7 jit_solution(6798456150365349560)
XLA Ops:
  0.0 8.9 %collective-permute-start = (bf16[1280,768]{1,0:T(8,128)(2,1)}, bf16[1280,768]{1,0:T(8,128)(2,1)}, u32[]{:S(2)}, u32[]{:S(2)}) collective-permute-start(bf16[1280,768]{1,0:T(8,128)(2,1)} %near.1), channel_id=1, source_target_pairs={{0,1},{1,0},{2,3},{3,2},{4,5},{5,4},{6,7},{7,6},{8,9},{9,8},{10,11... | collective-permute-start | bytes 5898248 | tf_op jit(solution)/shard_map/ppermute | solution.py:25
  10.5 9.5 %all-to-all-start = ((bf16[16,2,32,256]{3,2,1,0:T(8,128)(2,1)}), bf16[16,2,32,256]{3,2,1,0:T(8,128)(2,1)S(1)}, u32[]{:S(2)}, u32[]{:S(2)}) async-start(bf16[16,2,32,256]{3,2,1,0:T(8,128)(2,1)} %broadcast_in_dim.27), calls=%async_computation | async-start | bytes 1048576 | tf_op jit(solution)/shard_map/all_to_all | solution.py:16
  22.5 3.2 %collective-permute-start.1 = (bf16[64,1152]{1,0:T(8,128)(2,1)S(1)}, bf16[64,1152]{1,0:T(8,128)(2,1)S(1)}, u32[]{:S(2)}, u32[]{:S(2)}) collective-permute-start(bf16[64,1152]{1,0:T(8,128)(2,1)S(1)} %fusion.1.refs_0_), channel_id=1, source_target_pairs={{0,4},{1,5},{2,6},{3,7},{4,0},{5,1},{6,2},{7,3},{8,12},{9,13},{10,... | collective-permute-start | bytes 442376 | tf_op jit(solution)/shard_map/ppermute | solution.py:25
  25.7 4.5 %collective-permute-start.2 = (bf16[64,1152]{1,0:T(8,128)(2,1)S(1)}, bf16[64,1152]{1,0:T(8,128)(2,1)S(1)}, u32[]{:S(2)}, u32[]{:S(2)}) collective-permute-start(bf16[64,1152]{1,0:T(8,128)(2,1)S(1)} %fusion.1.refs_0_), channel_id=1, source_target_pairs={{0,8},{1,9},{2,10},{3,11},{4,12},{5,13},{6,14},{7,15},{8,0},{9,1},... | collective-permute-start | bytes 442376 | tf_op jit(solution)/shard_map/ppermute | solution.py:25
  30.2 1.9 %collective-permute-start.3 = (bf16[64,1152]{1,0:T(8,128)(2,1)S(1)}, bf16[64,1152]{1,0:T(8,128)(2,1)S(1)}, u32[]{:S(2)}, u32[]{:S(2)}) collective-permute-start(bf16[64,1152]{1,0:T(8,128)(2,1)S(1)} %fusion.1.refs_0_), channel_id=1, source_target_pairs={{0,12},{1,13},{2,14},{3,15},{4,8},{5,9},{6,10},{7,11},{8,4},{9,5},... | collective-permute-start | bytes 442376 | tf_op jit(solution)/shard_map/ppermute | solution.py:25
  32.2 3.0 %collective-permute-done.2.refs_2_ = bf16[64,1152]{1,0:T(8,128)(2,1)S(1)} collective-permute-done((bf16[64,1152]{1,0:T(8,128)(2,1)S(1)}, bf16[64,1152]{1,0:T(8,128)(2,1)S(1)}, u32[]{:S(2)}, u32[]{:S(2)}) %collective-permute-start.2) | collective-permute-done | bytes 147488 | tf_op jit(solution)/shard_map/ppermute | solution.py:25
  35.2 2.7 %collective-permute-done.3.refs_3_ = bf16[64,1152]{1,0:T(8,128)(2,1)S(1)} collective-permute-done((bf16[64,1152]{1,0:T(8,128)(2,1)S(1)}, bf16[64,1152]{1,0:T(8,128)(2,1)S(1)}, u32[]{:S(2)}, u32[]{:S(2)}) %collective-permute-start.3) | collective-permute-done | bytes 147488 | tf_op jit(solution)/shard_map/ppermute | solution.py:25
  37.9 3.1 %collective-permute-start.4 = (bf16[4,64,1152]{2,1,0:T(8,128)(2,1)S(1)}, bf16[4,64,1152]{2,1,0:T(8,128)(2,1)S(1)}, u32[]{:S(2)}, u32[]{:S(2)}) collective-permute-start(bf16[4,64,1152]{2,1,0:T(8,128)(2,1)S(1)} %shard_map.128.refs_0_), channel_id=1, source_target_pairs={{0,2},{1,3},{2,0},{3,1},{4,6},{5,7},{6,4},{7,5},{8,10},{9,11},{10,... | collective-permute-start | bytes 1769480 | tf_op jit(solution)/shard_map/ppermute | solution.py:25
  41.0 3.9 %collective-permute-start.5 = (bf16[4,64,1152]{2,1,0:T(8,128)(2,1)S(1)}, bf16[4,64,1152]{2,1,0:T(8,128)(2,1)S(1)}, u32[]{:S(2)}, u32[]{:S(2)}) collective-permute-start(bf16[4,64,1152]{2,1,0:T(8,128)(2,1)S(1)} %shard_map.128.refs_0_), channel_id=1, source_target_pairs={{0,1},{1,0},{2,3},{3,2},{4,5},{5,4},{6,7},{7,6},{8,9},{9,8},{10,11... | collective-permute-start | bytes 1769480 | tf_op jit(solution)/shard_map/ppermute | solution.py:25
  45.0 7.9 %collective-permute-done.4.refs_1_ = bf16[4,64,1152]{2,1,0:T(8,128)(2,1)S(1)} collective-permute-done((bf16[4,64,1152]{2,1,0:T(8,128)(2,1)S(1)}, bf16[4,64,1152]{2,1,0:T(8,128)(2,1)S(1)}, u32[]{:S(2)}, u32[]{:S(2)}) %collective-permute-start.4) | collective-permute-done | bytes 589856 | tf_op jit(solution)/shard_map/ppermute | solution.py:25
  52.9 4.6 %collective-permute-start.6 = (bf16[4,64,1152]{2,1,0:T(8,128)(2,1)S(1)}, bf16[4,64,1152]{2,1,0:T(8,128)(2,1)S(1)}, u32[]{:S(2)}, u32[]{:S(2)}) collective-permute-start(bf16[4,64,1152]{2,1,0:T(8,128)(2,1)S(1)} %collective-permute-done.4.refs_1_), channel_id=1, source_target_pairs={{0,1},{1,0},{2,3},{3,2},{4,5},{5,4},{6,7},{7,6},{8,9},{9,8},{10,11... | collective-permute-start | bytes 1769480 | tf_op jit(solution)/shard_map/ppermute | solution.py:25
  59.9 1.1 copy-done.4
  60.9 1.1 copy-done.6
  62.5 1.5 copy-done.2
  64.1 4.5 %shard_map.127 = (bf16[2560,768]{1,0:T(8,128)(2,1)S(1)}, bf16[128,768]{1,0:T(8,128)(2,1)}) custom-call(bf16[1280,768]{1,0:T(8,128)(2,1)S(1)} %copy-done.2, bf16[1280,768]{1,0:T(8,128)(2,1)} %collective-permute-done.far, s32[128,1]{1,0:T(8,128)S(1)} %copy.14.label), custom_call_target="tpu_custom_call" | custom-call | flops 1024 | bytes 1024 | tf_op jit(solution)/shard_map/pallas_call | solution.py:53
  68.6 1.9 %copy-done = bf16[2560,768]{1,0:T(8,128)(2,1)} copy-done((bf16[2560,768]{1,0:T(8,128)(2,1)}, bf16[2560,768]{1,0:T(8,128)(2,1)S(1)}, u32[]{:S(2)}) %copy-start) | copy-done | bytes 3932184
  70.4 4.8 %collective-permute-start.7 = (bf16[16,2,32,256]{3,2,1,0:T(8,128)(2,1)S(1)}, bf16[16,2,32,256]{3,2,1,0:T(8,128)(2,1)S(1)}, u32[]{:S(2)}, u32[]{:S(2)}) collective-permute-start(bf16[16,2,32,256]{3,2,1,0:T(8,128)(2,1)S(1)} %all-to-all-done.own), channel_id=1, source_target_pairs={{0,16},{16,0},{32,48},{48,32},{64,80},{80,64},{96,112},{112,96},{1... | collective-permute-start | bytes 1572872 | tf_op jit(solution)/shard_map/ppermute | solution.py:25
  75.2 4.1 %all-to-all-start.1 = ((bf16[8,16,768]{2,1,0:T(8,128)(2,1)}), bf16[8,16,768]{2,1,0:T(8,128)(2,1)S(1)}, u32[]{:S(2)}, u32[]{:S(2)}) async-start(bf16[8,16,768]{2,1,0:T(8,128)(2,1)} %bitcast.15), calls=%async_computation.1 | async-start | bytes 393216 | tf_op jit(solution)/shard_map/all_to_all | solution.py:16
  79.3 2.8 %collective-permute-start.8 = (bf16[16,2,32,256]{3,2,1,0:T(8,128)(2,1)S(1)}, bf16[16,2,32,256]{3,2,1,0:T(8,128)(2,1)}, u32[]{:S(2)}, u32[]{:S(2)}) collective-permute-start(bf16[16,2,32,256]{3,2,1,0:T(8,128)(2,1)S(1)} %all-to-all-done.own), channel_id=1, source_target_pairs={{0,1},{1,0},{2,3},{3,2},{4,5},{5,4},{6,7},{7,6},{8,9},{9,8},{10,11... | collective-permute-start | bytes 1572872 | tf_op jit(solution)/shard_map/ppermute | solution.py:25
  82.2 8.3 %all-to-all-done.1.label_parts = bf16[8,16,768]{2,1,0:T(8,128)(2,1)S(1)} async-done(((bf16[8,16,768]{2,1,0:T(8,128)(2,1)}), bf16[8,16,768]{2,1,0:T(8,128)(2,1)S(1)}, u32[]{:S(2)}, u32[]{:S(2)}) %all-to-all-start.1) | async-done | bytes 196640 | tf_op jit(solution)/shard_map/all_to_all | solution.py:16
  90.4 3.9 %collective-permute-start.9 = (bf16[16,2,32,256]{3,2,1,0:T(8,128)(2,1)S(1)}, bf16[16,2,32,256]{3,2,1,0:T(8,128)(2,1)}, u32[]{:S(2)}, u32[]{:S(2)}) collective-permute-start(bf16[16,2,32,256]{3,2,1,0:T(8,128)(2,1)S(1)} %collective-permute-done.7.other), channel_id=1, source_target_pairs={{0,1},{1,0},{2,3},{3,2},{4,5},{5,4},{6,7},{7,6},{8,9},{9,8},{10,11... | collective-permute-start | bytes 1572872 | tf_op jit(solution)/shard_map/ppermute | solution.py:25
  94.4 1.6 collective-permute-done.9.far_other
  96.0 2.2 %shard_map.131 = (bf16[2,1024,256]{2,1,0:T(8,128)(2,1)S(1)}, bf16[2,1024,256]{2,1,0:T(8,128)(2,1)S(1)}, f32[2,128,256]{2,1,0:T(8,128)S(1)}, bf16[128,1024]{1,0:T(8,128)(2,1)S(1)}) custom-call(s32[1]{0:T(128)} %bitcast.side, bf16[16,2,32,256]{3,2,1,0:T(8,128)(2,1)S(1)} %all-to-all-done.own, bf16[16,2,32,256]{3,2,1,0:T(8,128)(2,1)S(1)} %collective-permute-done.7.other, ...), custom_call_target="tpu_custom_call" | custom-call | tf_op jit(solution)/shard_map/pallas_call | solution.py:53
  98.2 9.4 %all_to_all.40.mixed = bf16[8,16,1024]{2,1,0:T(8,128)(2,1)S(1)} all-to-all(bf16[8,16,1024]{2,1,0:T(8,128)(2,1)S(1)} %bitcast.37), channel_id=1, replica_groups={{0,2,4,6,8,10,12,14},{1,3,5,7,9,11,13,15},{16,18,20,22,24,26,28,30},{17..., dimensions={0} | all-to-all | bytes 524288 | tf_op jit(solution)/shard_map/all_to_all | solution.py:16
  108.2 8.4 %all_to_all.41 = bf16[8,16,768]{2,1,0:T(8,128)(2,1)S(1)} all-to-all(bf16[8,16,768]{2,1,0:T(8,128)(2,1)S(1)} %get-tuple-element.43), channel_id=1, replica_groups={{0,2,4,6,8,10,12,14},{1,3,5,7,9,11,13,15},{16,18,20,22,24,26,28,30},{17..., dimensions={0} | all-to-all | bytes 393216 | tf_op jit(solution)/shard_map/all_to_all | solution.py:16
  116.6 2.6 %shard_map.133 = bf16[128,896]{1,0:T(8,128)(2,1)S(1)} custom-call(bf16[128,768]{1,0:T(8,128)(2,1)S(1)} %bitcast.36, bf16[2560,768]{1,0:T(8,128)(2,1)S(1)} %copy-done.1, s32[128,1]{1,0:T(8,128)S(1)} %copy.14.label), custom_call_target="tpu_custom_call" | custom-call | tf_op jit(solution)/shard_map/pallas_call | solution.py:53
  119.2 8.4 %all_to_all.42.back = bf16[8,16,896]{2,1,0:T(8,128)(2,1)S(1)} all-to-all(bf16[8,16,896]{2,1,0:T(8,128)(2,1)S(1)} %bitcast.35), channel_id=1, replica_groups={{0,2,4,6,8,10,12,14},{1,3,5,7,9,11,13,15},{16,18,20,22,24,26,28,30},{17..., dimensions={0} | all-to-all | bytes 458752 | tf_op jit(solution)/shard_map/all_to_all | solution.py:16
  128.5 8.5 %all_to_all.43 = bf16[8,16,1024]{2,1,0:T(8,128)(2,1)S(1)} all-to-all(bf16[8,16,1024]{2,1,0:T(8,128)(2,1)S(1)} %get-tuple-element.50), channel_id=1, replica_groups={{0,2,4,6,8,10,12,14},{1,3,5,7,9,11,13,15},{16,18,20,22,24,26,28,30},{17..., dimensions={0} | all-to-all | bytes 524288 | tf_op jit(solution)/shard_map/all_to_all | solution.py:16
  137.0 1.4 shard_map.135
  138.4 3.4 %all-to-all-start.6 = ((bf16[8,16,1024]{2,1,0:T(8,128)(2,1)}), bf16[8,16,1024]{2,1,0:T(8,128)(2,1)S(1)}, u32[]{:S(2)}, u32[]{:S(2)}) async-start(bf16[8,16,1024]{2,1,0:T(8,128)(2,1)} %bitcast.22), calls=%async_computation.6 | async-start | bytes 524288 | tf_op jit(solution)/shard_map/all_to_all | solution.py:16
  142.5 5.4 %all-to-all-done.6.parts = bf16[8,16,1024]{2,1,0:T(8,128)(2,1)S(1)} async-done(((bf16[8,16,1024]{2,1,0:T(8,128)(2,1)}), bf16[8,16,1024]{2,1,0:T(8,128)(2,1)S(1)}, u32[]{:S(2)}, u32[]{:S(2)}) %all-to-all-start.6) | async-done | bytes 262176 | tf_op jit(solution)/shard_map/all_to_all | solution.py:16
  148.3 14.6 %all_to_all.44.parts = f32[16,8,128]{2,1,0:T(8,128)S(1)} all-to-all(f32[16,8,128]{2,1,0:T(8,128)S(1)} %shard_map.136), channel_id=1, replica_groups=mesh['dp'=32,'txt'=16] {'txt'}, dimensions={0} | all-to-all | bytes 131072 | tf_op jit(solution)/shard_map/all_to_all | solution.py:16
  (50 shorter events, 9.5 us)
Async XLA Ops:
  0.0 57.5 %copy-start.12 = (s32[256]{0:T(256)S(1)}, s32[256]{0:T(256)}, u32[]{:S(2)}) copy-start(s32[256]{0:T(256)} %param.24) | copy-start | bytes 3076
  0.0 62.5 %collective-permute-start = (bf16[1280,768]{1,0:T(8,128)(2,1)}, bf16[1280,768]{1,0:T(8,128)(2,1)}, u32[]{:S(2)}, u32[]{:S(2)}) collective-permute-start(bf16[1280,768]{1,0:T(8,128)(2,1)} %near.1), channel_id=1, source_target_pairs={{0,1},{1,0},{2,3},{3,2},{4,5},{5,4},{6,7},{7,6},{8,9},{9,8},{10,11... | collective-permute-start | bytes 5898248 | tf_op jit(solution)/shard_map/ppermute | solution.py:25
  10.5 59.9 %all-to-all-start = ((bf16[16,2,32,256]{3,2,1,0:T(8,128)(2,1)}), bf16[16,2,32,256]{3,2,1,0:T(8,128)(2,1)S(1)}, u32[]{:S(2)}, u32[]{:S(2)}) async-start(bf16[16,2,32,256]{3,2,1,0:T(8,128)(2,1)} %broadcast_in_dim.27), calls=%async_computation | async-start | bytes 1048576 | tf_op jit(solution)/shard_map/all_to_all | solution.py:16
  21.5 40.7 %copy-start.8 = (f32[1024]{0:T(1024)S(1)}, f32[1024]{0:T(1024)}, u32[]{:S(2)}) copy-start(f32[1024]{0:T(1024)} %param.14) | copy-start | bytes 12292
  21.5 40.7 %copy-start.9 = (f32[1024]{0:T(1024)S(1)}, f32[1024]{0:T(1024)}, u32[]{:S(2)}) copy-start(f32[1024]{0:T(1024)} %param.15) | copy-start | bytes 12292
  22.5 9.7 %collective-permute-start.1 = (bf16[64,1152]{1,0:T(8,128)(2,1)S(1)}, bf16[64,1152]{1,0:T(8,128)(2,1)S(1)}, u32[]{:S(2)}, u32[]{:S(2)}) collective-permute-start(bf16[64,1152]{1,0:T(8,128)(2,1)S(1)} %fusion.1.refs_0_), channel_id=1, source_target_pairs={{0,4},{1,5},{2,6},{3,7},{4,0},{5,1},{6,2},{7,3},{8,12},{9,13},{10,... | collective-permute-start | bytes 442376 | tf_op jit(solution)/shard_map/ppermute | solution.py:25
  25.7 9.4 %collective-permute-start.2 = (bf16[64,1152]{1,0:T(8,128)(2,1)S(1)}, bf16[64,1152]{1,0:T(8,128)(2,1)S(1)}, u32[]{:S(2)}, u32[]{:S(2)}) collective-permute-start(bf16[64,1152]{1,0:T(8,128)(2,1)S(1)} %fusion.1.refs_0_), channel_id=1, source_target_pairs={{0,8},{1,9},{2,10},{3,11},{4,12},{5,13},{6,14},{7,15},{8,0},{9,1},... | collective-permute-start | bytes 442376 | tf_op jit(solution)/shard_map/ppermute | solution.py:25
  30.2 7.6 %collective-permute-start.3 = (bf16[64,1152]{1,0:T(8,128)(2,1)S(1)}, bf16[64,1152]{1,0:T(8,128)(2,1)S(1)}, u32[]{:S(2)}, u32[]{:S(2)}) collective-permute-start(bf16[64,1152]{1,0:T(8,128)(2,1)S(1)} %fusion.1.refs_0_), channel_id=1, source_target_pairs={{0,12},{1,13},{2,14},{3,15},{4,8},{5,9},{6,10},{7,11},{8,4},{9,5},... | collective-permute-start | bytes 442376 | tf_op jit(solution)/shard_map/ppermute | solution.py:25
  37.9 15.0 %collective-permute-start.4 = (bf16[4,64,1152]{2,1,0:T(8,128)(2,1)S(1)}, bf16[4,64,1152]{2,1,0:T(8,128)(2,1)S(1)}, u32[]{:S(2)}, u32[]{:S(2)}) collective-permute-start(bf16[4,64,1152]{2,1,0:T(8,128)(2,1)S(1)} %shard_map.128.refs_0_), channel_id=1, source_target_pairs={{0,2},{1,3},{2,0},{3,1},{4,6},{5,7},{6,4},{7,5},{8,10},{9,11},{10,... | collective-permute-start | bytes 1769480 | tf_op jit(solution)/shard_map/ppermute | solution.py:25
  41.0 16.6 %collective-permute-start.5 = (bf16[4,64,1152]{2,1,0:T(8,128)(2,1)S(1)}, bf16[4,64,1152]{2,1,0:T(8,128)(2,1)S(1)}, u32[]{:S(2)}, u32[]{:S(2)}) collective-permute-start(bf16[4,64,1152]{2,1,0:T(8,128)(2,1)S(1)} %shard_map.128.refs_0_), channel_id=1, source_target_pairs={{0,1},{1,0},{2,3},{3,2},{4,5},{5,4},{6,7},{7,6},{8,9},{9,8},{10,11... | collective-permute-start | bytes 1769480 | tf_op jit(solution)/shard_map/ppermute | solution.py:25
  52.9 6.2 %collective-permute-start.6 = (bf16[4,64,1152]{2,1,0:T(8,128)(2,1)S(1)}, bf16[4,64,1152]{2,1,0:T(8,128)(2,1)S(1)}, u32[]{:S(2)}, u32[]{:S(2)}) collective-permute-start(bf16[4,64,1152]{2,1,0:T(8,128)(2,1)S(1)} %collective-permute-done.4.refs_1_), channel_id=1, source_target_pairs={{0,1},{1,0},{2,3},{3,2},{4,5},{5,4},{6,7},{7,6},{8,9},{9,8},{10,11... | collective-permute-start | bytes 1769480 | tf_op jit(solution)/shard_map/ppermute | solution.py:25
  57.7 0.8 copy-start.3
  59.1 0.8 copy-start.5
  59.9 1.1 copy-start.4
  60.9 1.1 copy-start.6
  62.5 1.5 copy-start.2
  64.1 32.0 %copy-start.11 = (f32[256]{0:T(256)S(1)}, f32[256]{0:T(256)}, u32[]{:S(2)}) copy-start(f32[256]{0:T(256)} %param.17) | copy-start | bytes 3076
  68.6 1.9 %copy-start = (bf16[2560,768]{1,0:T(8,128)(2,1)}, bf16[2560,768]{1,0:T(8,128)(2,1)S(1)}, u32[]{:S(2)}) copy-start(bf16[2560,768]{1,0:T(8,128)(2,1)S(1)} %get-tuple-element.44.text_unit) | copy-start | bytes 11796484
  70.4 37.2 %copy-start.10 = (f32[1024]{0:T(1024)S(1)}, f32[1024]{0:T(1024)}, u32[]{:S(2)}) copy-start(f32[1024]{0:T(1024)} %param.19) | copy-start | bytes 12292
  70.4 20.0 %collective-permute-start.7 = (bf16[16,2,32,256]{3,2,1,0:T(8,128)(2,1)S(1)}, bf16[16,2,32,256]{3,2,1,0:T(8,128)(2,1)S(1)}, u32[]{:S(2)}, u32[]{:S(2)}) collective-permute-start(bf16[16,2,32,256]{3,2,1,0:T(8,128)(2,1)S(1)} %all-to-all-done.own), channel_id=1, source_target_pairs={{0,16},{16,0},{32,48},{48,32},{64,80},{80,64},{96,112},{112,96},{1... | collective-permute-start | bytes 1572872 | tf_op jit(solution)/shard_map/ppermute | solution.py:25
  75.2 15.2 %all-to-all-start.1 = ((bf16[8,16,768]{2,1,0:T(8,128)(2,1)}), bf16[8,16,768]{2,1,0:T(8,128)(2,1)S(1)}, u32[]{:S(2)}, u32[]{:S(2)}) async-start(bf16[8,16,768]{2,1,0:T(8,128)(2,1)} %bitcast.15), calls=%async_computation.1 | async-start | bytes 393216 | tf_op jit(solution)/shard_map/all_to_all | solution.py:16
  79.3 15.1 %collective-permute-start.8 = (bf16[16,2,32,256]{3,2,1,0:T(8,128)(2,1)S(1)}, bf16[16,2,32,256]{3,2,1,0:T(8,128)(2,1)}, u32[]{:S(2)}, u32[]{:S(2)}) collective-permute-start(bf16[16,2,32,256]{3,2,1,0:T(8,128)(2,1)S(1)} %all-to-all-done.own), channel_id=1, source_target_pairs={{0,1},{1,0},{2,3},{3,2},{4,5},{5,4},{6,7},{7,6},{8,9},{9,8},{10,11... | collective-permute-start | bytes 1572872 | tf_op jit(solution)/shard_map/ppermute | solution.py:25
  90.4 5.6 %collective-permute-start.9 = (bf16[16,2,32,256]{3,2,1,0:T(8,128)(2,1)S(1)}, bf16[16,2,32,256]{3,2,1,0:T(8,128)(2,1)}, u32[]{:S(2)}, u32[]{:S(2)}) collective-permute-start(bf16[16,2,32,256]{3,2,1,0:T(8,128)(2,1)S(1)} %collective-permute-done.7.other), channel_id=1, source_target_pairs={{0,1},{1,0},{2,3},{3,2},{4,5},{5,4},{6,7},{7,6},{8,9},{9,8},{10,11... | collective-permute-start | bytes 1572872 | tf_op jit(solution)/shard_map/ppermute | solution.py:25
  96.0 20.6 %copy-start.1 = (bf16[2560,768]{1,0:T(8,128)(2,1)S(1)}, bf16[2560,768]{1,0:T(8,128)(2,1)}, u32[]{:S(2)}) copy-start(bf16[2560,768]{1,0:T(8,128)(2,1)} %copy-done) | copy-start | bytes 11796484
  137.0 25.8 %copy-start.7 = (bf16[256,64]{0,1:T(8,128)(2,1)S(1)}, bf16[256,64]{0,1:T(8,128)(2,1)}, u32[]{:S(2)}) copy-start(bf16[256,64]{0,1:T(8,128)(2,1)} %param.13) | copy-start | bytes 98308
  138.4 9.5 %all-to-all-start.6 = ((bf16[8,16,1024]{2,1,0:T(8,128)(2,1)}), bf16[8,16,1024]{2,1,0:T(8,128)(2,1)S(1)}, u32[]{:S(2)}, u32[]{:S(2)}) async-start(bf16[8,16,1024]{2,1,0:T(8,128)(2,1)} %bitcast.22), calls=%async_computation.6 | async-start | bytes 524288 | tf_op jit(solution)/shard_map/all_to_all | solution.py:16

commit v5 on v4

--- a/solution.py
+++ b/solution.py
@@ -47,7 +47,7 @@
     return (scaled - first - normed * second) * rstd
 
 
-def vmem_call(body, outs, *args, scalars=0, cost=None, scratch=()):
+def vmem_call(body, outs, *args, scalars=0, cost=None, scratch=(), grant=12):
     smem = pl.BlockSpec(memory_space=pltpu.SMEM)
     vmem = pl.BlockSpec(memory_space=pltpu.VMEM)
     return pl.pallas_call(
@@ -55,7 +55,7 @@
         out_shape=[jax.ShapeDtypeStruct(s, d) for s, d in outs],
         in_specs=[smem] * scalars + [vmem] * (len(args) - scalars),
         out_specs=[vmem] * len(outs),
-        compiler_params=pltpu.CompilerParams(vmem_limit_bytes=32 << 20),
+        compiler_params=pltpu.CompilerParams(vmem_limit_bytes=grant << 20),
         cost_estimate=cost,
         scratch_shapes=[pltpu.VMEM(*spec) for spec in scratch],
     )(*args)
@@ -79,53 +79,66 @@
     label_text[...] = total.astype(BF)
 
 
+def split_kernel(near, other, proj, rest):
+    emb = proj.shape[3]
+    for k, part in enumerate((near, other)):
+        block = part[:, :emb]
+        for y in range(proj.shape[0]):
+            proj[y, k] = block
+        rest[k] = part[:, emb:]
+
+
 def stack_kernel(*refs):
     out = refs[-1]
     for k, part in enumerate(refs[:-1]):
         out[k] = part[...]
 
 
-def order_kernel(me, *refs):
-    sides, (proj, state, vectors, far_bias) = refs[:4], refs[4:]
-    emb = proj.shape[1]
-    share = sides[0].shape[1]
-    half = state.shape[1]
+def rows_kernel(me, near, far, gain, bias, own, lines, normed, far_bias, state, vectors):
+    n_txt = vectors.shape[0]
+    share = near.shape[2]
+    rows, half = own.shape[0], state.shape[1]
     at = me[0]
     first = lax.rem(at, 2) == 0
-    for side, bits in zip(sides, (0, 2, 1, 3)):
+    for core, side in enumerate((near, far)):
         for y in range(side.shape[0]):
-            owner = at ^ (4 * y + bits)
-            there = pl.multiple_of(owner * share, share)
-            proj[pl.ds(there, share), :] = side[y, :, :emb]
-            left = side[y, :, emb : emb + half]
-            right = side[y, :, emb + half : emb + 2 * half]
-            state[pl.ds(there, share), :] = jnp.where(first, left, right)
-            vectors[owner] = side[y, :8, emb + 2 * half :].astype(F32)
-    parts = sides[2][0, 8:16, emb + 2 * half :].astype(F32)
+            for x in range(side.shape[1]):
+                owner = at ^ (4 * y + 2 * x + core)
+                there = pl.multiple_of(owner * share, share)
+                left = side[y, x, :, :half]
+                right = side[y, x, :, half : 2 * half]
+                state[pl.ds(there, share), :] = jnp.where(first, left, right)
+                vectors[owner] = side[y, x, :8, 2 * half :].astype(F32)
+    parts = far[0, 0, 8:16, 2 * half :].astype(F32)
     for k in range(2):
         far_bias[:, 128 * k : 128 * k + 128] = (
             parts[k : k + 1] + parts[k + 2 : k + 3] + parts[k + 4 : k + 5]
         )
-
-
-def rows_kernel(me, state, vectors, gain, bias, own, lines, normed):
-    rows, half = own.shape[0], state.shape[1]
-    share = state.shape[0] // vectors.shape[0]
-    start = (me[0] // 2) * rows
-    at = lax.broadcasted_iota(jnp.int32, (rows, half), 1)
+    start = (at // 2) * rows
+    column = lax.broadcasted_iota(jnp.int32, (rows, half), 1)
     line = lax.broadcasted_iota(jnp.int32, (rows, half), 0)
-    pick = jnp.where(at == line + start, 1.0, 0.0).astype(BF)
+    pick = jnp.where(column == line + start, 1.0, 0.0).astype(BF)
     own[...] = lax.dot_general(pick, state[...], NT, preferred_element_type=F32)
-    for first in range(2):
+    for k in range(2):
         line = [
-            vectors[t, 3 * first : 3 * first + 1, :share]
-            + vectors[t, 3 * first + 1 : 3 * first + 2, :share]
-            + vectors[t, 3 * first + 2 : 3 * first + 3, :share]
-            for t in range(vectors.shape[0])
+            vectors[t, 3 * k : 3 * k + 1, :share]
+            + vectors[t, 3 * k + 1 : 3 * k + 2, :share]
+            + vectors[t, 3 * k + 2 : 3 * k + 3, :share]
+            for t in range(n_txt)
         ]
-        lines[first : first + 1, :] = jnp.concatenate(line, axis=1)
+        lines[k : k + 1, :] = jnp.concatenate(line, axis=1)
     xhat, _ = row_norm(state[...].astype(F32).T)
     normed[...] = (xhat * gain[...] + bias[...]).astype(BF)
+
+
+def proj_kernel(me, near, far, proj):
+    share = near.shape[2]
+    for core, side in enumerate((near, far)):
+        for y in range(side.shape[0]):
+            for x in range(side.shape[1]):
+                owner = 4 * y + (lax.rem(me[0], 4) ^ (2 * x + core))
+                there = pl.multiple_of(owner * share, share)
+                proj[pl.ds(there, share), :] = side[y, x]
 
 
 def mlp_kernel(side, own, other, far_own, far_other, normed, bias, far_bias, *outs):
@@ -139,7 +152,7 @@
             w_down[k, pl.ds(here, depth), :] = mine[z, 1]
             w_up[k, pl.ds(there, depth), :] = theirs[z, 0]
             w_down[k, pl.ds(there, depth), :] = theirs[z, 1]
-    total = jnp.zeros(mixed.shape, F32)
+    total = jnp.zeros(normed.shape, F32)
     for k, add in enumerate((bias, far_bias)):
         pre = jnp.dot(normed[...], w_up[k], preferred_element_type=F32) + add[...]
         pre_act[k] = pre
@@ -159,8 +172,14 @@
     normed_grad[...] = total.astype(BF)
 
 
-def softmax_kernel(unit_low, text_unit, label, back, logits):
+def softmax_kernel(arrived, text_unit, label, back, label_rows, logits, unit_low):
     half, emb = unit_low.shape
+    n = arrived.shape[0]
+    texts = jnp.zeros(label_rows.shape, F32)
+    for j in range(n):
+        unit_low[j * half // n : (j + 1) * half // n, :] = arrived[j, :, :emb]
+        texts += arrived[j, :, emb:].astype(F32)
+    label_rows[...] = texts
     n_block = 5
     step = text_unit.shape[0] // n_block
     top = None
@@ -194,8 +213,10 @@
     back[:, emb:] = stats.astype(BF)
 
 
-def embed_kernel(mixed, own, bias, lines, proj, sent, unit, norm, yhat, rstd):
+def embed_kernel(mixed, own, bias, lines, proj, label_text, sent, unit, norm, yhat, rstd):
     n = mixed.shape[0]
+    emb = unit.shape[1]
+    rows = own.shape[0]
     total = own[...] + bias[...]
     for j in range(n):
         total += mixed[j].astype(F32)
@@ -210,18 +231,17 @@
     unit[...] = vec
     low = vec.astype(BF)
     for j in range(n):
-        sent[j] = low
-
-
-def embed_back_kernel(back, label_parts, unit, norm, yhat, rstd, lines, proj, sent, grad):
+        sent[j, :, :emb] = low
+        sent[j, :, emb:] = label_text[j * rows : (j + 1) * rows, :]
+
+
+def embed_back_kernel(back, label_rows, unit, norm, yhat, rstd, lines, proj, sent, grad):
     n = back.shape[0]
     emb = unit.shape[1]
     stats = [back[j, :, emb:].astype(F32) for j in range(n)]
     top = stats[0][:, 0:1]
-    label_rows = label_parts[0].astype(F32)
     for j in range(1, n):
         top = jnp.maximum(top, stats[j][:, 0:1])
-        label_rows += label_parts[j].astype(F32)
     rest = jnp.zeros_like(top)
     hit = jnp.zeros_like(top)
     unit_grad = jnp.zeros(unit.shape, F32)
@@ -230,7 +250,7 @@
         rest += weight * (stats[j][:, 1:2] + stats[j][:, 2:3])
         hit += weight * (stats[j][:, 3:4] + stats[j][:, 4:5])
         unit_grad += weight * back[j, :, :emb].astype(F32)
-    unit_grad = (unit_grad - rest * label_rows) * (100.0 / (rest + hit))
+    unit_grad = (unit_grad - rest * label_rows[...]) * (100.0 / (rest + hit))
     vec = unit[...]
     along = jnp.sum(vec * unit_grad, axis=1, keepdims=True)
     emb_grad = ((unit_grad - vec * along) / norm[:, 0:1]).astype(BF)
@@ -307,60 +327,44 @@
     vectors = jnp.pad(vectors, ((0, share - vectors.shape[0]), (0, 0)))
     chain = jnp.concatenate([projection, resid.T, vectors], axis=1)
     far_texts = from_partner(texts, "txt", 1)
-    chain = [chain] + [from_partner(chain, "txt", 4 * k) for k in (1, 2, 3)]
-    (chain,) = vmem_call(
-        stack_kernel, (((len(chain), *chain[0].shape), BF),), *chain, cost=SMALL
-    )
-    chain_x = from_partner(chain, "txt", 2)
-    far_chain = from_partner(chain, "txt", 1)
-    far_chain_x = from_partner(chain_x, "txt", 1)
+    proj, rest = vmem_call(
+        split_kernel,
+        (((4, 2, share, emb), BF), ((2, share, images + 128), BF)),
+        chain,
+        from_partner(chain, "txt", 2),
+        cost=SMALL,
+    )
+    rest = [rest] + [from_partner(rest, "txt", 4 * k) for k in (1, 2, 3)]
+    (rest,) = vmem_call(stack_kernel, (((4, *rest[0].shape), BF),), *rest, cost=SMALL)
+    far_rest = from_partner(rest, "txt", 1)
     here = me.astype(jnp.int32).reshape(1)
-    proj, state, vectors, far_bias = vmem_call(
-        order_kernel,
-        (
-            ((WIDTH, emb), BF),
-            ((WIDTH, half), BF),
-            ((n_txt, 8, 128), F32),
-            ((1, hid), F32),
-        ),
+    own, lines, normed, far_bias = vmem_call(
+        rows_kernel,
+        (((rows, WIDTH), F32), ((8, WIDTH), F32), ((half, WIDTH), BF), ((1, hid), F32)),
         here,
-        chain,
-        chain_x,
-        far_chain,
-        far_chain_x,
-        scalars=1,
-        cost=SMALL,
-    )
-    own, lines, normed = vmem_call(
-        rows_kernel,
-        (((rows, WIDTH), F32), ((8, WIDTH), F32), ((half, WIDTH), BF)),
-        here,
-        state,
-        vectors,
+        rest,
+        far_rest,
         prenorm_gain[None],
         prenorm_bias[None],
         scalars=1,
         cost=SMALL,
+        scratch=(((WIDTH, half), BF), ((n_txt, 8, 128), F32)),
     )
 
     label = lax.dynamic_slice_in_dim(labels, core * half, half) - (me - core) * n_text
     inside = (label >= 0) & (label < 2 * n_text)
     label = jnp.where(core == 0, label, jnp.where(label < n_text, label + n_text, label - n_text))
     label = jnp.where(inside, label, -1)
-    text_unit, label_text = vmem_call(
-        text_kernel,
-        (((2 * n_text, emb), BF), ((half, emb), BF)),
-        texts,
-        far_texts,
-        label[:, None],
-        cost=SMALL,
-    )
-    mine, label_text, normed = lax.optimization_barrier((mine, label_text, normed))
+    mine, proj, normed = lax.optimization_barrier((mine, proj, normed))
     other = from_partner(mine, "dp", 1)
     far_mine = from_partner(mine, "txt", 1)
-    label_text = swapped(label_text.reshape(n_pair, rows, emb), "txt", cores)
-    other, label_text = lax.optimization_barrier((other, label_text))
+    along_y = [[b + 4 * y for y in range(4)] for b in range(4)]
+    proj = swapped(proj, "txt", along_y)
     far_other = from_partner(other, "txt", 1)
+    far_proj = from_partner(proj, "txt", 1)
+    (proj,) = vmem_call(
+        proj_kernel, (((WIDTH, emb), BF),), here, proj, far_proj, scalars=1, cost=SMALL
+    )
     side = lax.rem(lax.axis_index("dp"), 2).astype(jnp.int32).reshape(1)
     w_up, w_down, pre_act, mixed = vmem_call(
         mlp_kernel,
@@ -380,12 +384,21 @@
         far_bias,
         scalars=1,
     )
+    mixed, far_texts = lax.optimization_barrier((mixed, far_texts))
+    text_unit, label_text = vmem_call(
+        text_kernel,
+        (((2 * n_text, emb), BF), ((half, emb), BF)),
+        texts,
+        far_texts,
+        label[:, None],
+        cost=pl.CostEstimate(flops=2 * 2**30, bytes_accessed=12 << 20, transcendentals=0),
+    )
     mixed = swapped(mixed.reshape(n_pair, rows, WIDTH), "txt", cores)
 
     sent, unit_vec, emb_norm, yhat, rstd_out = vmem_call(
         embed_kernel,
         (
-            ((n_pair, rows, emb), BF),
+            ((n_pair, rows, 2 * emb), BF),
             ((rows, emb), F32),
             ((rows, 128), F32),
             ((rows, WIDTH), F32),
@@ -396,16 +409,17 @@
         down_bias[None],
         lines,
         proj,
-    )
-    unit_low = swapped(sent, "txt", cores).reshape(half, emb)
-
-    (back,) = vmem_call(
+        label_text,
+    )
+    arrived = swapped(sent, "txt", cores)
+
+    back, label_rows = vmem_call(
         softmax_kernel,
-        (((half, emb + 128), BF),),
-        unit_low,
+        (((half, emb + 128), BF), ((rows, emb), F32)),
+        arrived,
         text_unit,
         label[:, None],
-        scratch=(((half, 2 * n_text), F32),),
+        scratch=(((half, 2 * n_text), F32), ((half, emb), BF)),
     )
     back = back.reshape(n_pair, rows, emb + 128)
     back = swapped(back, "txt", cores)
@@ -414,7 +428,7 @@
         embed_back_kernel,
         (((n_pair, rows, WIDTH), BF), ((rows, WIDTH), F32)),
         back,
-        label_text,
+        label_rows,
         unit_vec,
         emb_norm,
         yhat,

time: 165 us -> 167 us (1.012)
  local copies, waits for them, and re-layouts: 8.24 us -> 18.1 us
  blocking collectives: 49.4 us -> 43.6 us
  waiting for transfers between devices: 29.4 us -> 25.2 us
    all_to_all x3 -> x4, starting transfers between devices: 17.1 us -> 27.9 us  [swapped(): return lax.all_to_all(x, axis, 0, 0, tiled=True, axis_index_groups=groups)]
    unnamed x26 -> x52, local copies, waits for them, and re-layouts: 7.2 us -> 17.1 us
    ppermute x10, starting transfers between devices: 41.7 us -> 32 us  [from_partner(): return lax.ppermute(x, axis, pairs)]
    all_to_all x3 -> x4, waiting for transfers between devices: 13.7 us -> 5.43 us  [swapped(): return lax.all_to_all(x, axis, 0, 0, tiled=True, axis_index_groups=groups)]
    all_to_all x5 -> x4, blocking collectives: 49.4 us -> 43.6 us  [swapped(): return lax.all_to_all(x, axis, 0, 0, tiled=True, axis_index_groups=groups)]
    ppermute x10, waiting for transfers between devices: 15.7 us -> 19.8 us  [from_partner(): return lax.ppermute(x, axis, pairs)]
    pallas_call x11 -> x12, Pallas kernels: 13.7 us -> 14.8 us  [vmem_call(): pl.pallas_call(body, out_shape=[jax.ShapeDtypeStruct(s, d) for s, d in ou...]
  transfers between devices with their start and end apart: 13 -> 14, of which waited for: 7 -> 6; matrix products, arithmetic and copies ran while one was open for 3% -> 2% of each run, Pallas kernels for 3% -> 4%
where the time goes in v5:
time: 167 us; the launch traced here: 166 us
  starting transfers between devices  59.9 us (36%)
  blocking collectives  43.6 us (26%)
  waiting for transfers between devices  25.2 us (15%)
  local copies, waits for them, and re-layouts  18.1 us (11%)
  Pallas kernels  14.8 us (9%)
  other arithmetic  3.16 us (2%)
    all_to_all x4, blocking collectives, swapped(): return lax.all_to_all(x, axis, 0, 0, tiled=True, axis_index_groups=groups)  43.6 us
    ppermute x10, starting transfers between devices, from_partner(): return lax.ppermute(x, axis, pairs)  32 us
    all_to_all x4, starting transfers between devices, swapped(): return lax.all_to_all(x, axis, 0, 0, tiled=True, axis_index_groups=groups)  27.9 us
    ppermute x10, waiting for transfers between devices, from_partner(): return lax.ppermute(x, axis, pairs)  19.8 us
    unnamed x52, local copies, waits for them, and re-layouts  17.1 us
    pallas_call x12, Pallas kernels, vmem_call(): pl.pallas_call(body, out_shape=[jax.ShapeDtypeStruct(s, d) for s, d in ou...  14.8 us
    all_to_all x4, waiting for transfers between devices, swapped(): return lax.all_to_all(x, axis, 0, 0, tiled=True, axis_index_groups=groups)  5.43 us
  transfers between devices with their start and end apart: 14, of which 6 were waited for; matrix products, arithmetic and copies ran while one was open for 2% of the time, Pallas kernels for 4%

profile of v5, /device:TPU:1, one launch (start us, length us, event | category | flops | bytes accessed | tf_op | source)
XLA Modules:
  0.0 165.9 jit_solution(787130177010249588)
XLA Ops:
  1.6 15.7 %all-to-all-start = ((bf16[16,2,32,256]{3,2,1,0:T(8,128)(2,1)}), bf16[16,2,32,256]{3,2,1,0:T(8,128)(2,1)S(1)}, u32[]{:S(2)}, u32[]{:S(2)}) async-start(bf16[16,2,32,256]{3,2,1,0:T(8,128)(2,1)} %broadcast_in_dim.27), calls=%async_computation | async-start | bytes 1048576 | tf_op jit(solution)/shard_map/all_to_all | solution.py:16
  17.4 2.9 %collective-permute-start.8 = (bf16[1280,768]{1,0:T(8,128)(2,1)}, bf16[1280,768]{1,0:T(8,128)(2,1)}, u32[]{:S(2)}, u32[]{:S(2)}) collective-permute-start(bf16[1280,768]{1,0:T(8,128)(2,1)} %near.1), channel_id=1, source_target_pairs={{0,1},{1,0},{2,3},{3,2},{4,5},{5,4},{6,7},{7,6},{8,9},{9,8},{10,11... | collective-permute-start | bytes 5898248 | tf_op jit(solution)/shard_map/ppermute | solution.py:25
  22.7 3.1 %collective-permute-start = (bf16[64,1152]{1,0:T(8,128)(2,1)S(1)}, bf16[64,1152]{1,0:T(8,128)(2,1)S(1)}, u32[]{:S(2)}, u32[]{:S(2)}) collective-permute-start(bf16[64,1152]{1,0:T(8,128)(2,1)S(1)} %fusion.1.near), channel_id=1, source_target_pairs={{0,2},{1,3},{2,0},{3,1},{4,6},{5,7},{6,4},{7,5},{8,10},{9,11},{10,... | collective-permute-start | bytes 442376 | tf_op jit(solution)/shard_map/ppermute | solution.py:25
  25.8 4.2 %collective-permute-done.other = bf16[64,1152]{1,0:T(8,128)(2,1)S(1)} collective-permute-done((bf16[64,1152]{1,0:T(8,128)(2,1)S(1)}, bf16[64,1152]{1,0:T(8,128)(2,1)S(1)}, u32[]{:S(2)}, u32[]{:S(2)}) %collective-permute-start) | collective-permute-done | bytes 147488 | tf_op jit(solution)/shard_map/ppermute | solution.py:25
  31.0 3.2 %collective-permute-start.1 = (bf16[2,64,384]{2,1,0:T(8,128)(2,1)S(1)}, bf16[2,64,384]{2,1,0:T(8,128)(2,1)S(1)}, u32[]{:S(2)}, u32[]{:S(2)}) collective-permute-start(bf16[2,64,384]{2,1,0:T(8,128)(2,1)S(1)} %get-tuple-element.32.refs_0_), channel_id=1, source_target_pairs={{0,4},{1,5},{2,6},{3,7},{4,0},{5,1},{6,2},{7,3},{8,12},{9,13},{10,... | collective-permute-start | bytes 294920 | tf_op jit(solution)/shard_map/ppermute | solution.py:25
  34.2 4.5 %collective-permute-start.2 = (bf16[2,64,384]{2,1,0:T(8,128)(2,1)S(1)}, bf16[2,64,384]{2,1,0:T(8,128)(2,1)S(1)}, u32[]{:S(2)}, u32[]{:S(2)}) collective-permute-start(bf16[2,64,384]{2,1,0:T(8,128)(2,1)S(1)} %get-tuple-element.32.refs_0_), channel_id=1, source_target_pairs={{0,8},{1,9},{2,10},{3,11},{4,12},{5,13},{6,14},{7,15},{8,0},{9,1},... | collective-permute-start | bytes 294920 | tf_op jit(solution)/shard_map/ppermute | solution.py:25
  38.7 1.9 %collective-permute-start.3 = (bf16[2,64,384]{2,1,0:T(8,128)(2,1)S(1)}, bf16[2,64,384]{2,1,0:T(8,128)(2,1)S(1)}, u32[]{:S(2)}, u32[]{:S(2)}) collective-permute-start(bf16[2,64,384]{2,1,0:T(8,128)(2,1)S(1)} %get-tuple-element.32.refs_0_), channel_id=1, source_target_pairs={{0,12},{1,13},{2,14},{3,15},{4,8},{5,9},{6,10},{7,11},{8,4},{9,5},... | collective-permute-start | bytes 294920 | tf_op jit(solution)/shard_map/ppermute | solution.py:25
  41.4 4.2 %collective-permute-done.3.refs_3_ = bf16[2,64,384]{2,1,0:T(8,128)(2,1)S(1)} collective-permute-done((bf16[2,64,384]{2,1,0:T(8,128)(2,1)S(1)}, bf16[2,64,384]{2,1,0:T(8,128)(2,1)S(1)}, u32[]{:S(2)}, u32[]{:S(2)}) %collective-permute-start.3) | collective-permute-done | bytes 98336 | tf_op jit(solution)/shard_map/ppermute | solution.py:25
  45.6 4.1 %collective-permute-start.4 = (bf16[4,2,64,384]{3,2,1,0:T(8,128)(2,1)S(1)}, bf16[4,2,64,384]{3,2,1,0:T(8,128)(2,1)S(1)}, u32[]{:S(2)}, u32[]{:S(2)}) collective-permute-start(bf16[4,2,64,384]{3,2,1,0:T(8,128)(2,1)S(1)} %shard_map.128.near), channel_id=1, source_target_pairs={{0,1},{1,0},{2,3},{3,2},{4,5},{5,4},{6,7},{7,6},{8,9},{9,8},{10,11... | collective-permute-start | bytes 1179656 | tf_op jit(solution)/shard_map/ppermute | solution.py:25
  49.8 1.3 collective-permute-done.4.far
  52.8 3.6 %all-to-all-start.2 = ((bf16[4,2,64,768]{3,2,1,0:T(8,128)(2,1)}), bf16[4,2,64,768]{3,2,1,0:T(8,128)(2,1)S(1)}, u32[]{:S(2)}, u32[]{:S(2)}) async-start(bf16[4,2,64,768]{3,2,1,0:T(8,128)(2,1)} %get-tuple-element.41), calls=%async_computation.2 | async-start | bytes 1572864 | tf_op jit(solution)/shard_map/all_to_all | solution.py:16
  56.4 4.7 %collective-permute-start.5 = (bf16[16,2,32,256]{3,2,1,0:T(8,128)(2,1)S(1)}, bf16[16,2,32,256]{3,2,1,0:T(8,128)(2,1)S(1)}, u32[]{:S(2)}, u32[]{:S(2)}) collective-permute-start(bf16[16,2,32,256]{3,2,1,0:T(8,128)(2,1)S(1)} %all-to-all-done.own), channel_id=1, source_target_pairs={{0,16},{16,0},{32,48},{48,32},{64,80},{80,64},{96,112},{112,96},{1... | collective-permute-start | bytes 1572872 | tf_op jit(solution)/shard_map/ppermute | solution.py:25
  61.1 2.6 %collective-permute-start.6 = (bf16[16,2,32,256]{3,2,1,0:T(8,128)(2,1)S(1)}, bf16[16,2,32,256]{3,2,1,0:T(8,128)(2,1)S(1)}, u32[]{:S(2)}, u32[]{:S(2)}) collective-permute-start(bf16[16,2,32,256]{3,2,1,0:T(8,128)(2,1)S(1)} %all-to-all-done.own), channel_id=1, source_target_pairs={{0,1},{1,0},{2,3},{3,2},{4,5},{5,4},{6,7},{7,6},{8,9},{9,8},{10,11... | collective-permute-start | bytes 1572872 | tf_op jit(solution)/shard_map/ppermute | solution.py:25
  63.7 9.3 %collective-permute-done.5.other = bf16[16,2,32,256]{3,2,1,0:T(8,128)(2,1)S(1)} collective-permute-done((bf16[16,2,32,256]{3,2,1,0:T(8,128)(2,1)S(1)}, bf16[16,2,32,256]{3,2,1,0:T(8,128)(2,1)S(1)}, u32[]{:S(2)}, u32[]{:S(2)}) %collective-permute-start.5) | collective-permute-done | bytes 524320 | tf_op jit(solution)/shard_map/ppermute | solution.py:25
  73.0 3.1 %collective-permute-start.7 = (bf16[16,2,32,256]{3,2,1,0:T(8,128)(2,1)S(1)}, bf16[16,2,32,256]{3,2,1,0:T(8,128)(2,1)S(1)}, u32[]{:S(2)}, u32[]{:S(2)}) collective-permute-start(bf16[16,2,32,256]{3,2,1,0:T(8,128)(2,1)S(1)} %collective-permute-done.5.other), channel_id=1, source_target_pairs={{0,1},{1,0},{2,3},{3,2},{4,5},{5,4},{6,7},{7,6},{8,9},{9,8},{10,11... | collective-permute-start | bytes 1572872 | tf_op jit(solution)/shard_map/ppermute | solution.py:25
  76.9 1.9 %collective-permute-start.9 = (bf16[4,2,64,768]{3,2,1,0:T(8,128)(2,1)S(1)}, bf16[4,2,64,768]{3,2,1,0:T(8,128)(2,1)}, u32[]{:S(2)}, u32[]{:S(2)}) collective-permute-start(bf16[4,2,64,768]{3,2,1,0:T(8,128)(2,1)S(1)} %all-to-all-done.2.near), channel_id=1, source_target_pairs={{0,1},{1,0},{2,3},{3,2},{4,5},{5,4},{6,7},{7,6},{8,9},{9,8},{10,11... | collective-permute-start | bytes 2359304 | tf_op jit(solution)/shard_map/ppermute | solution.py:25
  80.4 1.0 copy-done.5
  86.8 5.1 %all-to-all-start.1 = ((bf16[8,16,1024]{2,1,0:T(8,128)(2,1)}), bf16[8,16,1024]{2,1,0:T(8,128)(2,1)}, u32[]{:S(2)}, u32[]{:S(2)}) async-start(bf16[8,16,1024]{2,1,0:T(8,128)(2,1)} %bitcast.33), calls=%async_computation.1 | async-start | bytes 524288 | tf_op jit(solution)/shard_map/all_to_all | solution.py:16
  92.1 1.5 copy-done.24
  93.6 3.8 %shard_map.132 = (bf16[2560,768]{1,0:T(8,128)(2,1)S(1)}, bf16[128,768]{1,0:T(8,128)(2,1)S(1)}) custom-call(bf16[1280,768]{1,0:T(8,128)(2,1)S(1)} %copy-done.24, bf16[1280,768]{1,0:T(8,128)(2,1)} %collective-permute-done.8.far, s32[128,1]{1,0:T(8,128)S(1)} %copy.14.label), custom_call_target="tpu_custom_call" | custom-call | flops 2147483648 | bytes 12582912 | tf_op jit(solution)/shard_map/pallas_call | solution.py:53
  97.4 1.9 %copy-done = bf16[2560,768]{1,0:T(8,128)(2,1)} copy-done((bf16[2560,768]{1,0:T(8,128)(2,1)}, bf16[2560,768]{1,0:T(8,128)(2,1)S(1)}, u32[]{:S(2)}) %copy-start) | copy-done | bytes 3932184
  100.0 1.2 shard_map.131.proj
  102.9 1.5 shard_map.133
  104.4 12.3 %all_to_all.40.arrived = bf16[8,16,1536]{2,1,0:T(8,128)(2,1)S(1)} all-to-all(bf16[8,16,1536]{2,1,0:T(8,128)(2,1)S(1)} %get-tuple-element.44), channel_id=1, replica_groups={{0,2,4,6,8,10,12,14},{1,3,5,7,9,11,13,15},{16,18,20,22,24,26,28,30},{17..., dimensions={0} | all-to-all | bytes 786432 | tf_op jit(solution)/shard_map/all_to_all | solution.py:16
  116.7 2.1 %copy-done.1 = bf16[2560,768]{1,0:T(8,128)(2,1)S(1)} copy-done((bf16[2560,768]{1,0:T(8,128)(2,1)S(1)}, bf16[2560,768]{1,0:T(8,128)(2,1)}, u32[]{:S(2)}) %copy-start.1) | copy-done | bytes 3932184
  118.8 2.7 %shard_map.134 = (bf16[128,896]{1,0:T(8,128)(2,1)S(1)}, f32[16,768]{1,0:T(8,128)S(1)}) custom-call(bf16[8,16,1536]{2,1,0:T(8,128)(2,1)S(1)} %all_to_all.40.arrived, bf16[2560,768]{1,0:T(8,128)(2,1)S(1)} %copy-done.1, s32[128,1]{1,0:T(8,128)S(1)} %copy.14.label), custom_call_target="tpu_custom_call" | custom-call | tf_op jit(solution)/shard_map/pallas_call | solution.py:53
  121.5 8.5 %all_to_all.41.back = bf16[8,16,896]{2,1,0:T(8,128)(2,1)S(1)} all-to-all(bf16[8,16,896]{2,1,0:T(8,128)(2,1)S(1)} %bitcast.34), channel_id=1, replica_groups={{0,2,4,6,8,10,12,14},{1,3,5,7,9,11,13,15},{16,18,20,22,24,26,28,30},{17..., dimensions={0} | all-to-all | bytes 458752 | tf_op jit(solution)/shard_map/all_to_all | solution.py:16
  131.0 8.5 %all_to_all.42 = bf16[8,16,1024]{2,1,0:T(8,128)(2,1)S(1)} all-to-all(bf16[8,16,1024]{2,1,0:T(8,128)(2,1)S(1)} %get-tuple-element.52), channel_id=1, replica_groups={{0,2,4,6,8,10,12,14},{1,3,5,7,9,11,13,15},{16,18,20,22,24,26,28,30},{17..., dimensions={0} | all-to-all | bytes 524288 | tf_op jit(solution)/shard_map/all_to_all | solution.py:16
  139.5 1.4 shard_map.136
  140.9 3.4 %all-to-all-start.6 = ((bf16[8,16,1024]{2,1,0:T(8,128)(2,1)}), bf16[8,16,1024]{2,1,0:T(8,128)(2,1)S(1)}, u32[]{:S(2)}, u32[]{:S(2)}) async-start(bf16[8,16,1024]{2,1,0:T(8,128)(2,1)} %bitcast.20), calls=%async_computation.6 | async-start | bytes 524288 | tf_op jit(solution)/shard_map/all_to_all | solution.py:16
  145.0 5.4 %all-to-all-done.6.parts = bf16[8,16,1024]{2,1,0:T(8,128)(2,1)S(1)} async-done(((bf16[8,16,1024]{2,1,0:T(8,128)(2,1)}), bf16[8,16,1024]{2,1,0:T(8,128)(2,1)S(1)}, u32[]{:S(2)}, u32[]{:S(2)}) %all-to-all-start.6) | async-done | bytes 262176 | tf_op jit(solution)/shard_map/all_to_all | solution.py:16
  150.8 14.3 %all_to_all.43.parts = f32[16,8,128]{2,1,0:T(8,128)S(1)} all-to-all(f32[16,8,128]{2,1,0:T(8,128)S(1)} %shard_map.137), channel_id=1, replica_groups=mesh['dp'=32,'txt'=16] {'txt'}, dimensions={0} | all-to-all | bytes 131072 | tf_op jit(solution)/shard_map/all_to_all | solution.py:16
  (78 shorter events, 19.7 us)
Async XLA Ops:
  0.0 51.1 %copy-start.20 = (f32[1024]{0:T(1024)S(1)}, f32[1024]{0:T(1024)}, u32[]{:S(2)}) copy-start(f32[1024]{0:T(1024)} %param.14) | copy-start | bytes 12292
  0.0 51.1 %copy-start.21 = (f32[1024]{0:T(1024)S(1)}, f32[1024]{0:T(1024)}, u32[]{:S(2)}) copy-start(f32[1024]{0:T(1024)} %param.15) | copy-start | bytes 12292
  1.6 51.2 %all-to-all-start = ((bf16[16,2,32,256]{3,2,1,0:T(8,128)(2,1)}), bf16[16,2,32,256]{3,2,1,0:T(8,128)(2,1)S(1)}, u32[]{:S(2)}, u32[]{:S(2)}) async-start(bf16[16,2,32,256]{3,2,1,0:T(8,128)(2,1)} %broadcast_in_dim.27), calls=%async_computation | async-start | bytes 1048576 | tf_op jit(solution)/shard_map/all_to_all | solution.py:16
  17.4 63.0 %copy-start.23 = (f32[256]{0:T(256)S(1)}, f32[256]{0:T(256)}, u32[]{:S(2)}) copy-start(f32[256]{0:T(256)} %param.17) | copy-start | bytes 3076
  17.4 68.7 %collective-permute-start.8 = (bf16[1280,768]{1,0:T(8,128)(2,1)}, bf16[1280,768]{1,0:T(8,128)(2,1)}, u32[]{:S(2)}, u32[]{:S(2)}) collective-permute-start(bf16[1280,768]{1,0:T(8,128)(2,1)} %near.1), channel_id=1, source_target_pairs={{0,1},{1,0},{2,3},{3,2},{4,5},{5,4},{6,7},{7,6},{8,9},{9,8},{10,11... | collective-permute-start | bytes 5898248 | tf_op jit(solution)/shard_map/ppermute | solution.py:25
  22.7 7.4 %collective-permute-start = (bf16[64,1152]{1,0:T(8,128)(2,1)S(1)}, bf16[64,1152]{1,0:T(8,128)(2,1)S(1)}, u32[]{:S(2)}, u32[]{:S(2)}) collective-permute-start(bf16[64,1152]{1,0:T(8,128)(2,1)S(1)} %fusion.1.near), channel_id=1, source_target_pairs={{0,2},{1,3},{2,0},{3,1},{4,6},{5,7},{6,4},{7,5},{8,10},{9,11},{10,... | collective-permute-start | bytes 442376 | tf_op jit(solution)/shard_map/ppermute | solution.py:25
  31.0 9.7 %collective-permute-start.1 = (bf16[2,64,384]{2,1,0:T(8,128)(2,1)S(1)}, bf16[2,64,384]{2,1,0:T(8,128)(2,1)S(1)}, u32[]{:S(2)}, u32[]{:S(2)}) collective-permute-start(bf16[2,64,384]{2,1,0:T(8,128)(2,1)S(1)} %get-tuple-element.32.refs_0_), channel_id=1, source_target_pairs={{0,4},{1,5},{2,6},{3,7},{4,0},{5,1},{6,2},{7,3},{8,12},{9,13},{10,... | collective-permute-start | bytes 294920 | tf_op jit(solution)/shard_map/ppermute | solution.py:25
  34.2 7.2 %collective-permute-start.2 = (bf16[2,64,384]{2,1,0:T(8,128)(2,1)S(1)}, bf16[2,64,384]{2,1,0:T(8,128)(2,1)S(1)}, u32[]{:S(2)}, u32[]{:S(2)}) collective-permute-start(bf16[2,64,384]{2,1,0:T(8,128)(2,1)S(1)} %get-tuple-element.32.refs_0_), channel_id=1, source_target_pairs={{0,8},{1,9},{2,10},{3,11},{4,12},{5,13},{6,14},{7,15},{8,0},{9,1},... | collective-permute-start | bytes 294920 | tf_op jit(solution)/shard_map/ppermute | solution.py:25
  38.7 6.9 %collective-permute-start.3 = (bf16[2,64,384]{2,1,0:T(8,128)(2,1)S(1)}, bf16[2,64,384]{2,1,0:T(8,128)(2,1)S(1)}, u32[]{:S(2)}, u32[]{:S(2)}) collective-permute-start(bf16[2,64,384]{2,1,0:T(8,128)(2,1)S(1)} %get-tuple-element.32.refs_0_), channel_id=1, source_target_pairs={{0,12},{1,13},{2,14},{3,15},{4,8},{5,9},{6,10},{7,11},{8,4},{9,5},... | collective-permute-start | bytes 294920 | tf_op jit(solution)/shard_map/ppermute | solution.py:25
  45.6 5.5 %collective-permute-start.4 = (bf16[4,2,64,384]{3,2,1,0:T(8,128)(2,1)S(1)}, bf16[4,2,64,384]{3,2,1,0:T(8,128)(2,1)S(1)}, u32[]{:S(2)}, u32[]{:S(2)}) collective-permute-start(bf16[4,2,64,384]{3,2,1,0:T(8,128)(2,1)S(1)} %shard_map.128.near), channel_id=1, source_target_pairs={{0,1},{1,0},{2,3},{3,2},{4,5},{5,4},{6,7},{7,6},{8,9},{9,8},{10,11... | collective-permute-start | bytes 1179656 | tf_op jit(solution)/shard_map/ppermute | solution.py:25
  52.8 39.1 %copy-start.25 = (s32[256]{0:T(256)S(1)}, s32[256]{0:T(256)}, u32[]{:S(2)}) copy-start(s32[256]{0:T(256)} %param.24) | copy-start | bytes 3076
  52.8 24.1 %all-to-all-start.2 = ((bf16[4,2,64,768]{3,2,1,0:T(8,128)(2,1)}), bf16[4,2,64,768]{3,2,1,0:T(8,128)(2,1)S(1)}, u32[]{:S(2)}, u32[]{:S(2)}) async-start(bf16[4,2,64,768]{3,2,1,0:T(8,128)(2,1)} %get-tuple-element.41), calls=%async_computation.2 | async-start | bytes 1572864 | tf_op jit(solution)/shard_map/all_to_all | solution.py:16
  56.4 16.5 %collective-permute-start.5 = (bf16[16,2,32,256]{3,2,1,0:T(8,128)(2,1)S(1)}, bf16[16,2,32,256]{3,2,1,0:T(8,128)(2,1)S(1)}, u32[]{:S(2)}, u32[]{:S(2)}) collective-permute-start(bf16[16,2,32,256]{3,2,1,0:T(8,128)(2,1)S(1)} %all-to-all-done.own), channel_id=1, source_target_pairs={{0,16},{16,0},{32,48},{48,32},{64,80},{80,64},{96,112},{112,96},{1... | collective-permute-start | bytes 1572872 | tf_op jit(solution)/shard_map/ppermute | solution.py:25
  61.1 17.7 %collective-permute-start.6 = (bf16[16,2,32,256]{3,2,1,0:T(8,128)(2,1)S(1)}, bf16[16,2,32,256]{3,2,1,0:T(8,128)(2,1)S(1)}, u32[]{:S(2)}, u32[]{:S(2)}) collective-permute-start(bf16[16,2,32,256]{3,2,1,0:T(8,128)(2,1)S(1)} %all-to-all-done.own), channel_id=1, source_target_pairs={{0,1},{1,0},{2,3},{3,2},{4,5},{5,4},{6,7},{7,6},{8,9},{9,8},{10,11... | collective-permute-start | bytes 1572872 | tf_op jit(solution)/shard_map/ppermute | solution.py:25
  73.0 6.7 %collective-permute-start.7 = (bf16[16,2,32,256]{3,2,1,0:T(8,128)(2,1)S(1)}, bf16[16,2,32,256]{3,2,1,0:T(8,128)(2,1)S(1)}, u32[]{:S(2)}, u32[]{:S(2)}) collective-permute-start(bf16[16,2,32,256]{3,2,1,0:T(8,128)(2,1)S(1)} %collective-permute-done.5.other), channel_id=1, source_target_pairs={{0,1},{1,0},{2,3},{3,2},{4,5},{5,4},{6,7},{7,6},{8,9},{9,8},{10,11... | collective-permute-start | bytes 1572872 | tf_op jit(solution)/shard_map/ppermute | solution.py:25
  76.9 23.1 %collective-permute-start.9 = (bf16[4,2,64,768]{3,2,1,0:T(8,128)(2,1)S(1)}, bf16[4,2,64,768]{3,2,1,0:T(8,128)(2,1)}, u32[]{:S(2)}, u32[]{:S(2)}) collective-permute-start(bf16[4,2,64,768]{3,2,1,0:T(8,128)(2,1)S(1)} %all-to-all-done.2.near), channel_id=1, source_target_pairs={{0,1},{1,0},{2,3},{3,2},{4,5},{5,4},{6,7},{7,6},{8,9},{9,8},{10,11... | collective-permute-start | bytes 2359304 | tf_op jit(solution)/shard_map/ppermute | solution.py:25
  78.8 0.8 copy-start.6
  80.4 1.0 copy-start.5
  81.5 1.0 copy-start.7
  82.5 1.0 copy-start.9
  83.6 0.9 copy-start.11
  86.1 11.4 %copy-start.2 = (bf16[2,1024,256]{2,1,0:T(8,128)(2,1)}, bf16[2,1024,256]{2,1,0:T(8,128)(2,1)S(1)}, u32[]{:S(2)}) copy-start(bf16[2,1024,256]{2,1,0:T(8,128)(2,1)S(1)} %get-tuple-element.55.w_down) | copy-start | bytes 3145732
  86.8 14.5 %all-to-all-start.1 = ((bf16[8,16,1024]{2,1,0:T(8,128)(2,1)}), bf16[8,16,1024]{2,1,0:T(8,128)(2,1)}, u32[]{:S(2)}, u32[]{:S(2)}) async-start(bf16[8,16,1024]{2,1,0:T(8,128)(2,1)} %bitcast.33), calls=%async_computation.1 | async-start | bytes 524288 | tf_op jit(solution)/shard_map/all_to_all | solution.py:16
  92.1 1.5 copy-start.24
  97.4 1.9 %copy-start = (bf16[2560,768]{1,0:T(8,128)(2,1)}, bf16[2560,768]{1,0:T(8,128)(2,1)S(1)}, u32[]{:S(2)}) copy-start(bf16[2560,768]{1,0:T(8,128)(2,1)S(1)} %get-tuple-element.45.text_unit) | copy-start | bytes 11796484
  100.0 1.3 copy-start.22
  101.3 0.9 copy-start.16
  116.7 2.1 %copy-start.1 = (bf16[2560,768]{1,0:T(8,128)(2,1)S(1)}, bf16[2560,768]{1,0:T(8,128)(2,1)}, u32[]{:S(2)}) copy-start(bf16[2560,768]{1,0:T(8,128)(2,1)} %copy-done) | copy-start | bytes 11796484
  121.5 18.0 %copy-start.3 = (bf16[2,1024,256]{2,1,0:T(8,128)(2,1)S(1)}, bf16[2,1024,256]{2,1,0:T(8,128)(2,1)}, u32[]{:S(2)}) copy-start(bf16[2,1024,256]{2,1,0:T(8,128)(2,1)} %copy-done.2) | copy-start | bytes 3145732
  121.5 18.0 %copy-start.14 = (f32[2,128,256]{2,1,0:T(8,128)S(1)}, f32[2,128,256]{2,1,0:T(8,128)}, u32[]{:S(2)}) copy-start(f32[2,128,256]{2,1,0:T(8,128)} %copy-done.13) | copy-start | bytes 786436
  139.5 25.6 %copy-start.19 = (bf16[256,64]{0,1:T(8,128)(2,1)S(1)}, bf16[256,64]{0,1:T(8,128)(2,1)}, u32[]{:S(2)}) copy-start(bf16[256,64]{0,1:T(8,128)(2,1)} %param.13) | copy-start | bytes 98308
  140.9 9.5 %all-to-all-start.6 = ((bf16[8,16,1024]{2,1,0:T(8,128)(2,1)}), bf16[8,16,1024]{2,1,0:T(8,128)(2,1)S(1)}, u32[]{:S(2)}, u32[]{:S(2)}) async-start(bf16[8,16,1024]{2,1,0:T(8,128)(2,1)} %bitcast.20), calls=%async_computation.6 | async-start | bytes 524288 | tf_op jit(solution)/shard_map/all_to_all | solution.py:16
  (8 other events, 5.8 us)

commit v6 on v5

v6 whole, which is shorter than its diff:
```python
import jax
import jax.numpy as jnp
from jax import lax
from jax.experimental import pallas as pl
from jax.experimental.pallas import tpu as pltpu
from jax.sharding import PartitionSpec as P

WIDTH = 1024
BF = jnp.bfloat16
F32 = jnp.float32
NT = (((1,), (1,)), ((), ()))
SMALL = pl.CostEstimate(flops=1024, bytes_accessed=1024, transcendentals=0)


def swapped(x, axis, groups=None):
    return lax.all_to_all(x, axis, 0, 0, tiled=True, axis_index_groups=groups)


def copies(x, n):
    return jnp.broadcast_to(x, (n, *x.shape))


def from_partner(x, axis, bits):
    pairs = [(i, i ^ bits) for i in range(lax.axis_size(axis))]
    return lax.ppermute(x, axis, pairs)


def pieces(x, count):
    out = []
    for _ in range(count):
        part = lax.reduce_precision(x, 8, 7)
        out.append(part.astype(BF))
        x = x - part
    return out


def row_norm(rows):
    mean = jnp.mean(rows, axis=1, keepdims=True)
    var = jnp.mean(rows * rows, axis=1, keepdims=True) - mean * mean
    rstd = lax.rsqrt(var + 1e-05)
    return (rows - mean) * rstd, rstd


def norm_back(scaled, normed, rstd):
    first = jnp.mean(scaled, axis=1, keepdims=True)
    second = jnp.mean(scaled * normed, axis=1, keepdims=True)
    return (scaled - first - normed * second) * rstd


def call(body, outs, spaces, *args, cost=None, scratch=(), sems=0):
    kinds = {"v": pltpu.VMEM, "h": pltpu.HBM, "a": pl.ANY}
    specs = [pl.BlockSpec(memory_space=kinds[c]) for c in spaces]
    shapes = [pltpu.VMEM(*spec) for spec in scratch]
    if sems:
        shapes.append(pltpu.SemaphoreType.DMA((sems,)))
    return pl.pallas_call(
        body,
        out_shape=[
            pltpu.HBM(*out) if c == "h" else jax.ShapeDtypeStruct(*out)
            for c, out in zip(spaces[len(args) :], outs)
        ],
        in_specs=specs[: len(args)],
        out_specs=specs[len(args) :],
        scratch_shapes=shapes,
        compiler_params=pltpu.CompilerParams(vmem_limit_bytes=24 << 20),
        cost_estimate=cost,
    )(*(
        pltpu.with_memory_space_constraint(arg, pltpu.HBM) if c == "h" else arg
        for c, arg in zip(spaces, args)
    ))


def local_labels(labels, n_text):
    half = labels.shape[0] // 2
    me = lax.axis_index("txt")
    core = lax.rem(me, 2)
    label = labels[pl.ds(pl.multiple_of(core * half, half), half), :] - (me - core) * n_text
    inside = (label >= 0) & (label < 2 * n_text)
    turned = jnp.where(label < n_text, label + n_text, label - n_text)
    return jnp.where(inside, jnp.where(core == 0, label, turned), -1)


def text_kernel(near, far, labels, unit, label_text, held, sem):
    n_text = near.shape[0]
    half = label_text.shape[0]
    step = 256
    count = n_text // step
    loads = []
    for k in range(2 * count):
        side = near if k < count else far
        loads.append(
            pltpu.make_async_copy(
                side.at[pl.ds((k % count) * step, step)], held.at[pl.ds(k * step, step)], sem.at[k]
            )
        )
        loads[k].start()
    label = local_labels(labels, n_text)
    total = jnp.zeros(label_text.shape, F32)
    stores = []
    for k in range(2 * count):
        loads[k].wait()
        block = held[k * step : (k + 1) * step, :].astype(F32)
        squares = jnp.sum(block * block, axis=1, keepdims=True)
        low = (block / jnp.sqrt(squares + 1e-06)).astype(BF)
        held[k * step : (k + 1) * step, :] = low
        place = pl.ds(k * step, step)
        stores.append(
            pltpu.make_async_copy(held.at[place], unit.at[place], sem.at[2 * count + k])
        )
        stores[k].start()
        columns = lax.broadcasted_iota(jnp.int32, (half, step), 1) + k * step
        pick = jnp.where(columns == label, 1.0, 0.0).astype(BF)
        total += jnp.dot(pick, low, preferred_element_type=F32)
    label_text[...] = total.astype(BF)
    for store in stores:
        store.wait()


def split_kernel(near, other, proj, rest):
    emb = proj.shape[3]
    for k, part in enumerate((near, other)):
        block = part[:, :emb]
        for y in range(proj.shape[0]):
            proj[y, k] = block
        rest[k] = part[:, emb:]


def stack_kernel(*refs):
    out = refs[-1]
    for k, part in enumerate(refs[:-1]):
        out[k] = part[...]


def rows_kernel(near, far, gain, bias, own, lines, normed, far_bias, state, vectors):
    n_txt = vectors.shape[0]
    share = near.shape[2]
    rows, half = own.shape[0], state.shape[1]
    at = lax.axis_index("txt")
    first = lax.rem(at, 2) == 0
    for core, side in enumerate((near, far)):
        for y in range(side.shape[0]):
            for x in range(side.shape[1]):
                owner = at ^ (4 * y + 2 * x + core)
                there = pl.multiple_of(owner * share, share)
                left = side[y, x, :, :half]
                right = side[y, x, :, half : 2 * half]
                state[pl.ds(there, share), :] = jnp.where(first, left, right)
                vectors[owner] = side[y, x, :8, 2 * half :].astype(F32)
    parts = far[0, 0, 8:16, 2 * half :].astype(F32)
    for k in range(2):
        far_bias[:, 128 * k : 128 * k + 128] = (
            parts[k : k + 1] + parts[k + 2 : k + 3] + parts[k + 4 : k + 5]
        )
    start = (at // 2) * rows
    column = lax.broadcasted_iota(jnp.int32, (rows, half), 1)
    line = lax.broadcasted_iota(jnp.int32, (rows, half), 0)
    pick = jnp.where(column == line + start, 1.0, 0.0).astype(BF)
    own[...] = lax.dot_general(pick, state[...], NT, preferred_element_type=F32)
    for k in range(2):
        line = [
            vectors[t, 3 * k : 3 * k + 1, :share]
            + vectors[t, 3 * k + 1 : 3 * k + 2, :share]
            + vectors[t, 3 * k + 2 : 3 * k + 3, :share]
            for t in range(n_txt)
        ]
        lines[k : k + 1, :] = jnp.concatenate(line, axis=1)
    xhat, _ = row_norm(state[...].astype(F32).T)
    normed[...] = (xhat * gain[...] + bias[...]).astype(BF)


def ordered_proj(near, far, proj, sem):
    low = lax.rem(lax.axis_index("txt"), 4)
    loads = []
    for core, side in enumerate((near, far)):
        for x in range(2):
            k = 2 * x + core
            place = proj.at[:, low ^ k]
            loads.append(pltpu.make_async_copy(side.at[:, x], place, sem.at[k]))
            loads[-1].start()
    return loads


def ordered_weights(own, other, far_own, far_other, weights, sem):
    side = lax.rem(lax.axis_index("dp"), 2)
    loads = {}
    for matrix in weights:
        for k, pair in enumerate(((own, other), (far_own, far_other))):
            for x, part in enumerate(pair):
                place = weights[matrix].at[k, :, side if x == 0 else 1 - side]
                number = 4 * matrix + 2 * k + x
                load = pltpu.make_async_copy(part.at[:, matrix], place, sem.at[number])
                load.start()
                loads[matrix, k, x] = load
    return loads


def mlp_kernel(own, other, far_own, far_other, normed, bias, far_bias, *refs):
    pre_act, mixed, up, down, sem = refs
    width, hid = normed.shape[1], bias.shape[1]
    loads = ordered_weights(own, other, far_own, far_other, {0: up, 1: down}, sem)
    total = jnp.zeros(normed.shape, F32)
    for k, add in enumerate((bias, far_bias)):
        for matrix in range(2):
            for x in range(2):
                loads[matrix, k, x].wait()
        w_up = up[k].reshape(width, hid)
        pre = jnp.dot(normed[...], w_up, preferred_element_type=F32) + add[...]
        pre_act[k] = pre
        hidden = (pre * jax.nn.sigmoid(1.702 * pre)).astype(BF)
        w_down = down[k].reshape(width, hid)
        total += lax.dot_general(hidden, w_down, NT, preferred_element_type=F32)
    mixed[...] = total.astype(BF)


def mlp_back_kernel(own, other, far_own, far_other, arrived, pre_act, *refs):
    normed_grad, up, down, sem = refs
    width, hid = arrived.shape[1], pre_act.shape[2]
    loads = ordered_weights(own, other, far_own, far_other, {1: down, 0: up}, sem)
    total = jnp.zeros(normed_grad.shape, F32)
    for k in range(2):
        for x in range(2):
            loads[1, k, x].wait()
        w_down = down[k].reshape(width, hid)
        hid_grad = jnp.dot(arrived[...], w_down, preferred_element_type=F32)
        pre = pre_act[k]
        gate = jax.nn.sigmoid(1.702 * pre)
        act_grad = (hid_grad * (gate + 1.702 * pre * gate * (1.0 - gate))).astype(BF)
        for x in range(2):
            loads[0, k, x].wait()
        w_up = up[k].reshape(width, hid)
        total += lax.dot_general(act_grad, w_up, NT, preferred_element_type=F32)
    normed_grad[...] = total.astype(BF)


def softmax_kernel(arrived, text_unit, labels, back, label_rows, logits, unit_low, held, sem):
    half, emb = unit_low.shape
    n = arrived.shape[0]
    n_block = 5
    step = text_unit.shape[0] // n_block
    loads = []
    for k in range(n_block):
        place = pl.ds(k * step, step)
        loads.append(pltpu.make_async_copy(text_unit.at[place], held.at[place], sem.at[k]))
        loads[k].start()
    texts = jnp.zeros(label_rows.shape, F32)
    for j in range(n):
        unit_low[j * half // n : (j + 1) * half // n, :] = arrived[j, :, :emb]
        texts += arrived[j, :, emb:].astype(F32)
    label_rows[...] = texts
    label = local_labels(labels, text_unit.shape[0] // 2)
    top = None
    for k in range(n_block):
        loads[k].wait()
        texts = held[k * step : (k + 1) * step, :]
        block = 100.0 * lax.dot_general(unit_low[...], texts, NT, preferred_element_type=F32)
        logits[:, k * step : (k + 1) * step] = block
        block = jnp.max(block, axis=1, keepdims=True)
        top = block if top is None else jnp.maximum(top, block)
    top = top.astype(BF).astype(F32)
    rest = jnp.zeros_like(top)
    hit = jnp.zeros_like(top)
    total = jnp.zeros((half, emb), F32)
    for k in range(n_block):
        block = jnp.exp(logits[:, k * step : (k + 1) * step] - top)
        columns = lax.broadcasted_iota(jnp.int32, (half, step), 1) + k * step
        target = columns == label
        others = jnp.where(target, 0.0, block)
        rest += jnp.sum(others, axis=1, keepdims=True)
        hit += jnp.sum(jnp.where(target, block, 0.0), axis=1, keepdims=True)
        total += jnp.dot(
            others.astype(BF), held[k * step : (k + 1) * step, :], preferred_element_type=F32
        )
    back[:, :emb] = total.astype(BF)
    lane = lax.broadcasted_iota(jnp.int32, (half, 128), 1)
    rest_high = rest.astype(BF).astype(F32)
    hit_high = hit.astype(BF).astype(F32)
    stats = jnp.zeros((half, 128), F32)
    for k, value in enumerate((top, rest_high, rest - rest_high, hit_high, hit - hit_high)):
        stats = jnp.where(lane == k, value, stats)
    back[:, emb:] = stats.astype(BF)


def embed_kernel(mixed, own, bias, lines, near, far, label_text, *refs):
    sent, unit, norm, yhat, rstd, proj, sem = refs
    loads = ordered_proj(near, far, proj, sem)
    n = mixed.shape[0]
    emb = unit.shape[1]
    rows = own.shape[0]
    total = own[...] + bias[...]
    for j in range(n):
        total += mixed[j].astype(F32)
    normed, scale = row_norm(total)
    yhat[...] = normed
    rstd[...] = jnp.broadcast_to(scale, rstd.shape)
    post_normed = (normed * lines[0:1, :] + lines[1:2, :]).astype(BF)
    for load in loads:
        load.wait()
    w_proj = proj[...].reshape(-1, emb)
    embedding = jnp.dot(post_normed, w_proj, preferred_element_type=F32)
    length = jnp.sqrt(jnp.sum(embedding * embedding, axis=1, keepdims=True) + 1e-06)
    norm[...] = jnp.broadcast_to(length, norm.shape)
    vec = embedding / length
    unit[...] = vec
    low = vec.astype(BF)
    for j in range(n):
        sent[j, :, :emb] = low
        sent[j, :, emb:] = label_text[j * rows : (j + 1) * rows, :]


def embed_back_kernel(back, label_rows, unit, norm, yhat, rstd, lines, near, far, *refs):
    sent, grad, proj, sem = refs
    loads = ordered_proj(near, far, proj, sem)
    n = back.shape[0]
    emb = unit.shape[1]
    stats = [back[j, :, emb:].astype(F32) for j in range(n)]
    top = stats[0][:, 0:1]
    for j in range(1, n):
        top = jnp.maximum(top, stats[j][:, 0:1])
    rest = jnp.zeros_like(top)
    hit = jnp.zeros_like(top)
    unit_grad = jnp.zeros(unit.shape, F32)
    for j in range(n):
        weight = jnp.exp(stats[j][:, 0:1] - top)
        rest += weight * (stats[j][:, 1:2] + stats[j][:, 2:3])
        hit += weight * (stats[j][:, 3:4] + stats[j][:, 4:5])
        unit_grad += weight * back[j, :, :emb].astype(F32)
    unit_grad = (unit_grad - rest * label_rows[...]) * (100.0 / (rest + hit))
    vec = unit[...]
    along = jnp.sum(vec * unit_grad, axis=1, keepdims=True)
    emb_grad = ((unit_grad - vec * along) / norm[:, 0:1]).astype(BF)
    for load in loads:
        load.wait()
    w_proj = proj[...].reshape(-1, emb)
    post_grad = lax.dot_general(emb_grad, w_proj, NT, preferred_element_type=F32)
    out_grad = norm_back(post_grad * lines[0:1, :], yhat[...], rstd[:, 0:1])
    grad[...] = out_grad
    low = out_grad.astype(BF)
    for j in range(n):
        sent[j] = low


def change_kernel(parts, gain, own, out_grad, step, sent):
    n, half, _ = sent.shape
    share = own.shape[1] // n
    total = parts[0].astype(F32)
    for j in range(1, parts.shape[0]):
        total += parts[j].astype(F32)
    xhat, scale = row_norm(own[...])
    grad = out_grad[...] + norm_back(total * gain[...], xhat, scale)
    rms = jnp.sqrt(jnp.mean(grad * grad, axis=1, keepdims=True) + 1e-06)
    change = step[0:1, 0:1] * grad / rms
    for j in range(n):
        block = change[:, j * share : (j + 1) * share]
        sent[j, :, :share] = block[:half]
        sent[j, :, share:] = block[half:]


def result_kernel(parts, resid, out):
    n, _, width = parts.shape
    share = width // 2
    blocks = []
    for c in range(2):
        for g in range(n // 2):
            block = parts[2 * g + c]
            blocks += [block[:, :share], block[:, share:]]
    change = jnp.concatenate(blocks, axis=0)
    out[...] = resid[...].astype(F32) + change.T


def local(
    resid,
    prenorm_gain,
    prenorm_bias,
    up_weight,
    up_bias,
    down_weight,
    down_bias,
    post_gain,
    post_bias,
    projection,
    texts,
    labels,
    step_size,
):
    n_txt, n_dp = lax.axis_size("txt"), lax.axis_size("dp")
    n_z, n_pair = n_dp // 2, n_txt // 2
    images, share = resid.shape
    half = images // 2
    rows = images // n_txt
    hid = up_weight.shape[1]
    n_text, emb = texts.shape
    cores = [[2 * i + c for i in range(n_pair)] for c in range(2)]
    along_y = [[b + 4 * y for y in range(4)] for b in range(4)]
    along_z = [[2 * z + x for z in range(n_z)] for x in range(2)]

    mine = jnp.stack([up_weight, down_weight.T], axis=0)
    mine = swapped(copies(mine, n_z), "dp", along_z)

    vectors = jnp.stack(pieces(post_gain, 3) + pieces(post_bias, 3))
    vectors = jnp.pad(vectors, ((0, 2), (0, 128 - share)))
    bias_parts = jnp.stack(pieces(up_bias, 3)).reshape(3 * hid // 128, 128)
    vectors = jnp.concatenate([vectors, bias_parts])
    vectors = jnp.pad(vectors, ((0, share - vectors.shape[0]), (0, 0)))
    chain = jnp.concatenate([projection, resid.T, vectors], axis=1)
    chain, labels = lax.optimization_barrier((chain, labels[:, None]))
    far_texts = from_partner(texts, "txt", 1)
    proj, rest = call(
        split_kernel,
        (((4, 2, share, emb), BF), ((2, share, images + 128), BF)),
        "vvvv",
        chain,
        from_partner(chain, "txt", 2),
        cost=SMALL,
    )
    rest = [rest] + [from_partner(rest, "txt", 4 * k) for k in (1, 2, 3)]
    (rest,) = call(stack_kernel, (((4, *rest[0].shape), BF),), "vvvvv", *rest, cost=SMALL)
    far_rest = from_partner(rest, "txt", 1)
    own, lines, normed, far_bias = call(
        rows_kernel,
        (((rows, WIDTH), F32), ((8, WIDTH), F32), ((half, WIDTH), BF), ((1, hid), F32)),
        "vvvvvvvv",
        rest,
        far_rest,
        prenorm_gain[None],
        prenorm_bias[None],
        cost=SMALL,
        scratch=(((WIDTH, half), BF), ((n_txt, 8, 128), F32)),
    )

    mine, proj, normed = lax.optimization_barrier((mine, proj, normed))
    other = from_partner(mine, "dp", 1)
    far_mine = from_partner(mine, "txt", 1)
    proj = swapped(proj, "txt", along_y)
    far_other = from_partner(other, "txt", 1)
    far_proj = from_partner(proj, "txt", 1)
    weights = (mine, other, far_mine, far_other)
    held = ((2, n_z, 2, WIDTH // n_dp, hid), BF)
    pre_act, mixed = call(
        mlp_kernel,
        (((2, half, hid), F32), ((half, WIDTH), BF)),
        "aaaavvvvv",
        *weights,
        normed,
        up_bias[None],
        far_bias,
        scratch=(held, held),
        sems=8,
    )
    mixed, far_texts = lax.optimization_barrier((mixed, far_texts))
    text_unit, label_text = call(
        text_kernel,
        (((2 * n_text, emb), BF), ((half, emb), BF)),
        "hhvhv",
        texts,
        far_texts,
        labels,
        cost=pl.CostEstimate(flops=2**31, bytes_accessed=12 << 20, transcendentals=0),
        scratch=(((2 * n_text, emb), BF),),
        sems=4 * n_text // 256,
    )
    mixed = swapped(mixed.reshape(n_pair, rows, WIDTH), "txt", cores)

    held_proj = ((4, 4, share, emb), BF)
    sent, unit_vec, emb_norm, yhat, rstd_out = call(
        embed_kernel,
        (
            ((n_pair, rows, 2 * emb), BF),
            ((rows, emb), F32),
            ((rows, 128), F32),
            ((rows, WIDTH), F32),
            ((rows, 128), F32),
        ),
        "vvvvhhvvvvvv",
        mixed,
        own,
        down_bias[None],
        lines,
        proj,
        far_proj,
        label_text,
        scratch=(held_proj,),
        sems=4,
    )
    arrived = swapped(sent, "txt", cores)

    back, label_rows = call(
        softmax_kernel,
        (((half, emb + 128), BF), ((rows, emb), F32)),
        "vhvvv",
        arrived,
        text_unit,
        labels,
        scratch=(((half, 2 * n_text), F32), ((half, emb), BF), ((2 * n_text, emb), BF)),
        sems=5,
    )
    back = swapped(back.reshape(n_pair, rows, emb + 128), "txt", cores)

    sent, out_grad = call(
        embed_back_kernel,
        (((n_pair, rows, WIDTH), BF), ((rows, WIDTH), F32)),
        "vvvvvvvhhvv",
        back,
        label_rows,
        unit_vec,
        emb_norm,
        yhat,
        rstd_out,
        lines,
        proj,
        far_proj,
        scratch=(held_proj,),
        sems=4,
    )
    out_low = swapped(sent, "txt", cores).reshape(half, WIDTH)

    (normed_grad,) = call(
        mlp_back_kernel,
        (((half, WIDTH), BF),),
        "aaaavvv",
        *weights,
        out_low,
        pre_act,
        scratch=(held, held),
        sems=8,
    )
    normed_grad = swapped(normed_grad.reshape(n_pair, rows, WIDTH), "txt", cores)
    (change,) = call(
        change_kernel,
        (((n_txt, rows // 2, 2 * share), F32),),
        "vvvvvv",
        normed_grad,
        prenorm_gain[None],
        own,
        out_grad,
        step_size[None],
    )
    change = swapped(change, "txt")
    (out,) = call(result_kernel, (((share, images), F32),), "vvv", change, resid.T)
    return out.T


def solution(mesh):
    placed = (
        P("dp", "txt"),
        P(),
        P(),
        P("dp", "txt"),
        P("txt"),
        P("txt", "dp"),
        P(),
        P("txt"),
        P("txt"),
        P("txt", None),
        P("txt", None),
        P("dp"),
        P(),
    )
    return jax.shard_map(
        local, mesh=mesh, in_specs=placed, out_specs=P("dp", "txt"), check_vma=False
    )
```

time: 167 us -> 155 us (0.928)
  local copies, waits for them, and re-layouts: 18.1 us -> 1.11 us
  Pallas kernels: 14.8 us -> 20 us
  blocking collectives: 43.6 us -> 41.7 us
    unnamed x52 -> x12, local copies, waits for them, and re-layouts: 17.1 us -> 0.03 us
    all_to_all x4, waiting for transfers between devices: 5.43 us -> 14.7 us  [swapped(): return lax.all_to_all(x, axis, 0, 0, tiled=True, axis_index_groups=groups)]
    ppermute x10, waiting for transfers between devices: 19.8 us -> 12 us  [from_partner(): return lax.ppermute(x, axis, pairs)]
    pallas_call x12 -> x11, Pallas kernels: 14.8 us -> 20 us  [call(): pl.pallas_call(body, out_shape=[pltpu.HBM(*out) if c == 'h' else jax.Shap...]
    all_to_all x4, blocking collectives: 43.6 us -> 41.7 us  [swapped(): return lax.all_to_all(x, axis, 0, 0, tiled=True, axis_index_groups=groups)]
  transfers between devices with their start and end apart: 14 -> 14, of which waited for: 6 -> 8; matrix products, arithmetic and copies ran while one was open for 2% -> 2% of each run, Pallas kernels for 4% -> 5%
where the time goes in v6:
time: 155 us; the launch traced here: 154 us
  starting transfers between devices  60.4 us (39%)
  blocking collectives  41.7 us (27%)
  waiting for transfers between devices  26.7 us (17%)
  Pallas kernels  20 us (13%)
  other arithmetic  3.08 us (2%)
    all_to_all x4, blocking collectives, swapped(): return lax.all_to_all(x, axis, 0, 0, tiled=True, axis_index_groups=groups)  41.7 us
    ppermute x10, starting transfers between devices, from_partner(): return lax.ppermute(x, axis, pairs)  31.9 us
    all_to_all x4, starting transfers between devices, swapped(): return lax.all_to_all(x, axis, 0, 0, tiled=True, axis_index_groups=groups)  28.5 us
    pallas_call x11, Pallas kernels, call(): pl.pallas_call(body, out_shape=[pltpu.HBM(*out) if c == 'h' else jax.Shap...  20 us
    all_to_all x4, waiting for transfers between devices, swapped(): return lax.all_to_all(x, axis, 0, 0, tiled=True, axis_index_groups=groups)  14.7 us
    ppermute x10, waiting for transfers between devices, from_partner(): return lax.ppermute(x, axis, pairs)  12 us
  transfers between devices with their start and end apart: 14, of which 8 were waited for; matrix products, arithmetic and copies ran while one was open for 2% of the time, Pallas kernels for 5%

profile of v6, /device:TPU:1, one launch (start us, length us, event | category | flops | bytes accessed | tf_op | source)
XLA Modules:
  0.0 154.0 jit_solution(4987491622031508158)
XLA Ops:
  1.7 15.7 %all-to-all-start = ((bf16[16,2,32,256]{3,2,1,0:T(8,128)(2,1)}), bf16[16,2,32,256]{3,2,1,0:T(8,128)(2,1)S(1)}, u32[]{:S(2)}, u32[]{:S(2)}) async-start(bf16[16,2,32,256]{3,2,1,0:T(8,128)(2,1)} %broadcast_in_dim.22), calls=%async_computation | async-start | bytes 1048576 | tf_op jit(solution)/shard_map/all_to_all | solution.py:16
  17.4 2.9 %collective-permute-start.8 = (bf16[1280,768]{1,0:T(8,128)(2,1)}, bf16[1280,768]{1,0:T(8,128)(2,1)}, u32[]{:S(2)}, u32[]{:S(2)}) collective-permute-start(bf16[1280,768]{1,0:T(8,128)(2,1)} %near.1), channel_id=1, source_target_pairs={{0,1},{1,0},{2,3},{3,2},{4,5},{5,4},{6,7},{7,6},{8,9},{9,8},{10,11... | collective-permute-start | bytes 5898248 | tf_op jit(solution)/shard_map/ppermute | solution.py:25
  22.7 3.1 %collective-permute-start = (bf16[64,1152]{1,0:T(8,128)(2,1)S(1)}, bf16[64,1152]{1,0:T(8,128)(2,1)S(1)}, u32[]{:S(2)}, u32[]{:S(2)}) collective-permute-start(bf16[64,1152]{1,0:T(8,128)(2,1)S(1)} %fusion.1.near), channel_id=1, source_target_pairs={{0,2},{1,3},{2,0},{3,1},{4,6},{5,7},{6,4},{7,5},{8,10},{9,11},{10,... | collective-permute-start | bytes 442376 | tf_op jit(solution)/shard_map/ppermute | solution.py:25
  25.8 4.2 %collective-permute-done.other = bf16[64,1152]{1,0:T(8,128)(2,1)S(1)} collective-permute-done((bf16[64,1152]{1,0:T(8,128)(2,1)S(1)}, bf16[64,1152]{1,0:T(8,128)(2,1)S(1)}, u32[]{:S(2)}, u32[]{:S(2)}) %collective-permute-start) | collective-permute-done | bytes 147488 | tf_op jit(solution)/shard_map/ppermute | solution.py:25
  30.0 1.0 shard_map.127
  31.0 3.2 %collective-permute-start.1 = (bf16[2,64,384]{2,1,0:T(8,128)(2,1)S(1)}, bf16[2,64,384]{2,1,0:T(8,128)(2,1)S(1)}, u32[]{:S(2)}, u32[]{:S(2)}) collective-permute-start(bf16[2,64,384]{2,1,0:T(8,128)(2,1)S(1)} %get-tuple-element.33.refs_0_), channel_id=1, source_target_pairs={{0,4},{1,5},{2,6},{3,7},{4,0},{5,1},{6,2},{7,3},{8,12},{9,13},{10,... | collective-permute-start | bytes 294920 | tf_op jit(solution)/shard_map/ppermute | solution.py:25
  34.2 4.5 %collective-permute-start.2 = (bf16[2,64,384]{2,1,0:T(8,128)(2,1)S(1)}, bf16[2,64,384]{2,1,0:T(8,128)(2,1)S(1)}, u32[]{:S(2)}, u32[]{:S(2)}) collective-permute-start(bf16[2,64,384]{2,1,0:T(8,128)(2,1)S(1)} %get-tuple-element.33.refs_0_), channel_id=1, source_target_pairs={{0,8},{1,9},{2,10},{3,11},{4,12},{5,13},{6,14},{7,15},{8,0},{9,1},... | collective-permute-start | bytes 294920 | tf_op jit(solution)/shard_map/ppermute | solution.py:25
  38.7 1.9 %collective-permute-start.3 = (bf16[2,64,384]{2,1,0:T(8,128)(2,1)S(1)}, bf16[2,64,384]{2,1,0:T(8,128)(2,1)S(1)}, u32[]{:S(2)}, u32[]{:S(2)}) collective-permute-start(bf16[2,64,384]{2,1,0:T(8,128)(2,1)S(1)} %get-tuple-element.33.refs_0_), channel_id=1, source_target_pairs={{0,12},{1,13},{2,14},{3,15},{4,8},{5,9},{6,10},{7,11},{8,4},{9,5},... | collective-permute-start | bytes 294920 | tf_op jit(solution)/shard_map/ppermute | solution.py:25
  41.4 4.2 %collective-permute-done.3.refs_3_ = bf16[2,64,384]{2,1,0:T(8,128)(2,1)S(1)} collective-permute-done((bf16[2,64,384]{2,1,0:T(8,128)(2,1)S(1)}, bf16[2,64,384]{2,1,0:T(8,128)(2,1)S(1)}, u32[]{:S(2)}, u32[]{:S(2)}) %collective-permute-start.3) | collective-permute-done | bytes 98336 | tf_op jit(solution)/shard_map/ppermute | solution.py:25
  45.6 4.1 %collective-permute-start.4 = (bf16[4,2,64,384]{3,2,1,0:T(8,128)(2,1)S(1)}, bf16[4,2,64,384]{3,2,1,0:T(8,128)(2,1)S(1)}, u32[]{:S(2)}, u32[]{:S(2)}) collective-permute-start(bf16[4,2,64,384]{3,2,1,0:T(8,128)(2,1)S(1)} %shard_map.128.near), channel_id=1, source_target_pairs={{0,1},{1,0},{2,3},{3,2},{4,5},{5,4},{6,7},{7,6},{8,9},{9,8},{10,11... | collective-permute-start | bytes 1179656 | tf_op jit(solution)/shard_map/ppermute | solution.py:25
  49.8 1.3 collective-permute-done.4.far
  51.5 4.2 %all-to-all-start.2 = ((bf16[4,2,64,768]{3,2,1,0:T(8,128)(2,1)}), bf16[4,2,64,768]{3,2,1,0:T(8,128)(2,1)}, u32[]{:S(2)}, u32[]{:S(2)}) async-start(bf16[4,2,64,768]{3,2,1,0:T(8,128)(2,1)} %get-tuple-element.42), calls=%async_computation.2 | async-start | bytes 1572864 | tf_op jit(solution)/shard_map/all_to_all | solution.py:16
  55.7 4.7 %collective-permute-start.5 = (bf16[16,2,32,256]{3,2,1,0:T(8,128)(2,1)S(1)}, bf16[16,2,32,256]{3,2,1,0:T(8,128)(2,1)S(1)}, u32[]{:S(2)}, u32[]{:S(2)}) collective-permute-start(bf16[16,2,32,256]{3,2,1,0:T(8,128)(2,1)S(1)} %all-to-all-done.own), channel_id=1, source_target_pairs={{0,16},{16,0},{32,48},{48,32},{64,80},{80,64},{96,112},{112,96},{1... | collective-permute-start | bytes 1572872 | tf_op jit(solution)/shard_map/ppermute | solution.py:25
  60.4 7.4 %all-to-all-done.2.near = bf16[4,2,64,768]{3,2,1,0:T(8,128)(2,1)} async-done(((bf16[4,2,64,768]{3,2,1,0:T(8,128)(2,1)}), bf16[4,2,64,768]{3,2,1,0:T(8,128)(2,1)}, u32[]{:S(2)}, u32[]{:S(2)}) %all-to-all-start.2) | async-done | bytes 786464 | tf_op jit(solution)/shard_map/all_to_all | solution.py:16
  67.8 3.1 %collective-permute-start.9 = (bf16[4,2,64,768]{3,2,1,0:T(8,128)(2,1)}, bf16[4,2,64,768]{3,2,1,0:T(8,128)(2,1)}, u32[]{:S(2)}, u32[]{:S(2)}) collective-permute-start(bf16[4,2,64,768]{3,2,1,0:T(8,128)(2,1)} %all-to-all-done.2.near), channel_id=1, source_target_pairs={{0,1},{1,0},{2,3},{3,2},{4,5},{5,4},{6,7},{7,6},{8,9},{9,8},{10,11... | collective-permute-start | bytes 2359304 | tf_op jit(solution)/shard_map/ppermute | solution.py:25
  70.9 1.9 %collective-permute-start.6 = (bf16[16,2,32,256]{3,2,1,0:T(8,128)(2,1)S(1)}, bf16[16,2,32,256]{3,2,1,0:T(8,128)(2,1)S(1)}, u32[]{:S(2)}, u32[]{:S(2)}) collective-permute-start(bf16[16,2,32,256]{3,2,1,0:T(8,128)(2,1)S(1)} %all-to-all-done.own), channel_id=1, source_target_pairs={{0,1},{1,0},{2,3},{3,2},{4,5},{5,4},{6,7},{7,6},{8,9},{9,8},{10,11... | collective-permute-start | bytes 1572872 | tf_op jit(solution)/shard_map/ppermute | solution.py:25
  72.9 2.5 %collective-permute-start.7 = (bf16[16,2,32,256]{3,2,1,0:T(8,128)(2,1)S(1)}, bf16[16,2,32,256]{3,2,1,0:T(8,128)(2,1)S(1)}, u32[]{:S(2)}, u32[]{:S(2)}) collective-permute-start(bf16[16,2,32,256]{3,2,1,0:T(8,128)(2,1)S(1)} %collective-permute-done.5.other), channel_id=1, source_target_pairs={{0,1},{1,0},{2,3},{3,2},{4,5},{5,4},{6,7},{7,6},{8,9},{9,8},{10,11... | collective-permute-start | bytes 1572872 | tf_op jit(solution)/shard_map/ppermute | solution.py:25
  75.4 1.5 collective-permute-done.7.far_other
  76.9 1.9 %shard_map.130 = (f32[2,128,256]{2,1,0:T(8,128)S(1)}, bf16[128,1024]{1,0:T(8,128)(2,1)}) custom-call(bf16[16,2,32,256]{3,2,1,0:T(8,128)(2,1)S(1)} %all-to-all-done.own, bf16[16,2,32,256]{3,2,1,0:T(8,128)(2,1)S(1)} %collective-permute-done.5.other, bf16[16,2,32,256]{3,2,1,0:T(8,128)(2,1)S(1)} %collective-permute-done.6.far_own, ...), custom_call_target="tpu_custom_call" | custom-call | tf_op jit(solution)/shard_map/pallas_call | solution.py:56
  78.8 5.1 %all-to-all-start.1 = ((bf16[8,16,1024]{2,1,0:T(8,128)(2,1)}), bf16[8,16,1024]{2,1,0:T(8,128)(2,1)S(1)}, u32[]{:S(2)}, u32[]{:S(2)}) async-start(bf16[8,16,1024]{2,1,0:T(8,128)(2,1)} %bitcast.14), calls=%async_computation.1 | async-start | bytes 524288 | tf_op jit(solution)/shard_map/all_to_all | solution.py:16
  84.1 4.7 %shard_map.131 = (bf16[2560,768]{1,0:T(8,128)(2,1)}, bf16[128,768]{1,0:T(8,128)(2,1)S(1)}) custom-call(bf16[1280,768]{1,0:T(8,128)(2,1)} %near.1, bf16[1280,768]{1,0:T(8,128)(2,1)} %collective-permute-done.8.far, s32[256,1]{1,0:T(8,128)S(1)} %copy.14.labels), custom_call_target="tpu_custom_call" | custom-call | flops 2147483648 | bytes 12582912 | tf_op jit(solution)/shard_map/pallas_call | solution.py:56
  88.8 1.8 %all-to-all-done.1.mixed = bf16[8,16,1024]{2,1,0:T(8,128)(2,1)S(1)} async-done(((bf16[8,16,1024]{2,1,0:T(8,128)(2,1)}), bf16[8,16,1024]{2,1,0:T(8,128)(2,1)S(1)}, u32[]{:S(2)}, u32[]{:S(2)}) %all-to-all-start.1) | async-done | bytes 262176 | tf_op jit(solution)/shard_map/all_to_all | solution.py:16
  90.7 1.9 %shard_map.132 = (bf16[8,16,1536]{2,1,0:T(8,128)(2,1)S(1)}, f32[16,768]{1,0:T(8,128)S(1)}, f32[16,128]{1,0:T(8,128)S(1)}, f32[16,1024]{1,0:T(8,128)S(1)}, f32[16,128]{1,0:T(8,128)S(1)}) custom-call(bf16[8,16,1024]{2,1,0:T(8,128)(2,1)S(1)} %all-to-all-done.1.mixed, f32[16,1024]{1,0:T(8,128)S(1)} %get-tuple-element.40.own, f32[1,1024]{1,0:T(1,128)S(1)} %bitcast.36, ...), custom_call_target="tpu_custom_call" | custom-call | tf_op jit(solution)/shard_map/pallas_call | solution.py:56
  92.5 10.5 %all_to_all.40.arrived = bf16[8,16,1536]{2,1,0:T(8,128)(2,1)S(1)} all-to-all(bf16[8,16,1536]{2,1,0:T(8,128)(2,1)S(1)} %get-tuple-element.46), channel_id=1, replica_groups={{0,2,4,6,8,10,12,14},{1,3,5,7,9,11,13,15},{16,18,20,22,24,26,28,30},{17..., dimensions={0} | all-to-all | bytes 786432 | tf_op jit(solution)/shard_map/all_to_all | solution.py:16
  103.0 4.7 %shard_map.133 = (bf16[128,896]{1,0:T(8,128)(2,1)S(1)}, f32[16,768]{1,0:T(8,128)S(1)}) custom-call(bf16[8,16,1536]{2,1,0:T(8,128)(2,1)S(1)} %all_to_all.40.arrived, bf16[2560,768]{1,0:T(8,128)(2,1)} %get-tuple-element.47.text_unit, s32[256,1]{1,0:T(8,128)S(1)} %copy.14.labels), custom_call_target="tpu_custom_call" | custom-call | tf_op jit(solution)/shard_map/pallas_call | solution.py:56
  107.8 8.4 %all_to_all.41.back = bf16[8,16,896]{2,1,0:T(8,128)(2,1)S(1)} all-to-all(bf16[8,16,896]{2,1,0:T(8,128)(2,1)S(1)} %bitcast.30), channel_id=1, replica_groups={{0,2,4,6,8,10,12,14},{1,3,5,7,9,11,13,15},{16,18,20,22,24,26,28,30},{17..., dimensions={0} | all-to-all | bytes 458752 | tf_op jit(solution)/shard_map/all_to_all | solution.py:16
  116.2 2.3 %shard_map.134 = (bf16[8,16,1024]{2,1,0:T(8,128)(2,1)S(1)}, f32[16,1024]{1,0:T(8,128)S(1)}) custom-call(bf16[8,16,896]{2,1,0:T(8,128)(2,1)S(1)} %all_to_all.41.back, f32[16,768]{1,0:T(8,128)S(1)} %get-tuple-element.49.label_rows, f32[16,768]{1,0:T(8,128)S(1)} %get-tuple-element.50.unit, f32[16,128]{1,0:T(8,128)S(1)} %get-tuple-element.51.norm, ...), custom_call_target="tpu_custom_call" | custom-call | tf_op jit(solution)/shard_map/pallas_call | solution.py:56
  118.5 8.5 %all_to_all.42 = bf16[8,16,1024]{2,1,0:T(8,128)(2,1)S(1)} all-to-all(bf16[8,16,1024]{2,1,0:T(8,128)(2,1)S(1)} %get-tuple-element.54), channel_id=1, replica_groups={{0,2,4,6,8,10,12,14},{1,3,5,7,9,11,13,15},{16,18,20,22,24,26,28,30},{17..., dimensions={0} | all-to-all | bytes 524288 | tf_op jit(solution)/shard_map/all_to_all | solution.py:16
  127.0 2.0 %shard_map.135 = bf16[128,1024]{1,0:T(8,128)(2,1)} custom-call(bf16[16,2,32,256]{3,2,1,0:T(8,128)(2,1)S(1)} %all-to-all-done.own, bf16[16,2,32,256]{3,2,1,0:T(8,128)(2,1)S(1)} %collective-permute-done.5.other, bf16[16,2,32,256]{3,2,1,0:T(8,128)(2,1)S(1)} %collective-permute-done.6.far_own, bf16[16,2,32,256]{3,2,1,0:T(8,128)(2,1)S(1)} %collective-permute-done.7.far_other, ...), custom_call_target="tpu_custom_call" | custom-call | tf_op jit(solution)/shard_map/pallas_call | solution.py:56
  129.0 3.4 %all-to-all-start.6 = ((bf16[8,16,1024]{2,1,0:T(8,128)(2,1)}), bf16[8,16,1024]{2,1,0:T(8,128)(2,1)S(1)}, u32[]{:S(2)}, u32[]{:S(2)}) async-start(bf16[8,16,1024]{2,1,0:T(8,128)(2,1)} %bitcast.18), calls=%async_computation.6 | async-start | bytes 524288 | tf_op jit(solution)/shard_map/all_to_all | solution.py:16
  133.1 5.4 %all-to-all-done.6.parts = bf16[8,16,1024]{2,1,0:T(8,128)(2,1)S(1)} async-done(((bf16[8,16,1024]{2,1,0:T(8,128)(2,1)}), bf16[8,16,1024]{2,1,0:T(8,128)(2,1)S(1)}, u32[]{:S(2)}, u32[]{:S(2)}) %all-to-all-start.6) | async-done | bytes 262176 | tf_op jit(solution)/shard_map/all_to_all | solution.py:16
  138.9 14.3 %all_to_all.43.parts = f32[16,8,128]{2,1,0:T(8,128)S(1)} all-to-all(f32[16,8,128]{2,1,0:T(8,128)S(1)} %shard_map.136), channel_id=1, replica_groups=mesh['dp'=32,'txt'=16] {'txt'}, dimensions={0} | all-to-all | bytes 131072 | tf_op jit(solution)/shard_map/all_to_all | solution.py:16
  (36 shorter events, 6.5 us)
Async XLA Ops:
  0.0 51.1 %copy-start.1 = (f32[1024]{0:T(1024)S(1)}, f32[1024]{0:T(1024)}, u32[]{:S(2)}) copy-start(f32[1024]{0:T(1024)} %param.14) | copy-start | bytes 12292
  0.0 51.1 %copy-start.2 = (f32[1024]{0:T(1024)S(1)}, f32[1024]{0:T(1024)}, u32[]{:S(2)}) copy-start(f32[1024]{0:T(1024)} %param.15) | copy-start | bytes 12292
  1.7 49.8 %all-to-all-start = ((bf16[16,2,32,256]{3,2,1,0:T(8,128)(2,1)}), bf16[16,2,32,256]{3,2,1,0:T(8,128)(2,1)S(1)}, u32[]{:S(2)}, u32[]{:S(2)}) async-start(bf16[16,2,32,256]{3,2,1,0:T(8,128)(2,1)} %broadcast_in_dim.22), calls=%async_computation | async-start | bytes 1048576 | tf_op jit(solution)/shard_map/all_to_all | solution.py:16
  17.4 59.5 %copy-start.4 = (f32[256]{0:T(256)S(1)}, f32[256]{0:T(256)}, u32[]{:S(2)}) copy-start(f32[256]{0:T(256)} %param.17) | copy-start | bytes 3076
  17.4 61.4 %collective-permute-start.8 = (bf16[1280,768]{1,0:T(8,128)(2,1)}, bf16[1280,768]{1,0:T(8,128)(2,1)}, u32[]{:S(2)}, u32[]{:S(2)}) collective-permute-start(bf16[1280,768]{1,0:T(8,128)(2,1)} %near.1), channel_id=1, source_target_pairs={{0,1},{1,0},{2,3},{3,2},{4,5},{5,4},{6,7},{7,6},{8,9},{9,8},{10,11... | collective-permute-start | bytes 5898248 | tf_op jit(solution)/shard_map/ppermute | solution.py:25
  22.7 7.4 %collective-permute-start = (bf16[64,1152]{1,0:T(8,128)(2,1)S(1)}, bf16[64,1152]{1,0:T(8,128)(2,1)S(1)}, u32[]{:S(2)}, u32[]{:S(2)}) collective-permute-start(bf16[64,1152]{1,0:T(8,128)(2,1)S(1)} %fusion.1.near), channel_id=1, source_target_pairs={{0,2},{1,3},{2,0},{3,1},{4,6},{5,7},{6,4},{7,5},{8,10},{9,11},{10,... | collective-permute-start | bytes 442376 | tf_op jit(solution)/shard_map/ppermute | solution.py:25
  31.0 9.7 %collective-permute-start.1 = (bf16[2,64,384]{2,1,0:T(8,128)(2,1)S(1)}, bf16[2,64,384]{2,1,0:T(8,128)(2,1)S(1)}, u32[]{:S(2)}, u32[]{:S(2)}) collective-permute-start(bf16[2,64,384]{2,1,0:T(8,128)(2,1)S(1)} %get-tuple-element.33.refs_0_), channel_id=1, source_target_pairs={{0,4},{1,5},{2,6},{3,7},{4,0},{5,1},{6,2},{7,3},{8,12},{9,13},{10,... | collective-permute-start | bytes 294920 | tf_op jit(solution)/shard_map/ppermute | solution.py:25
  34.2 7.2 %collective-permute-start.2 = (bf16[2,64,384]{2,1,0:T(8,128)(2,1)S(1)}, bf16[2,64,384]{2,1,0:T(8,128)(2,1)S(1)}, u32[]{:S(2)}, u32[]{:S(2)}) collective-permute-start(bf16[2,64,384]{2,1,0:T(8,128)(2,1)S(1)} %get-tuple-element.33.refs_0_), channel_id=1, source_target_pairs={{0,8},{1,9},{2,10},{3,11},{4,12},{5,13},{6,14},{7,15},{8,0},{9,1},... | collective-permute-start | bytes 294920 | tf_op jit(solution)/shard_map/ppermute | solution.py:25
  38.7 6.9 %collective-permute-start.3 = (bf16[2,64,384]{2,1,0:T(8,128)(2,1)S(1)}, bf16[2,64,384]{2,1,0:T(8,128)(2,1)S(1)}, u32[]{:S(2)}, u32[]{:S(2)}) collective-permute-start(bf16[2,64,384]{2,1,0:T(8,128)(2,1)S(1)} %get-tuple-element.33.refs_0_), channel_id=1, source_target_pairs={{0,12},{1,13},{2,14},{3,15},{4,8},{5,9},{6,10},{7,11},{8,4},{9,5},... | collective-permute-start | bytes 294920 | tf_op jit(solution)/shard_map/ppermute | solution.py:25
  45.6 5.5 %collective-permute-start.4 = (bf16[4,2,64,384]{3,2,1,0:T(8,128)(2,1)S(1)}, bf16[4,2,64,384]{3,2,1,0:T(8,128)(2,1)S(1)}, u32[]{:S(2)}, u32[]{:S(2)}) collective-permute-start(bf16[4,2,64,384]{3,2,1,0:T(8,128)(2,1)S(1)} %shard_map.128.near), channel_id=1, source_target_pairs={{0,1},{1,0},{2,3},{3,2},{4,5},{5,4},{6,7},{7,6},{8,9},{9,8},{10,11... | collective-permute-start | bytes 1179656 | tf_op jit(solution)/shard_map/ppermute | solution.py:25
  51.5 32.4 %copy-start.5 = (s32[256]{0:T(256)S(1)}, s32[256]{0:T(256)}, u32[]{:S(2)}) copy-start(s32[256]{0:T(256)} %param.24) | copy-start | bytes 3076
  51.5 16.3 %all-to-all-start.2 = ((bf16[4,2,64,768]{3,2,1,0:T(8,128)(2,1)}), bf16[4,2,64,768]{3,2,1,0:T(8,128)(2,1)}, u32[]{:S(2)}, u32[]{:S(2)}) async-start(bf16[4,2,64,768]{3,2,1,0:T(8,128)(2,1)} %get-tuple-element.42), calls=%async_computation.2 | async-start | bytes 1572864 | tf_op jit(solution)/shard_map/all_to_all | solution.py:16
  55.7 17.1 %collective-permute-start.5 = (bf16[16,2,32,256]{3,2,1,0:T(8,128)(2,1)S(1)}, bf16[16,2,32,256]{3,2,1,0:T(8,128)(2,1)S(1)}, u32[]{:S(2)}, u32[]{:S(2)}) collective-permute-start(bf16[16,2,32,256]{3,2,1,0:T(8,128)(2,1)S(1)} %all-to-all-done.own), channel_id=1, source_target_pairs={{0,16},{16,0},{32,48},{48,32},{64,80},{80,64},{96,112},{112,96},{1... | collective-permute-start | bytes 1572872 | tf_op jit(solution)/shard_map/ppermute | solution.py:25
  67.8 22.8 %collective-permute-start.9 = (bf16[4,2,64,768]{3,2,1,0:T(8,128)(2,1)}, bf16[4,2,64,768]{3,2,1,0:T(8,128)(2,1)}, u32[]{:S(2)}, u32[]{:S(2)}) collective-permute-start(bf16[4,2,64,768]{3,2,1,0:T(8,128)(2,1)} %all-to-all-done.2.near), channel_id=1, source_target_pairs={{0,1},{1,0},{2,3},{3,2},{4,5},{5,4},{6,7},{7,6},{8,9},{9,8},{10,11... | collective-permute-start | bytes 2359304 | tf_op jit(solution)/shard_map/ppermute | solution.py:25
  70.9 4.4 %collective-permute-start.6 = (bf16[16,2,32,256]{3,2,1,0:T(8,128)(2,1)S(1)}, bf16[16,2,32,256]{3,2,1,0:T(8,128)(2,1)S(1)}, u32[]{:S(2)}, u32[]{:S(2)}) collective-permute-start(bf16[16,2,32,256]{3,2,1,0:T(8,128)(2,1)S(1)} %all-to-all-done.own), channel_id=1, source_target_pairs={{0,1},{1,0},{2,3},{3,2},{4,5},{5,4},{6,7},{7,6},{8,9},{9,8},{10,11... | collective-permute-start | bytes 1572872 | tf_op jit(solution)/shard_map/ppermute | solution.py:25
  72.9 4.0 %collective-permute-start.7 = (bf16[16,2,32,256]{3,2,1,0:T(8,128)(2,1)S(1)}, bf16[16,2,32,256]{3,2,1,0:T(8,128)(2,1)S(1)}, u32[]{:S(2)}, u32[]{:S(2)}) collective-permute-start(bf16[16,2,32,256]{3,2,1,0:T(8,128)(2,1)S(1)} %collective-permute-done.5.other), channel_id=1, source_target_pairs={{0,1},{1,0},{2,3},{3,2},{4,5},{5,4},{6,7},{7,6},{8,9},{9,8},{10,11... | collective-permute-start | bytes 1572872 | tf_op jit(solution)/shard_map/ppermute | solution.py:25
  78.8 11.8 %all-to-all-start.1 = ((bf16[8,16,1024]{2,1,0:T(8,128)(2,1)}), bf16[8,16,1024]{2,1,0:T(8,128)(2,1)S(1)}, u32[]{:S(2)}, u32[]{:S(2)}) async-start(bf16[8,16,1024]{2,1,0:T(8,128)(2,1)} %bitcast.14), calls=%async_computation.1 | async-start | bytes 524288 | tf_op jit(solution)/shard_map/all_to_all | solution.py:16
  84.1 6.6 %copy-start.3 = (f32[1024]{0:T(1024)S(1)}, f32[1024]{0:T(1024)}, u32[]{:S(2)}) copy-start(f32[1024]{0:T(1024)} %param.19) | copy-start | bytes 12292
  127.0 26.2 %copy-start = (bf16[256,64]{0,1:T(8,128)(2,1)S(1)}, bf16[256,64]{0,1:T(8,128)(2,1)}, u32[]{:S(2)}) copy-start(bf16[256,64]{0,1:T(8,128)(2,1)} %param.13) | copy-start | bytes 98308
  129.0 9.5 %all-to-all-start.6 = ((bf16[8,16,1024]{2,1,0:T(8,128)(2,1)}), bf16[8,16,1024]{2,1,0:T(8,128)(2,1)S(1)}, u32[]{:S(2)}, u32[]{:S(2)}) async-start(bf16[8,16,1024]{2,1,0:T(8,128)(2,1)} %bitcast.18), calls=%async_computation.6 | async-start | bytes 524288 | tf_op jit(solution)/shard_map/all_to_all | solution.py:16

commit v7 on v6

--- a/solution.py
+++ b/solution.py
@@ -23,15 +23,6 @@
 def from_partner(x, axis, bits):
     pairs = [(i, i ^ bits) for i in range(lax.axis_size(axis))]
     return lax.ppermute(x, axis, pairs)
-
-
-def pieces(x, count):
-    out = []
-    for _ in range(count):
-        part = lax.reduce_precision(x, 8, 7)
-        out.append(part.astype(BF))
-        x = x - part
-    return out
 
 
 def row_norm(rows):
@@ -114,6 +105,32 @@
     label_text[...] = total.astype(BF)
     for store in stores:
         store.wait()
+
+
+def message_kernel(projection, resid, gain, bias, up_bias, out):
+    emb, images = projection.shape[1], resid.shape[1]
+
+    def parts(value):
+        found = []
+        for _ in range(3):
+            part = value.astype(BF).astype(F32)
+            found.append(part)
+            value = value - part
+        return found
+
+    out[:, :emb] = projection[...]
+    out[:, emb : emb + images] = resid[...]
+    blank = jnp.zeros((1, 128 - gain.shape[1]), F32)
+    lines = [
+        jnp.concatenate([part, blank], axis=1)
+        for part in parts(gain[...]) + parts(bias[...])
+    ]
+    lines += [jnp.zeros((1, 128), F32)] * 2
+    lines += [part[:, 128 * k : 128 * k + 128] for part in parts(up_bias[...]) for k in range(2)]
+    lines += [jnp.zeros((1, 128), F32)] * 2
+    lines = jnp.concatenate(lines, axis=0)
+    out[:, emb + images :] = jnp.zeros((out.shape[0], 128), BF)
+    out[: lines.shape[0], emb + images :] = lines.astype(BF)
 
 
 def split_kernel(near, other, proj, rest):
@@ -168,16 +185,33 @@
     normed[...] = (xhat * gain[...] + bias[...]).astype(BF)
 
 
-def ordered_proj(near, far, proj, sem):
+def in_arrival_order(rows, share):
     low = lax.rem(lax.axis_index("txt"), 4)
-    loads = []
-    for core, side in enumerate((near, far)):
+    sides = ([], [])
+    for y in range(rows.shape[1] // (4 * share)):
+        pair = [rows[:, (4 * y + 2 * x) * share : (4 * y + 2 * x + 2) * share] for x in range(2)]
         for x in range(2):
-            k = 2 * x + core
-            place = proj.at[:, low ^ k]
-            loads.append(pltpu.make_async_copy(side.at[:, x], place, sem.at[k]))
-            loads[-1].start()
-    return loads
+            block = jnp.where(low < 2, pair[x], pair[1 - x])
+            first, second = block[:, :share], block[:, share:]
+            even = lax.rem(low, 2) == 0
+            sides[0].append(jnp.where(even, first, second))
+            sides[1].append(jnp.where(even, second, first))
+    return [jnp.concatenate(side, axis=1) for side in sides]
+
+
+def in_natural_order(near, far, share):
+    low = lax.rem(lax.axis_index("txt"), 4)
+    even = lax.rem(low, 2) == 0
+    blocks = []
+    for y in range(near.shape[1] // (2 * share)):
+        pair = []
+        for x in range(2):
+            place = slice((2 * y + x) * share, (2 * y + x + 1) * share)
+            first = jnp.where(even, near[:, place], far[:, place])
+            second = jnp.where(even, far[:, place], near[:, place])
+            pair.append(jnp.concatenate([first, second], axis=1))
+        blocks += [jnp.where(low < 2, pair[x], pair[1 - x]) for x in range(2)]
+    return jnp.concatenate(blocks, axis=1)
 
 
 def ordered_weights(own, other, far_own, far_other, weights, sem):
@@ -281,8 +315,7 @@
 
 
 def embed_kernel(mixed, own, bias, lines, near, far, label_text, *refs):
-    sent, unit, norm, yhat, rstd, proj, sem = refs
-    loads = ordered_proj(near, far, proj, sem)
+    sent, unit, norm, yhat, rstd = refs
     n = mixed.shape[0]
     emb = unit.shape[1]
     rows = own.shape[0]
@@ -292,11 +325,11 @@
     normed, scale = row_norm(total)
     yhat[...] = normed
     rstd[...] = jnp.broadcast_to(scale, rstd.shape)
-    post_normed = (normed * lines[0:1, :] + lines[1:2, :]).astype(BF)
-    for load in loads:
-        load.wait()
-    w_proj = proj[...].reshape(-1, emb)
-    embedding = jnp.dot(post_normed, w_proj, preferred_element_type=F32)
+    post_normed = normed * lines[0:1, :] + lines[1:2, :]
+    embedding = jnp.zeros(unit.shape, F32)
+    for side, part in zip((near, far), in_arrival_order(post_normed, near.shape[2])):
+        w_proj = side[...].reshape(-1, emb)
+        embedding += jnp.dot(part.astype(BF), w_proj, preferred_element_type=F32)
     length = jnp.sqrt(jnp.sum(embedding * embedding, axis=1, keepdims=True) + 1e-06)
     norm[...] = jnp.broadcast_to(length, norm.shape)
     vec = embedding / length
@@ -308,8 +341,7 @@
 
 
 def embed_back_kernel(back, label_rows, unit, norm, yhat, rstd, lines, near, far, *refs):
-    sent, grad, proj, sem = refs
-    loads = ordered_proj(near, far, proj, sem)
+    sent, grad = refs
     n = back.shape[0]
     emb = unit.shape[1]
     stats = [back[j, :, emb:].astype(F32) for j in range(n)]
@@ -328,10 +360,15 @@
     vec = unit[...]
     along = jnp.sum(vec * unit_grad, axis=1, keepdims=True)
     emb_grad = ((unit_grad - vec * along) / norm[:, 0:1]).astype(BF)
-    for load in loads:
-        load.wait()
-    w_proj = proj[...].reshape(-1, emb)
-    post_grad = lax.dot_general(emb_grad, w_proj, NT, preferred_element_type=F32)
+    post_grad = in_natural_order(
+        *(
+            lax.dot_general(
+                emb_grad, side[...].reshape(-1, emb), NT, preferred_element_type=F32
+            )
+            for side in (near, far)
+        ),
+        near.shape[2],
+    )
     out_grad = norm_back(post_grad * lines[0:1, :], yhat[...], rstd[:, 0:1])
     grad[...] = out_grad
     low = out_grad.astype(BF)
@@ -396,14 +433,18 @@
     mine = jnp.stack([up_weight, down_weight.T], axis=0)
     mine = swapped(copies(mine, n_z), "dp", along_z)
 
-    vectors = jnp.stack(pieces(post_gain, 3) + pieces(post_bias, 3))
-    vectors = jnp.pad(vectors, ((0, 2), (0, 128 - share)))
-    bias_parts = jnp.stack(pieces(up_bias, 3)).reshape(3 * hid // 128, 128)
-    vectors = jnp.concatenate([vectors, bias_parts])
-    vectors = jnp.pad(vectors, ((0, share - vectors.shape[0]), (0, 0)))
-    chain = jnp.concatenate([projection, resid.T, vectors], axis=1)
+    (chain,) = call(
+        message_kernel,
+        (((share, emb + images + 128), BF),),
+        "vvvvvv",
+        projection,
+        resid.T,
+        post_gain[None],
+        post_bias[None],
+        up_bias[None],
+        cost=SMALL,
+    )
     chain, labels = lax.optimization_barrier((chain, labels[:, None]))
-    far_texts = from_partner(texts, "txt", 1)
     proj, rest = call(
         split_kernel,
         (((4, 2, share, emb), BF), ((2, share, images + 128), BF)),
@@ -427,18 +468,18 @@
         scratch=(((WIDTH, half), BF), ((n_txt, 8, 128), F32)),
     )
 
-    mine, proj, normed = lax.optimization_barrier((mine, proj, normed))
+    mine, proj, normed, far_texts = lax.optimization_barrier((mine, proj, normed, texts))
     other = from_partner(mine, "dp", 1)
     far_mine = from_partner(mine, "txt", 1)
+    far_texts = from_partner(far_texts, "txt", 1)
     proj = swapped(proj, "txt", along_y)
     far_other = from_partner(other, "txt", 1)
-    far_proj = from_partner(proj, "txt", 1)
     weights = (mine, other, far_mine, far_other)
     held = ((2, n_z, 2, WIDTH // n_dp, hid), BF)
     pre_act, mixed = call(
         mlp_kernel,
         (((2, half, hid), F32), ((half, WIDTH), BF)),
-        "aaaavvvvv",
+        "hhaavvvvv",
         *weights,
         normed,
         up_bias[None],
@@ -446,7 +487,8 @@
         scratch=(held, held),
         sems=8,
     )
-    mixed, far_texts = lax.optimization_barrier((mixed, far_texts))
+    mixed, far_texts, proj = lax.optimization_barrier((mixed, far_texts, proj))
+    far_proj = from_partner(proj, "txt", 1)
     text_unit, label_text = call(
         text_kernel,
         (((2 * n_text, emb), BF), ((half, emb), BF)),
@@ -460,7 +502,6 @@
     )
     mixed = swapped(mixed.reshape(n_pair, rows, WIDTH), "txt", cores)
 
-    held_proj = ((4, 4, share, emb), BF)
     sent, unit_vec, emb_norm, yhat, rstd_out = call(
         embed_kernel,
         (
@@ -470,7 +511,7 @@
             ((rows, WIDTH), F32),
             ((rows, 128), F32),
         ),
-        "vvvvhhvvvvvv",
+        "vvvvvvvvvvvv",
         mixed,
         own,
         down_bias[None],
@@ -478,8 +519,6 @@
         proj,
         far_proj,
         label_text,
-        scratch=(held_proj,),
-        sems=4,
     )
     arrived = swapped(sent, "txt", cores)
 
@@ -498,7 +537,7 @@
     sent, out_grad = call(
         embed_back_kernel,
         (((n_pair, rows, WIDTH), BF), ((rows, WIDTH), F32)),
-        "vvvvvvvhhvv",
+        "vvvvvvvvvvv",
         back,
         label_rows,
         unit_vec,
@@ -508,15 +547,13 @@
         lines,
         proj,
         far_proj,
-        scratch=(held_proj,),
-        sems=4,
     )
     out_low = swapped(sent, "txt", cores).reshape(half, WIDTH)
 
     (normed_grad,) = call(
         mlp_back_kernel,
         (((half, WIDTH), BF),),
-        "aaaavvv",
+        "hhaavvv",
         *weights,
         out_low,
         pre_act,

time: 155 us -> 153 us (0.987)
  local copies, waits for them, and re-layouts: 1.11 us -> 5.42 us
  other arithmetic: 3.08 us -> 0.76 us
  starting transfers between devices: 60.4 us -> 58.4 us
    all_to_all x4, waiting for transfers between devices: 14.7 us -> 7.74 us  [swapped(): return lax.all_to_all(x, axis, 0, 0, tiled=True, axis_index_groups=groups)]
    ppermute x10, waiting for transfers between devices: 12 us -> 17.5 us  [from_partner(): return lax.ppermute(x, axis, pairs)]
    unnamed x12 -> x26, local copies, waits for them, and re-layouts: 0.03 us -> 4.42 us
    all_to_all x4, starting transfers between devices: 28.5 us -> 26.1 us  [swapped(): return lax.all_to_all(x, axis, 0, 0, tiled=True, axis_index_groups=groups)]
    pallas_call x11 -> x12, Pallas kernels: 20 us -> 19.5 us  [call(): pl.pallas_call(body, out_shape=[pltpu.HBM(*out) if c == 'h' else jax.Shap...]
  transfers between devices with their start and end apart: 14 -> 14, of which waited for: 8 -> 8; matrix products, arithmetic and copies ran while one was open for 2% -> 0% of each run, Pallas kernels for 5% -> 6%
where the time goes in v7:
time: 153 us; the launch traced here: 151 us
  starting transfers between devices  58.4 us (38%)
  blocking collectives  41.1 us (27%)
  waiting for transfers between devices  25.3 us (17%)
  Pallas kernels  19.5 us (13%)
  local copies, waits for them, and re-layouts  5.42 us (4%)
    all_to_all x4, blocking collectives, swapped(): return lax.all_to_all(x, axis, 0, 0, tiled=True, axis_index_groups=groups)  41.1 us
    ppermute x10, starting transfers between devices, from_partner(): return lax.ppermute(x, axis, pairs)  32.4 us
    all_to_all x4, starting transfers between devices, swapped(): return lax.all_to_all(x, axis, 0, 0, tiled=True, axis_index_groups=groups)  26.1 us
    pallas_call x12, Pallas kernels, call(): pl.pallas_call(body, out_shape=[pltpu.HBM(*out) if c == 'h' else jax.Shap...  19.5 us
    ppermute x10, waiting for transfers between devices, from_partner(): return lax.ppermute(x, axis, pairs)  17.5 us
    all_to_all x4, waiting for transfers between devices, swapped(): return lax.all_to_all(x, axis, 0, 0, tiled=True, axis_index_groups=groups)  7.74 us
    unnamed x26, local copies, waits for them, and re-layouts  4.42 us
  transfers between devices with their start and end apart: 14, of which 8 were waited for; matrix products, arithmetic and copies ran while one was open for 0% of the time, Pallas kernels for 6%

profile of v7, /device:TPU:1, one launch (start us, length us, event | category | flops | bytes accessed | tf_op | source)
XLA Modules:
  0.0 151.5 jit_solution(14364288345259073660)
XLA Ops:
  1.6 15.7 %all-to-all-start = ((bf16[16,2,32,256]{3,2,1,0:T(8,128)(2,1)}), bf16[16,2,32,256]{3,2,1,0:T(8,128)(2,1)S(1)}, u32[]{:S(2)}, u32[]{:S(2)}) async-start(bf16[16,2,32,256]{3,2,1,0:T(8,128)(2,1)} %broadcast_in_dim.29), calls=%async_computation | async-start | bytes 1048576 | tf_op jit(solution)/shard_map/all_to_all | solution.py:16
  21.1 3.1 %collective-permute-start = (bf16[64,1152]{1,0:T(8,128)(2,1)S(1)}, bf16[64,1152]{1,0:T(8,128)(2,1)S(1)}, u32[]{:S(2)}, u32[]{:S(2)}) collective-permute-start(bf16[64,1152]{1,0:T(8,128)(2,1)S(1)} %shard_map.127.near), channel_id=1, source_target_pairs={{0,2},{1,3},{2,0},{3,1},{4,6},{5,7},{6,4},{7,5},{8,10},{9,11},{10,... | collective-permute-start | bytes 442376 | tf_op jit(solution)/shard_map/ppermute | solution.py:25
  24.2 3.2 %collective-permute-done.other = bf16[64,1152]{1,0:T(8,128)(2,1)S(1)} collective-permute-done((bf16[64,1152]{1,0:T(8,128)(2,1)S(1)}, bf16[64,1152]{1,0:T(8,128)(2,1)S(1)}, u32[]{:S(2)}, u32[]{:S(2)}) %collective-permute-start) | collective-permute-done | bytes 147488 | tf_op jit(solution)/shard_map/ppermute | solution.py:25
  27.4 0.9 shard_map.128
  28.3 3.2 %collective-permute-start.1 = (bf16[2,64,384]{2,1,0:T(8,128)(2,1)S(1)}, bf16[2,64,384]{2,1,0:T(8,128)(2,1)S(1)}, u32[]{:S(2)}, u32[]{:S(2)}) collective-permute-start(bf16[2,64,384]{2,1,0:T(8,128)(2,1)S(1)} %get-tuple-element.35.refs_0_), channel_id=1, source_target_pairs={{0,4},{1,5},{2,6},{3,7},{4,0},{5,1},{6,2},{7,3},{8,12},{9,13},{10,... | collective-permute-start | bytes 294920 | tf_op jit(solution)/shard_map/ppermute | solution.py:25
  31.5 4.5 %collective-permute-start.2 = (bf16[2,64,384]{2,1,0:T(8,128)(2,1)S(1)}, bf16[2,64,384]{2,1,0:T(8,128)(2,1)S(1)}, u32[]{:S(2)}, u32[]{:S(2)}) collective-permute-start(bf16[2,64,384]{2,1,0:T(8,128)(2,1)S(1)} %get-tuple-element.35.refs_0_), channel_id=1, source_target_pairs={{0,8},{1,9},{2,10},{3,11},{4,12},{5,13},{6,14},{7,15},{8,0},{9,1},... | collective-permute-start | bytes 294920 | tf_op jit(solution)/shard_map/ppermute | solution.py:25
  36.0 1.9 %collective-permute-start.3 = (bf16[2,64,384]{2,1,0:T(8,128)(2,1)S(1)}, bf16[2,64,384]{2,1,0:T(8,128)(2,1)S(1)}, u32[]{:S(2)}, u32[]{:S(2)}) collective-permute-start(bf16[2,64,384]{2,1,0:T(8,128)(2,1)S(1)} %get-tuple-element.35.refs_0_), channel_id=1, source_target_pairs={{0,12},{1,13},{2,14},{3,15},{4,8},{5,9},{6,10},{7,11},{8,4},{9,5},... | collective-permute-start | bytes 294920 | tf_op jit(solution)/shard_map/ppermute | solution.py:25
  38.0 1.7 %collective-permute-done.2.refs_2_ = bf16[2,64,384]{2,1,0:T(8,128)(2,1)S(1)} collective-permute-done((bf16[2,64,384]{2,1,0:T(8,128)(2,1)S(1)}, bf16[2,64,384]{2,1,0:T(8,128)(2,1)S(1)}, u32[]{:S(2)}, u32[]{:S(2)}) %collective-permute-start.2) | collective-permute-done | bytes 98336 | tf_op jit(solution)/shard_map/ppermute | solution.py:25
  39.7 3.2 %collective-permute-done.3.refs_3_ = bf16[2,64,384]{2,1,0:T(8,128)(2,1)S(1)} collective-permute-done((bf16[2,64,384]{2,1,0:T(8,128)(2,1)S(1)}, bf16[2,64,384]{2,1,0:T(8,128)(2,1)S(1)}, u32[]{:S(2)}, u32[]{:S(2)}) %collective-permute-start.3) | collective-permute-done | bytes 98336 | tf_op jit(solution)/shard_map/ppermute | solution.py:25
  42.9 5.2 %collective-permute-start.4 = (bf16[4,2,64,384]{3,2,1,0:T(8,128)(2,1)S(1)}, bf16[4,2,64,384]{3,2,1,0:T(8,128)(2,1)S(1)}, u32[]{:S(2)}, u32[]{:S(2)}) collective-permute-start(bf16[4,2,64,384]{3,2,1,0:T(8,128)(2,1)S(1)} %shard_map.129.near), channel_id=1, source_target_pairs={{0,1},{1,0},{2,3},{3,2},{4,5},{5,4},{6,7},{7,6},{8,9},{9,8},{10,11... | collective-permute-start | bytes 1179656 | tf_op jit(solution)/shard_map/ppermute | solution.py:25
  48.1 1.3 collective-permute-done.4.far
  49.9 2.3 %collective-permute-start.8 = (bf16[1280,768]{1,0:T(8,128)(2,1)}, bf16[1280,768]{1,0:T(8,128)(2,1)}, u32[]{:S(2)}, u32[]{:S(2)}) collective-permute-start(bf16[1280,768]{1,0:T(8,128)(2,1)} %near.1), channel_id=1, source_target_pairs={{0,1},{1,0},{2,3},{3,2},{4,5},{5,4},{6,7},{7,6},{8,9},{9,8},{10,11... | collective-permute-start | bytes 5898248 | tf_op jit(solution)/shard_map/ppermute | solution.py:25
  52.2 4.7 %collective-permute-start.5 = (bf16[16,2,32,256]{3,2,1,0:T(8,128)(2,1)S(1)}, bf16[16,2,32,256]{3,2,1,0:T(8,128)(2,1)}, u32[]{:S(2)}, u32[]{:S(2)}) collective-permute-start(bf16[16,2,32,256]{3,2,1,0:T(8,128)(2,1)S(1)} %all-to-all-done.own), channel_id=1, source_target_pairs={{0,16},{16,0},{32,48},{48,32},{64,80},{80,64},{96,112},{112,96},{1... | collective-permute-start | bytes 1572872 | tf_op jit(solution)/shard_map/ppermute | solution.py:25
  56.9 3.5 %all-to-all-start.1 = ((bf16[4,2,64,768]{3,2,1,0:T(8,128)(2,1)}), bf16[4,2,64,768]{3,2,1,0:T(8,128)(2,1)S(1)}, u32[]{:S(2)}, u32[]{:S(2)}) async-start(bf16[4,2,64,768]{3,2,1,0:T(8,128)(2,1)} %get-tuple-element.42), calls=%async_computation.1 | async-start | bytes 1572864 | tf_op jit(solution)/shard_map/all_to_all | solution.py:16
  60.4 2.3 %collective-permute-start.6 = (bf16[16,2,32,256]{3,2,1,0:T(8,128)(2,1)S(1)}, bf16[16,2,32,256]{3,2,1,0:T(8,128)(2,1)S(1)}, u32[]{:S(2)}, u32[]{:S(2)}) collective-permute-start(bf16[16,2,32,256]{3,2,1,0:T(8,128)(2,1)S(1)} %all-to-all-done.own), channel_id=1, source_target_pairs={{0,1},{1,0},{2,3},{3,2},{4,5},{5,4},{6,7},{7,6},{8,9},{9,8},{10,11... | collective-permute-start | bytes 1572872 | tf_op jit(solution)/shard_map/ppermute | solution.py:25
  62.7 6.4 %collective-permute-done.5.other = bf16[16,2,32,256]{3,2,1,0:T(8,128)(2,1)} collective-permute-done((bf16[16,2,32,256]{3,2,1,0:T(8,128)(2,1)S(1)}, bf16[16,2,32,256]{3,2,1,0:T(8,128)(2,1)}, u32[]{:S(2)}, u32[]{:S(2)}) %collective-permute-start.5) | collective-permute-done | bytes 524320 | tf_op jit(solution)/shard_map/ppermute | solution.py:25
  69.1 2.9 %collective-permute-start.7 = (bf16[16,2,32,256]{3,2,1,0:T(8,128)(2,1)}, bf16[16,2,32,256]{3,2,1,0:T(8,128)(2,1)S(1)}, u32[]{:S(2)}, u32[]{:S(2)}) collective-permute-start(bf16[16,2,32,256]{3,2,1,0:T(8,128)(2,1)} %collective-permute-done.5.other), channel_id=1, source_target_pairs={{0,1},{1,0},{2,3},{3,2},{4,5},{5,4},{6,7},{7,6},{8,9},{9,8},{10,11... | collective-permute-start | bytes 1572872 | tf_op jit(solution)/shard_map/ppermute | solution.py:25
  72.0 1.7 %collective-permute-done.7.far_other = bf16[16,2,32,256]{3,2,1,0:T(8,128)(2,1)S(1)} collective-permute-done((bf16[16,2,32,256]{3,2,1,0:T(8,128)(2,1)}, bf16[16,2,32,256]{3,2,1,0:T(8,128)(2,1)S(1)}, u32[]{:S(2)}, u32[]{:S(2)}) %collective-permute-start.7) | collective-permute-done | bytes 524320 | tf_op jit(solution)/shard_map/ppermute | solution.py:25
  73.7 3.0 %shard_map.131 = (f32[2,128,256]{2,1,0:T(8,128)S(1)}, bf16[128,1024]{1,0:T(8,128)(2,1)}) custom-call(bf16[16,2,32,256]{3,2,1,0:T(8,128)(2,1)} %copy-done.11, bf16[16,2,32,256]{3,2,1,0:T(8,128)(2,1)} %collective-permute-done.5.other, bf16[16,2,32,256]{3,2,1,0:T(8,128)(2,1)S(1)} %collective-permute-done.6.far_own, ...), custom_call_target="tpu_custom_call" | custom-call | tf_op jit(solution)/shard_map/pallas_call | solution.py:47
  76.7 2.3 %collective-permute-start.9 = (bf16[4,2,64,768]{3,2,1,0:T(8,128)(2,1)S(1)}, bf16[4,2,64,768]{3,2,1,0:T(8,128)(2,1)S(1)}, u32[]{:S(2)}, u32[]{:S(2)}) collective-permute-start(bf16[4,2,64,768]{3,2,1,0:T(8,128)(2,1)S(1)} %all-to-all-done.1.near), channel_id=1, source_target_pairs={{0,1},{1,0},{2,3},{3,2},{4,5},{5,4},{6,7},{7,6},{8,9},{9,8},{10,11... | collective-permute-start | bytes 2359304 | tf_op jit(solution)/shard_map/ppermute | solution.py:25
  78.9 3.4 %all-to-all-start.2 = ((bf16[8,16,1024]{2,1,0:T(8,128)(2,1)}), bf16[8,16,1024]{2,1,0:T(8,128)(2,1)S(1)}, u32[]{:S(2)}, u32[]{:S(2)}) async-start(bf16[8,16,1024]{2,1,0:T(8,128)(2,1)} %bitcast.10), calls=%async_computation.2 | async-start | bytes 524288 | tf_op jit(solution)/shard_map/all_to_all | solution.py:16
  82.5 4.7 %shard_map.132 = (bf16[2560,768]{1,0:T(8,128)(2,1)}, bf16[128,768]{1,0:T(8,128)(2,1)S(1)}) custom-call(bf16[1280,768]{1,0:T(8,128)(2,1)} %near.1, bf16[1280,768]{1,0:T(8,128)(2,1)} %collective-permute-done.8.far, s32[256,1]{1,0:T(8,128)S(1)} %copy.14.labels), custom_call_target="tpu_custom_call" | custom-call | flops 2147483648 | bytes 12582912 | tf_op jit(solution)/shard_map/pallas_call | solution.py:47
  87.3 2.3 %all-to-all-done.2.mixed = bf16[8,16,1024]{2,1,0:T(8,128)(2,1)S(1)} async-done(((bf16[8,16,1024]{2,1,0:T(8,128)(2,1)}), bf16[8,16,1024]{2,1,0:T(8,128)(2,1)S(1)}, u32[]{:S(2)}, u32[]{:S(2)}) %all-to-all-start.2) | async-done | bytes 262176 | tf_op jit(solution)/shard_map/all_to_all | solution.py:16
  91.0 10.4 %all_to_all.40.arrived = bf16[8,16,1536]{2,1,0:T(8,128)(2,1)S(1)} all-to-all(bf16[8,16,1536]{2,1,0:T(8,128)(2,1)S(1)} %get-tuple-element.50), channel_id=1, replica_groups={{0,2,4,6,8,10,12,14},{1,3,5,7,9,11,13,15},{16,18,20,22,24,26,28,30},{17..., dimensions={0} | all-to-all | bytes 786432 | tf_op jit(solution)/shard_map/all_to_all | solution.py:16
  101.4 4.7 %shard_map.134 = (bf16[128,896]{1,0:T(8,128)(2,1)S(1)}, f32[16,768]{1,0:T(8,128)S(1)}) custom-call(bf16[8,16,1536]{2,1,0:T(8,128)(2,1)S(1)} %all_to_all.40.arrived, bf16[2560,768]{1,0:T(8,128)(2,1)} %get-tuple-element.51.text_unit, s32[256,1]{1,0:T(8,128)S(1)} %copy.14.labels), custom_call_target="tpu_custom_call" | custom-call | tf_op jit(solution)/shard_map/pallas_call | solution.py:47
  106.2 8.4 %all_to_all.41.back = bf16[8,16,896]{2,1,0:T(8,128)(2,1)S(1)} all-to-all(bf16[8,16,896]{2,1,0:T(8,128)(2,1)S(1)} %bitcast.20), channel_id=1, replica_groups={{0,2,4,6,8,10,12,14},{1,3,5,7,9,11,13,15},{16,18,20,22,24,26,28,30},{17..., dimensions={0} | all-to-all | bytes 458752 | tf_op jit(solution)/shard_map/all_to_all | solution.py:16
  114.5 1.0 shard_map.135
  115.5 8.7 %all_to_all.42 = bf16[8,16,1024]{2,1,0:T(8,128)(2,1)S(1)} all-to-all(bf16[8,16,1024]{2,1,0:T(8,128)(2,1)S(1)} %get-tuple-element.58), channel_id=1, replica_groups={{0,2,4,6,8,10,12,14},{1,3,5,7,9,11,13,15},{16,18,20,22,24,26,28,30},{17..., dimensions={0} | all-to-all | bytes 524288 | tf_op jit(solution)/shard_map/all_to_all | solution.py:16
  124.2 2.9 %shard_map.136 = bf16[128,1024]{1,0:T(8,128)(2,1)} custom-call(bf16[16,2,32,256]{3,2,1,0:T(8,128)(2,1)} %copy-done.11, bf16[16,2,32,256]{3,2,1,0:T(8,128)(2,1)} %collective-permute-done.5.other, bf16[16,2,32,256]{3,2,1,0:T(8,128)(2,1)S(1)} %collective-permute-done.6.far_own, bf16[16,2,32,256]{3,2,1,0:T(8,128)(2,1)S(1)} %collective-permute-done.7.far_other, ...), custom_call_target="tpu_custom_call" | custom-call | tf_op jit(solution)/shard_map/pallas_call | solution.py:47
  127.1 3.4 %all-to-all-start.6 = ((bf16[8,16,1024]{2,1,0:T(8,128)(2,1)}), bf16[8,16,1024]{2,1,0:T(8,128)(2,1)S(1)}, u32[]{:S(2)}, u32[]{:S(2)}) async-start(bf16[8,16,1024]{2,1,0:T(8,128)(2,1)} %bitcast.14), calls=%async_computation.6 | async-start | bytes 524288 | tf_op jit(solution)/shard_map/all_to_all | solution.py:16
  131.2 5.4 %all-to-all-done.6.parts = bf16[8,16,1024]{2,1,0:T(8,128)(2,1)S(1)} async-done(((bf16[8,16,1024]{2,1,0:T(8,128)(2,1)}), bf16[8,16,1024]{2,1,0:T(8,128)(2,1)S(1)}, u32[]{:S(2)}, u32[]{:S(2)}) %all-to-all-start.6) | async-done | bytes 262176 | tf_op jit(solution)/shard_map/all_to_all | solution.py:16
  137.0 13.7 %all_to_all.43.parts = f32[16,8,128]{2,1,0:T(8,128)S(1)} all-to-all(f32[16,8,128]{2,1,0:T(8,128)S(1)} %shard_map.137), channel_id=1, replica_groups=mesh['dp'=32,'txt'=16] {'txt'}, dimensions={0} | all-to-all | bytes 131072 | tf_op jit(solution)/shard_map/all_to_all | solution.py:16
  (41 shorter events, 8.5 us)
Async XLA Ops:
  0.0 49.5 %copy-start.5 = (f32[1024]{0:T(1024)S(1)}, f32[1024]{0:T(1024)}, u32[]{:S(2)}) copy-start(f32[1024]{0:T(1024)} %param.14) | copy-start | bytes 12292
  0.0 49.5 %copy-start.6 = (f32[1024]{0:T(1024)S(1)}, f32[1024]{0:T(1024)}, u32[]{:S(2)}) copy-start(f32[1024]{0:T(1024)} %param.15) | copy-start | bytes 12292
  1.6 48.2 %all-to-all-start = ((bf16[16,2,32,256]{3,2,1,0:T(8,128)(2,1)}), bf16[16,2,32,256]{3,2,1,0:T(8,128)(2,1)S(1)}, u32[]{:S(2)}, u32[]{:S(2)}) async-start(bf16[16,2,32,256]{3,2,1,0:T(8,128)(2,1)} %broadcast_in_dim.29), calls=%async_computation | async-start | bytes 1048576 | tf_op jit(solution)/shard_map/all_to_all | solution.py:16
  17.4 0.8 copy-start.2
  18.1 0.9 copy-start.4
  19.0 0.7 copy-start.8
  19.7 0.7 copy-start.9
  20.4 0.7 copy-start.10
  21.1 6.3 %collective-permute-start = (bf16[64,1152]{1,0:T(8,128)(2,1)S(1)}, bf16[64,1152]{1,0:T(8,128)(2,1)S(1)}, u32[]{:S(2)}, u32[]{:S(2)}) collective-permute-start(bf16[64,1152]{1,0:T(8,128)(2,1)S(1)} %shard_map.127.near), channel_id=1, source_target_pairs={{0,2},{1,3},{2,0},{3,1},{4,6},{5,7},{6,4},{7,5},{8,10},{9,11},{10,... | collective-permute-start | bytes 442376 | tf_op jit(solution)/shard_map/ppermute | solution.py:25
  28.3 9.7 %collective-permute-start.1 = (bf16[2,64,384]{2,1,0:T(8,128)(2,1)S(1)}, bf16[2,64,384]{2,1,0:T(8,128)(2,1)S(1)}, u32[]{:S(2)}, u32[]{:S(2)}) collective-permute-start(bf16[2,64,384]{2,1,0:T(8,128)(2,1)S(1)} %get-tuple-element.35.refs_0_), channel_id=1, source_target_pairs={{0,4},{1,5},{2,6},{3,7},{4,0},{5,1},{6,2},{7,3},{8,12},{9,13},{10,... | collective-permute-start | bytes 294920 | tf_op jit(solution)/shard_map/ppermute | solution.py:25
  31.5 8.2 %collective-permute-start.2 = (bf16[2,64,384]{2,1,0:T(8,128)(2,1)S(1)}, bf16[2,64,384]{2,1,0:T(8,128)(2,1)S(1)}, u32[]{:S(2)}, u32[]{:S(2)}) collective-permute-start(bf16[2,64,384]{2,1,0:T(8,128)(2,1)S(1)} %get-tuple-element.35.refs_0_), channel_id=1, source_target_pairs={{0,8},{1,9},{2,10},{3,11},{4,12},{5,13},{6,14},{7,15},{8,0},{9,1},... | collective-permute-start | bytes 294920 | tf_op jit(solution)/shard_map/ppermute | solution.py:25
  36.0 6.9 %collective-permute-start.3 = (bf16[2,64,384]{2,1,0:T(8,128)(2,1)S(1)}, bf16[2,64,384]{2,1,0:T(8,128)(2,1)S(1)}, u32[]{:S(2)}, u32[]{:S(2)}) collective-permute-start(bf16[2,64,384]{2,1,0:T(8,128)(2,1)S(1)} %get-tuple-element.35.refs_0_), channel_id=1, source_target_pairs={{0,12},{1,13},{2,14},{3,15},{4,8},{5,9},{6,10},{7,11},{8,4},{9,5},... | collective-permute-start | bytes 294920 | tf_op jit(solution)/shard_map/ppermute | solution.py:25
  42.9 6.5 %collective-permute-start.4 = (bf16[4,2,64,384]{3,2,1,0:T(8,128)(2,1)S(1)}, bf16[4,2,64,384]{3,2,1,0:T(8,128)(2,1)S(1)}, u32[]{:S(2)}, u32[]{:S(2)}) collective-permute-start(bf16[4,2,64,384]{3,2,1,0:T(8,128)(2,1)S(1)} %shard_map.129.near), channel_id=1, source_target_pairs={{0,1},{1,0},{2,3},{3,2},{4,5},{5,4},{6,7},{7,6},{8,9},{9,8},{10,11... | collective-permute-start | bytes 1179656 | tf_op jit(solution)/shard_map/ppermute | solution.py:25
  49.9 26.8 %copy-start = (f32[8,1024]{1,0:T(8,128)}, f32[8,1024]{1,0:T(8,128)S(1)}, u32[]{:S(2)}) copy-start(f32[8,1024]{1,0:T(8,128)S(1)} %get-tuple-element.45.lines) | copy-start | bytes 98308
  49.9 23.8 %copy-start.11 = (bf16[16,2,32,256]{3,2,1,0:T(8,128)(2,1)}, bf16[16,2,32,256]{3,2,1,0:T(8,128)(2,1)S(1)}, u32[]{:S(2)}) copy-start(bf16[16,2,32,256]{3,2,1,0:T(8,128)(2,1)S(1)} %all-to-all-done.own) | copy-start | bytes 1572868
  49.9 32.5 %copy-start.12 = (s32[256]{0:T(256)S(1)}, s32[256]{0:T(256)}, u32[]{:S(2)}) copy-start(s32[256]{0:T(256)} %param.24) | copy-start | bytes 3076
  49.9 26.8 %collective-permute-start.8 = (bf16[1280,768]{1,0:T(8,128)(2,1)}, bf16[1280,768]{1,0:T(8,128)(2,1)}, u32[]{:S(2)}, u32[]{:S(2)}) collective-permute-start(bf16[1280,768]{1,0:T(8,128)(2,1)} %near.1), channel_id=1, source_target_pairs={{0,1},{1,0},{2,3},{3,2},{4,5},{5,4},{6,7},{7,6},{8,9},{9,8},{10,11... | collective-permute-start | bytes 5898248 | tf_op jit(solution)/shard_map/ppermute | solution.py:25
  52.2 16.9 %collective-permute-start.5 = (bf16[16,2,32,256]{3,2,1,0:T(8,128)(2,1)S(1)}, bf16[16,2,32,256]{3,2,1,0:T(8,128)(2,1)}, u32[]{:S(2)}, u32[]{:S(2)}) collective-permute-start(bf16[16,2,32,256]{3,2,1,0:T(8,128)(2,1)S(1)} %all-to-all-done.own), channel_id=1, source_target_pairs={{0,16},{16,0},{32,48},{48,32},{64,80},{80,64},{96,112},{112,96},{1... | collective-permute-start | bytes 1572872 | tf_op jit(solution)/shard_map/ppermute | solution.py:25
  56.9 19.8 %all-to-all-start.1 = ((bf16[4,2,64,768]{3,2,1,0:T(8,128)(2,1)}), bf16[4,2,64,768]{3,2,1,0:T(8,128)(2,1)S(1)}, u32[]{:S(2)}, u32[]{:S(2)}) async-start(bf16[4,2,64,768]{3,2,1,0:T(8,128)(2,1)} %get-tuple-element.42), calls=%async_computation.1 | async-start | bytes 1572864 | tf_op jit(solution)/shard_map/all_to_all | solution.py:16
  60.4 11.6 %collective-permute-start.6 = (bf16[16,2,32,256]{3,2,1,0:T(8,128)(2,1)S(1)}, bf16[16,2,32,256]{3,2,1,0:T(8,128)(2,1)S(1)}, u32[]{:S(2)}, u32[]{:S(2)}) collective-permute-start(bf16[16,2,32,256]{3,2,1,0:T(8,128)(2,1)S(1)} %all-to-all-done.own), channel_id=1, source_target_pairs={{0,1},{1,0},{2,3},{3,2},{4,5},{5,4},{6,7},{7,6},{8,9},{9,8},{10,11... | collective-permute-start | bytes 1572872 | tf_op jit(solution)/shard_map/ppermute | solution.py:25
  69.1 4.6 %collective-permute-start.7 = (bf16[16,2,32,256]{3,2,1,0:T(8,128)(2,1)}, bf16[16,2,32,256]{3,2,1,0:T(8,128)(2,1)S(1)}, u32[]{:S(2)}, u32[]{:S(2)}) collective-permute-start(bf16[16,2,32,256]{3,2,1,0:T(8,128)(2,1)} %collective-permute-done.5.other), channel_id=1, source_target_pairs={{0,1},{1,0},{2,3},{3,2},{4,5},{5,4},{6,7},{7,6},{8,9},{9,8},{10,11... | collective-permute-start | bytes 1572872 | tf_op jit(solution)/shard_map/ppermute | solution.py:25
  76.7 12.9 %collective-permute-start.9 = (bf16[4,2,64,768]{3,2,1,0:T(8,128)(2,1)S(1)}, bf16[4,2,64,768]{3,2,1,0:T(8,128)(2,1)S(1)}, u32[]{:S(2)}, u32[]{:S(2)}) collective-permute-start(bf16[4,2,64,768]{3,2,1,0:T(8,128)(2,1)S(1)} %all-to-all-done.1.near), channel_id=1, source_target_pairs={{0,1},{1,0},{2,3},{3,2},{4,5},{5,4},{6,7},{7,6},{8,9},{9,8},{10,11... | collective-permute-start | bytes 2359304 | tf_op jit(solution)/shard_map/ppermute | solution.py:25
  78.9 10.6 %all-to-all-start.2 = ((bf16[8,16,1024]{2,1,0:T(8,128)(2,1)}), bf16[8,16,1024]{2,1,0:T(8,128)(2,1)S(1)}, u32[]{:S(2)}, u32[]{:S(2)}) async-start(bf16[8,16,1024]{2,1,0:T(8,128)(2,1)} %bitcast.10), calls=%async_computation.2 | async-start | bytes 524288 | tf_op jit(solution)/shard_map/all_to_all | solution.py:16
  82.5 7.1 %copy-start.7 = (f32[1024]{0:T(1024)S(1)}, f32[1024]{0:T(1024)}, u32[]{:S(2)}) copy-start(f32[1024]{0:T(1024)} %param.19) | copy-start | bytes 12292
  89.6 0.8 copy-start.1
  124.2 26.5 %copy-start.3 = (bf16[256,64]{0,1:T(8,128)(2,1)S(1)}, bf16[256,64]{0,1:T(8,128)(2,1)}, u32[]{:S(2)}) copy-start(bf16[256,64]{0,1:T(8,128)(2,1)} %param.13) | copy-start | bytes 98308
  127.1 9.5 %all-to-all-start.6 = ((bf16[8,16,1024]{2,1,0:T(8,128)(2,1)}), bf16[8,16,1024]{2,1,0:T(8,128)(2,1)S(1)}, u32[]{:S(2)}, u32[]{:S(2)}) async-start(bf16[8,16,1024]{2,1,0:T(8,128)(2,1)} %bitcast.14), calls=%async_computation.6 | async-start | bytes 524288 | tf_op jit(solution)/shard_map/all_to_all | solution.py:16

commit v8 on v7

--- a/solution.py
+++ b/solution.py
@@ -14,10 +14,6 @@
 
 def swapped(x, axis, groups=None):
     return lax.all_to_all(x, axis, 0, 0, tiled=True, axis_index_groups=groups)
-
-
-def copies(x, n):
-    return jnp.broadcast_to(x, (n, *x.shape))
 
 
 def from_partner(x, axis, bits):
@@ -107,8 +103,27 @@
         store.wait()
 
 
-def message_kernel(projection, resid, gain, bias, up_bias, out):
+def copies_kernel(up, down, out, sem):
+    loads = [
+        pltpu.make_async_copy(part, out.at[0, k], sem.at[k]) for k, part in enumerate((up, down))
+    ]
+    for load in loads:
+        load.start()
+    for load in loads:
+        load.wait()
+    for z in range(1, out.shape[0]):
+        out[z] = out[0]
+
+
+def message_kernel(projection, resid, gain, bias, up_bias, out, gains, biases, ups, sem):
     emb, images = projection.shape[1], resid.shape[1]
+    places = (out.at[:, :emb], out.at[:, emb : emb + images], gains, biases, ups)
+    loads = [
+        pltpu.make_async_copy(part, place, sem.at[k])
+        for k, (part, place) in enumerate(zip((projection, resid, gain, bias, up_bias), places))
+    ]
+    for load in loads:
+        load.start()
 
     def parts(value):
         found = []
@@ -118,15 +133,14 @@
             value = value - part
         return found
 
-    out[:, :emb] = projection[...]
-    out[:, emb : emb + images] = resid[...]
+    for load in loads:
+        load.wait()
     blank = jnp.zeros((1, 128 - gain.shape[1]), F32)
     lines = [
-        jnp.concatenate([part, blank], axis=1)
-        for part in parts(gain[...]) + parts(bias[...])
+        jnp.concatenate([part, blank], axis=1) for part in parts(gains[...]) + parts(biases[...])
     ]
     lines += [jnp.zeros((1, 128), F32)] * 2
-    lines += [part[:, 128 * k : 128 * k + 128] for part in parts(up_bias[...]) for k in range(2)]
+    lines += [part[:, 128 * k : 128 * k + 128] for part in parts(ups[...]) for k in range(2)]
     lines += [jnp.zeros((1, 128), F32)] * 2
     lines = jnp.concatenate(lines, axis=0)
     out[:, emb + images :] = jnp.zeros((out.shape[0], 128), BF)
@@ -232,17 +246,20 @@
     pre_act, mixed, up, down, sem = refs
     width, hid = normed.shape[1], bias.shape[1]
     loads = ordered_weights(own, other, far_own, far_other, {0: up, 1: down}, sem)
-    total = jnp.zeros(normed.shape, F32)
+    hidden = []
     for k, add in enumerate((bias, far_bias)):
-        for matrix in range(2):
-            for x in range(2):
-                loads[matrix, k, x].wait()
+        for x in range(2):
+            loads[0, k, x].wait()
         w_up = up[k].reshape(width, hid)
         pre = jnp.dot(normed[...], w_up, preferred_element_type=F32) + add[...]
         pre_act[k] = pre
-        hidden = (pre * jax.nn.sigmoid(1.702 * pre)).astype(BF)
+        hidden.append((pre * jax.nn.sigmoid(1.702 * pre)).astype(BF))
+    total = jnp.zeros(normed.shape, F32)
+    for k in range(2):
+        for x in range(2):
+            loads[1, k, x].wait()
         w_down = down[k].reshape(width, hid)
-        total += lax.dot_general(hidden, w_down, NT, preferred_element_type=F32)
+        total += lax.dot_general(hidden[k], w_down, NT, preferred_element_type=F32)
     mixed[...] = total.astype(BF)
 
 
@@ -250,7 +267,7 @@
     normed_grad, up, down, sem = refs
     width, hid = arrived.shape[1], pre_act.shape[2]
     loads = ordered_weights(own, other, far_own, far_other, {1: down, 0: up}, sem)
-    total = jnp.zeros(normed_grad.shape, F32)
+    act_grad = []
     for k in range(2):
         for x in range(2):
             loads[1, k, x].wait()
@@ -258,11 +275,13 @@
         hid_grad = jnp.dot(arrived[...], w_down, preferred_element_type=F32)
         pre = pre_act[k]
         gate = jax.nn.sigmoid(1.702 * pre)
-        act_grad = (hid_grad * (gate + 1.702 * pre * gate * (1.0 - gate))).astype(BF)
+        act_grad.append((hid_grad * (gate + 1.702 * pre * gate * (1.0 - gate))).astype(BF))
+    total = jnp.zeros(normed_grad.shape, F32)
+    for k in range(2):
         for x in range(2):
             loads[0, k, x].wait()
         w_up = up[k].reshape(width, hid)
-        total += lax.dot_general(act_grad, w_up, NT, preferred_element_type=F32)
+        total += lax.dot_general(act_grad[k], w_up, NT, preferred_element_type=F32)
     normed_grad[...] = total.astype(BF)
 
 
@@ -430,21 +449,31 @@
     along_y = [[b + 4 * y for y in range(4)] for b in range(4)]
     along_z = [[2 * z + x for z in range(n_z)] for x in range(2)]
 
-    mine = jnp.stack([up_weight, down_weight.T], axis=0)
-    mine = swapped(copies(mine, n_z), "dp", along_z)
+    (mine,) = call(
+        copies_kernel,
+        (((n_z, 2, WIDTH // n_dp, hid), BF),),
+        "hhv",
+        up_weight,
+        down_weight.T,
+        sems=2,
+    )
+    mine = swapped(mine, "dp", along_z)
 
     (chain,) = call(
         message_kernel,
         (((share, emb + images + 128), BF),),
-        "vvvvvv",
+        "hhhhhv",
         projection,
         resid.T,
         post_gain[None],
         post_bias[None],
         up_bias[None],
         cost=SMALL,
-    )
-    chain, labels = lax.optimization_barrier((chain, labels[:, None]))
+        scratch=(((1, share), F32), ((1, share), F32), ((1, hid), F32)),
+        sems=5,
+    )
+    chain, labels, far_texts = lax.optimization_barrier((chain, labels[:, None], texts))
+    far_texts = from_partner(far_texts, "txt", 1)
     proj, rest = call(
         split_kernel,
         (((4, 2, share, emb), BF), ((2, share, images + 128), BF)),
@@ -453,8 +482,10 @@
         from_partner(chain, "txt", 2),
         cost=SMALL,
     )
-    rest = [rest] + [from_partner(rest, "txt", 4 * k) for k in (1, 2, 3)]
-    (rest,) = call(stack_kernel, (((4, *rest[0].shape), BF),), "vvvvv", *rest, cost=SMALL)
+    for bits in (4, 8):
+        both = (rest, from_partner(rest, "txt", bits))
+        (rest,) = call(stack_kernel, (((2, *rest.shape), BF),), "vvv", *both, cost=SMALL)
+    rest = rest.reshape(4, 2, share, images + 128)
     far_rest = from_partner(rest, "txt", 1)
     own, lines, normed, far_bias = call(
         rows_kernel,
@@ -468,10 +499,9 @@
         scratch=(((WIDTH, half), BF), ((n_txt, 8, 128), F32)),
     )
 
-    mine, proj, normed, far_texts = lax.optimization_barrier((mine, proj, normed, texts))
+    mine, proj, normed = lax.optimization_barrier((mine, proj, normed))
     other = from_partner(mine, "dp", 1)
     far_mine = from_partner(mine, "txt", 1)
-    far_texts = from_partner(far_texts, "txt", 1)
     proj = swapped(proj, "txt", along_y)
     far_other = from_partner(other, "txt", 1)
     weights = (mine, other, far_mine, far_other)

time: 153 us -> 152 us (level)
  local copies, waits for them, and re-layouts: 5.42 us -> 0.93 us
  Pallas kernels: 19.5 us -> 22 us
    unnamed x26 -> x18, local copies, waits for them, and re-layouts: 4.42 us -> 0.8 us
    pallas_call x12 -> x14, Pallas kernels: 19.5 us -> 22 us  [call(): pl.pallas_call(body, out_shape=[pltpu.HBM(*out) if c == 'h' else jax.Shap...]
    all_to_all x4, starting transfers between devices: 26.1 us -> 28.5 us  [swapped(): return lax.all_to_all(x, axis, 0, 0, tiled=True, axis_index_groups=groups)]
    ppermute x10 -> x9, starting transfers between devices: 32.4 us -> 31.3 us  [from_partner(): return lax.ppermute(x, axis, pairs)]
    ppermute x10 -> x9, waiting for transfers between devices: 17.5 us -> 18.1 us  [from_partner(): return lax.ppermute(x, axis, pairs)]
  transfers between devices with their start and end apart: 14 -> 13, of which waited for: 8 -> 8; matrix products, arithmetic and copies ran while one was open for 0% -> 0% of each run, Pallas kernels for 6% -> 7%
where the time goes in v8:
time: 152 us; the launch traced here: 151 us
  starting transfers between devices  59.8 us (39%)
  blocking collectives  41.5 us (27%)
  waiting for transfers between devices  25.6 us (17%)
  Pallas kernels  22 us (14%)
    all_to_all x4, blocking collectives, swapped(): return lax.all_to_all(x, axis, 0, 0, tiled=True, axis_index_groups=groups)  41.5 us
    ppermute x9, starting transfers between devices, from_partner(): return lax.ppermute(x, axis, pairs)  31.3 us
    all_to_all x4, starting transfers between devices, swapped(): return lax.all_to_all(x, axis, 0, 0, tiled=True, axis_index_groups=groups)  28.5 us
    pallas_call x14, Pallas kernels, call(): pl.pallas_call(body, out_shape=[pltpu.HBM(*out) if c == 'h' else jax.Shap...  22 us
    ppermute x9, waiting for transfers between devices, from_partner(): return lax.ppermute(x, axis, pairs)  18.1 us
    all_to_all x4, waiting for transfers between devices, swapped(): return lax.all_to_all(x, axis, 0, 0, tiled=True, axis_index_groups=groups)  7.49 us
  transfers between devices with their start and end apart: 13, of which 8 were waited for; matrix products, arithmetic and copies ran while one was open for 0% of the time, Pallas kernels for 7%

profile of v8, /device:TPU:1, one launch (start us, length us, event | category | flops | bytes accessed | tf_op | source)
XLA Modules:
  0.0 150.7 jit_solution(713288718259821218)
XLA Ops:
  0.0 1.6 %shard_map.127 = bf16[16,2,32,256]{3,2,1,0:T(8,128)(2,1)} custom-call(bf16[32,256]{1,0:T(8,128)(2,1)} %up.1, bf16[32,256]{1,0:T(8,128)(2,1)} %bitcast.29), custom_call_target="tpu_custom_call" | custom-call | tf_op jit(solution)/shard_map/pallas_call | solution.py:43
  1.6 15.8 %all-to-all-start = ((bf16[16,2,32,256]{3,2,1,0:T(8,128)(2,1)}), bf16[16,2,32,256]{3,2,1,0:T(8,128)(2,1)S(1)}, u32[]{:S(2)}, u32[]{:S(2)}) async-start(bf16[16,2,32,256]{3,2,1,0:T(8,128)(2,1)} %shard_map.127), calls=%async_computation | async-start | bytes 1048576 | tf_op jit(solution)/shard_map/all_to_all | solution.py:16
  17.4 1.0 shard_map.128.near
  18.4 2.9 %collective-permute-start.7 = (bf16[1280,768]{1,0:T(8,128)(2,1)}, bf16[1280,768]{1,0:T(8,128)(2,1)}, u32[]{:S(2)}, u32[]{:S(2)}) collective-permute-start(bf16[1280,768]{1,0:T(8,128)(2,1)} %near.1), channel_id=1, source_target_pairs={{0,1},{1,0},{2,3},{3,2},{4,5},{5,4},{6,7},{7,6},{8,9},{9,8},{10,11... | collective-permute-start | bytes 5898248 | tf_op jit(solution)/shard_map/ppermute | solution.py:21
  21.3 3.1 %collective-permute-start = (bf16[64,1152]{1,0:T(8,128)(2,1)S(1)}, bf16[64,1152]{1,0:T(8,128)(2,1)S(1)}, u32[]{:S(2)}, u32[]{:S(2)}) collective-permute-start(bf16[64,1152]{1,0:T(8,128)(2,1)S(1)} %shard_map.128.near), channel_id=1, source_target_pairs={{0,2},{1,3},{2,0},{3,1},{4,6},{5,7},{6,4},{7,5},{8,10},{9,11},{10,... | collective-permute-start | bytes 442376 | tf_op jit(solution)/shard_map/ppermute | solution.py:21
  24.4 4.2 %collective-permute-done.other = bf16[64,1152]{1,0:T(8,128)(2,1)S(1)} collective-permute-done((bf16[64,1152]{1,0:T(8,128)(2,1)S(1)}, bf16[64,1152]{1,0:T(8,128)(2,1)S(1)}, u32[]{:S(2)}, u32[]{:S(2)}) %collective-permute-start) | collective-permute-done | bytes 147488 | tf_op jit(solution)/shard_map/ppermute | solution.py:21
  29.6 3.2 %collective-permute-start.1 = (bf16[2,64,384]{2,1,0:T(8,128)(2,1)S(1)}, bf16[2,64,384]{2,1,0:T(8,128)(2,1)S(1)}, u32[]{:S(2)}, u32[]{:S(2)}) collective-permute-start(bf16[2,64,384]{2,1,0:T(8,128)(2,1)S(1)} %get-tuple-element.35.refs_0_), channel_id=1, source_target_pairs={{0,4},{1,5},{2,6},{3,7},{4,0},{5,1},{6,2},{7,3},{8,12},{9,13},{10,... | collective-permute-start | bytes 294920 | tf_op jit(solution)/shard_map/ppermute | solution.py:21
  32.8 2.4 %collective-permute-done.1.refs_1_ = bf16[2,64,384]{2,1,0:T(8,128)(2,1)S(1)} collective-permute-done((bf16[2,64,384]{2,1,0:T(8,128)(2,1)S(1)}, bf16[2,64,384]{2,1,0:T(8,128)(2,1)S(1)}, u32[]{:S(2)}, u32[]{:S(2)}) %collective-permute-start.1) | collective-permute-done | bytes 98336 | tf_op jit(solution)/shard_map/ppermute | solution.py:21
  35.3 4.8 %collective-permute-start.2 = (bf16[2,2,64,384]{3,2,1,0:T(8,128)(2,1)S(1)}, bf16[2,2,64,384]{3,2,1,0:T(8,128)(2,1)S(1)}, u32[]{:S(2)}, u32[]{:S(2)}) collective-permute-start(bf16[2,2,64,384]{3,2,1,0:T(8,128)(2,1)S(1)} %shard_map.130.refs_0_), channel_id=1, source_target_pairs={{0,8},{1,9},{2,10},{3,11},{4,12},{5,13},{6,14},{7,15},{8,0},{9,1},... | collective-permute-start | bytes 589832 | tf_op jit(solution)/shard_map/ppermute | solution.py:21
  40.1 3.4 %collective-permute-done.2.refs_1_ = bf16[2,2,64,384]{3,2,1,0:T(8,128)(2,1)S(1)} collective-permute-done((bf16[2,2,64,384]{3,2,1,0:T(8,128)(2,1)S(1)}, bf16[2,2,64,384]{3,2,1,0:T(8,128)(2,1)S(1)}, u32[]{:S(2)}, u32[]{:S(2)}) %collective-permute-start.2) | collective-permute-done | bytes 196640 | tf_op jit(solution)/shard_map/ppermute | solution.py:21
  43.5 4.4 %collective-permute-start.3 = (bf16[4,2,64,384]{3,2,1,0:T(8,128)(2,1)S(1)}, bf16[4,2,64,384]{3,2,1,0:T(8,128)(2,1)S(1)}, u32[]{:S(2)}, u32[]{:S(2)}) collective-permute-start(bf16[4,2,64,384]{3,2,1,0:T(8,128)(2,1)S(1)} %bitcast.17), channel_id=1, source_target_pairs={{0,1},{1,0},{2,3},{3,2},{4,5},{5,4},{6,7},{7,6},{8,9},{9,8},{10,11... | collective-permute-start | bytes 1179656 | tf_op jit(solution)/shard_map/ppermute | solution.py:21
  47.9 1.3 collective-permute-done.3.far
  49.7 4.7 %collective-permute-start.4 = (bf16[16,2,32,256]{3,2,1,0:T(8,128)(2,1)S(1)}, bf16[16,2,32,256]{3,2,1,0:T(8,128)(2,1)}, u32[]{:S(2)}, u32[]{:S(2)}) collective-permute-start(bf16[16,2,32,256]{3,2,1,0:T(8,128)(2,1)S(1)} %all-to-all-done.own), channel_id=1, source_target_pairs={{0,16},{16,0},{32,48},{48,32},{64,80},{80,64},{96,112},{112,96},{1... | collective-permute-start | bytes 1572872 | tf_op jit(solution)/shard_map/ppermute | solution.py:21
  54.4 4.2 %all-to-all-start.1 = ((bf16[4,2,64,768]{3,2,1,0:T(8,128)(2,1)}), bf16[4,2,64,768]{3,2,1,0:T(8,128)(2,1)S(1)}, u32[]{:S(2)}, u32[]{:S(2)}) async-start(bf16[4,2,64,768]{3,2,1,0:T(8,128)(2,1)} %get-tuple-element.42), calls=%async_computation.1 | async-start | bytes 1572864 | tf_op jit(solution)/shard_map/all_to_all | solution.py:16
  58.6 2.8 %collective-permute-start.5 = (bf16[16,2,32,256]{3,2,1,0:T(8,128)(2,1)S(1)}, bf16[16,2,32,256]{3,2,1,0:T(8,128)(2,1)S(1)}, u32[]{:S(2)}, u32[]{:S(2)}) collective-permute-start(bf16[16,2,32,256]{3,2,1,0:T(8,128)(2,1)S(1)} %all-to-all-done.own), channel_id=1, source_target_pairs={{0,1},{1,0},{2,3},{3,2},{4,5},{5,4},{6,7},{7,6},{8,9},{9,8},{10,11... | collective-permute-start | bytes 1572872 | tf_op jit(solution)/shard_map/ppermute | solution.py:21
  61.4 4.9 %collective-permute-done.4.other = bf16[16,2,32,256]{3,2,1,0:T(8,128)(2,1)} collective-permute-done((bf16[16,2,32,256]{3,2,1,0:T(8,128)(2,1)S(1)}, bf16[16,2,32,256]{3,2,1,0:T(8,128)(2,1)}, u32[]{:S(2)}, u32[]{:S(2)}) %collective-permute-start.4) | collective-permute-done | bytes 524320 | tf_op jit(solution)/shard_map/ppermute | solution.py:21
  66.3 3.1 %collective-permute-start.6 = (bf16[16,2,32,256]{3,2,1,0:T(8,128)(2,1)}, bf16[16,2,32,256]{3,2,1,0:T(8,128)(2,1)S(1)}, u32[]{:S(2)}, u32[]{:S(2)}) collective-permute-start(bf16[16,2,32,256]{3,2,1,0:T(8,128)(2,1)} %collective-permute-done.4.other), channel_id=1, source_target_pairs={{0,1},{1,0},{2,3},{3,2},{4,5},{5,4},{6,7},{7,6},{8,9},{9,8},{10,11... | collective-permute-start | bytes 1572872 | tf_op jit(solution)/shard_map/ppermute | solution.py:21
  69.5 1.7 %collective-permute-done.6.far_other = bf16[16,2,32,256]{3,2,1,0:T(8,128)(2,1)S(1)} collective-permute-done((bf16[16,2,32,256]{3,2,1,0:T(8,128)(2,1)}, bf16[16,2,32,256]{3,2,1,0:T(8,128)(2,1)S(1)}, u32[]{:S(2)}, u32[]{:S(2)}) %collective-permute-start.6) | collective-permute-done | bytes 524320 | tf_op jit(solution)/shard_map/ppermute | solution.py:21
  71.2 2.9 %shard_map.133 = (f32[2,128,256]{2,1,0:T(8,128)S(1)}, bf16[128,1024]{1,0:T(8,128)(2,1)}) custom-call(bf16[16,2,32,256]{3,2,1,0:T(8,128)(2,1)} %copy-done.7, bf16[16,2,32,256]{3,2,1,0:T(8,128)(2,1)} %collective-permute-done.4.other, bf16[16,2,32,256]{3,2,1,0:T(8,128)(2,1)S(1)} %collective-permute-done.5.far_own, ...), custom_call_target="tpu_custom_call" | custom-call | tf_op jit(solution)/shard_map/pallas_call | solution.py:43
  74.1 2.3 %collective-permute-start.8 = (bf16[4,2,64,768]{3,2,1,0:T(8,128)(2,1)S(1)}, bf16[4,2,64,768]{3,2,1,0:T(8,128)(2,1)S(1)}, u32[]{:S(2)}, u32[]{:S(2)}) collective-permute-start(bf16[4,2,64,768]{3,2,1,0:T(8,128)(2,1)S(1)} %all-to-all-done.1.near), channel_id=1, source_target_pairs={{0,1},{1,0},{2,3},{3,2},{4,5},{5,4},{6,7},{7,6},{8,9},{9,8},{10,11... | collective-permute-start | bytes 2359304 | tf_op jit(solution)/shard_map/ppermute | solution.py:21
  76.4 5.1 %all-to-all-start.2 = ((bf16[8,16,1024]{2,1,0:T(8,128)(2,1)}), bf16[8,16,1024]{2,1,0:T(8,128)(2,1)S(1)}, u32[]{:S(2)}, u32[]{:S(2)}) async-start(bf16[8,16,1024]{2,1,0:T(8,128)(2,1)} %bitcast.9), calls=%async_computation.2 | async-start | bytes 524288 | tf_op jit(solution)/shard_map/all_to_all | solution.py:16
  81.7 4.7 %shard_map.134 = (bf16[2560,768]{1,0:T(8,128)(2,1)}, bf16[128,768]{1,0:T(8,128)(2,1)S(1)}) custom-call(bf16[1280,768]{1,0:T(8,128)(2,1)} %near.1, bf16[1280,768]{1,0:T(8,128)(2,1)} %collective-permute-done.7.far, s32[256,1]{1,0:T(8,128)S(1)} %copy.14.labels), custom_call_target="tpu_custom_call" | custom-call | flops 2147483648 | bytes 12582912 | tf_op jit(solution)/shard_map/pallas_call | solution.py:43
  86.4 2.1 %all-to-all-done.2.mixed = bf16[8,16,1024]{2,1,0:T(8,128)(2,1)S(1)} async-done(((bf16[8,16,1024]{2,1,0:T(8,128)(2,1)}), bf16[8,16,1024]{2,1,0:T(8,128)(2,1)S(1)}, u32[]{:S(2)}, u32[]{:S(2)}) %all-to-all-start.2) | async-done | bytes 262176 | tf_op jit(solution)/shard_map/all_to_all | solution.py:16
  89.9 10.6 %all_to_all.40.arrived = bf16[8,16,1536]{2,1,0:T(8,128)(2,1)S(1)} all-to-all(bf16[8,16,1536]{2,1,0:T(8,128)(2,1)S(1)} %get-tuple-element.50), channel_id=1, replica_groups={{0,2,4,6,8,10,12,14},{1,3,5,7,9,11,13,15},{16,18,20,22,24,26,28,30},{17..., dimensions={0} | all-to-all | bytes 786432 | tf_op jit(solution)/shard_map/all_to_all | solution.py:16
  100.5 4.7 %shard_map.136 = (bf16[128,896]{1,0:T(8,128)(2,1)S(1)}, f32[16,768]{1,0:T(8,128)S(1)}) custom-call(bf16[8,16,1536]{2,1,0:T(8,128)(2,1)S(1)} %all_to_all.40.arrived, bf16[2560,768]{1,0:T(8,128)(2,1)} %get-tuple-element.51.text_unit, s32[256,1]{1,0:T(8,128)S(1)} %copy.14.labels), custom_call_target="tpu_custom_call" | custom-call | tf_op jit(solution)/shard_map/pallas_call | solution.py:43
  105.3 8.4 %all_to_all.41.back = bf16[8,16,896]{2,1,0:T(8,128)(2,1)S(1)} all-to-all(bf16[8,16,896]{2,1,0:T(8,128)(2,1)S(1)} %bitcast.20), channel_id=1, replica_groups={{0,2,4,6,8,10,12,14},{1,3,5,7,9,11,13,15},{16,18,20,22,24,26,28,30},{17..., dimensions={0} | all-to-all | bytes 458752 | tf_op jit(solution)/shard_map/all_to_all | solution.py:16
  113.7 1.0 shard_map.137
  114.6 8.7 %all_to_all.42 = bf16[8,16,1024]{2,1,0:T(8,128)(2,1)S(1)} all-to-all(bf16[8,16,1024]{2,1,0:T(8,128)(2,1)S(1)} %get-tuple-element.58), channel_id=1, replica_groups={{0,2,4,6,8,10,12,14},{1,3,5,7,9,11,13,15},{16,18,20,22,24,26,28,30},{17..., dimensions={0} | all-to-all | bytes 524288 | tf_op jit(solution)/shard_map/all_to_all | solution.py:16
  123.3 2.9 %shard_map.138 = bf16[128,1024]{1,0:T(8,128)(2,1)} custom-call(bf16[16,2,32,256]{3,2,1,0:T(8,128)(2,1)} %copy-done.7, bf16[16,2,32,256]{3,2,1,0:T(8,128)(2,1)} %collective-permute-done.4.other, bf16[16,2,32,256]{3,2,1,0:T(8,128)(2,1)S(1)} %collective-permute-done.5.far_own, bf16[16,2,32,256]{3,2,1,0:T(8,128)(2,1)S(1)} %collective-permute-done.6.far_other, ...), custom_call_target="tpu_custom_call" | custom-call | tf_op jit(solution)/shard_map/pallas_call | solution.py:43
  126.2 3.4 %all-to-all-start.6 = ((bf16[8,16,1024]{2,1,0:T(8,128)(2,1)}), bf16[8,16,1024]{2,1,0:T(8,128)(2,1)S(1)}, u32[]{:S(2)}, u32[]{:S(2)}) async-start(bf16[8,16,1024]{2,1,0:T(8,128)(2,1)} %bitcast.13), calls=%async_computation.6 | async-start | bytes 524288 | tf_op jit(solution)/shard_map/all_to_all | solution.py:16
  130.3 5.4 %all-to-all-done.6.parts = bf16[8,16,1024]{2,1,0:T(8,128)(2,1)S(1)} async-done(((bf16[8,16,1024]{2,1,0:T(8,128)(2,1)}), bf16[8,16,1024]{2,1,0:T(8,128)(2,1)S(1)}, u32[]{:S(2)}, u32[]{:S(2)}) %all-to-all-start.6) | async-done | bytes 262176 | tf_op jit(solution)/shard_map/all_to_all | solution.py:16
  136.1 13.8 %all_to_all.43.parts = f32[16,8,128]{2,1,0:T(8,128)S(1)} all-to-all(f32[16,8,128]{2,1,0:T(8,128)S(1)} %shard_map.139), channel_id=1, replica_groups=mesh['dp'=32,'txt'=16] {'txt'}, dimensions={0} | all-to-all | bytes 131072 | tf_op jit(solution)/shard_map/all_to_all | solution.py:16
  (31 shorter events, 4.2 us)
Async XLA Ops:
  0.0 49.3 %copy-start.3 = (f32[1024]{0:T(1024)S(1)}, f32[1024]{0:T(1024)}, u32[]{:S(2)}) copy-start(f32[1024]{0:T(1024)} %param.14) | copy-start | bytes 12292
  0.0 49.3 %copy-start.4 = (f32[1024]{0:T(1024)S(1)}, f32[1024]{0:T(1024)}, u32[]{:S(2)}) copy-start(f32[1024]{0:T(1024)} %param.15) | copy-start | bytes 12292
  1.6 48.0 %all-to-all-start = ((bf16[16,2,32,256]{3,2,1,0:T(8,128)(2,1)}), bf16[16,2,32,256]{3,2,1,0:T(8,128)(2,1)S(1)}, u32[]{:S(2)}, u32[]{:S(2)}) async-start(bf16[16,2,32,256]{3,2,1,0:T(8,128)(2,1)} %shard_map.127), calls=%async_computation | async-start | bytes 1048576 | tf_op jit(solution)/shard_map/all_to_all | solution.py:16
  18.4 52.8 %copy-start.6 = (f32[256]{0:T(256)S(1)}, f32[256]{0:T(256)}, u32[]{:S(2)}) copy-start(f32[256]{0:T(256)} %param.17) | copy-start | bytes 3076
  18.4 55.7 %collective-permute-start.7 = (bf16[1280,768]{1,0:T(8,128)(2,1)}, bf16[1280,768]{1,0:T(8,128)(2,1)}, u32[]{:S(2)}, u32[]{:S(2)}) collective-permute-start(bf16[1280,768]{1,0:T(8,128)(2,1)} %near.1), channel_id=1, source_target_pairs={{0,1},{1,0},{2,3},{3,2},{4,5},{5,4},{6,7},{7,6},{8,9},{9,8},{10,11... | collective-permute-start | bytes 5898248 | tf_op jit(solution)/shard_map/ppermute | solution.py:21
  21.3 7.4 %collective-permute-start = (bf16[64,1152]{1,0:T(8,128)(2,1)S(1)}, bf16[64,1152]{1,0:T(8,128)(2,1)S(1)}, u32[]{:S(2)}, u32[]{:S(2)}) collective-permute-start(bf16[64,1152]{1,0:T(8,128)(2,1)S(1)} %shard_map.128.near), channel_id=1, source_target_pairs={{0,2},{1,3},{2,0},{3,1},{4,6},{5,7},{6,4},{7,5},{8,10},{9,11},{10,... | collective-permute-start | bytes 442376 | tf_op jit(solution)/shard_map/ppermute | solution.py:21
  29.6 5.6 %collective-permute-start.1 = (bf16[2,64,384]{2,1,0:T(8,128)(2,1)S(1)}, bf16[2,64,384]{2,1,0:T(8,128)(2,1)S(1)}, u32[]{:S(2)}, u32[]{:S(2)}) collective-permute-start(bf16[2,64,384]{2,1,0:T(8,128)(2,1)S(1)} %get-tuple-element.35.refs_0_), channel_id=1, source_target_pairs={{0,4},{1,5},{2,6},{3,7},{4,0},{5,1},{6,2},{7,3},{8,12},{9,13},{10,... | collective-permute-start | bytes 294920 | tf_op jit(solution)/shard_map/ppermute | solution.py:21
  35.3 8.2 %collective-permute-start.2 = (bf16[2,2,64,384]{3,2,1,0:T(8,128)(2,1)S(1)}, bf16[2,2,64,384]{3,2,1,0:T(8,128)(2,1)S(1)}, u32[]{:S(2)}, u32[]{:S(2)}) collective-permute-start(bf16[2,2,64,384]{3,2,1,0:T(8,128)(2,1)S(1)} %shard_map.130.refs_0_), channel_id=1, source_target_pairs={{0,8},{1,9},{2,10},{3,11},{4,12},{5,13},{6,14},{7,15},{8,0},{9,1},... | collective-permute-start | bytes 589832 | tf_op jit(solution)/shard_map/ppermute | solution.py:21
  43.5 5.7 %collective-permute-start.3 = (bf16[4,2,64,384]{3,2,1,0:T(8,128)(2,1)S(1)}, bf16[4,2,64,384]{3,2,1,0:T(8,128)(2,1)S(1)}, u32[]{:S(2)}, u32[]{:S(2)}) collective-permute-start(bf16[4,2,64,384]{3,2,1,0:T(8,128)(2,1)S(1)} %bitcast.17), channel_id=1, source_target_pairs={{0,1},{1,0},{2,3},{3,2},{4,5},{5,4},{6,7},{7,6},{8,9},{9,8},{10,11... | collective-permute-start | bytes 1179656 | tf_op jit(solution)/shard_map/ppermute | solution.py:21
  49.7 24.4 %copy-start = (f32[8,1024]{1,0:T(8,128)}, f32[8,1024]{1,0:T(8,128)S(1)}, u32[]{:S(2)}) copy-start(f32[8,1024]{1,0:T(8,128)S(1)} %get-tuple-element.45.lines) | copy-start | bytes 98308
  49.7 21.5 %copy-start.7 = (bf16[16,2,32,256]{3,2,1,0:T(8,128)(2,1)}, bf16[16,2,32,256]{3,2,1,0:T(8,128)(2,1)S(1)}, u32[]{:S(2)}) copy-start(bf16[16,2,32,256]{3,2,1,0:T(8,128)(2,1)S(1)} %all-to-all-done.own) | copy-start | bytes 1572868
  49.7 31.9 %copy-start.8 = (s32[256]{0:T(256)S(1)}, s32[256]{0:T(256)}, u32[]{:S(2)}) copy-start(s32[256]{0:T(256)} %param.24) | copy-start | bytes 3076
  49.7 16.6 %collective-permute-start.4 = (bf16[16,2,32,256]{3,2,1,0:T(8,128)(2,1)S(1)}, bf16[16,2,32,256]{3,2,1,0:T(8,128)(2,1)}, u32[]{:S(2)}, u32[]{:S(2)}) collective-permute-start(bf16[16,2,32,256]{3,2,1,0:T(8,128)(2,1)S(1)} %all-to-all-done.own), channel_id=1, source_target_pairs={{0,16},{16,0},{32,48},{48,32},{64,80},{80,64},{96,112},{112,96},{1... | collective-permute-start | bytes 1572872 | tf_op jit(solution)/shard_map/ppermute | solution.py:21
  54.4 19.8 %all-to-all-start.1 = ((bf16[4,2,64,768]{3,2,1,0:T(8,128)(2,1)}), bf16[4,2,64,768]{3,2,1,0:T(8,128)(2,1)S(1)}, u32[]{:S(2)}, u32[]{:S(2)}) async-start(bf16[4,2,64,768]{3,2,1,0:T(8,128)(2,1)} %get-tuple-element.42), calls=%async_computation.1 | async-start | bytes 1572864 | tf_op jit(solution)/shard_map/all_to_all | solution.py:16
  58.6 10.9 %collective-permute-start.5 = (bf16[16,2,32,256]{3,2,1,0:T(8,128)(2,1)S(1)}, bf16[16,2,32,256]{3,2,1,0:T(8,128)(2,1)S(1)}, u32[]{:S(2)}, u32[]{:S(2)}) collective-permute-start(bf16[16,2,32,256]{3,2,1,0:T(8,128)(2,1)S(1)} %all-to-all-done.own), channel_id=1, source_target_pairs={{0,1},{1,0},{2,3},{3,2},{4,5},{5,4},{6,7},{7,6},{8,9},{9,8},{10,11... | collective-permute-start | bytes 1572872 | tf_op jit(solution)/shard_map/ppermute | solution.py:21
  66.3 4.8 %collective-permute-start.6 = (bf16[16,2,32,256]{3,2,1,0:T(8,128)(2,1)}, bf16[16,2,32,256]{3,2,1,0:T(8,128)(2,1)S(1)}, u32[]{:S(2)}, u32[]{:S(2)}) collective-permute-start(bf16[16,2,32,256]{3,2,1,0:T(8,128)(2,1)} %collective-permute-done.4.other), channel_id=1, source_target_pairs={{0,1},{1,0},{2,3},{3,2},{4,5},{5,4},{6,7},{7,6},{8,9},{9,8},{10,11... | collective-permute-start | bytes 1572872 | tf_op jit(solution)/shard_map/ppermute | solution.py:21
  74.1 14.4 %collective-permute-start.8 = (bf16[4,2,64,768]{3,2,1,0:T(8,128)(2,1)S(1)}, bf16[4,2,64,768]{3,2,1,0:T(8,128)(2,1)S(1)}, u32[]{:S(2)}, u32[]{:S(2)}) collective-permute-start(bf16[4,2,64,768]{3,2,1,0:T(8,128)(2,1)S(1)} %all-to-all-done.1.near), channel_id=1, source_target_pairs={{0,1},{1,0},{2,3},{3,2},{4,5},{5,4},{6,7},{7,6},{8,9},{9,8},{10,11... | collective-permute-start | bytes 2359304 | tf_op jit(solution)/shard_map/ppermute | solution.py:21
  76.4 12.1 %all-to-all-start.2 = ((bf16[8,16,1024]{2,1,0:T(8,128)(2,1)}), bf16[8,16,1024]{2,1,0:T(8,128)(2,1)S(1)}, u32[]{:S(2)}, u32[]{:S(2)}) async-start(bf16[8,16,1024]{2,1,0:T(8,128)(2,1)} %bitcast.9), calls=%async_computation.2 | async-start | bytes 524288 | tf_op jit(solution)/shard_map/all_to_all | solution.py:16
  81.7 6.8 %copy-start.5 = (f32[1024]{0:T(1024)S(1)}, f32[1024]{0:T(1024)}, u32[]{:S(2)}) copy-start(f32[1024]{0:T(1024)} %param.19) | copy-start | bytes 12292
  88.5 0.8 copy-start.1
  123.3 26.6 %copy-start.2 = (bf16[256,64]{0,1:T(8,128)(2,1)S(1)}, bf16[256,64]{0,1:T(8,128)(2,1)}, u32[]{:S(2)}) copy-start(bf16[256,64]{0,1:T(8,128)(2,1)} %param.13) | copy-start | bytes 98308
  126.2 9.5 %all-to-all-start.6 = ((bf16[8,16,1024]{2,1,0:T(8,128)(2,1)}), bf16[8,16,1024]{2,1,0:T(8,128)(2,1)S(1)}, u32[]{:S(2)}, u32[]{:S(2)}) async-start(bf16[8,16,1024]{2,1,0:T(8,128)(2,1)} %bitcast.13), calls=%async_computation.6 | async-start | bytes 524288 | tf_op jit(solution)/shard_map/all_to_all | solution.py:16

commit v9 on v8

--- a/solution.py
+++ b/solution.py
@@ -115,12 +115,15 @@
         out[z] = out[0]
 
 
-def message_kernel(projection, resid, gain, bias, up_bias, out, gains, biases, ups, sem):
+def message_kernel(projection, resid, gain, bias, up_bias, step, *refs):
+    out, gains, biases, ups, steps, sem = refs
     emb, images = projection.shape[1], resid.shape[1]
-    places = (out.at[:, :emb], out.at[:, emb : emb + images], gains, biases, ups)
+    places = (out.at[:, :emb], out.at[:, emb : emb + images], gains, biases, ups, steps)
     loads = [
         pltpu.make_async_copy(part, place, sem.at[k])
-        for k, (part, place) in enumerate(zip((projection, resid, gain, bias, up_bias), places))
+        for k, (part, place) in enumerate(
+            zip((projection, resid, gain, bias, up_bias, step), places)
+        )
     ]
     for load in loads:
         load.start()
@@ -141,19 +144,24 @@
     ]
     lines += [jnp.zeros((1, 128), F32)] * 2
     lines += [part[:, 128 * k : 128 * k + 128] for part in parts(ups[...]) for k in range(2)]
-    lines += [jnp.zeros((1, 128), F32)] * 2
+    lines.append(jnp.concatenate(parts(steps[:, 0:1]) + [jnp.zeros((1, 125), F32)], axis=1))
+    lines.append(jnp.zeros((1, 128), F32))
     lines = jnp.concatenate(lines, axis=0)
     out[:, emb + images :] = jnp.zeros((out.shape[0], 128), BF)
     out[: lines.shape[0], emb + images :] = lines.astype(BF)
 
 
-def split_kernel(near, other, proj, rest):
+def proj_copies_kernel(near, other, proj):
     emb = proj.shape[3]
     for k, part in enumerate((near, other)):
         block = part[:, :emb]
         for y in range(proj.shape[0]):
             proj[y, k] = block
-        rest[k] = part[:, emb:]
+
+
+def rest_kernel(near, other, rest):
+    for k, part in enumerate((near, other)):
+        rest[k] = part[:, part.shape[1] - rest.shape[2] :]
 
 
 def stack_kernel(*refs):
@@ -162,10 +170,11 @@
         out[k] = part[...]
 
 
-def rows_kernel(near, far, gain, bias, own, lines, normed, far_bias, state, vectors):
+def rows_kernel(near, far, gain, bias, kept, normed, far_bias, state, vectors):
     n_txt = vectors.shape[0]
     share = near.shape[2]
-    rows, half = own.shape[0], state.shape[1]
+    half = state.shape[1]
+    rows = 2 * half // n_txt
     at = lax.axis_index("txt")
     first = lax.rem(at, 2) == 0
     for core, side in enumerate((near, far)):
@@ -186,7 +195,7 @@
     column = lax.broadcasted_iota(jnp.int32, (rows, half), 1)
     line = lax.broadcasted_iota(jnp.int32, (rows, half), 0)
     pick = jnp.where(column == line + start, 1.0, 0.0).astype(BF)
-    own[...] = lax.dot_general(pick, state[...], NT, preferred_element_type=F32)
+    kept[:rows, :] = lax.dot_general(pick, state[...], NT, preferred_element_type=F32)
     for k in range(2):
         line = [
             vectors[t, 3 * k : 3 * k + 1, :share]
@@ -194,7 +203,10 @@
             + vectors[t, 3 * k + 2 : 3 * k + 3, :share]
             for t in range(n_txt)
         ]
-        lines[k : k + 1, :] = jnp.concatenate(line, axis=1)
+        kept[rows + k : rows + k + 1, :] = jnp.concatenate(line, axis=1)
+    step = near[0, 0, 8:16, 2 * half :].astype(F32)[6:7, :]
+    step = jnp.sum(step, axis=1, keepdims=True)
+    kept[rows + 2 :, :] = jnp.broadcast_to(step, (kept.shape[0] - rows - 2, kept.shape[1]))
     xhat, _ = row_norm(state[...].astype(F32).T)
     normed[...] = (xhat * gain[...] + bias[...]).astype(BF)
 
@@ -228,60 +240,76 @@
     return jnp.concatenate(blocks, axis=1)
 
 
-def ordered_weights(own, other, far_own, far_other, weights, sem):
+def start_loads(own, other, weights, sem):
     side = lax.rem(lax.axis_index("dp"), 2)
     loads = {}
     for matrix in weights:
-        for k, pair in enumerate(((own, other), (far_own, far_other))):
-            for x, part in enumerate(pair):
-                place = weights[matrix].at[k, :, side if x == 0 else 1 - side]
-                number = 4 * matrix + 2 * k + x
-                load = pltpu.make_async_copy(part.at[:, matrix], place, sem.at[number])
-                load.start()
-                loads[matrix, k, x] = load
+        for x, part in enumerate((own, other)):
+            place = weights[matrix].at[:, side if x == 0 else 1 - side]
+            load = pltpu.make_async_copy(part.at[:, matrix], place, sem.at[2 * matrix + x])
+            load.start()
+            loads[matrix, x] = load
     return loads
 
 
-def mlp_kernel(own, other, far_own, far_other, normed, bias, far_bias, *refs):
-    pre_act, mixed, up, down, sem = refs
-    width, hid = normed.shape[1], bias.shape[1]
-    loads = ordered_weights(own, other, far_own, far_other, {0: up, 1: down}, sem)
-    hidden = []
-    for k, add in enumerate((bias, far_bias)):
-        for x in range(2):
-            loads[0, k, x].wait()
-        w_up = up[k].reshape(width, hid)
-        pre = jnp.dot(normed[...], w_up, preferred_element_type=F32) + add[...]
-        pre_act[k] = pre
-        hidden.append((pre * jax.nn.sigmoid(1.702 * pre)).astype(BF))
-    total = jnp.zeros(normed.shape, F32)
-    for k in range(2):
-        for x in range(2):
-            loads[1, k, x].wait()
-        w_down = down[k].reshape(width, hid)
-        total += lax.dot_general(hidden[k], w_down, NT, preferred_element_type=F32)
+def placed_weights(own, other, matrix, held):
+    side = lax.rem(lax.axis_index("dp"), 2)
+    for z in range(own.shape[0]):
+        held[z, side] = own[z, matrix]
+        held[z, 1 - side] = other[z, matrix]
+    return held[...].reshape(-1, own.shape[3])
+
+
+def hidden_units(normed, w_up, bias, pre_act):
+    pre = jnp.dot(normed[...], w_up, preferred_element_type=F32) + bias[...]
+    pre_act[...] = pre
+    return (pre * jax.nn.sigmoid(1.702 * pre)).astype(BF)
+
+
+def act_gradient(arrived, w_down, pre_act):
+    hid_grad = jnp.dot(arrived[...], w_down, preferred_element_type=F32)
+    pre = pre_act[...]
+    gate = jax.nn.sigmoid(1.702 * pre)
+    return (hid_grad * (gate + 1.702 * pre * gate * (1.0 - gate))).astype(BF)
+
+
+def mlp_near_kernel(own, other, normed, bias, pre_act, part, up, down, held_pre_act, sem):
+    loads = start_loads(own, other, {0: up, 1: down}, sem)
+    for x in range(2):
+        loads[0, x].wait()
+    hidden = hidden_units(normed, up[...].reshape(-1, bias.shape[1]), bias, held_pre_act)
+    store = pltpu.make_async_copy(held_pre_act, pre_act, sem.at[4])
+    store.start()
+    for x in range(2):
+        loads[1, x].wait()
+    w_down = down[...].reshape(-1, bias.shape[1])
+    part[...] = lax.dot_general(hidden, w_down, NT, preferred_element_type=F32)
+    store.wait()
+
+
+def mlp_far_kernel(own, other, normed, bias, part, pre_act, mixed, up, down):
+    hidden = hidden_units(normed, placed_weights(own, other, 0, up), bias, pre_act)
+    w_down = placed_weights(own, other, 1, down)
+    total = part[...] + lax.dot_general(hidden, w_down, NT, preferred_element_type=F32)
     mixed[...] = total.astype(BF)
 
 
-def mlp_back_kernel(own, other, far_own, far_other, arrived, pre_act, *refs):
-    normed_grad, up, down, sem = refs
-    width, hid = arrived.shape[1], pre_act.shape[2]
-    loads = ordered_weights(own, other, far_own, far_other, {1: down, 0: up}, sem)
-    act_grad = []
-    for k in range(2):
-        for x in range(2):
-            loads[1, k, x].wait()
-        w_down = down[k].reshape(width, hid)
-        hid_grad = jnp.dot(arrived[...], w_down, preferred_element_type=F32)
-        pre = pre_act[k]
-        gate = jax.nn.sigmoid(1.702 * pre)
-        act_grad.append((hid_grad * (gate + 1.702 * pre * gate * (1.0 - gate))).astype(BF))
-    total = jnp.zeros(normed_grad.shape, F32)
-    for k in range(2):
-        for x in range(2):
-            loads[0, k, x].wait()
-        w_up = up[k].reshape(width, hid)
-        total += lax.dot_general(act_grad[k], w_up, NT, preferred_element_type=F32)
+def mlp_back_kernel(own, other, far_own, far_other, arrived, pre_act, far_pre_act, *refs):
+    normed_grad, up, down, far_up, far_down, sem = refs
+    hid = pre_act.shape[1]
+    loads = start_loads(own, other, {1: down, 0: up}, sem)
+    act_grad = act_gradient(
+        arrived, placed_weights(far_own, far_other, 1, far_down), far_pre_act
+    )
+    w_up = placed_weights(far_own, far_other, 0, far_up)
+    total = lax.dot_general(act_grad, w_up, NT, preferred_element_type=F32)
+    for x in range(2):
+        loads[1, x].wait()
+    act_grad = act_gradient(arrived, down[...].reshape(-1, hid), pre_act)
+    for x in range(2):
+        loads[0, x].wait()
+    w_up = up[...].reshape(-1, hid)
+    total += lax.dot_general(act_grad, w_up, NT, preferred_element_type=F32)
     normed_grad[...] = total.astype(BF)
 
 
@@ -290,9 +318,10 @@
     n = arrived.shape[0]
     n_block = 5
     step = text_unit.shape[0] // n_block
+    cut = step // 4
     loads = []
-    for k in range(n_block):
-        place = pl.ds(k * step, step)
+    for k in range(4 * n_block):
+        place = pl.ds(k * cut, cut)
         loads.append(pltpu.make_async_copy(text_unit.at[place], held.at[place], sem.at[k]))
         loads[k].start()
     texts = jnp.zeros(label_rows.shape, F32)
@@ -303,7 +332,8 @@
     label = local_labels(labels, text_unit.shape[0] // 2)
     top = None
     for k in range(n_block):
-        loads[k].wait()
+        for load in loads[4 * k : 4 * k + 4]:
+            load.wait()
         texts = held[k * step : (k + 1) * step, :]
         block = 100.0 * lax.dot_general(unit_low[...], texts, NT, preferred_element_type=F32)
         logits[:, k * step : (k + 1) * step] = block
@@ -333,18 +363,18 @@
     back[:, emb:] = stats.astype(BF)
 
 
-def embed_kernel(mixed, own, bias, lines, near, far, label_text, *refs):
+def embed_kernel(mixed, kept, bias, near, far, label_text, *refs):
     sent, unit, norm, yhat, rstd = refs
     n = mixed.shape[0]
     emb = unit.shape[1]
-    rows = own.shape[0]
-    total = own[...] + bias[...]
+    rows = mixed.shape[1]
+    total = kept[:rows, :] + bias[...]
     for j in range(n):
         total += mixed[j].astype(F32)
     normed, scale = row_norm(total)
     yhat[...] = normed
     rstd[...] = jnp.broadcast_to(scale, rstd.shape)
-    post_normed = normed * lines[0:1, :] + lines[1:2, :]
+    post_normed = normed * kept[rows : rows + 1, :] + kept[rows + 1 : rows + 2, :]
     embedding = jnp.zeros(unit.shape, F32)
     for side, part in zip((near, far), in_arrival_order(post_normed, near.shape[2])):
         w_proj = side[...].reshape(-1, emb)
@@ -359,9 +389,9 @@
         sent[j, :, emb:] = label_text[j * rows : (j + 1) * rows, :]
 
 
-def embed_back_kernel(back, label_rows, unit, norm, yhat, rstd, lines, near, far, *refs):
+def embed_back_kernel(back, label_rows, unit, norm, yhat, rstd, kept, near, far, *refs):
     sent, grad = refs
-    n = back.shape[0]
+    n, rows = back.shape[:2]
     emb = unit.shape[1]
     stats = [back[j, :, emb:].astype(F32) for j in range(n)]
     top = stats[0][:, 0:1]
@@ -388,23 +418,24 @@
         ),
         near.shape[2],
     )
-    out_grad = norm_back(post_grad * lines[0:1, :], yhat[...], rstd[:, 0:1])
+    out_grad = norm_back(post_grad * kept[rows : rows + 1, :], yhat[...], rstd[:, 0:1])
     grad[...] = out_grad
     low = out_grad.astype(BF)
     for j in range(n):
         sent[j] = low
 
 
-def change_kernel(parts, gain, own, out_grad, step, sent):
+def change_kernel(parts, gain, kept, out_grad, sent):
     n, half, _ = sent.shape
-    share = own.shape[1] // n
+    rows = out_grad.shape[0]
+    share = out_grad.shape[1] // n
     total = parts[0].astype(F32)
     for j in range(1, parts.shape[0]):
         total += parts[j].astype(F32)
-    xhat, scale = row_norm(own[...])
+    xhat, scale = row_norm(kept[:rows, :])
     grad = out_grad[...] + norm_back(total * gain[...], xhat, scale)
     rms = jnp.sqrt(jnp.mean(grad * grad, axis=1, keepdims=True) + 1e-06)
-    change = step[0:1, 0:1] * grad / rms
+    change = kept[rows + 2 : rows + 3, 0:1] * grad / rms
     for j in range(n):
         block = change[:, j * share : (j + 1) * share]
         sent[j, :, :share] = block[:half]
@@ -462,35 +493,31 @@
     (chain,) = call(
         message_kernel,
         (((share, emb + images + 128), BF),),
-        "hhhhhv",
+        "hhhhhhv",
         projection,
         resid.T,
         post_gain[None],
         post_bias[None],
         up_bias[None],
+        jnp.broadcast_to(step_size, (1, 128)),
         cost=SMALL,
-        scratch=(((1, share), F32), ((1, share), F32), ((1, hid), F32)),
-        sems=5,
+        scratch=(((1, share), F32), ((1, share), F32), ((1, hid), F32), ((1, 128), F32)),
+        sems=6,
     )
     chain, labels, far_texts = lax.optimization_barrier((chain, labels[:, None], texts))
     far_texts = from_partner(far_texts, "txt", 1)
-    proj, rest = call(
-        split_kernel,
-        (((4, 2, share, emb), BF), ((2, share, images + 128), BF)),
-        "vvvv",
-        chain,
-        from_partner(chain, "txt", 2),
-        cost=SMALL,
-    )
+    both = (chain, from_partner(chain, "txt", 2))
+    (rest,) = call(rest_kernel, (((2, share, images + 128), BF),), "vvv", *both, cost=SMALL)
+    (proj,) = call(proj_copies_kernel, (((4, 2, share, emb), BF),), "vvv", *both, cost=SMALL)
     for bits in (4, 8):
         both = (rest, from_partner(rest, "txt", bits))
         (rest,) = call(stack_kernel, (((2, *rest.shape), BF),), "vvv", *both, cost=SMALL)
     rest = rest.reshape(4, 2, share, images + 128)
     far_rest = from_partner(rest, "txt", 1)
-    own, lines, normed, far_bias = call(
+    kept, normed, far_bias = call(
         rows_kernel,
-        (((rows, WIDTH), F32), ((8, WIDTH), F32), ((half, WIDTH), BF), ((1, hid), F32)),
-        "vvvvvvvv",
+        (((rows + 8, WIDTH), F32), ((half, WIDTH), BF), ((1, hid), F32)),
+        "vvvvvvv",
         rest,
         far_rest,
         prenorm_gain[None],
@@ -504,18 +531,28 @@
     far_mine = from_partner(mine, "txt", 1)
     proj = swapped(proj, "txt", along_y)
     far_other = from_partner(other, "txt", 1)
-    weights = (mine, other, far_mine, far_other)
-    held = ((2, n_z, 2, WIDTH // n_dp, hid), BF)
-    pre_act, mixed = call(
-        mlp_kernel,
-        (((2, half, hid), F32), ((half, WIDTH), BF)),
-        "hhaavvvvv",
-        *weights,
+    held = ((n_z, 2, WIDTH // n_dp, hid), BF)
+    pre_act, part = call(
+        mlp_near_kernel,
+        (((half, hid), F32), ((half, WIDTH), F32)),
+        "hhvvhv",
+        mine,
+        other,
         normed,
         up_bias[None],
+        scratch=(held, held, ((half, hid), F32)),
+        sems=5,
+    )
+    far_pre_act, mixed = call(
+        mlp_far_kernel,
+        (((half, hid), F32), ((half, WIDTH), BF)),
+        "vvvvvvv",
+        far_mine,
+        far_other,
+        normed,
         far_bias,
+        part,
         scratch=(held, held),
-        sems=8,
     )
     mixed, far_texts, proj = lax.optimization_barrier((mixed, far_texts, proj))
     far_proj = from_partner(proj, "txt", 1)
@@ -541,11 +578,10 @@
             ((rows, WIDTH), F32),
             ((rows, 128), F32),
         ),
-        "vvvvvvvvvvvv",
+        "vvvvvvvvvvv",
         mixed,
-        own,
+        kept,
         down_bias[None],
-        lines,
         proj,
         far_proj,
         label_text,
@@ -560,7 +596,7 @@
         text_unit,
         labels,
         scratch=(((half, 2 * n_text), F32), ((half, emb), BF), ((2 * n_text, emb), BF)),
-        sems=5,
+        sems=20,
     )
     back = swapped(back.reshape(n_pair, rows, emb + 128), "txt", cores)
 
@@ -574,7 +610,7 @@
         emb_norm,
         yhat,
         rstd_out,
-        lines,
+        kept,
         proj,
         far_proj,
     )
@@ -583,23 +619,26 @@
     (normed_grad,) = call(
         mlp_back_kernel,
         (((half, WIDTH), BF),),
-        "hhaavvv",
-        *weights,
+        "hhvvvvvv",
+        mine,
+        other,
+        far_mine,
+        far_other,
         out_low,
         pre_act,
-        scratch=(held, held),
-        sems=8,
+        far_pre_act,
+        scratch=(held, held, held, held),
+        sems=4,
     )
     normed_grad = swapped(normed_grad.reshape(n_pair, rows, WIDTH), "txt", cores)
     (change,) = call(
         change_kernel,
         (((n_txt, rows // 2, 2 * share), F32),),
-        "vvvvvv",
+        "vvvvv",
         normed_grad,
         prenorm_gain[None],
-        own,
+        kept,
         out_grad,
-        step_size[None],
     )
     change = swapped(change, "txt")
     (out,) = call(result_kernel, (((share, images), F32),), "vvv", change, resid.T)

time: 152 us -> 149 us (0.980)
  blocking collectives: 41.5 us -> 50.7 us
  waiting for transfers between devices: 25.6 us -> 17.6 us
  starting transfers between devices: 59.8 us -> 56 us
    all_to_all x4 -> x5, blocking collectives: 41.5 us -> 50.7 us  [swapped(): return lax.all_to_all(x, axis, 0, 0, tiled=True, axis_index_groups=groups)]
    all_to_all x4 -> x3, waiting for transfers between devices: 7.49 us -> 1.71 us  [swapped(): return lax.all_to_all(x, axis, 0, 0, tiled=True, axis_index_groups=groups)]
    all_to_all x4 -> x3, starting transfers between devices: 28.5 us -> 25.1 us  [swapped(): return lax.all_to_all(x, axis, 0, 0, tiled=True, axis_index_groups=groups)]
    ppermute x9, waiting for transfers between devices: 18.1 us -> 15.9 us  [from_partner(): return lax.ppermute(x, axis, pairs)]
    pallas_call x14 -> x16, Pallas kernels: 22 us -> 21.8 us  [call(): pl.pallas_call(body, out_shape=[pltpu.HBM(*out) if c == 'h' else jax.Shap...]
  transfers between devices with their start and end apart: 13 -> 12, of which waited for: 8 -> 6; matrix products, arithmetic and copies ran while one was open for 0% -> 0% of each run, Pallas kernels for 7% -> 7%
where the time goes in v9:
time: 149 us; the launch traced here: 148 us
  starting transfers between devices  56 us (38%)
  blocking collectives  50.7 us (34%)
  Pallas kernels  21.8 us (15%)
  waiting for transfers between devices  17.6 us (12%)
    all_to_all x5, blocking collectives, swapped(): return lax.all_to_all(x, axis, 0, 0, tiled=True, axis_index_groups=groups)  50.7 us
    ppermute x9, starting transfers between devices, from_partner(): return lax.ppermute(x, axis, pairs)  30.8 us
    all_to_all x3, starting transfers between devices, swapped(): return lax.all_to_all(x, axis, 0, 0, tiled=True, axis_index_groups=groups)  25.1 us
    pallas_call x16, Pallas kernels, call(): pl.pallas_call(body, out_shape=[pltpu.HBM(*out) if c == 'h' else jax.Shap...  21.8 us
    ppermute x9, waiting for transfers between devices, from_partner(): return lax.ppermute(x, axis, pairs)  15.9 us
  transfers between devices with their start and end apart: 12, of which 6 were waited for; matrix products, arithmetic and copies ran while one was open for 0% of the time, Pallas kernels for 7%

profile of v9, /device:TPU:1, one launch (start us, length us, event | category | flops | bytes accessed | tf_op | source)
XLA Modules:
  0.0 147.7 jit_solution(3331582364465409175)
XLA Ops:
  0.0 1.6 %shard_map.130 = bf16[16,2,32,256]{3,2,1,0:T(8,128)(2,1)} custom-call(bf16[32,256]{1,0:T(8,128)(2,1)} %up.1, bf16[32,256]{1,0:T(8,128)(2,1)} %bitcast.30), custom_call_target="tpu_custom_call" | custom-call | tf_op jit(solution)/shard_map/pallas_call | solution.py:43
  1.6 15.8 %all-to-all-start = ((bf16[16,2,32,256]{3,2,1,0:T(8,128)(2,1)}), bf16[16,2,32,256]{3,2,1,0:T(8,128)(2,1)}, u32[]{:S(2)}, u32[]{:S(2)}) async-start(bf16[16,2,32,256]{3,2,1,0:T(8,128)(2,1)} %shard_map.130), calls=%async_computation | async-start | bytes 1048576 | tf_op jit(solution)/shard_map/all_to_all | solution.py:16
  18.7 1.0 shard_map.131.near
  19.7 2.9 %collective-permute-start.7 = (bf16[1280,768]{1,0:T(8,128)(2,1)}, bf16[1280,768]{1,0:T(8,128)(2,1)}, u32[]{:S(2)}, u32[]{:S(2)}) collective-permute-start(bf16[1280,768]{1,0:T(8,128)(2,1)} %near.1), channel_id=1, source_target_pairs={{0,1},{1,0},{2,3},{3,2},{4,5},{5,4},{6,7},{7,6},{8,9},{9,8},{10,11... | collective-permute-start | bytes 5898248 | tf_op jit(solution)/shard_map/ppermute | solution.py:21
  22.6 3.1 %collective-permute-start = (bf16[64,1152]{1,0:T(8,128)(2,1)S(1)}, bf16[64,1152]{1,0:T(8,128)(2,1)S(1)}, u32[]{:S(2)}, u32[]{:S(2)}) collective-permute-start(bf16[64,1152]{1,0:T(8,128)(2,1)S(1)} %shard_map.131.near), channel_id=1, source_target_pairs={{0,2},{1,3},{2,0},{3,1},{4,6},{5,7},{6,4},{7,5},{8,10},{9,11},{10,... | collective-permute-start | bytes 442376 | tf_op jit(solution)/shard_map/ppermute | solution.py:21
  25.7 4.3 %collective-permute-done.other = bf16[64,1152]{1,0:T(8,128)(2,1)S(1)} collective-permute-done((bf16[64,1152]{1,0:T(8,128)(2,1)S(1)}, bf16[64,1152]{1,0:T(8,128)(2,1)S(1)}, u32[]{:S(2)}, u32[]{:S(2)}) %collective-permute-start) | collective-permute-done | bytes 147488 | tf_op jit(solution)/shard_map/ppermute | solution.py:21
  30.1 3.2 %collective-permute-start.1 = (bf16[2,64,384]{2,1,0:T(8,128)(2,1)S(1)}, bf16[2,64,384]{2,1,0:T(8,128)(2,1)S(1)}, u32[]{:S(2)}, u32[]{:S(2)}) collective-permute-start(bf16[2,64,384]{2,1,0:T(8,128)(2,1)S(1)} %shard_map.133.refs_0_), channel_id=1, source_target_pairs={{0,4},{1,5},{2,6},{3,7},{4,0},{5,1},{6,2},{7,3},{8,12},{9,13},{10,... | collective-permute-start | bytes 294920 | tf_op jit(solution)/shard_map/ppermute | solution.py:21
  33.3 2.5 %collective-permute-done.1.refs_1_ = bf16[2,64,384]{2,1,0:T(8,128)(2,1)S(1)} collective-permute-done((bf16[2,64,384]{2,1,0:T(8,128)(2,1)S(1)}, bf16[2,64,384]{2,1,0:T(8,128)(2,1)S(1)}, u32[]{:S(2)}, u32[]{:S(2)}) %collective-permute-start.1) | collective-permute-done | bytes 98336 | tf_op jit(solution)/shard_map/ppermute | solution.py:21
  35.9 4.8 %collective-permute-start.2 = (bf16[2,2,64,384]{3,2,1,0:T(8,128)(2,1)S(1)}, bf16[2,2,64,384]{3,2,1,0:T(8,128)(2,1)S(1)}, u32[]{:S(2)}, u32[]{:S(2)}) collective-permute-start(bf16[2,2,64,384]{3,2,1,0:T(8,128)(2,1)S(1)} %shard_map.134.refs_0_), channel_id=1, source_target_pairs={{0,8},{1,9},{2,10},{3,11},{4,12},{5,13},{6,14},{7,15},{8,0},{9,1},... | collective-permute-start | bytes 589832 | tf_op jit(solution)/shard_map/ppermute | solution.py:21
  40.7 3.6 %collective-permute-done.2.refs_1_ = bf16[2,2,64,384]{3,2,1,0:T(8,128)(2,1)S(1)} collective-permute-done((bf16[2,2,64,384]{3,2,1,0:T(8,128)(2,1)S(1)}, bf16[2,2,64,384]{3,2,1,0:T(8,128)(2,1)S(1)}, u32[]{:S(2)}, u32[]{:S(2)}) %collective-permute-start.2) | collective-permute-done | bytes 196640 | tf_op jit(solution)/shard_map/ppermute | solution.py:21
  44.4 4.2 %collective-permute-start.3 = (bf16[4,2,64,384]{3,2,1,0:T(8,128)(2,1)S(1)}, bf16[4,2,64,384]{3,2,1,0:T(8,128)(2,1)S(1)}, u32[]{:S(2)}, u32[]{:S(2)}) collective-permute-start(bf16[4,2,64,384]{3,2,1,0:T(8,128)(2,1)S(1)} %bitcast.17), channel_id=1, source_target_pairs={{0,1},{1,0},{2,3},{3,2},{4,5},{5,4},{6,7},{7,6},{8,9},{9,8},{10,11... | collective-permute-start | bytes 1179656 | tf_op jit(solution)/shard_map/ppermute | solution.py:21
  48.5 0.9 shard_map.132
  50.3 4.7 %collective-permute-start.4 = (bf16[16,2,32,256]{3,2,1,0:T(8,128)(2,1)}, bf16[16,2,32,256]{3,2,1,0:T(8,128)(2,1)}, u32[]{:S(2)}, u32[]{:S(2)}) collective-permute-start(bf16[16,2,32,256]{3,2,1,0:T(8,128)(2,1)} %all-to-all-done.own), channel_id=1, source_target_pairs={{0,16},{16,0},{32,48},{48,32},{64,80},{80,64},{96,112},{112,96},{1... | collective-permute-start | bytes 1572872 | tf_op jit(solution)/shard_map/ppermute | solution.py:21
  54.9 4.2 %all-to-all-start.1 = ((bf16[4,2,64,768]{3,2,1,0:T(8,128)(2,1)}), bf16[4,2,64,768]{3,2,1,0:T(8,128)(2,1)S(1)}, u32[]{:S(2)}, u32[]{:S(2)}) async-start(bf16[4,2,64,768]{3,2,1,0:T(8,128)(2,1)} %shard_map.132), calls=%async_computation.1 | async-start | bytes 1572864 | tf_op jit(solution)/shard_map/all_to_all | solution.py:16
  59.1 3.0 %collective-permute-start.5 = (bf16[16,2,32,256]{3,2,1,0:T(8,128)(2,1)}, bf16[16,2,32,256]{3,2,1,0:T(8,128)(2,1)S(1)}, u32[]{:S(2)}, u32[]{:S(2)}) collective-permute-start(bf16[16,2,32,256]{3,2,1,0:T(8,128)(2,1)} %all-to-all-done.own), channel_id=1, source_target_pairs={{0,1},{1,0},{2,3},{3,2},{4,5},{5,4},{6,7},{7,6},{8,9},{9,8},{10,11... | collective-permute-start | bytes 1572872 | tf_op jit(solution)/shard_map/ppermute | solution.py:21
  62.1 5.0 %collective-permute-done.4.other = bf16[16,2,32,256]{3,2,1,0:T(8,128)(2,1)} collective-permute-done((bf16[16,2,32,256]{3,2,1,0:T(8,128)(2,1)}, bf16[16,2,32,256]{3,2,1,0:T(8,128)(2,1)}, u32[]{:S(2)}, u32[]{:S(2)}) %collective-permute-start.4) | collective-permute-done | bytes 524320 | tf_op jit(solution)/shard_map/ppermute | solution.py:21
  67.1 3.1 %collective-permute-start.6 = (bf16[16,2,32,256]{3,2,1,0:T(8,128)(2,1)}, bf16[16,2,32,256]{3,2,1,0:T(8,128)(2,1)S(1)}, u32[]{:S(2)}, u32[]{:S(2)}) collective-permute-start(bf16[16,2,32,256]{3,2,1,0:T(8,128)(2,1)} %collective-permute-done.4.other), channel_id=1, source_target_pairs={{0,1},{1,0},{2,3},{3,2},{4,5},{5,4},{6,7},{7,6},{8,9},{9,8},{10,11... | collective-permute-start | bytes 1572872 | tf_op jit(solution)/shard_map/ppermute | solution.py:21
  70.2 2.0 %shard_map.137 = (f32[128,256]{1,0:T(8,128)}, f32[128,1024]{1,0:T(8,128)S(1)}) custom-call(bf16[16,2,32,256]{3,2,1,0:T(8,128)(2,1)} %all-to-all-done.own, bf16[16,2,32,256]{3,2,1,0:T(8,128)(2,1)} %collective-permute-done.4.other, bf16[128,1024]{1,0:T(8,128)(2,1)S(1)} %get-tuple-element.35.normed, f32[1,256]{1,0:T(1,128)S(1)} %bitcast.29), custom_call_target="tpu_custom_call" | custom-call | tf_op jit(solution)/shard_map/pallas_call | solution.py:43
  72.3 1.3 shard_map.138
  73.6 1.9 %collective-permute-start.8 = (bf16[4,2,64,768]{3,2,1,0:T(8,128)(2,1)S(1)}, bf16[4,2,64,768]{3,2,1,0:T(8,128)(2,1)S(1)}, u32[]{:S(2)}, u32[]{:S(2)}) collective-permute-start(bf16[4,2,64,768]{3,2,1,0:T(8,128)(2,1)S(1)} %all-to-all-done.1.near), channel_id=1, source_target_pairs={{0,1},{1,0},{2,3},{3,2},{4,5},{5,4},{6,7},{7,6},{8,9},{9,8},{10,11... | collective-permute-start | bytes 2359304 | tf_op jit(solution)/shard_map/ppermute | solution.py:21
  75.6 5.1 %all-to-all-start.2 = ((bf16[8,16,1024]{2,1,0:T(8,128)(2,1)}), bf16[8,16,1024]{2,1,0:T(8,128)(2,1)S(1)}, u32[]{:S(2)}, u32[]{:S(2)}) async-start(bf16[8,16,1024]{2,1,0:T(8,128)(2,1)} %bitcast.10), calls=%async_computation.2 | async-start | bytes 524288 | tf_op jit(solution)/shard_map/all_to_all | solution.py:16
  80.9 4.7 %shard_map.139 = (bf16[2560,768]{1,0:T(8,128)(2,1)}, bf16[128,768]{1,0:T(8,128)(2,1)S(1)}) custom-call(bf16[1280,768]{1,0:T(8,128)(2,1)} %near.1, bf16[1280,768]{1,0:T(8,128)(2,1)} %collective-permute-done.7.far, s32[256,1]{1,0:T(8,128)S(1)} %copy.14.labels), custom_call_target="tpu_custom_call" | custom-call | flops 2147483648 | bytes 12582912 | tf_op jit(solution)/shard_map/pallas_call | solution.py:43
  85.6 1.7 %all-to-all-done.2.mixed = bf16[8,16,1024]{2,1,0:T(8,128)(2,1)S(1)} async-done(((bf16[8,16,1024]{2,1,0:T(8,128)(2,1)}), bf16[8,16,1024]{2,1,0:T(8,128)(2,1)S(1)}, u32[]{:S(2)}, u32[]{:S(2)}) %all-to-all-start.2) | async-done | bytes 262176 | tf_op jit(solution)/shard_map/all_to_all | solution.py:16
  88.0 10.7 %all_to_all.40.arrived = bf16[8,16,1536]{2,1,0:T(8,128)(2,1)S(1)} all-to-all(bf16[8,16,1536]{2,1,0:T(8,128)(2,1)S(1)} %get-tuple-element.47), channel_id=1, replica_groups={{0,2,4,6,8,10,12,14},{1,3,5,7,9,11,13,15},{16,18,20,22,24,26,28,30},{17..., dimensions={0} | all-to-all | bytes 786432 | tf_op jit(solution)/shard_map/all_to_all | solution.py:16
  98.6 5.0 %shard_map.141 = (bf16[128,896]{1,0:T(8,128)(2,1)S(1)}, f32[16,768]{1,0:T(8,128)S(1)}) custom-call(bf16[8,16,1536]{2,1,0:T(8,128)(2,1)S(1)} %all_to_all.40.arrived, bf16[2560,768]{1,0:T(8,128)(2,1)} %get-tuple-element.48.text_unit, s32[256,1]{1,0:T(8,128)S(1)} %copy.14.labels), custom_call_target="tpu_custom_call" | custom-call | tf_op jit(solution)/shard_map/pallas_call | solution.py:43
  103.6 8.5 %all_to_all.41.back = bf16[8,16,896]{2,1,0:T(8,128)(2,1)S(1)} all-to-all(bf16[8,16,896]{2,1,0:T(8,128)(2,1)S(1)} %bitcast.21), channel_id=1, replica_groups={{0,2,4,6,8,10,12,14},{1,3,5,7,9,11,13,15},{16,18,20,22,24,26,28,30},{17..., dimensions={0} | all-to-all | bytes 458752 | tf_op jit(solution)/shard_map/all_to_all | solution.py:16
  112.1 1.0 shard_map.142
  113.1 8.5 %all_to_all.42 = bf16[8,16,1024]{2,1,0:T(8,128)(2,1)S(1)} all-to-all(bf16[8,16,1024]{2,1,0:T(8,128)(2,1)S(1)} %get-tuple-element.55), channel_id=1, replica_groups={{0,2,4,6,8,10,12,14},{1,3,5,7,9,11,13,15},{16,18,20,22,24,26,28,30},{17..., dimensions={0} | all-to-all | bytes 524288 | tf_op jit(solution)/shard_map/all_to_all | solution.py:16
  121.7 1.9 %shard_map.143 = bf16[128,1024]{1,0:T(8,128)(2,1)S(1)} custom-call(bf16[16,2,32,256]{3,2,1,0:T(8,128)(2,1)} %all-to-all-done.own, bf16[16,2,32,256]{3,2,1,0:T(8,128)(2,1)} %collective-permute-done.4.other, bf16[16,2,32,256]{3,2,1,0:T(8,128)(2,1)S(1)} %collective-permute-done.5.own.far_own, ...), custom_call_target="tpu_custom_call" | custom-call | tf_op jit(solution)/shard_map/pallas_call | solution.py:43
  123.6 8.5 %all_to_all.43.parts = bf16[8,16,1024]{2,1,0:T(8,128)(2,1)S(1)} all-to-all(bf16[8,16,1024]{2,1,0:T(8,128)(2,1)S(1)} %bitcast.20), channel_id=1, replica_groups={{0,2,4,6,8,10,12,14},{1,3,5,7,9,11,13,15},{16,18,20,22,24,26,28,30},{17..., dimensions={0} | all-to-all | bytes 524288 | tf_op jit(solution)/shard_map/all_to_all | solution.py:16
  132.5 14.4 %all_to_all.44.parts = f32[16,8,128]{2,1,0:T(8,128)S(1)} all-to-all(f32[16,8,128]{2,1,0:T(8,128)S(1)} %shard_map.144), channel_id=1, replica_groups=mesh['dp'=32,'txt'=16] {'txt'}, dimensions={0} | all-to-all | bytes 131072 | tf_op jit(solution)/shard_map/all_to_all | solution.py:16
  147.0 0.8 shard_map.145
  (29 shorter events, 2.6 us)
Async XLA Ops:
  1.6 48.3 %copy-start.2 = (f32[1024]{0:T(1024)S(1)}, f32[1024]{0:T(1024)}, u32[]{:S(2)}) copy-start(f32[1024]{0:T(1024)} %param.14) | copy-start | bytes 12292
  1.6 48.3 %copy-start.3 = (f32[1024]{0:T(1024)S(1)}, f32[1024]{0:T(1024)}, u32[]{:S(2)}) copy-start(f32[1024]{0:T(1024)} %param.15) | copy-start | bytes 12292
  1.6 48.6 %all-to-all-start = ((bf16[16,2,32,256]{3,2,1,0:T(8,128)(2,1)}), bf16[16,2,32,256]{3,2,1,0:T(8,128)(2,1)}, u32[]{:S(2)}, u32[]{:S(2)}) async-start(bf16[16,2,32,256]{3,2,1,0:T(8,128)(2,1)} %shard_map.130), calls=%async_computation | async-start | bytes 1048576 | tf_op jit(solution)/shard_map/all_to_all | solution.py:16
  19.7 53.9 %collective-permute-start.7 = (bf16[1280,768]{1,0:T(8,128)(2,1)}, bf16[1280,768]{1,0:T(8,128)(2,1)}, u32[]{:S(2)}, u32[]{:S(2)}) collective-permute-start(bf16[1280,768]{1,0:T(8,128)(2,1)} %near.1), channel_id=1, source_target_pairs={{0,1},{1,0},{2,3},{3,2},{4,5},{5,4},{6,7},{7,6},{8,9},{9,8},{10,11... | collective-permute-start | bytes 5898248 | tf_op jit(solution)/shard_map/ppermute | solution.py:21
  22.6 7.5 %collective-permute-start = (bf16[64,1152]{1,0:T(8,128)(2,1)S(1)}, bf16[64,1152]{1,0:T(8,128)(2,1)S(1)}, u32[]{:S(2)}, u32[]{:S(2)}) collective-permute-start(bf16[64,1152]{1,0:T(8,128)(2,1)S(1)} %shard_map.131.near), channel_id=1, source_target_pairs={{0,2},{1,3},{2,0},{3,1},{4,6},{5,7},{6,4},{7,5},{8,10},{9,11},{10,... | collective-permute-start | bytes 442376 | tf_op jit(solution)/shard_map/ppermute | solution.py:21
  30.1 5.8 %collective-permute-start.1 = (bf16[2,64,384]{2,1,0:T(8,128)(2,1)S(1)}, bf16[2,64,384]{2,1,0:T(8,128)(2,1)S(1)}, u32[]{:S(2)}, u32[]{:S(2)}) collective-permute-start(bf16[2,64,384]{2,1,0:T(8,128)(2,1)S(1)} %shard_map.133.refs_0_), channel_id=1, source_target_pairs={{0,4},{1,5},{2,6},{3,7},{4,0},{5,1},{6,2},{7,3},{8,12},{9,13},{10,... | collective-permute-start | bytes 294920 | tf_op jit(solution)/shard_map/ppermute | solution.py:21
  35.9 34.4 %copy-start.5 = (f32[256]{0:T(256)S(1)}, f32[256]{0:T(256)}, u32[]{:S(2)}) copy-start(f32[256]{0:T(256)} %param.17) | copy-start | bytes 3076
  35.9 8.5 %collective-permute-start.2 = (bf16[2,2,64,384]{3,2,1,0:T(8,128)(2,1)S(1)}, bf16[2,2,64,384]{3,2,1,0:T(8,128)(2,1)S(1)}, u32[]{:S(2)}, u32[]{:S(2)}) collective-permute-start(bf16[2,2,64,384]{3,2,1,0:T(8,128)(2,1)S(1)} %shard_map.134.refs_0_), channel_id=1, source_target_pairs={{0,8},{1,9},{2,10},{3,11},{4,12},{5,13},{6,14},{7,15},{8,0},{9,1},... | collective-permute-start | bytes 589832 | tf_op jit(solution)/shard_map/ppermute | solution.py:21
  44.4 5.5 %collective-permute-start.3 = (bf16[4,2,64,384]{3,2,1,0:T(8,128)(2,1)S(1)}, bf16[4,2,64,384]{3,2,1,0:T(8,128)(2,1)S(1)}, u32[]{:S(2)}, u32[]{:S(2)}) collective-permute-start(bf16[4,2,64,384]{3,2,1,0:T(8,128)(2,1)S(1)} %bitcast.17), channel_id=1, source_target_pairs={{0,1},{1,0},{2,3},{3,2},{4,5},{5,4},{6,7},{7,6},{8,9},{9,8},{10,11... | collective-permute-start | bytes 1179656 | tf_op jit(solution)/shard_map/ppermute | solution.py:21
  50.3 16.9 %collective-permute-start.4 = (bf16[16,2,32,256]{3,2,1,0:T(8,128)(2,1)}, bf16[16,2,32,256]{3,2,1,0:T(8,128)(2,1)}, u32[]{:S(2)}, u32[]{:S(2)}) collective-permute-start(bf16[16,2,32,256]{3,2,1,0:T(8,128)(2,1)} %all-to-all-done.own), channel_id=1, source_target_pairs={{0,16},{16,0},{32,48},{48,32},{64,80},{80,64},{96,112},{112,96},{1... | collective-permute-start | bytes 1572872 | tf_op jit(solution)/shard_map/ppermute | solution.py:21
  54.9 18.7 %all-to-all-start.1 = ((bf16[4,2,64,768]{3,2,1,0:T(8,128)(2,1)}), bf16[4,2,64,768]{3,2,1,0:T(8,128)(2,1)S(1)}, u32[]{:S(2)}, u32[]{:S(2)}) async-start(bf16[4,2,64,768]{3,2,1,0:T(8,128)(2,1)} %shard_map.132), calls=%async_computation.1 | async-start | bytes 1572864 | tf_op jit(solution)/shard_map/all_to_all | solution.py:16
  59.1 21.6 %copy-start.6 = (s32[256]{0:T(256)S(1)}, s32[256]{0:T(256)}, u32[]{:S(2)}) copy-start(s32[256]{0:T(256)} %param.24) | copy-start | bytes 3076
  59.1 13.1 %collective-permute-start.5 = (bf16[16,2,32,256]{3,2,1,0:T(8,128)(2,1)}, bf16[16,2,32,256]{3,2,1,0:T(8,128)(2,1)S(1)}, u32[]{:S(2)}, u32[]{:S(2)}) collective-permute-start(bf16[16,2,32,256]{3,2,1,0:T(8,128)(2,1)} %all-to-all-done.own), channel_id=1, source_target_pairs={{0,1},{1,0},{2,3},{3,2},{4,5},{5,4},{6,7},{7,6},{8,9},{9,8},{10,11... | collective-permute-start | bytes 1572872 | tf_op jit(solution)/shard_map/ppermute | solution.py:21
  67.1 5.1 %collective-permute-start.6 = (bf16[16,2,32,256]{3,2,1,0:T(8,128)(2,1)}, bf16[16,2,32,256]{3,2,1,0:T(8,128)(2,1)S(1)}, u32[]{:S(2)}, u32[]{:S(2)}) collective-permute-start(bf16[16,2,32,256]{3,2,1,0:T(8,128)(2,1)} %collective-permute-done.4.other), channel_id=1, source_target_pairs={{0,1},{1,0},{2,3},{3,2},{4,5},{5,4},{6,7},{7,6},{8,9},{9,8},{10,11... | collective-permute-start | bytes 1572872 | tf_op jit(solution)/shard_map/ppermute | solution.py:21
  73.6 13.7 %collective-permute-start.8 = (bf16[4,2,64,768]{3,2,1,0:T(8,128)(2,1)S(1)}, bf16[4,2,64,768]{3,2,1,0:T(8,128)(2,1)S(1)}, u32[]{:S(2)}, u32[]{:S(2)}) collective-permute-start(bf16[4,2,64,768]{3,2,1,0:T(8,128)(2,1)S(1)} %all-to-all-done.1.near), channel_id=1, source_target_pairs={{0,1},{1,0},{2,3},{3,2},{4,5},{5,4},{6,7},{7,6},{8,9},{9,8},{10,11... | collective-permute-start | bytes 2359304 | tf_op jit(solution)/shard_map/ppermute | solution.py:21
  75.6 11.7 %all-to-all-start.2 = ((bf16[8,16,1024]{2,1,0:T(8,128)(2,1)}), bf16[8,16,1024]{2,1,0:T(8,128)(2,1)S(1)}, u32[]{:S(2)}, u32[]{:S(2)}) async-start(bf16[8,16,1024]{2,1,0:T(8,128)(2,1)} %bitcast.10), calls=%async_computation.2 | async-start | bytes 524288 | tf_op jit(solution)/shard_map/all_to_all | solution.py:16
  80.8 6.5 %copy-start.4 = (f32[1024]{0:T(1024)S(1)}, f32[1024]{0:T(1024)}, u32[]{:S(2)}) copy-start(f32[1024]{0:T(1024)} %param.19) | copy-start | bytes 12292
  103.6 18.0 %copy-start = (f32[128,256]{1,0:T(8,128)S(1)}, f32[128,256]{1,0:T(8,128)}, u32[]{:S(2)}) copy-start(f32[128,256]{1,0:T(8,128)} %get-tuple-element.56.pre_act) | copy-start | bytes 393220
  121.7 25.3 %copy-start.1 = (bf16[256,64]{0,1:T(8,128)(2,1)S(1)}, bf16[256,64]{0,1:T(8,128)(2,1)}, u32[]{:S(2)}) copy-start(bf16[256,64]{0,1:T(8,128)(2,1)} %param.13) | copy-start | bytes 98308

commit v10 on v9

--- a/solution.py
+++ b/solution.py
@@ -105,24 +105,24 @@
 
 def copies_kernel(up, down, out, sem):
     loads = [
-        pltpu.make_async_copy(part, out.at[0, k], sem.at[k]) for k, part in enumerate((up, down))
+        pltpu.make_async_copy(part, out.at[z, k], sem.at[2 * z + k])
+        for z in range(out.shape[0])
+        for k, part in enumerate((up, down))
     ]
     for load in loads:
         load.start()
     for load in loads:
         load.wait()
-    for z in range(1, out.shape[0]):
-        out[z] = out[0]
-
-
-def message_kernel(projection, resid, gain, bias, up_bias, step, *refs):
-    out, gains, biases, ups, steps, sem = refs
+
+
+def message_kernel(projection, resid, gain, bias, up_bias, *refs):
+    out, gains, biases, ups, sem = refs
     emb, images = projection.shape[1], resid.shape[1]
-    places = (out.at[:, :emb], out.at[:, emb : emb + images], gains, biases, ups, steps)
+    places = (out.at[:, :emb], out.at[:, emb : emb + images], gains, biases, ups)
     loads = [
         pltpu.make_async_copy(part, place, sem.at[k])
         for k, (part, place) in enumerate(
-            zip((projection, resid, gain, bias, up_bias, step), places)
+            zip((projection, resid, gain, bias, up_bias), places)
         )
     ]
     for load in loads:
@@ -144,8 +144,7 @@
     ]
     lines += [jnp.zeros((1, 128), F32)] * 2
     lines += [part[:, 128 * k : 128 * k + 128] for part in parts(ups[...]) for k in range(2)]
-    lines.append(jnp.concatenate(parts(steps[:, 0:1]) + [jnp.zeros((1, 125), F32)], axis=1))
-    lines.append(jnp.zeros((1, 128), F32))
+    lines += [jnp.zeros((1, 128), F32)] * 2
     lines = jnp.concatenate(lines, axis=0)
     out[:, emb + images :] = jnp.zeros((out.shape[0], 128), BF)
     out[: lines.shape[0], emb + images :] = lines.astype(BF)
@@ -170,7 +169,7 @@
         out[k] = part[...]
 
 
-def rows_kernel(near, far, gain, bias, kept, normed, far_bias, state, vectors):
+def rows_kernel(near, far, gain, bias, step, kept, normed, far_bias, state, vectors):
     n_txt = vectors.shape[0]
     share = near.shape[2]
     half = state.shape[1]
@@ -204,9 +203,9 @@
             for t in range(n_txt)
         ]
         kept[rows + k : rows + k + 1, :] = jnp.concatenate(line, axis=1)
-    step = near[0, 0, 8:16, 2 * half :].astype(F32)[6:7, :]
-    step = jnp.sum(step, axis=1, keepdims=True)
-    kept[rows + 2 :, :] = jnp.broadcast_to(step, (kept.shape[0] - rows - 2, kept.shape[1]))
+    kept[rows + 2 :, :] = jnp.broadcast_to(
+        step[0:1, 0:1], (kept.shape[0] - rows - 2, kept.shape[1])
+    )
     xhat, _ = row_norm(state[...].astype(F32).T)
     normed[...] = (xhat * gain[...] + bias[...]).astype(BF)
 
@@ -313,7 +312,7 @@
     normed_grad[...] = total.astype(BF)
 
 
-def softmax_kernel(arrived, text_unit, labels, back, label_rows, logits, unit_low, held, sem):
+def softmax_kernel(arrived, text_unit, labels, back, label_rows, unit_low, held, sem):
     half, emb = unit_low.shape
     n = arrived.shape[0]
     n_block = 5
@@ -336,23 +335,24 @@
             load.wait()
         texts = held[k * step : (k + 1) * step, :]
         block = 100.0 * lax.dot_general(unit_low[...], texts, NT, preferred_element_type=F32)
-        logits[:, k * step : (k + 1) * step] = block
-        block = jnp.max(block, axis=1, keepdims=True)
-        top = block if top is None else jnp.maximum(top, block)
-    top = top.astype(BF).astype(F32)
-    rest = jnp.zeros_like(top)
-    hit = jnp.zeros_like(top)
-    total = jnp.zeros((half, emb), F32)
-    for k in range(n_block):
-        block = jnp.exp(logits[:, k * step : (k + 1) * step] - top)
+        highest = jnp.max(block, axis=1, keepdims=True).astype(BF).astype(F32)
+        if k:
+            highest = jnp.maximum(top, highest)
+            scale = jnp.exp(top - highest)
+        top = highest
+        block = jnp.exp(block - top)
         columns = lax.broadcasted_iota(jnp.int32, (half, step), 1) + k * step
         target = columns == label
         others = jnp.where(target, 0.0, block)
-        rest += jnp.sum(others, axis=1, keepdims=True)
-        hit += jnp.sum(jnp.where(target, block, 0.0), axis=1, keepdims=True)
-        total += jnp.dot(
-            others.astype(BF), held[k * step : (k + 1) * step, :], preferred_element_type=F32
-        )
+        new_rest = jnp.sum(others, axis=1, keepdims=True)
+        new_hit = jnp.sum(jnp.where(target, block, 0.0), axis=1, keepdims=True)
+        new_total = jnp.dot(others.astype(BF), texts, preferred_element_type=F32)
+        if k:
+            rest = rest * scale + new_rest
+            hit = hit * scale + new_hit
+            total = total * scale + new_total
+        else:
+            rest, hit, total = new_rest, new_hit, new_total
     back[:, :emb] = total.astype(BF)
     lane = lax.broadcasted_iota(jnp.int32, (half, 128), 1)
     rest_high = rest.astype(BF).astype(F32)
@@ -483,26 +483,25 @@
     (mine,) = call(
         copies_kernel,
         (((n_z, 2, WIDTH // n_dp, hid), BF),),
-        "hhv",
+        "hhh",
         up_weight,
         down_weight.T,
-        sems=2,
+        sems=2 * n_z,
     )
     mine = swapped(mine, "dp", along_z)
 
     (chain,) = call(
         message_kernel,
         (((share, emb + images + 128), BF),),
-        "hhhhhhv",
+        "hhhhhv",
         projection,
         resid.T,
         post_gain[None],
         post_bias[None],
         up_bias[None],
-        jnp.broadcast_to(step_size, (1, 128)),
         cost=SMALL,
-        scratch=(((1, share), F32), ((1, share), F32), ((1, hid), F32), ((1, 128), F32)),
-        sems=6,
+        scratch=(((1, share), F32), ((1, share), F32), ((1, hid), F32)),
+        sems=5,
     )
     chain, labels, far_texts = lax.optimization_barrier((chain, labels[:, None], texts))
     far_texts = from_partner(far_texts, "txt", 1)
@@ -517,11 +516,12 @@
     kept, normed, far_bias = call(
         rows_kernel,
         (((rows + 8, WIDTH), F32), ((half, WIDTH), BF), ((1, hid), F32)),
-        "vvvvvvv",
+        "vvvvvvvv",
         rest,
         far_rest,
         prenorm_gain[None],
         prenorm_bias[None],
+        jnp.broadcast_to(step_size, (1, 128)),
         cost=SMALL,
         scratch=(((WIDTH, half), BF), ((n_txt, 8, 128), F32)),
     )
@@ -595,7 +595,7 @@
         arrived,
         text_unit,
         labels,
-        scratch=(((half, 2 * n_text), F32), ((half, emb), BF), ((2 * n_text, emb), BF)),
+        scratch=(((half, emb), BF), ((2 * n_text, emb), BF)),
         sems=20,
     )
     back = swapped(back.reshape(n_pair, rows, emb + 128), "txt", cores)

time: 149 us -> 163 us (1.094)
  Pallas kernels: 21.8 us -> 37.7 us
    pallas_call x16, Pallas kernels: 21.8 us -> 37.7 us  [call(): pl.pallas_call(body, out_shape=[pltpu.HBM(*out) if c == 'h' else jax.Shap...]
  transfers between devices with their start and end apart: 12 -> 12, of which waited for: 6 -> 5; matrix products, arithmetic and copies ran while one was open for 0% -> 0% of each run, Pallas kernels for 7% -> 6%
where the time goes in v10:
time: 163 us; the launch traced here: 162 us
  starting transfers between devices  55.4 us (34%)
  blocking collectives  50.7 us (31%)
  Pallas kernels  37.7 us (23%)
  waiting for transfers between devices  17.5 us (11%)
    all_to_all x5, blocking collectives, swapped(): return lax.all_to_all(x, axis, 0, 0, tiled=True, axis_index_groups=groups)  50.7 us
    pallas_call x16, Pallas kernels, call(): pl.pallas_call(body, out_shape=[pltpu.HBM(*out) if c == 'h' else jax.Shap...  37.7 us
    ppermute x9, starting transfers between devices, from_partner(): return lax.ppermute(x, axis, pairs)  30.3 us
    all_to_all x3, starting transfers between devices, swapped(): return lax.all_to_all(x, axis, 0, 0, tiled=True, axis_index_groups=groups)  25.1 us
    ppermute x9, waiting for transfers between devices, from_partner(): return lax.ppermute(x, axis, pairs)  15.9 us
  transfers between devices with their start and end apart: 12, of which 5 were waited for; matrix products, arithmetic and copies ran while one was open for 0% of the time, Pallas kernels for 6%

profile of v10, /device:TPU:1, one launch (start us, length us, event | category | flops | bytes accessed | tf_op | source)
XLA Modules:
  0.0 162.5 jit_solution(13401416022648014251)
XLA Ops:
  0.0 17.3 %shard_map.130 = bf16[16,2,32,256]{3,2,1,0:T(8,128)(2,1)} custom-call(bf16[32,256]{1,0:T(8,128)(2,1)} %up.1, bf16[32,256]{1,0:T(8,128)(2,1)} %bitcast.30), custom_call_target="tpu_custom_call" | custom-call | tf_op jit(solution)/shard_map/pallas_call | solution.py:43
  17.3 15.8 %all-to-all-start = ((bf16[16,2,32,256]{3,2,1,0:T(8,128)(2,1)}), bf16[16,2,32,256]{3,2,1,0:T(8,128)(2,1)}, u32[]{:S(2)}, u32[]{:S(2)}) async-start(bf16[16,2,32,256]{3,2,1,0:T(8,128)(2,1)} %shard_map.130), calls=%async_computation | async-start | bytes 1048576 | tf_op jit(solution)/shard_map/all_to_all | solution.py:16
  33.1 1.0 shard_map.131.near
  34.1 2.9 %collective-permute-start.7 = (bf16[1280,768]{1,0:T(8,128)(2,1)}, bf16[1280,768]{1,0:T(8,128)(2,1)}, u32[]{:S(2)}, u32[]{:S(2)}) collective-permute-start(bf16[1280,768]{1,0:T(8,128)(2,1)} %near.1), channel_id=1, source_target_pairs={{0,1},{1,0},{2,3},{3,2},{4,5},{5,4},{6,7},{7,6},{8,9},{9,8},{10,11... | collective-permute-start | bytes 5898248 | tf_op jit(solution)/shard_map/ppermute | solution.py:21
  37.0 3.1 %collective-permute-start = (bf16[64,1152]{1,0:T(8,128)(2,1)S(1)}, bf16[64,1152]{1,0:T(8,128)(2,1)S(1)}, u32[]{:S(2)}, u32[]{:S(2)}) collective-permute-start(bf16[64,1152]{1,0:T(8,128)(2,1)S(1)} %shard_map.131.near), channel_id=1, source_target_pairs={{0,2},{1,3},{2,0},{3,1},{4,6},{5,7},{6,4},{7,5},{8,10},{9,11},{10,... | collective-permute-start | bytes 442376 | tf_op jit(solution)/shard_map/ppermute | solution.py:21
  40.1 4.2 %collective-permute-done.other = bf16[64,1152]{1,0:T(8,128)(2,1)S(1)} collective-permute-done((bf16[64,1152]{1,0:T(8,128)(2,1)S(1)}, bf16[64,1152]{1,0:T(8,128)(2,1)S(1)}, u32[]{:S(2)}, u32[]{:S(2)}) %collective-permute-start) | collective-permute-done | bytes 147488 | tf_op jit(solution)/shard_map/ppermute | solution.py:21
  44.3 3.2 %collective-permute-start.1 = (bf16[2,64,384]{2,1,0:T(8,128)(2,1)S(1)}, bf16[2,64,384]{2,1,0:T(8,128)(2,1)S(1)}, u32[]{:S(2)}, u32[]{:S(2)}) collective-permute-start(bf16[2,64,384]{2,1,0:T(8,128)(2,1)S(1)} %shard_map.133.refs_0_), channel_id=1, source_target_pairs={{0,4},{1,5},{2,6},{3,7},{4,0},{5,1},{6,2},{7,3},{8,12},{9,13},{10,... | collective-permute-start | bytes 294920 | tf_op jit(solution)/shard_map/ppermute | solution.py:21
  47.6 2.5 %collective-permute-done.1.refs_1_ = bf16[2,64,384]{2,1,0:T(8,128)(2,1)S(1)} collective-permute-done((bf16[2,64,384]{2,1,0:T(8,128)(2,1)S(1)}, bf16[2,64,384]{2,1,0:T(8,128)(2,1)S(1)}, u32[]{:S(2)}, u32[]{:S(2)}) %collective-permute-start.1) | collective-permute-done | bytes 98336 | tf_op jit(solution)/shard_map/ppermute | solution.py:21
  50.1 4.8 %collective-permute-start.2 = (bf16[2,2,64,384]{3,2,1,0:T(8,128)(2,1)S(1)}, bf16[2,2,64,384]{3,2,1,0:T(8,128)(2,1)S(1)}, u32[]{:S(2)}, u32[]{:S(2)}) collective-permute-start(bf16[2,2,64,384]{3,2,1,0:T(8,128)(2,1)S(1)} %shard_map.134.refs_0_), channel_id=1, source_target_pairs={{0,8},{1,9},{2,10},{3,11},{4,12},{5,13},{6,14},{7,15},{8,0},{9,1},... | collective-permute-start | bytes 589832 | tf_op jit(solution)/shard_map/ppermute | solution.py:21
  55.0 3.5 %collective-permute-done.2.refs_1_ = bf16[2,2,64,384]{3,2,1,0:T(8,128)(2,1)S(1)} collective-permute-done((bf16[2,2,64,384]{3,2,1,0:T(8,128)(2,1)S(1)}, bf16[2,2,64,384]{3,2,1,0:T(8,128)(2,1)S(1)}, u32[]{:S(2)}, u32[]{:S(2)}) %collective-permute-start.2) | collective-permute-done | bytes 196640 | tf_op jit(solution)/shard_map/ppermute | solution.py:21
  58.5 4.3 %collective-permute-start.3 = (bf16[4,2,64,384]{3,2,1,0:T(8,128)(2,1)S(1)}, bf16[4,2,64,384]{3,2,1,0:T(8,128)(2,1)S(1)}, u32[]{:S(2)}, u32[]{:S(2)}) collective-permute-start(bf16[4,2,64,384]{3,2,1,0:T(8,128)(2,1)S(1)} %bitcast.17), channel_id=1, source_target_pairs={{0,1},{1,0},{2,3},{3,2},{4,5},{5,4},{6,7},{7,6},{8,9},{9,8},{10,11... | collective-permute-start | bytes 1179656 | tf_op jit(solution)/shard_map/ppermute | solution.py:21
  63.5 0.9 shard_map.132
  64.9 4.7 %collective-permute-start.4 = (bf16[16,2,32,256]{3,2,1,0:T(8,128)(2,1)}, bf16[16,2,32,256]{3,2,1,0:T(8,128)(2,1)S(1)}, u32[]{:S(2)}, u32[]{:S(2)}) collective-permute-start(bf16[16,2,32,256]{3,2,1,0:T(8,128)(2,1)} %all-to-all-done.own), channel_id=1, source_target_pairs={{0,16},{16,0},{32,48},{48,32},{64,80},{80,64},{96,112},{112,96},{1... | collective-permute-start | bytes 1572872 | tf_op jit(solution)/shard_map/ppermute | solution.py:21
  69.5 4.2 %all-to-all-start.1 = ((bf16[4,2,64,768]{3,2,1,0:T(8,128)(2,1)}), bf16[4,2,64,768]{3,2,1,0:T(8,128)(2,1)S(1)}, u32[]{:S(2)}, u32[]{:S(2)}) async-start(bf16[4,2,64,768]{3,2,1,0:T(8,128)(2,1)} %shard_map.132), calls=%async_computation.1 | async-start | bytes 1572864 | tf_op jit(solution)/shard_map/all_to_all | solution.py:16
  73.7 2.7 %collective-permute-start.5 = (bf16[16,2,32,256]{3,2,1,0:T(8,128)(2,1)}, bf16[16,2,32,256]{3,2,1,0:T(8,128)(2,1)S(1)}, u32[]{:S(2)}, u32[]{:S(2)}) collective-permute-start(bf16[16,2,32,256]{3,2,1,0:T(8,128)(2,1)} %all-to-all-done.own), channel_id=1, source_target_pairs={{0,1},{1,0},{2,3},{3,2},{4,5},{5,4},{6,7},{7,6},{8,9},{9,8},{10,11... | collective-permute-start | bytes 1572872 | tf_op jit(solution)/shard_map/ppermute | solution.py:21
  76.4 5.5 %collective-permute-done.4.other = bf16[16,2,32,256]{3,2,1,0:T(8,128)(2,1)S(1)} collective-permute-done((bf16[16,2,32,256]{3,2,1,0:T(8,128)(2,1)}, bf16[16,2,32,256]{3,2,1,0:T(8,128)(2,1)S(1)}, u32[]{:S(2)}, u32[]{:S(2)}) %collective-permute-start.4) | collective-permute-done | bytes 524320 | tf_op jit(solution)/shard_map/ppermute | solution.py:21
  82.0 2.8 %collective-permute-start.6 = (bf16[16,2,32,256]{3,2,1,0:T(8,128)(2,1)S(1)}, bf16[16,2,32,256]{3,2,1,0:T(8,128)(2,1)S(1)}, u32[]{:S(2)}, u32[]{:S(2)}) collective-permute-start(bf16[16,2,32,256]{3,2,1,0:T(8,128)(2,1)S(1)} %collective-permute-done.4.other), channel_id=1, source_target_pairs={{0,1},{1,0},{2,3},{3,2},{4,5},{5,4},{6,7},{7,6},{8,9},{9,8},{10,11... | collective-permute-start | bytes 1572872 | tf_op jit(solution)/shard_map/ppermute | solution.py:21
  84.8 2.0 %shard_map.137 = (f32[128,256]{1,0:T(8,128)}, f32[128,1024]{1,0:T(8,128)S(1)}) custom-call(bf16[16,2,32,256]{3,2,1,0:T(8,128)(2,1)} %all-to-all-done.own, bf16[16,2,32,256]{3,2,1,0:T(8,128)(2,1)} %copy-done.6, bf16[128,1024]{1,0:T(8,128)(2,1)S(1)} %get-tuple-element.35.normed, f32[1,256]{1,0:T(1,128)S(1)} %bitcast.29), custom_call_target="tpu_custom_call" | custom-call | tf_op jit(solution)/shard_map/pallas_call | solution.py:43
  86.8 1.3 shard_map.138
  88.1 1.9 %collective-permute-start.8 = (bf16[4,2,64,768]{3,2,1,0:T(8,128)(2,1)S(1)}, bf16[4,2,64,768]{3,2,1,0:T(8,128)(2,1)S(1)}, u32[]{:S(2)}, u32[]{:S(2)}) collective-permute-start(bf16[4,2,64,768]{3,2,1,0:T(8,128)(2,1)S(1)} %all-to-all-done.1.near), channel_id=1, source_target_pairs={{0,1},{1,0},{2,3},{3,2},{4,5},{5,4},{6,7},{7,6},{8,9},{9,8},{10,11... | collective-permute-start | bytes 2359304 | tf_op jit(solution)/shard_map/ppermute | solution.py:21
  90.0 5.1 %all-to-all-start.2 = ((bf16[8,16,1024]{2,1,0:T(8,128)(2,1)}), bf16[8,16,1024]{2,1,0:T(8,128)(2,1)S(1)}, u32[]{:S(2)}, u32[]{:S(2)}) async-start(bf16[8,16,1024]{2,1,0:T(8,128)(2,1)} %bitcast.10), calls=%async_computation.2 | async-start | bytes 524288 | tf_op jit(solution)/shard_map/all_to_all | solution.py:16
  95.3 4.7 %shard_map.139 = (bf16[2560,768]{1,0:T(8,128)(2,1)}, bf16[128,768]{1,0:T(8,128)(2,1)S(1)}) custom-call(bf16[1280,768]{1,0:T(8,128)(2,1)} %near.1, bf16[1280,768]{1,0:T(8,128)(2,1)} %collective-permute-done.7.far, s32[256,1]{1,0:T(8,128)S(1)} %copy.14.labels), custom_call_target="tpu_custom_call" | custom-call | flops 2147483648 | bytes 12582912 | tf_op jit(solution)/shard_map/pallas_call | solution.py:43
  100.1 1.7 %all-to-all-done.2.mixed = bf16[8,16,1024]{2,1,0:T(8,128)(2,1)S(1)} async-done(((bf16[8,16,1024]{2,1,0:T(8,128)(2,1)}), bf16[8,16,1024]{2,1,0:T(8,128)(2,1)S(1)}, u32[]{:S(2)}, u32[]{:S(2)}) %all-to-all-start.2) | async-done | bytes 262176 | tf_op jit(solution)/shard_map/all_to_all | solution.py:16
  102.4 10.7 %all_to_all.40.arrived = bf16[8,16,1536]{2,1,0:T(8,128)(2,1)S(1)} all-to-all(bf16[8,16,1536]{2,1,0:T(8,128)(2,1)S(1)} %get-tuple-element.47), channel_id=1, replica_groups={{0,2,4,6,8,10,12,14},{1,3,5,7,9,11,13,15},{16,18,20,22,24,26,28,30},{17..., dimensions={0} | all-to-all | bytes 786432 | tf_op jit(solution)/shard_map/all_to_all | solution.py:16
  113.1 5.2 %shard_map.141 = (bf16[128,896]{1,0:T(8,128)(2,1)S(1)}, f32[16,768]{1,0:T(8,128)S(1)}) custom-call(bf16[8,16,1536]{2,1,0:T(8,128)(2,1)S(1)} %all_to_all.40.arrived, bf16[2560,768]{1,0:T(8,128)(2,1)} %get-tuple-element.48.text_unit, s32[256,1]{1,0:T(8,128)S(1)} %copy.14.labels), custom_call_target="tpu_custom_call" | custom-call | tf_op jit(solution)/shard_map/pallas_call | solution.py:43
  118.3 8.5 %all_to_all.41.back = bf16[8,16,896]{2,1,0:T(8,128)(2,1)S(1)} all-to-all(bf16[8,16,896]{2,1,0:T(8,128)(2,1)S(1)} %bitcast.21), channel_id=1, replica_groups={{0,2,4,6,8,10,12,14},{1,3,5,7,9,11,13,15},{16,18,20,22,24,26,28,30},{17..., dimensions={0} | all-to-all | bytes 458752 | tf_op jit(solution)/shard_map/all_to_all | solution.py:16
  126.8 1.0 shard_map.142
  127.8 8.5 %all_to_all.42 = bf16[8,16,1024]{2,1,0:T(8,128)(2,1)S(1)} all-to-all(bf16[8,16,1024]{2,1,0:T(8,128)(2,1)S(1)} %get-tuple-element.55), channel_id=1, replica_groups={{0,2,4,6,8,10,12,14},{1,3,5,7,9,11,13,15},{16,18,20,22,24,26,28,30},{17..., dimensions={0} | all-to-all | bytes 524288 | tf_op jit(solution)/shard_map/all_to_all | solution.py:16
  136.4 1.9 %shard_map.143 = bf16[128,1024]{1,0:T(8,128)(2,1)S(1)} custom-call(bf16[16,2,32,256]{3,2,1,0:T(8,128)(2,1)} %all-to-all-done.own, bf16[16,2,32,256]{3,2,1,0:T(8,128)(2,1)} %copy-done.6, bf16[16,2,32,256]{3,2,1,0:T(8,128)(2,1)S(1)} %collective-permute-done.5.own.far_own, bf16[16,2,32,256]{3,2,1,0:T(8,128)(2,1)S(1)} %collective-permute-done.6.other.far_other, ...), custom_call_target="tpu_custom_call" | custom-call | tf_op jit(solution)/shard_map/pallas_call | solution.py:43
  138.3 8.5 %all_to_all.43.parts = bf16[8,16,1024]{2,1,0:T(8,128)(2,1)S(1)} all-to-all(bf16[8,16,1024]{2,1,0:T(8,128)(2,1)S(1)} %bitcast.20), channel_id=1, replica_groups={{0,2,4,6,8,10,12,14},{1,3,5,7,9,11,13,15},{16,18,20,22,24,26,28,30},{17..., dimensions={0} | all-to-all | bytes 524288 | tf_op jit(solution)/shard_map/all_to_all | solution.py:16
  147.3 14.4 %all_to_all.44.parts = f32[16,8,128]{2,1,0:T(8,128)S(1)} all-to-all(f32[16,8,128]{2,1,0:T(8,128)S(1)} %shard_map.144), channel_id=1, replica_groups=mesh['dp'=32,'txt'=16] {'txt'}, dimensions={0} | all-to-all | bytes 131072 | tf_op jit(solution)/shard_map/all_to_all | solution.py:16
  161.7 0.8 shard_map.145
  (31 shorter events, 1.7 us)
Async XLA Ops:
  17.3 47.1 %copy-start.2 = (f32[1024]{0:T(1024)S(1)}, f32[1024]{0:T(1024)}, u32[]{:S(2)}) copy-start(f32[1024]{0:T(1024)} %param.14) | copy-start | bytes 12292
  17.3 47.1 %copy-start.3 = (f32[1024]{0:T(1024)S(1)}, f32[1024]{0:T(1024)}, u32[]{:S(2)}) copy-start(f32[1024]{0:T(1024)} %param.15) | copy-start | bytes 12292
  17.3 47.6 %all-to-all-start = ((bf16[16,2,32,256]{3,2,1,0:T(8,128)(2,1)}), bf16[16,2,32,256]{3,2,1,0:T(8,128)(2,1)}, u32[]{:S(2)}, u32[]{:S(2)}) async-start(bf16[16,2,32,256]{3,2,1,0:T(8,128)(2,1)} %shard_map.130), calls=%async_computation | async-start | bytes 1048576 | tf_op jit(solution)/shard_map/all_to_all | solution.py:16
  34.1 54.0 %collective-permute-start.7 = (bf16[1280,768]{1,0:T(8,128)(2,1)}, bf16[1280,768]{1,0:T(8,128)(2,1)}, u32[]{:S(2)}, u32[]{:S(2)}) collective-permute-start(bf16[1280,768]{1,0:T(8,128)(2,1)} %near.1), channel_id=1, source_target_pairs={{0,1},{1,0},{2,3},{3,2},{4,5},{5,4},{6,7},{7,6},{8,9},{9,8},{10,11... | collective-permute-start | bytes 5898248 | tf_op jit(solution)/shard_map/ppermute | solution.py:21
  37.0 7.4 %collective-permute-start = (bf16[64,1152]{1,0:T(8,128)(2,1)S(1)}, bf16[64,1152]{1,0:T(8,128)(2,1)S(1)}, u32[]{:S(2)}, u32[]{:S(2)}) collective-permute-start(bf16[64,1152]{1,0:T(8,128)(2,1)S(1)} %shard_map.131.near), channel_id=1, source_target_pairs={{0,2},{1,3},{2,0},{3,1},{4,6},{5,7},{6,4},{7,5},{8,10},{9,11},{10,... | collective-permute-start | bytes 442376 | tf_op jit(solution)/shard_map/ppermute | solution.py:21
  44.3 5.8 %collective-permute-start.1 = (bf16[2,64,384]{2,1,0:T(8,128)(2,1)S(1)}, bf16[2,64,384]{2,1,0:T(8,128)(2,1)S(1)}, u32[]{:S(2)}, u32[]{:S(2)}) collective-permute-start(bf16[2,64,384]{2,1,0:T(8,128)(2,1)S(1)} %shard_map.133.refs_0_), channel_id=1, source_target_pairs={{0,4},{1,5},{2,6},{3,7},{4,0},{5,1},{6,2},{7,3},{8,12},{9,13},{10,... | collective-permute-start | bytes 294920 | tf_op jit(solution)/shard_map/ppermute | solution.py:21
  50.1 34.6 %copy-start.5 = (f32[256]{0:T(256)S(1)}, f32[256]{0:T(256)}, u32[]{:S(2)}) copy-start(f32[256]{0:T(256)} %param.17) | copy-start | bytes 3076
  50.1 8.4 %collective-permute-start.2 = (bf16[2,2,64,384]{3,2,1,0:T(8,128)(2,1)S(1)}, bf16[2,2,64,384]{3,2,1,0:T(8,128)(2,1)S(1)}, u32[]{:S(2)}, u32[]{:S(2)}) collective-permute-start(bf16[2,2,64,384]{3,2,1,0:T(8,128)(2,1)S(1)} %shard_map.134.refs_0_), channel_id=1, source_target_pairs={{0,8},{1,9},{2,10},{3,11},{4,12},{5,13},{6,14},{7,15},{8,0},{9,1},... | collective-permute-start | bytes 589832 | tf_op jit(solution)/shard_map/ppermute | solution.py:21
  58.5 5.9 %collective-permute-start.3 = (bf16[4,2,64,384]{3,2,1,0:T(8,128)(2,1)S(1)}, bf16[4,2,64,384]{3,2,1,0:T(8,128)(2,1)S(1)}, u32[]{:S(2)}, u32[]{:S(2)}) collective-permute-start(bf16[4,2,64,384]{3,2,1,0:T(8,128)(2,1)S(1)} %bitcast.17), channel_id=1, source_target_pairs={{0,1},{1,0},{2,3},{3,2},{4,5},{5,4},{6,7},{7,6},{8,9},{9,8},{10,11... | collective-permute-start | bytes 1179656 | tf_op jit(solution)/shard_map/ppermute | solution.py:21
  64.9 17.1 %collective-permute-start.4 = (bf16[16,2,32,256]{3,2,1,0:T(8,128)(2,1)}, bf16[16,2,32,256]{3,2,1,0:T(8,128)(2,1)S(1)}, u32[]{:S(2)}, u32[]{:S(2)}) collective-permute-start(bf16[16,2,32,256]{3,2,1,0:T(8,128)(2,1)} %all-to-all-done.own), channel_id=1, source_target_pairs={{0,16},{16,0},{32,48},{48,32},{64,80},{80,64},{96,112},{112,96},{1... | collective-permute-start | bytes 1572872 | tf_op jit(solution)/shard_map/ppermute | solution.py:21
  69.5 18.6 %all-to-all-start.1 = ((bf16[4,2,64,768]{3,2,1,0:T(8,128)(2,1)}), bf16[4,2,64,768]{3,2,1,0:T(8,128)(2,1)S(1)}, u32[]{:S(2)}, u32[]{:S(2)}) async-start(bf16[4,2,64,768]{3,2,1,0:T(8,128)(2,1)} %shard_map.132), calls=%async_computation.1 | async-start | bytes 1572864 | tf_op jit(solution)/shard_map/all_to_all | solution.py:16
  73.7 21.4 %copy-start.7 = (s32[256]{0:T(256)S(1)}, s32[256]{0:T(256)}, u32[]{:S(2)}) copy-start(s32[256]{0:T(256)} %param.24) | copy-start | bytes 3076
  73.7 13.0 %collective-permute-start.5 = (bf16[16,2,32,256]{3,2,1,0:T(8,128)(2,1)}, bf16[16,2,32,256]{3,2,1,0:T(8,128)(2,1)S(1)}, u32[]{:S(2)}, u32[]{:S(2)}) collective-permute-start(bf16[16,2,32,256]{3,2,1,0:T(8,128)(2,1)} %all-to-all-done.own), channel_id=1, source_target_pairs={{0,1},{1,0},{2,3},{3,2},{4,5},{5,4},{6,7},{7,6},{8,9},{9,8},{10,11... | collective-permute-start | bytes 1572872 | tf_op jit(solution)/shard_map/ppermute | solution.py:21
  82.0 2.8 %copy-start.6 = (bf16[16,2,32,256]{3,2,1,0:T(8,128)(2,1)}, bf16[16,2,32,256]{3,2,1,0:T(8,128)(2,1)S(1)}, u32[]{:S(2)}) copy-start(bf16[16,2,32,256]{3,2,1,0:T(8,128)(2,1)S(1)} %collective-permute-done.4.other) | copy-start | bytes 1572868
  82.0 4.8 %collective-permute-start.6 = (bf16[16,2,32,256]{3,2,1,0:T(8,128)(2,1)S(1)}, bf16[16,2,32,256]{3,2,1,0:T(8,128)(2,1)S(1)}, u32[]{:S(2)}, u32[]{:S(2)}) collective-permute-start(bf16[16,2,32,256]{3,2,1,0:T(8,128)(2,1)S(1)} %collective-permute-done.4.other), channel_id=1, source_target_pairs={{0,1},{1,0},{2,3},{3,2},{4,5},{5,4},{6,7},{7,6},{8,9},{9,8},{10,11... | collective-permute-start | bytes 1572872 | tf_op jit(solution)/shard_map/ppermute | solution.py:21
  88.1 13.6 %collective-permute-start.8 = (bf16[4,2,64,768]{3,2,1,0:T(8,128)(2,1)S(1)}, bf16[4,2,64,768]{3,2,1,0:T(8,128)(2,1)S(1)}, u32[]{:S(2)}, u32[]{:S(2)}) collective-permute-start(bf16[4,2,64,768]{3,2,1,0:T(8,128)(2,1)S(1)} %all-to-all-done.1.near), channel_id=1, source_target_pairs={{0,1},{1,0},{2,3},{3,2},{4,5},{5,4},{6,7},{7,6},{8,9},{9,8},{10,11... | collective-permute-start | bytes 2359304 | tf_op jit(solution)/shard_map/ppermute | solution.py:21
  90.0 11.7 %all-to-all-start.2 = ((bf16[8,16,1024]{2,1,0:T(8,128)(2,1)}), bf16[8,16,1024]{2,1,0:T(8,128)(2,1)S(1)}, u32[]{:S(2)}, u32[]{:S(2)}) async-start(bf16[8,16,1024]{2,1,0:T(8,128)(2,1)} %bitcast.10), calls=%async_computation.2 | async-start | bytes 524288 | tf_op jit(solution)/shard_map/all_to_all | solution.py:16
  95.3 6.4 %copy-start.4 = (f32[1024]{0:T(1024)S(1)}, f32[1024]{0:T(1024)}, u32[]{:S(2)}) copy-start(f32[1024]{0:T(1024)} %param.19) | copy-start | bytes 12292
  118.3 18.1 %copy-start = (f32[128,256]{1,0:T(8,128)S(1)}, f32[128,256]{1,0:T(8,128)}, u32[]{:S(2)}) copy-start(f32[128,256]{1,0:T(8,128)} %get-tuple-element.56.pre_act) | copy-start | bytes 393220
  136.4 25.3 %copy-start.1 = (bf16[256,64]{0,1:T(8,128)(2,1)S(1)}, bf16[256,64]{0,1:T(8,128)(2,1)}, u32[]{:S(2)}) copy-start(bf16[256,64]{0,1:T(8,128)(2,1)} %param.13) | copy-start | bytes 98308

commit v11 on v9

--- a/solution.py
+++ b/solution.py
@@ -115,14 +115,14 @@
         out[z] = out[0]
 
 
-def message_kernel(projection, resid, gain, bias, up_bias, step, *refs):
-    out, gains, biases, ups, steps, sem = refs
+def message_kernel(projection, resid, gain, bias, up_bias, *refs):
+    out, gains, biases, ups, sem = refs
     emb, images = projection.shape[1], resid.shape[1]
-    places = (out.at[:, :emb], out.at[:, emb : emb + images], gains, biases, ups, steps)
+    places = (out.at[:, :emb], out.at[:, emb : emb + images], gains, biases, ups)
     loads = [
         pltpu.make_async_copy(part, place, sem.at[k])
         for k, (part, place) in enumerate(
-            zip((projection, resid, gain, bias, up_bias, step), places)
+            zip((projection, resid, gain, bias, up_bias), places)
         )
     ]
     for load in loads:
@@ -144,8 +144,7 @@
     ]
     lines += [jnp.zeros((1, 128), F32)] * 2
     lines += [part[:, 128 * k : 128 * k + 128] for part in parts(ups[...]) for k in range(2)]
-    lines.append(jnp.concatenate(parts(steps[:, 0:1]) + [jnp.zeros((1, 125), F32)], axis=1))
-    lines.append(jnp.zeros((1, 128), F32))
+    lines += [jnp.zeros((1, 128), F32)] * 2
     lines = jnp.concatenate(lines, axis=0)
     out[:, emb + images :] = jnp.zeros((out.shape[0], 128), BF)
     out[: lines.shape[0], emb + images :] = lines.astype(BF)
@@ -170,7 +169,7 @@
         out[k] = part[...]
 
 
-def rows_kernel(near, far, gain, bias, kept, normed, far_bias, state, vectors):
+def rows_kernel(near, far, gain, bias, step, kept, normed, far_bias, state, vectors):
     n_txt = vectors.shape[0]
     share = near.shape[2]
     half = state.shape[1]
@@ -204,9 +203,9 @@
             for t in range(n_txt)
         ]
         kept[rows + k : rows + k + 1, :] = jnp.concatenate(line, axis=1)
-    step = near[0, 0, 8:16, 2 * half :].astype(F32)[6:7, :]
-    step = jnp.sum(step, axis=1, keepdims=True)
-    kept[rows + 2 :, :] = jnp.broadcast_to(step, (kept.shape[0] - rows - 2, kept.shape[1]))
+    kept[rows + 2 :, :] = jnp.broadcast_to(
+        step[0:1, 0:1], (kept.shape[0] - rows - 2, kept.shape[1])
+    )
     xhat, _ = row_norm(state[...].astype(F32).T)
     normed[...] = (xhat * gain[...] + bias[...]).astype(BF)
 
@@ -318,10 +317,9 @@
     n = arrived.shape[0]
     n_block = 5
     step = text_unit.shape[0] // n_block
-    cut = step // 4
     loads = []
-    for k in range(4 * n_block):
-        place = pl.ds(k * cut, cut)
+    for k in range(n_block):
+        place = pl.ds(k * step, step)
         loads.append(pltpu.make_async_copy(text_unit.at[place], held.at[place], sem.at[k]))
         loads[k].start()
     texts = jnp.zeros(label_rows.shape, F32)
@@ -332,8 +330,7 @@
     label = local_labels(labels, text_unit.shape[0] // 2)
     top = None
     for k in range(n_block):
-        for load in loads[4 * k : 4 * k + 4]:
-            load.wait()
+        loads[k].wait()
         texts = held[k * step : (k + 1) * step, :]
         block = 100.0 * lax.dot_general(unit_low[...], texts, NT, preferred_element_type=F32)
         logits[:, k * step : (k + 1) * step] = block
@@ -493,16 +490,15 @@
     (chain,) = call(
         message_kernel,
         (((share, emb + images + 128), BF),),
-        "hhhhhhv",
+        "hhhhhv",
         projection,
         resid.T,
         post_gain[None],
         post_bias[None],
         up_bias[None],
-        jnp.broadcast_to(step_size, (1, 128)),
         cost=SMALL,
-        scratch=(((1, share), F32), ((1, share), F32), ((1, hid), F32), ((1, 128), F32)),
-        sems=6,
+        scratch=(((1, share), F32), ((1, share), F32), ((1, hid), F32)),
+        sems=5,
     )
     chain, labels, far_texts = lax.optimization_barrier((chain, labels[:, None], texts))
     far_texts = from_partner(far_texts, "txt", 1)
@@ -517,11 +513,12 @@
     kept, normed, far_bias = call(
         rows_kernel,
         (((rows + 8, WIDTH), F32), ((half, WIDTH), BF), ((1, hid), F32)),
-        "vvvvvvv",
+        "vvvvvvvv",
         rest,
         far_rest,
         prenorm_gain[None],
         prenorm_bias[None],
+        jnp.broadcast_to(step_size, (1, 128)),
         cost=SMALL,
         scratch=(((WIDTH, half), BF), ((n_txt, 8, 128), F32)),
     )
@@ -596,7 +593,7 @@
         text_unit,
         labels,
         scratch=(((half, 2 * n_text), F32), ((half, emb), BF), ((2 * n_text, emb), BF)),
-        sems=20,
+        sems=5,
     )
     back = swapped(back.reshape(n_pair, rows, emb + 128), "txt", cores)
 

time: 149 us -> 147 us (0.987)
  transfers between devices with their start and end apart: 12 -> 12, of which waited for: 6 -> 5; matrix products, arithmetic and copies ran while one was open for 0% -> 0% of each run, Pallas kernels for 7% -> 7%
where the time goes in v11:
time: 147 us; the launch traced here: 146 us
  starting transfers between devices  55.5 us (38%)
  blocking collectives  50.7 us (34%)
  Pallas kernels  21.5 us (15%)
  waiting for transfers between devices  17.7 us (12%)
    all_to_all x5, blocking collectives, swapped(): return lax.all_to_all(x, axis, 0, 0, tiled=True, axis_index_groups=groups)  50.7 us
    ppermute x9, starting transfers between devices, from_partner(): return lax.ppermute(x, axis, pairs)  30.3 us
    all_to_all x3, starting transfers between devices, swapped(): return lax.all_to_all(x, axis, 0, 0, tiled=True, axis_index_groups=groups)  25.1 us
    pallas_call x16, Pallas kernels, call(): pl.pallas_call(body, out_shape=[pltpu.HBM(*out) if c == 'h' else jax.Shap...  21.5 us
    ppermute x9, waiting for transfers between devices, from_partner(): return lax.ppermute(x, axis, pairs)  16 us
  transfers between devices with their start and end apart: 12, of which 5 were waited for; matrix products, arithmetic and copies ran while one was open for 0% of the time, Pallas kernels for 7%

profile of v11, /device:TPU:1, one launch (start us, length us, event | category | flops | bytes accessed | tf_op | source)
XLA Modules:
  0.0 146.4 jit_solution(932074165170989721)
XLA Ops:
  0.0 1.6 %shard_map.130 = bf16[16,2,32,256]{3,2,1,0:T(8,128)(2,1)} custom-call(bf16[32,256]{1,0:T(8,128)(2,1)} %up.1, bf16[32,256]{1,0:T(8,128)(2,1)} %bitcast.30), custom_call_target="tpu_custom_call" | custom-call | tf_op jit(solution)/shard_map/pallas_call | solution.py:43
  1.6 15.8 %all-to-all-start = ((bf16[16,2,32,256]{3,2,1,0:T(8,128)(2,1)}), bf16[16,2,32,256]{3,2,1,0:T(8,128)(2,1)}, u32[]{:S(2)}, u32[]{:S(2)}) async-start(bf16[16,2,32,256]{3,2,1,0:T(8,128)(2,1)} %shard_map.130), calls=%async_computation | async-start | bytes 1048576 | tf_op jit(solution)/shard_map/all_to_all | solution.py:16
  17.4 1.0 shard_map.131.near
  18.4 2.9 %collective-permute-start.7 = (bf16[1280,768]{1,0:T(8,128)(2,1)}, bf16[1280,768]{1,0:T(8,128)(2,1)}, u32[]{:S(2)}, u32[]{:S(2)}) collective-permute-start(bf16[1280,768]{1,0:T(8,128)(2,1)} %near.1), channel_id=1, source_target_pairs={{0,1},{1,0},{2,3},{3,2},{4,5},{5,4},{6,7},{7,6},{8,9},{9,8},{10,11... | collective-permute-start | bytes 5898248 | tf_op jit(solution)/shard_map/ppermute | solution.py:21
  21.3 3.1 %collective-permute-start = (bf16[64,1152]{1,0:T(8,128)(2,1)S(1)}, bf16[64,1152]{1,0:T(8,128)(2,1)S(1)}, u32[]{:S(2)}, u32[]{:S(2)}) collective-permute-start(bf16[64,1152]{1,0:T(8,128)(2,1)S(1)} %shard_map.131.near), channel_id=1, source_target_pairs={{0,2},{1,3},{2,0},{3,1},{4,6},{5,7},{6,4},{7,5},{8,10},{9,11},{10,... | collective-permute-start | bytes 442376 | tf_op jit(solution)/shard_map/ppermute | solution.py:21
  24.4 4.2 %collective-permute-done.other = bf16[64,1152]{1,0:T(8,128)(2,1)S(1)} collective-permute-done((bf16[64,1152]{1,0:T(8,128)(2,1)S(1)}, bf16[64,1152]{1,0:T(8,128)(2,1)S(1)}, u32[]{:S(2)}, u32[]{:S(2)}) %collective-permute-start) | collective-permute-done | bytes 147488 | tf_op jit(solution)/shard_map/ppermute | solution.py:21
  28.7 3.2 %collective-permute-start.1 = (bf16[2,64,384]{2,1,0:T(8,128)(2,1)S(1)}, bf16[2,64,384]{2,1,0:T(8,128)(2,1)S(1)}, u32[]{:S(2)}, u32[]{:S(2)}) collective-permute-start(bf16[2,64,384]{2,1,0:T(8,128)(2,1)S(1)} %shard_map.133.refs_0_), channel_id=1, source_target_pairs={{0,4},{1,5},{2,6},{3,7},{4,0},{5,1},{6,2},{7,3},{8,12},{9,13},{10,... | collective-permute-start | bytes 294920 | tf_op jit(solution)/shard_map/ppermute | solution.py:21
  31.9 2.5 %collective-permute-done.1.refs_1_ = bf16[2,64,384]{2,1,0:T(8,128)(2,1)S(1)} collective-permute-done((bf16[2,64,384]{2,1,0:T(8,128)(2,1)S(1)}, bf16[2,64,384]{2,1,0:T(8,128)(2,1)S(1)}, u32[]{:S(2)}, u32[]{:S(2)}) %collective-permute-start.1) | collective-permute-done | bytes 98336 | tf_op jit(solution)/shard_map/ppermute | solution.py:21
  34.5 4.8 %collective-permute-start.2 = (bf16[2,2,64,384]{3,2,1,0:T(8,128)(2,1)S(1)}, bf16[2,2,64,384]{3,2,1,0:T(8,128)(2,1)S(1)}, u32[]{:S(2)}, u32[]{:S(2)}) collective-permute-start(bf16[2,2,64,384]{3,2,1,0:T(8,128)(2,1)S(1)} %shard_map.134.refs_0_), channel_id=1, source_target_pairs={{0,8},{1,9},{2,10},{3,11},{4,12},{5,13},{6,14},{7,15},{8,0},{9,1},... | collective-permute-start | bytes 589832 | tf_op jit(solution)/shard_map/ppermute | solution.py:21
  39.3 3.5 %collective-permute-done.2.refs_1_ = bf16[2,2,64,384]{3,2,1,0:T(8,128)(2,1)S(1)} collective-permute-done((bf16[2,2,64,384]{3,2,1,0:T(8,128)(2,1)S(1)}, bf16[2,2,64,384]{3,2,1,0:T(8,128)(2,1)S(1)}, u32[]{:S(2)}, u32[]{:S(2)}) %collective-permute-start.2) | collective-permute-done | bytes 196640 | tf_op jit(solution)/shard_map/ppermute | solution.py:21
  42.9 4.3 %collective-permute-start.3 = (bf16[4,2,64,384]{3,2,1,0:T(8,128)(2,1)S(1)}, bf16[4,2,64,384]{3,2,1,0:T(8,128)(2,1)S(1)}, u32[]{:S(2)}, u32[]{:S(2)}) collective-permute-start(bf16[4,2,64,384]{3,2,1,0:T(8,128)(2,1)S(1)} %bitcast.17), channel_id=1, source_target_pairs={{0,1},{1,0},{2,3},{3,2},{4,5},{5,4},{6,7},{7,6},{8,9},{9,8},{10,11... | collective-permute-start | bytes 1179656 | tf_op jit(solution)/shard_map/ppermute | solution.py:21
  47.8 0.9 shard_map.132
  49.2 4.7 %collective-permute-start.4 = (bf16[16,2,32,256]{3,2,1,0:T(8,128)(2,1)}, bf16[16,2,32,256]{3,2,1,0:T(8,128)(2,1)}, u32[]{:S(2)}, u32[]{:S(2)}) collective-permute-start(bf16[16,2,32,256]{3,2,1,0:T(8,128)(2,1)} %all-to-all-done.own), channel_id=1, source_target_pairs={{0,16},{16,0},{32,48},{48,32},{64,80},{80,64},{96,112},{112,96},{1... | collective-permute-start | bytes 1572872 | tf_op jit(solution)/shard_map/ppermute | solution.py:21
  53.9 4.2 %all-to-all-start.1 = ((bf16[4,2,64,768]{3,2,1,0:T(8,128)(2,1)}), bf16[4,2,64,768]{3,2,1,0:T(8,128)(2,1)S(1)}, u32[]{:S(2)}, u32[]{:S(2)}) async-start(bf16[4,2,64,768]{3,2,1,0:T(8,128)(2,1)} %shard_map.132), calls=%async_computation.1 | async-start | bytes 1572864 | tf_op jit(solution)/shard_map/all_to_all | solution.py:16
  58.1 2.7 %collective-permute-start.5 = (bf16[16,2,32,256]{3,2,1,0:T(8,128)(2,1)}, bf16[16,2,32,256]{3,2,1,0:T(8,128)(2,1)S(1)}, u32[]{:S(2)}, u32[]{:S(2)}) collective-permute-start(bf16[16,2,32,256]{3,2,1,0:T(8,128)(2,1)} %all-to-all-done.own), channel_id=1, source_target_pairs={{0,1},{1,0},{2,3},{3,2},{4,5},{5,4},{6,7},{7,6},{8,9},{9,8},{10,11... | collective-permute-start | bytes 1572872 | tf_op jit(solution)/shard_map/ppermute | solution.py:21
  60.7 5.6 %collective-permute-done.4.other = bf16[16,2,32,256]{3,2,1,0:T(8,128)(2,1)} collective-permute-done((bf16[16,2,32,256]{3,2,1,0:T(8,128)(2,1)}, bf16[16,2,32,256]{3,2,1,0:T(8,128)(2,1)}, u32[]{:S(2)}, u32[]{:S(2)}) %collective-permute-start.4) | collective-permute-done | bytes 524320 | tf_op jit(solution)/shard_map/ppermute | solution.py:21
  66.4 2.8 %collective-permute-start.6 = (bf16[16,2,32,256]{3,2,1,0:T(8,128)(2,1)}, bf16[16,2,32,256]{3,2,1,0:T(8,128)(2,1)S(1)}, u32[]{:S(2)}, u32[]{:S(2)}) collective-permute-start(bf16[16,2,32,256]{3,2,1,0:T(8,128)(2,1)} %collective-permute-done.4.other), channel_id=1, source_target_pairs={{0,1},{1,0},{2,3},{3,2},{4,5},{5,4},{6,7},{7,6},{8,9},{9,8},{10,11... | collective-permute-start | bytes 1572872 | tf_op jit(solution)/shard_map/ppermute | solution.py:21
  69.2 2.0 %shard_map.137 = (f32[128,256]{1,0:T(8,128)}, f32[128,1024]{1,0:T(8,128)S(1)}) custom-call(bf16[16,2,32,256]{3,2,1,0:T(8,128)(2,1)} %all-to-all-done.own, bf16[16,2,32,256]{3,2,1,0:T(8,128)(2,1)} %collective-permute-done.4.other, bf16[128,1024]{1,0:T(8,128)(2,1)S(1)} %get-tuple-element.35.normed, f32[1,256]{1,0:T(1,128)S(1)} %bitcast.29), custom_call_target="tpu_custom_call" | custom-call | tf_op jit(solution)/shard_map/pallas_call | solution.py:43
  71.2 1.3 shard_map.138
  72.5 1.9 %collective-permute-start.8 = (bf16[4,2,64,768]{3,2,1,0:T(8,128)(2,1)S(1)}, bf16[4,2,64,768]{3,2,1,0:T(8,128)(2,1)S(1)}, u32[]{:S(2)}, u32[]{:S(2)}) collective-permute-start(bf16[4,2,64,768]{3,2,1,0:T(8,128)(2,1)S(1)} %all-to-all-done.1.near), channel_id=1, source_target_pairs={{0,1},{1,0},{2,3},{3,2},{4,5},{5,4},{6,7},{7,6},{8,9},{9,8},{10,11... | collective-permute-start | bytes 2359304 | tf_op jit(solution)/shard_map/ppermute | solution.py:21
  74.5 5.1 %all-to-all-start.2 = ((bf16[8,16,1024]{2,1,0:T(8,128)(2,1)}), bf16[8,16,1024]{2,1,0:T(8,128)(2,1)S(1)}, u32[]{:S(2)}, u32[]{:S(2)}) async-start(bf16[8,16,1024]{2,1,0:T(8,128)(2,1)} %bitcast.10), calls=%async_computation.2 | async-start | bytes 524288 | tf_op jit(solution)/shard_map/all_to_all | solution.py:16
  79.8 4.7 %shard_map.139 = (bf16[2560,768]{1,0:T(8,128)(2,1)}, bf16[128,768]{1,0:T(8,128)(2,1)S(1)}) custom-call(bf16[1280,768]{1,0:T(8,128)(2,1)} %near.1, bf16[1280,768]{1,0:T(8,128)(2,1)} %collective-permute-done.7.far, s32[256,1]{1,0:T(8,128)S(1)} %copy.14.labels), custom_call_target="tpu_custom_call" | custom-call | flops 2147483648 | bytes 12582912 | tf_op jit(solution)/shard_map/pallas_call | solution.py:43
  84.5 1.7 %all-to-all-done.2.mixed = bf16[8,16,1024]{2,1,0:T(8,128)(2,1)S(1)} async-done(((bf16[8,16,1024]{2,1,0:T(8,128)(2,1)}), bf16[8,16,1024]{2,1,0:T(8,128)(2,1)S(1)}, u32[]{:S(2)}, u32[]{:S(2)}) %all-to-all-start.2) | async-done | bytes 262176 | tf_op jit(solution)/shard_map/all_to_all | solution.py:16
  86.9 10.7 %all_to_all.40.arrived = bf16[8,16,1536]{2,1,0:T(8,128)(2,1)S(1)} all-to-all(bf16[8,16,1536]{2,1,0:T(8,128)(2,1)S(1)} %get-tuple-element.47), channel_id=1, replica_groups={{0,2,4,6,8,10,12,14},{1,3,5,7,9,11,13,15},{16,18,20,22,24,26,28,30},{17..., dimensions={0} | all-to-all | bytes 786432 | tf_op jit(solution)/shard_map/all_to_all | solution.py:16
  97.6 4.7 %shard_map.141 = (bf16[128,896]{1,0:T(8,128)(2,1)S(1)}, f32[16,768]{1,0:T(8,128)S(1)}) custom-call(bf16[8,16,1536]{2,1,0:T(8,128)(2,1)S(1)} %all_to_all.40.arrived, bf16[2560,768]{1,0:T(8,128)(2,1)} %get-tuple-element.48.text_unit, s32[256,1]{1,0:T(8,128)S(1)} %copy.14.labels), custom_call_target="tpu_custom_call" | custom-call | tf_op jit(solution)/shard_map/pallas_call | solution.py:43
  102.3 8.5 %all_to_all.41.back = bf16[8,16,896]{2,1,0:T(8,128)(2,1)S(1)} all-to-all(bf16[8,16,896]{2,1,0:T(8,128)(2,1)S(1)} %bitcast.21), channel_id=1, replica_groups={{0,2,4,6,8,10,12,14},{1,3,5,7,9,11,13,15},{16,18,20,22,24,26,28,30},{17..., dimensions={0} | all-to-all | bytes 458752 | tf_op jit(solution)/shard_map/all_to_all | solution.py:16
  110.8 1.0 shard_map.142
  111.8 8.5 %all_to_all.42 = bf16[8,16,1024]{2,1,0:T(8,128)(2,1)S(1)} all-to-all(bf16[8,16,1024]{2,1,0:T(8,128)(2,1)S(1)} %get-tuple-element.55), channel_id=1, replica_groups={{0,2,4,6,8,10,12,14},{1,3,5,7,9,11,13,15},{16,18,20,22,24,26,28,30},{17..., dimensions={0} | all-to-all | bytes 524288 | tf_op jit(solution)/shard_map/all_to_all | solution.py:16
  120.4 1.9 %shard_map.143 = bf16[128,1024]{1,0:T(8,128)(2,1)S(1)} custom-call(bf16[16,2,32,256]{3,2,1,0:T(8,128)(2,1)} %all-to-all-done.own, bf16[16,2,32,256]{3,2,1,0:T(8,128)(2,1)} %collective-permute-done.4.other, bf16[16,2,32,256]{3,2,1,0:T(8,128)(2,1)S(1)} %collective-permute-done.5.own.far_own, ...), custom_call_target="tpu_custom_call" | custom-call | tf_op jit(solution)/shard_map/pallas_call | solution.py:43
  122.3 8.5 %all_to_all.43.parts = bf16[8,16,1024]{2,1,0:T(8,128)(2,1)S(1)} all-to-all(bf16[8,16,1024]{2,1,0:T(8,128)(2,1)S(1)} %bitcast.20), channel_id=1, replica_groups={{0,2,4,6,8,10,12,14},{1,3,5,7,9,11,13,15},{16,18,20,22,24,26,28,30},{17..., dimensions={0} | all-to-all | bytes 524288 | tf_op jit(solution)/shard_map/all_to_all | solution.py:16
  131.2 14.4 %all_to_all.44.parts = f32[16,8,128]{2,1,0:T(8,128)S(1)} all-to-all(f32[16,8,128]{2,1,0:T(8,128)S(1)} %shard_map.144), channel_id=1, replica_groups=mesh['dp'=32,'txt'=16] {'txt'}, dimensions={0} | all-to-all | bytes 131072 | tf_op jit(solution)/shard_map/all_to_all | solution.py:16
  145.6 0.8 shard_map.145
  (29 shorter events, 1.7 us)
Async XLA Ops:
  1.6 47.1 %copy-start.2 = (f32[1024]{0:T(1024)S(1)}, f32[1024]{0:T(1024)}, u32[]{:S(2)}) copy-start(f32[1024]{0:T(1024)} %param.14) | copy-start | bytes 12292
  1.6 47.1 %copy-start.3 = (f32[1024]{0:T(1024)S(1)}, f32[1024]{0:T(1024)}, u32[]{:S(2)}) copy-start(f32[1024]{0:T(1024)} %param.15) | copy-start | bytes 12292
  1.6 47.6 %all-to-all-start = ((bf16[16,2,32,256]{3,2,1,0:T(8,128)(2,1)}), bf16[16,2,32,256]{3,2,1,0:T(8,128)(2,1)}, u32[]{:S(2)}, u32[]{:S(2)}) async-start(bf16[16,2,32,256]{3,2,1,0:T(8,128)(2,1)} %shard_map.130), calls=%async_computation | async-start | bytes 1048576 | tf_op jit(solution)/shard_map/all_to_all | solution.py:16
  18.4 54.1 %collective-permute-start.7 = (bf16[1280,768]{1,0:T(8,128)(2,1)}, bf16[1280,768]{1,0:T(8,128)(2,1)}, u32[]{:S(2)}, u32[]{:S(2)}) collective-permute-start(bf16[1280,768]{1,0:T(8,128)(2,1)} %near.1), channel_id=1, source_target_pairs={{0,1},{1,0},{2,3},{3,2},{4,5},{5,4},{6,7},{7,6},{8,9},{9,8},{10,11... | collective-permute-start | bytes 5898248 | tf_op jit(solution)/shard_map/ppermute | solution.py:21
  21.3 7.4 %collective-permute-start = (bf16[64,1152]{1,0:T(8,128)(2,1)S(1)}, bf16[64,1152]{1,0:T(8,128)(2,1)S(1)}, u32[]{:S(2)}, u32[]{:S(2)}) collective-permute-start(bf16[64,1152]{1,0:T(8,128)(2,1)S(1)} %shard_map.131.near), channel_id=1, source_target_pairs={{0,2},{1,3},{2,0},{3,1},{4,6},{5,7},{6,4},{7,5},{8,10},{9,11},{10,... | collective-permute-start | bytes 442376 | tf_op jit(solution)/shard_map/ppermute | solution.py:21
  28.7 5.8 %collective-permute-start.1 = (bf16[2,64,384]{2,1,0:T(8,128)(2,1)S(1)}, bf16[2,64,384]{2,1,0:T(8,128)(2,1)S(1)}, u32[]{:S(2)}, u32[]{:S(2)}) collective-permute-start(bf16[2,64,384]{2,1,0:T(8,128)(2,1)S(1)} %shard_map.133.refs_0_), channel_id=1, source_target_pairs={{0,4},{1,5},{2,6},{3,7},{4,0},{5,1},{6,2},{7,3},{8,12},{9,13},{10,... | collective-permute-start | bytes 294920 | tf_op jit(solution)/shard_map/ppermute | solution.py:21
  34.5 34.7 %copy-start.5 = (f32[256]{0:T(256)S(1)}, f32[256]{0:T(256)}, u32[]{:S(2)}) copy-start(f32[256]{0:T(256)} %param.17) | copy-start | bytes 3076
  34.5 8.4 %collective-permute-start.2 = (bf16[2,2,64,384]{3,2,1,0:T(8,128)(2,1)S(1)}, bf16[2,2,64,384]{3,2,1,0:T(8,128)(2,1)S(1)}, u32[]{:S(2)}, u32[]{:S(2)}) collective-permute-start(bf16[2,2,64,384]{3,2,1,0:T(8,128)(2,1)S(1)} %shard_map.134.refs_0_), channel_id=1, source_target_pairs={{0,8},{1,9},{2,10},{3,11},{4,12},{5,13},{6,14},{7,15},{8,0},{9,1},... | collective-permute-start | bytes 589832 | tf_op jit(solution)/shard_map/ppermute | solution.py:21
  42.9 5.9 %collective-permute-start.3 = (bf16[4,2,64,384]{3,2,1,0:T(8,128)(2,1)S(1)}, bf16[4,2,64,384]{3,2,1,0:T(8,128)(2,1)S(1)}, u32[]{:S(2)}, u32[]{:S(2)}) collective-permute-start(bf16[4,2,64,384]{3,2,1,0:T(8,128)(2,1)S(1)} %bitcast.17), channel_id=1, source_target_pairs={{0,1},{1,0},{2,3},{3,2},{4,5},{5,4},{6,7},{7,6},{8,9},{9,8},{10,11... | collective-permute-start | bytes 1179656 | tf_op jit(solution)/shard_map/ppermute | solution.py:21
  49.2 17.2 %collective-permute-start.4 = (bf16[16,2,32,256]{3,2,1,0:T(8,128)(2,1)}, bf16[16,2,32,256]{3,2,1,0:T(8,128)(2,1)}, u32[]{:S(2)}, u32[]{:S(2)}) collective-permute-start(bf16[16,2,32,256]{3,2,1,0:T(8,128)(2,1)} %all-to-all-done.own), channel_id=1, source_target_pairs={{0,16},{16,0},{32,48},{48,32},{64,80},{80,64},{96,112},{112,96},{1... | collective-permute-start | bytes 1572872 | tf_op jit(solution)/shard_map/ppermute | solution.py:21
  53.9 18.7 %all-to-all-start.1 = ((bf16[4,2,64,768]{3,2,1,0:T(8,128)(2,1)}), bf16[4,2,64,768]{3,2,1,0:T(8,128)(2,1)S(1)}, u32[]{:S(2)}, u32[]{:S(2)}) async-start(bf16[4,2,64,768]{3,2,1,0:T(8,128)(2,1)} %shard_map.132), calls=%async_computation.1 | async-start | bytes 1572864 | tf_op jit(solution)/shard_map/all_to_all | solution.py:16
  58.1 21.6 %copy-start.6 = (s32[256]{0:T(256)S(1)}, s32[256]{0:T(256)}, u32[]{:S(2)}) copy-start(s32[256]{0:T(256)} %param.24) | copy-start | bytes 3076
  58.1 13.1 %collective-permute-start.5 = (bf16[16,2,32,256]{3,2,1,0:T(8,128)(2,1)}, bf16[16,2,32,256]{3,2,1,0:T(8,128)(2,1)S(1)}, u32[]{:S(2)}, u32[]{:S(2)}) collective-permute-start(bf16[16,2,32,256]{3,2,1,0:T(8,128)(2,1)} %all-to-all-done.own), channel_id=1, source_target_pairs={{0,1},{1,0},{2,3},{3,2},{4,5},{5,4},{6,7},{7,6},{8,9},{9,8},{10,11... | collective-permute-start | bytes 1572872 | tf_op jit(solution)/shard_map/ppermute | solution.py:21
  66.4 4.8 %collective-permute-start.6 = (bf16[16,2,32,256]{3,2,1,0:T(8,128)(2,1)}, bf16[16,2,32,256]{3,2,1,0:T(8,128)(2,1)S(1)}, u32[]{:S(2)}, u32[]{:S(2)}) collective-permute-start(bf16[16,2,32,256]{3,2,1,0:T(8,128)(2,1)} %collective-permute-done.4.other), channel_id=1, source_target_pairs={{0,1},{1,0},{2,3},{3,2},{4,5},{5,4},{6,7},{7,6},{8,9},{9,8},{10,11... | collective-permute-start | bytes 1572872 | tf_op jit(solution)/shard_map/ppermute | solution.py:21
  72.5 13.7 %collective-permute-start.8 = (bf16[4,2,64,768]{3,2,1,0:T(8,128)(2,1)S(1)}, bf16[4,2,64,768]{3,2,1,0:T(8,128)(2,1)S(1)}, u32[]{:S(2)}, u32[]{:S(2)}) collective-permute-start(bf16[4,2,64,768]{3,2,1,0:T(8,128)(2,1)S(1)} %all-to-all-done.1.near), channel_id=1, source_target_pairs={{0,1},{1,0},{2,3},{3,2},{4,5},{5,4},{6,7},{7,6},{8,9},{9,8},{10,11... | collective-permute-start | bytes 2359304 | tf_op jit(solution)/shard_map/ppermute | solution.py:21
  74.5 11.7 %all-to-all-start.2 = ((bf16[8,16,1024]{2,1,0:T(8,128)(2,1)}), bf16[8,16,1024]{2,1,0:T(8,128)(2,1)S(1)}, u32[]{:S(2)}, u32[]{:S(2)}) async-start(bf16[8,16,1024]{2,1,0:T(8,128)(2,1)} %bitcast.10), calls=%async_computation.2 | async-start | bytes 524288 | tf_op jit(solution)/shard_map/all_to_all | solution.py:16
  79.8 6.5 %copy-start.4 = (f32[1024]{0:T(1024)S(1)}, f32[1024]{0:T(1024)}, u32[]{:S(2)}) copy-start(f32[1024]{0:T(1024)} %param.19) | copy-start | bytes 12292
  102.3 18.0 %copy-start = (f32[128,256]{1,0:T(8,128)S(1)}, f32[128,256]{1,0:T(8,128)}, u32[]{:S(2)}) copy-start(f32[128,256]{1,0:T(8,128)} %get-tuple-element.56.pre_act) | copy-start | bytes 393220
  120.3 25.3 %copy-start.1 = (bf16[256,64]{0,1:T(8,128)(2,1)S(1)}, bf16[256,64]{0,1:T(8,128)(2,1)}, u32[]{:S(2)}) copy-start(bf16[256,64]{0,1:T(8,128)(2,1)} %param.13) | copy-start | bytes 98308
